TPU v7x, 32 devices: a whole 2x2x4 slice. The times are simulated.
32 devices in a mesh: lat: 8 (over y, x, core), lon: 4 (over z).
Axes of the slice: x: 2, y: 2, z: 4, core: 2. Of those that a mesh axis runs over, the one named last changes fastest.
Arguments:
- ocean_state: bfloat16 [1, 96, 640, 768], P(None, 'lat', None, 'lon'), may hold values from -6 to 6
- zonal_kernel: bfloat16 [2, 5, 256, 640], replicated, may hold values from -0.15625 to 0.15625
- norm_gain: bfloat16 [2, 640], replicated, may hold values from 0.099609375 to 1.8984375
- input_weight: bfloat16 [2, 640, 1280], replicated, may hold values from -0.25 to 0.25
- output_weight: bfloat16 [2, 1280, 640], replicated, may hold values from -0.15625 to 0.15625
Outputs:
- state_out: bfloat16 [1, 96, 640, 768], P(None, 'lat', None, 'lon')
All inputs are finite; a program needn't handle non-finite values.
Results may differ from a plain program's by a relative error of at most 0.009.
Values may be sent and summed in bfloat16 or wider, within the bound.
No kernel may reach another device: no remote copies, remote signals or barrier semaphores. Data moves between devices by JAX's collectives and lax.ppermute only.
A program may use at most 128 MiB of HBM per device.

v0:
```python
import jax
import jax.numpy as jnp
from jax import lax
from jax.sharding import PartitionSpec as P

W = 768
TAPS = 256
KROWS = 5
BLOCKS = 2


def extended(block, sides, width):
    for axis, dim in sides:
        count = lax.axis_size(axis)
        forward = [(i, i + 1) for i in range(count - 1)]
        backward = [(target, source) for source, target in forward]
        low = lax.ppermute(
            lax.slice_in_dim(block, block.shape[dim] - width, None, axis=dim), axis, forward
        )
        high = lax.ppermute(lax.slice_in_dim(block, 0, width, axis=dim), axis, backward)
        block = jnp.concatenate([low, block, high], axis=dim)
    return block


def real_basis(length, offsets):
    half_width = length // 2
    column = jnp.arange(length, dtype=jnp.int32)[None, :]
    frequency = column % half_width
    phases = offsets[:, None] * frequency % length
    angles = 2.0 * jnp.pi / length * phases.astype(jnp.float32)
    parity = (1 - 2 * (offsets % 2)).astype(jnp.float32)[:, None]
    sine_part = jnp.where(frequency == 0, parity, jnp.sin(angles))
    return jnp.where(column < half_width, jnp.cos(angles), sine_part)


def latitude_weights(row_start, row_count, total_rows):
    row_index = row_start + jnp.arange(row_count, dtype=jnp.int32)
    return jnp.sin(jnp.pi * (row_index.astype(jnp.float32) + 0.5) / total_rows)


def transform(rows_in, row_start, total_rows, forward):
    weights = latitude_weights(row_start, rows_in.shape[1], total_rows)
    weighted = rows_in.astype(jnp.float32) * weights[None, :, None, None]
    flat = weighted.reshape(-1, weighted.shape[3])
    return jnp.dot(flat, forward, precision=lax.Precision.HIGH).reshape(weighted.shape)


def untransform(spectra, inverse):
    flat = spectra.reshape(-1, spectra.shape[3])
    return jnp.dot(flat, inverse, precision=lax.Precision.HIGH).reshape(spectra.shape)


def kernel_factors(kernel_layer, first_channel, share_count, tap_basis):
    kernel_piece = lax.dynamic_slice_in_dim(kernel_layer, first_channel, share_count, 2).astype(
        jnp.float32
    )
    spectra = jnp.einsum("rtc,tk->rck", kernel_piece, tap_basis, precision=lax.Precision.HIGH)
    half_width = spectra.shape[2] // 2
    real_part = spectra[..., :half_width]
    sine_part = spectra[..., half_width:]
    keeper = (jnp.arange(half_width) >= 1).astype(jnp.float32)
    return (real_part, keeper * sine_part, keeper * real_part + (1.0 - keeper) * sine_part)


def apply_factor(spectra, factors, offset):
    real_factor, cross_factor, sine_factor = factors
    half_width = spectra.shape[3] // 2
    real_part = spectra[..., :half_width]
    sine_part = spectra[..., half_width:]
    new_real = real_part * real_factor[offset] - sine_part * cross_factor[offset]
    new_sine = real_part * cross_factor[offset] + sine_part * sine_factor[offset]
    return jnp.concatenate([new_real, new_sine], axis=3)


def rows_from_padded(padded, factors, row_count):
    summed = apply_factor(padded[:, 0:row_count], factors, 0)
    for offset in range(1, KROWS):
        summed = summed + apply_factor(padded[:, offset : offset + row_count], factors, offset)
    return summed


def feed_forward(mixed_grid, gain_layer, input_layer, output_layer):
    values = mixed_grid.astype(jnp.float32)
    average = jnp.mean(values, axis=2, keepdims=True)
    variance = jnp.mean(jnp.square(values - average), axis=2, keepdims=True)
    scaled = (
        (values - average)
        * lax.rsqrt(variance + 1e-05)
        * gain_layer.astype(jnp.float32)[None, None, :, None]
    )
    normed = scaled.astype(jnp.bfloat16)
    hidden = jnp.einsum("brcw,cf->brwf", normed, input_layer, preferred_element_type=jnp.float32)
    hidden = jax.nn.gelu(hidden, approximate=False).astype(jnp.bfloat16)
    projected = jnp.einsum(
        "brwf,fc->brcw", hidden, output_layer, preferred_element_type=jnp.float32
    )
    return (values + projected).astype(jnp.bfloat16)


def body(ocean_state, zonal_kernel, norm_gain, input_weight, output_weight):
    rim_rows = KROWS // 2
    lat_rows = ocean_state.shape[1]
    total_rows = lat_rows * lax.axis_size("lat")
    forward = real_basis(W, jnp.arange(W, dtype=jnp.int32))
    column_scale = jnp.where(jnp.arange(W) % (W // 2) == 0, 1.0, 2.0).astype(jnp.float32)
    inverse = column_scale[:, None] * forward.T / W
    tap_basis = real_basis(W, jnp.arange(TAPS, dtype=jnp.int32) - TAPS // 2)
    current = ocean_state
    for layer_index in range(BLOCKS):
        swapped = lax.all_to_all(current, "lon", split_axis=2, concat_axis=3, tiled=True)
        share_count = swapped.shape[2]
        first_channel = lax.axis_index("lon") * share_count
        first_row = lax.axis_index("lat") * lat_rows
        factors = kernel_factors(zonal_kernel[layer_index], first_channel, share_count, tap_basis)
        rimmed = extended(swapped, (("lat", 1),), rim_rows)
        signal = transform(rimmed, first_row - rim_rows, total_rows, forward)
        convolved = untransform(rows_from_padded(signal, factors, lat_rows), inverse)
        mixed_out = (
            swapped.astype(jnp.float32) + jax.nn.gelu(convolved, approximate=False)
        ).astype(jnp.bfloat16)
        mixed_grid = lax.all_to_all(mixed_out, "lon", split_axis=3, concat_axis=2, tiled=True)
        current = feed_forward(
            mixed_grid,
            norm_gain[layer_index],
            input_weight[layer_index],
            output_weight[layer_index],
        )
    return current


def solution(mesh):
    in_specs = (P(None, "lat", None, "lon"), P(), P(), P(), P())
    out_specs = P(None, "lat", None, "lon")
    return jax.shard_map(body, mesh=mesh, in_specs=in_specs, out_specs=out_specs, check_vma=False)
```

profile of v0, /device:TPU:2, one launch (start us, length us, event | category | flops | bytes accessed | tf_op | source)
XLA Modules:
  0.0 845.0 jit_solution(962291879979350326)
XLA Ops:
  0.0 8.2 copy.64
  8.2 5.3 all-to-all-start
  14.0 4.5 fusion.160
  19.4 4.5 fusion.158
  23.9 2.2 slice_multiply_fusion.3
  28.2 101.2 %all-to-all-done = bf16[1,12,640,192]{3,1,0,2:T(8,128)(2,1)} async-done(((bf16[1,12,640,192]{3,1,0,2:T(8,128)(2,1)}), bf16[1,12,640,192]{3,1,0,2:T(8,128)(2,1)}, u32[]{:S(2)}, u32[]{:S(2)}) %all-to-all-start) | async-done | bytes 2949152 | tf_op jit(solution)/shard_map/all_to_all | solution.py:110
  129.5 3.9 copy.65
  133.4 5.3 copy.66
  138.6 6.6 all_to_all.43
  148.4 3.6 collective-permute-start.1
  152.7 11.7 %multiply_multiply_fusion.22.clone.2 = f32[768,768]{1,0:T(8,128)} fusion(f32[768]{0:T(1024)S(1)} %get-tuple-element.88, s32[768]{0:T(1024)S(1)} %get-tuple-element.87, f32[768]{0:T(1024)S(1)} %broadcast_select_fusion, pred[768]{0:T(1024)(128)(4,1)S(1)} %get-tuple-element.90, pred[768]{0:T(1024)(128)(4,1)S(1)} %get-tuple-element.89), kind=kLoop, calls=%fused_computation.187.clone.1.clone.clone.clone | loop fusion | flops 7667712 | bytes 2370048 | tf_op jit(solution)/shard_map/mul | solution.py:119
  164.4 7.8 concatenate.129
  172.3 22.0 %fusion.104 = f32[1,16,160,768]{3,2,1,0:T(8,128)S(1)} fusion(bf16[2,160,768]{2,1,0:T(8,128)(2,1)} %bitcast.4, bf16[12,160,768]{2,1,0:T(8,128)(2,1)} %concatenate.129, bf16[2,160,768]{2,1,0:T(8,128)(2,1)} %bitcast.2, f32[16]{0:T(128)S(1)} %multiply_sine_fusion, f32[768]{0:T(1024)S(1)} %get-tuple-element.88, s32[768]{0:T(1024)S(1)} %get-tuple-element.87, ...), kind=kOutput, calls=%fused_computation.153 | convolution fusion | flops 9074049024 | bytes 11804224 | tf_op jit(solution)/shard_map/dot_general | solution.py:45
  194.4 3.4 multiply_subtract_fusion.9
  197.9 5.0 multiply_subtract_fusion.5
  202.9 5.0 multiply_subtract_fusion.7
  207.9 14.2 %negate_multiply_fusion.3 = (f32[1920,768]{1,0:T(8,128)S(1)}, f32[1920,768]{1,0:T(8,128)S(1)}) fusion(f32[1920,384]{1,0:T(8,128)} %bitcast.207, f32[1920,384]{1,0:T(8,128)} %bitcast.206, f32[1920,384]{1,0:T(8,128)} %bitcast.200, f32[1920,384]{1,0:T(8,128)} %bitcast.201, f32[1920,384]{1,0:T(8,128)} %bitcast.199, f32[1920,384]{1,0:T(8,128)} %bitcast.198, ...), kind=kOutput, calls=%fused_computation.132 | convolution fusion | flops 6812467200 | bytes 43646976 | tf_op jit(solution)/shard_map/dot_general | solution.py:50
  222.2 14.5 %fusion.27 = bf16[1,12,160,768]{3,2,1,0:T(8,128)(2,1)} fusion(f32[1,12,160,768]{3,2,1,0:T(8,128)S(1)} %bitcast.185, f32[1,12,160,768]{3,2,1,0:T(8,128)S(1)} %bitcast.184, bf16[1,12,160,768]{3,2,1,0:T(8,128)(2,1)} %copy-done.3), kind=kLoop, calls=%fused_computation.58 | loop fusion | flops 94371840 | bytes 17694720 | tf_op jit(solution)/shard_map/convert_element_type | solution.py:120
  236.7 10.2 %copy.69 = bf16[1,12,160,768]{2,1,0,3:T(8,128)(2,1)} copy(bf16[1,12,160,768]{3,2,1,0:T(8,128)(2,1)} %fusion.27) | data formatting | bytes 5898240 | tf_op jit(solution)/shard_map/convert_element_type | solution.py:120
  246.9 10.0 %reshape.1252 = bf16[4,2,184320]{2,1,0:T(2,128)(2,1)} reshape(bf16[768,1,12,160]{3,2,1,0:T(8,128)(2,1)} %bitcast.180) | data formatting | bytes 5898240
  257.0 4.1 all-to-all-start.1
  261.9 65.9 %all-to-all-done.1 = bf16[4,2,184320]{2,1,0:T(2,128)(2,1)S(1)} async-done(((bf16[4,2,184320]{2,1,0:T(2,128)(2,1)}), bf16[4,2,184320]{2,1,0:T(2,128)(2,1)S(1)}, u32[]{:S(2)}, u32[]{:S(2)}) %all-to-all-start.1) | async-done | bytes 2949152 | tf_op jit(solution)/shard_map/all_to_all | solution.py:121
  327.8 9.5 %reshape.1253 = bf16[768,1,12,160]{3,2,1,0:T(8,128)(2,1)} reshape(bf16[4,2,184320]{2,1,0:T(2,128)(2,1)S(1)} %all-to-all-done.1) | data formatting | bytes 5898240
  337.3 7.2 copy.70
  344.5 7.3 reshape.1242
  351.8 4.3 bitcast_reduce_fusion.1
  357.2 2.3 multiply_reduce_fusion.1
  359.6 2.5 multiply_convert_fusion.1
  362.1 2.7 copy.73
  364.7 4.5 copy.71
  369.2 8.7 %copy.75 = f32[1,12,640,192]{2,3,1,0:T(8,128)} copy(f32[1,12,640,192]{3,2,1,0:T(8,128)} %bitcast.178) | data formatting | bytes 11796480 | tf_op jit(solution)/shard_map/convert_element_type | solution.py:83
  378.0 10.2 %fusion.86 = (u16[192,1280]{1,0:T(8,128)(2,1)S(1)}, u16[192,1280]{1,0:T(8,128)(2,1)S(1)}, f32[12,192,1280]{2,1,0:T(8,128)S(1)}) fusion(bf16[12,640,192]{2,1,0:T(8,128)(2,1)} %bitcast.210, bf16[2,640,1280]{2,1,0:T(8,128)(2,1)S(1)} %copy-done.46), kind=kOutput, calls=%fused_computation.133 | convolution fusion | flops 3812720640 | bytes 17367040 | tf_op jit(solution)/shard_map/brcw,cf->brwf/dot_general | solution.py:92
  388.2 30.0 %fusion.73 = bf16[1,12,640,192]{2,3,1,0:T(8,128)(2,1)S(1)} fusion(f32[1,12,640,192]{2,3,1,0:T(8,128)S(1)} %copy-done.4, f32[12,192,1280]{2,1,0:T(8,128)S(1)} %get-tuple-element.85, u16[192,1280]{1,0:T(8,128)(2,1)S(1)} %get-tuple-element.8, u16[192,1280]{1,0:T(8,128)(2,1)S(1)} %get-tuple-element.7, bf16[2,1280,640]{2,1,0:T(8,128)(2,1)S(1)} %copy-done.48), kind=kOutput, calls=%fused_computation.106 | convolution fusion | flops 3984261120 | bytes 23265280 | tf_op jit(solution)/shard_map/brwf,fc->brcw/dot_general | solution.py:94
  418.3 11.5 %copy.76 = bf16[1,12,640,192]{3,1,0,2:T(8,128)(2,1)} copy(bf16[1,12,640,192]{2,3,1,0:T(8,128)(2,1)S(1)} %fusion.73) | data formatting | bytes 5898240 | tf_op jit(solution)/shard_map/convert_element_type | solution.py:97
  429.8 5.2 all-to-all-start.2
  435.9 2.5 slice_bitcast_fusion.1
  438.3 111.9 %all-to-all-done.2 = bf16[1,12,640,192]{3,1,0,2:T(8,128)(2,1)} async-done(((bf16[1,12,640,192]{3,1,0,2:T(8,128)(2,1)}), bf16[1,12,640,192]{3,1,0,2:T(8,128)(2,1)}, u32[]{:S(2)}, u32[]{:S(2)}) %all-to-all-start.2) | async-done | bytes 2949152 | tf_op jit(solution)/shard_map/all_to_all | solution.py:110
  550.2 3.9 copy.77
  554.1 4.9 copy.78
  559.0 6.6 all_to_all.48
  568.9 3.6 collective-permute-start.3
  572.5 2.5 slice_bitcast_fusion
  575.0 11.7 %multiply_multiply_fusion.21.clone.5 = f32[768,768]{1,0:T(8,128)} fusion(f32[768]{0:T(1024)S(1)} %copy-done.37, s32[768]{0:T(1024)S(1)} %copy-done.35, f32[768]{0:T(1024)S(1)} %copy-done.39, pred[768]{0:T(1024)(128)(4,1)S(1)} %copy-done.45, pred[768]{0:T(1024)(128)(4,1)S(1)} %copy-done.43), kind=kLoop, calls=%fused_computation.187.clone.clone.clone.clone.2 | loop fusion | flops 7667712 | bytes 2370048 | tf_op jit(solution)/shard_map/mul | solution.py:119
  586.7 8.0 concatenate.148
  594.8 22.1 %fusion.107 = f32[1,16,160,768]{3,2,1,0:T(8,128)S(1)} fusion(bf16[2,160,768]{2,1,0:T(8,128)(2,1)} %bitcast.50, bf16[12,160,768]{2,1,0:T(8,128)(2,1)} %concatenate.148, bf16[2,160,768]{2,1,0:T(8,128)(2,1)} %bitcast.48, f32[16]{0:T(128)S(1)} %copy-done.51, f32[768]{0:T(1024)S(1)} %copy-done.37, s32[768]{0:T(1024)S(1)} %copy-done.35, ...), kind=kOutput, calls=%fused_computation.154 | convolution fusion | flops 9074049024 | bytes 11804224 | tf_op jit(solution)/shard_map/dot_general | solution.py:45
  617.0 3.4 multiply_subtract_fusion.4
  620.4 5.0 multiply_subtract_fusion
  625.5 5.0 multiply_subtract_fusion.2
  630.5 14.4 %negate_multiply_fusion.2 = (f32[1920,768]{1,0:T(8,128)S(1)}, f32[1920,768]{1,0:T(8,128)S(1)}) fusion(f32[1920,384]{1,0:T(8,128)} %bitcast.209, f32[1920,384]{1,0:T(8,128)} %bitcast.208, f32[1920,384]{1,0:T(8,128)} %bitcast.204, f32[1920,384]{1,0:T(8,128)} %bitcast.205, f32[1920,384]{1,0:T(8,128)} %bitcast.203, f32[1920,384]{1,0:T(8,128)} %bitcast.202, ...), kind=kOutput, calls=%fused_computation.119 | convolution fusion | flops 6812467200 | bytes 43646976 | tf_op jit(solution)/shard_map/dot_general | solution.py:50
  644.9 14.5 %fusion.31 = bf16[1,12,160,768]{3,2,1,0:T(8,128)(2,1)} fusion(f32[1,12,160,768]{3,2,1,0:T(8,128)S(1)} %bitcast.187, f32[1,12,160,768]{3,2,1,0:T(8,128)S(1)} %bitcast.186, bf16[1,12,160,768]{3,2,1,0:T(8,128)(2,1)} %copy-done.2), kind=kLoop, calls=%fused_computation.62 | loop fusion | flops 94371840 | bytes 17694720 | tf_op jit(solution)/shard_map/convert_element_type | solution.py:120
  659.4 10.2 %copy.81 = bf16[1,12,160,768]{2,1,0,3:T(8,128)(2,1)} copy(bf16[1,12,160,768]{3,2,1,0:T(8,128)(2,1)} %fusion.31) | data formatting | bytes 5898240 | tf_op jit(solution)/shard_map/convert_element_type | solution.py:120
  669.7 10.0 %reshape.1254 = bf16[4,2,184320]{2,1,0:T(2,128)(2,1)} reshape(bf16[768,1,12,160]{3,2,1,0:T(8,128)(2,1)} %bitcast.182) | data formatting | bytes 5898240
  679.7 3.9 all-to-all-start.3
  683.8 66.5 %all-to-all-done.3 = bf16[4,2,184320]{2,1,0:T(2,128)(2,1)S(1)} async-done(((bf16[4,2,184320]{2,1,0:T(2,128)(2,1)}), bf16[4,2,184320]{2,1,0:T(2,128)(2,1)S(1)}, u32[]{:S(2)}, u32[]{:S(2)}) %all-to-all-start.3) | async-done | bytes 2949152 | tf_op jit(solution)/shard_map/all_to_all | solution.py:121
  750.3 9.5 %reshape.1255 = bf16[768,1,12,160]{3,2,1,0:T(8,128)(2,1)} reshape(bf16[4,2,184320]{2,1,0:T(2,128)(2,1)S(1)} %all-to-all-done.3) | data formatting | bytes 5898240
  759.8 7.2 copy.82
  767.0 7.3 reshape.1243
  774.3 4.3 bitcast_reduce_fusion
  779.7 2.3 multiply_reduce_fusion
  782.0 2.5 multiply_convert_fusion
  786.5 12.2 %fusion.87 = (u16[192,1280]{1,0:T(8,128)(2,1)}, u16[192,1280]{1,0:T(8,128)(2,1)}, f32[12,192,1280]{2,1,0:T(8,128)}) fusion(bf16[12,640,192]{2,1,0:T(8,128)(2,1)S(1)} %bitcast.211, bf16[2,640,1280]{2,1,0:T(8,128)(2,1)S(1)} %copy-done.47), kind=kOutput, calls=%fused_computation.134 | convolution fusion | flops 3812720640 | bytes 18350080 | tf_op jit(solution)/shard_map/brcw,cf->brwf/dot_general | solution.py:92
  798.7 4.4 copy.83
  803.1 8.6 %copy.87 = f32[1,12,640,192]{2,3,1,0:T(8,128)} copy(f32[1,12,640,192]{3,2,1,0:T(8,128)} %bitcast.179) | data formatting | bytes 11796480 | tf_op jit(solution)/shard_map/convert_element_type | solution.py:83
  811.7 32.9 %fusion.72 = bf16[1,12,640,192]{2,3,1,0:T(8,128)(2,1)} fusion(f32[1,12,640,192]{2,3,1,0:T(8,128)} %copy.87, f32[12,192,1280]{2,1,0:T(8,128)} %get-tuple-element.86, u16[192,1280]{1,0:T(8,128)(2,1)} %get-tuple-element.6, u16[192,1280]{1,0:T(8,128)(2,1)} %get-tuple-element.5, bf16[2,1280,640]{2,1,0:T(8,128)(2,1)S(1)} %copy-done.49), kind=kOutput, calls=%fused_computation.104 | convolution fusion | flops 3984261120 | bytes 23265280 | tf_op jit(solution)/shard_map/brwf,fc->brcw/dot_general | solution.py:94
  (134 shorter events, 16.7 us)
Async XLA Ops:
  8.2 5.4 copy-start.7
  8.2 121.3 %all-to-all-start = ((bf16[1,12,640,192]{3,1,0,2:T(8,128)(2,1)}), bf16[1,12,640,192]{3,1,0,2:T(8,128)(2,1)}, u32[]{:S(2)}, u32[]{:S(2)}) async-start(bf16[1,12,640,192]{3,1,0,2:T(8,128)(2,1)} %copy.64), calls=%async_computation | async-start | bytes 10485760 | tf_op jit(solution)/shard_map/all_to_all | solution.py:110
  13.6 158.6 %copy-start.42 = (pred[768]{0:T(1024)(128)(4,1)}, pred[768]{0:T(1024)(128)(4,1)S(1)}, u32[]{:S(2)}) copy-start(pred[768]{0:T(1024)(128)(4,1)S(1)} %get-tuple-element.89) | copy-start | bytes 2308
  13.6 158.6 %copy-start.44 = (pred[768]{0:T(1024)(128)(4,1)}, pred[768]{0:T(1024)(128)(4,1)S(1)}, u32[]{:S(2)}) copy-start(pred[768]{0:T(1024)(128)(4,1)S(1)} %get-tuple-element.90) | copy-start | bytes 2308
  13.7 158.6 %copy-start.34 = (s32[768]{0:T(1024)}, s32[768]{0:T(1024)S(1)}, u32[]{:S(2)}) copy-start(s32[768]{0:T(1024)S(1)} %get-tuple-element.87) | copy-start | bytes 9220
  13.7 158.6 %copy-start.36 = (f32[768]{0:T(1024)}, f32[768]{0:T(1024)S(1)}, u32[]{:S(2)}) copy-start(f32[768]{0:T(1024)S(1)} %get-tuple-element.88) | copy-start | bytes 9220
  23.9 3.3 copy-start.5
  145.3 49.0 %copy-start.3 = (bf16[1,12,160,768]{3,2,1,0:T(8,128)(2,1)}, bf16[1,12,160,768]{3,2,1,0:T(8,128)(2,1)S(1)}, u32[]{:S(2)}) copy-start(bf16[1,12,160,768]{3,2,1,0:T(8,128)(2,1)S(1)} %all_to_all.43) | copy-start | bytes 8847364
  146.5 25.7 %collective-permute-start = (bf16[1,2,160,768]{3,2,1,0:T(8,128)(2,1)}, bf16[1,2,160,768]{3,2,1,0:T(8,128)(2,1)}, u32[]{:S(2)}, u32[]{:S(2)}) collective-permute-start(bf16[1,2,160,768]{3,2,1,0:T(8,128)(2,1)} %get-tuple-element.47), channel_id=1, source_target_pairs={{0,4},{4,8},{8,12},{12,16},{16,20},{20,24},{24,28},{1,5},{5,9},{9,... | collective-permute-start | bytes 1474568 | tf_op jit(solution)/shard_map/ppermute | solution.py:17
  148.4 23.8 %collective-permute-start.1 = (bf16[1,2,160,768]{3,2,1,0:T(8,128)(2,1)}, bf16[1,2,160,768]{3,2,1,0:T(8,128)(2,1)}, u32[]{:S(2)}, u32[]{:S(2)}) collective-permute-start(bf16[1,2,160,768]{3,2,1,0:T(8,128)(2,1)} %get-tuple-element.48), channel_id=1, source_target_pairs={{4,0},{8,4},{12,8},{16,12},{20,16},{24,20},{28,24},{5,1},{9,5},{13... | collective-permute-start | bytes 1474568 | tf_op jit(solution)/shard_map/ppermute | solution.py:20
  152.1 42.2 %copy-start.50 = (f32[16]{0:T(128)}, f32[16]{0:T(128)S(1)}, u32[]{:S(2)}) copy-start(f32[16]{0:T(128)S(1)} %multiply_sine_fusion) | copy-start | bytes 196
  152.1 0.6 copy-start.38
  172.2 22.1 %copy-start.28 = (f32[160,384]{1,0:T(8,128)S(1)}, f32[160,384]{1,0:T(8,128)}, u32[]{:S(2)}) copy-start(f32[160,384]{1,0:T(8,128)} %get-tuple-element.62) | copy-start | bytes 737284
  172.2 22.1 %copy-start.31 = (f32[160,384]{1,0:T(8,128)S(1)}, f32[160,384]{1,0:T(8,128)}, u32[]{:S(2)}) copy-start(f32[160,384]{1,0:T(8,128)} %get-tuple-element.77) | copy-start | bytes 737284
  172.2 22.1 %copy-start.32 = (f32[160,384]{1,0:T(8,128)S(1)}, f32[160,384]{1,0:T(8,128)}, u32[]{:S(2)}) copy-start(f32[160,384]{1,0:T(8,128)} %get-tuple-element.82) | copy-start | bytes 737284
  194.4 3.4 copy-start.8
  194.4 3.4 copy-start.9
  194.4 3.4 copy-start.20
  194.4 3.4 copy-start.21
  194.4 3.4 copy-start.22
  194.4 3.4 copy-start.23
  197.8 5.1 copy-start.12
  197.9 5.1 copy-start.13
  197.9 5.1 copy-start.16
  197.9 5.1 copy-start.17
  246.9 14.1 %copy-start.41 = (bf16[2,640]{1,0:T(2,128)(2,1)S(1)}, bf16[2,640]{1,0:T(2,128)(2,1)}, u32[]{:S(2)}) copy-start(bf16[2,640]{1,0:T(2,128)(2,1)} %param.7) | copy-start | bytes 7684
  257.0 70.8 %all-to-all-start.1 = ((bf16[4,2,184320]{2,1,0:T(2,128)(2,1)}), bf16[4,2,184320]{2,1,0:T(2,128)(2,1)S(1)}, u32[]{:S(2)}, u32[]{:S(2)}) async-start(bf16[4,2,184320]{2,1,0:T(2,128)(2,1)} %reshape.1252), calls=%async_computation.1 | async-start | bytes 5898240 | tf_op jit(solution)/shard_map/all_to_all | solution.py:121
  351.8 5.5 copy-start.1
  369.2 8.7 %copy-start.46 = (bf16[2,640,1280]{2,1,0:T(8,128)(2,1)S(1)}, bf16[2,640,1280]{2,1,0:T(8,128)(2,1)}, u32[]{:S(2)}) copy-start(bf16[2,640,1280]{2,1,0:T(8,128)(2,1)} %param.8) | copy-start | bytes 9830404
  378.0 10.3 %copy-start.4 = (f32[1,12,640,192]{2,3,1,0:T(8,128)S(1)}, f32[1,12,640,192]{2,3,1,0:T(8,128)}, u32[]{:S(2)}) copy-start(f32[1,12,640,192]{2,3,1,0:T(8,128)} %copy.75) | copy-start | bytes 17694724
  378.0 10.3 %copy-start.48 = (bf16[2,1280,640]{2,1,0:T(8,128)(2,1)S(1)}, bf16[2,1280,640]{2,1,0:T(8,128)(2,1)}, u32[]{:S(2)}) copy-start(bf16[2,1280,640]{2,1,0:T(8,128)(2,1)} %param.9) | copy-start | bytes 9830404
  429.8 5.2 copy-start.6
  429.8 120.5 %all-to-all-start.2 = ((bf16[1,12,640,192]{3,1,0,2:T(8,128)(2,1)}), bf16[1,12,640,192]{3,1,0,2:T(8,128)(2,1)}, u32[]{:S(2)}, u32[]{:S(2)}) async-start(bf16[1,12,640,192]{3,1,0,2:T(8,128)(2,1)} %copy.76), calls=%async_computation.2 | async-start | bytes 10485760 | tf_op jit(solution)/shard_map/all_to_all | solution.py:110
  559.0 16.0 %copy-start.35 = (s32[768]{0:T(1024)S(1)}, s32[768]{0:T(1024)}, u32[]{:S(2)}) copy-start(s32[768]{0:T(1024)} %copy-done.34) | copy-start | bytes 9220
  559.0 16.0 %copy-start.37 = (f32[768]{0:T(1024)S(1)}, f32[768]{0:T(1024)}, u32[]{:S(2)}) copy-start(f32[768]{0:T(1024)} %copy-done.36) | copy-start | bytes 9220
  559.0 16.0 %copy-start.39 = (f32[768]{0:T(1024)S(1)}, f32[768]{0:T(1024)}, u32[]{:S(2)}) copy-start(f32[768]{0:T(1024)} %copy-done.38) | copy-start | bytes 9220
  559.0 16.0 %copy-start.43 = (pred[768]{0:T(1024)(128)(4,1)S(1)}, pred[768]{0:T(1024)(128)(4,1)}, u32[]{:S(2)}) copy-start(pred[768]{0:T(1024)(128)(4,1)} %copy-done.42) | copy-start | bytes 2308
  559.0 16.0 %copy-start.45 = (pred[768]{0:T(1024)(128)(4,1)S(1)}, pred[768]{0:T(1024)(128)(4,1)}, u32[]{:S(2)}) copy-start(pred[768]{0:T(1024)(128)(4,1)} %copy-done.44) | copy-start | bytes 2308
  565.7 29.0 %copy-start.2 = (bf16[1,12,160,768]{3,2,1,0:T(8,128)(2,1)}, bf16[1,12,160,768]{3,2,1,0:T(8,128)(2,1)S(1)}, u32[]{:S(2)}) copy-start(bf16[1,12,160,768]{3,2,1,0:T(8,128)(2,1)S(1)} %all_to_all.48) | copy-start | bytes 8847364
  566.8 27.9 %copy-start.51 = (f32[16]{0:T(128)S(1)}, f32[16]{0:T(128)}, u32[]{:S(2)}) copy-start(f32[16]{0:T(128)} %copy-done.50) | copy-start | bytes 196
  566.8 27.9 %collective-permute-start.2 = (bf16[1,2,160,768]{3,2,1,0:T(8,128)(2,1)}, bf16[1,2,160,768]{3,2,1,0:T(8,128)(2,1)}, u32[]{:S(2)}, u32[]{:S(2)}) collective-permute-start(bf16[1,2,160,768]{3,2,1,0:T(8,128)(2,1)} %get-tuple-element.45), channel_id=1, source_target_pairs={{0,4},{4,8},{8,12},{12,16},{16,20},{20,24},{24,28},{1,5},{5,9},{9,... | collective-permute-start | bytes 1474568 | tf_op jit(solution)/shard_map/ppermute | solution.py:17
  568.9 25.9 %collective-permute-start.3 = (bf16[1,2,160,768]{3,2,1,0:T(8,128)(2,1)}, bf16[1,2,160,768]{3,2,1,0:T(8,128)(2,1)}, u32[]{:S(2)}, u32[]{:S(2)}) collective-permute-start(bf16[1,2,160,768]{3,2,1,0:T(8,128)(2,1)} %get-tuple-element.46), channel_id=1, source_target_pairs={{4,0},{8,4},{12,8},{16,12},{20,16},{24,20},{28,24},{5,1},{9,5},{13... | collective-permute-start | bytes 1474568 | tf_op jit(solution)/shard_map/ppermute | solution.py:20
  594.7 22.1 %copy-start.29 = (f32[160,384]{1,0:T(8,128)S(1)}, f32[160,384]{1,0:T(8,128)}, u32[]{:S(2)}) copy-start(f32[160,384]{1,0:T(8,128)} %get-tuple-element.57) | copy-start | bytes 737284
  594.8 22.1 %copy-start.30 = (f32[160,384]{1,0:T(8,128)S(1)}, f32[160,384]{1,0:T(8,128)}, u32[]{:S(2)}) copy-start(f32[160,384]{1,0:T(8,128)} %get-tuple-element.67) | copy-start | bytes 737284
  594.8 22.1 %copy-start.33 = (f32[160,384]{1,0:T(8,128)S(1)}, f32[160,384]{1,0:T(8,128)}, u32[]{:S(2)}) copy-start(f32[160,384]{1,0:T(8,128)} %get-tuple-element.72) | copy-start | bytes 737284
  616.9 3.4 copy-start.14
  616.9 3.4 copy-start.15
  616.9 3.4 copy-start.18
  616.9 3.4 copy-start.19
  616.9 3.4 copy-start.26
  616.9 3.4 copy-start.27
  620.4 5.1 copy-start.10
  620.4 5.1 copy-start.11
  620.4 5.1 copy-start.24
  620.4 5.1 copy-start.25
  669.7 13.9 %copy-start.40 = (f32[640]{0:T(1024)S(1)}, f32[640]{0:T(1024)}, u32[]{:S(2)}) copy-start(f32[640]{0:T(1024)} %get-tuple-element.9) | copy-start | bytes 7684
  679.7 70.6 %all-to-all-start.3 = ((bf16[4,2,184320]{2,1,0:T(2,128)(2,1)}), bf16[4,2,184320]{2,1,0:T(2,128)(2,1)S(1)}, u32[]{:S(2)}, u32[]{:S(2)}) async-start(bf16[4,2,184320]{2,1,0:T(2,128)(2,1)} %reshape.1254), calls=%async_computation.3 | async-start | bytes 5898240 | tf_op jit(solution)/shard_map/all_to_all | solution.py:121
  774.3 5.5 copy-start
  784.6 1.9 copy-start.47
  803.1 8.6 %copy-start.49 = (bf16[2,1280,640]{2,1,0:T(8,128)(2,1)S(1)}, bf16[2,1280,640]{2,1,0:T(8,128)(2,1)}, u32[]{:S(2)}) copy-start(bf16[2,1280,640]{2,1,0:T(8,128)(2,1)} %param.9) | copy-start | bytes 9830404
where the time goes:
time: 856 us; the launch traced here: 845 us
  waiting for transfers between devices  346 us (40%)
  local copies, waits for them, and re-layouts  201 us (23%)
  matrix products  167 us (20%)
  other arithmetic  100 us (12%)
  starting transfers between devices  29.7 us (3%)
    all_to_all x2, waiting for transfers between devices, body(): lax.all_to_all(current, 'lon', split_axis=2, concat_axis=3, tiled=True)  213 us
    all_to_all x2, waiting for transfers between devices, body(): lax.all_to_all(mixed_out, 'lon', split_axis=3, concat_axis=2, tiled=True)  132 us
    dot_general x2, matrix products, feed_forward(): jnp.einsum('brwf,fc->brcw', hidden, output_layer, preferred_element_type=...  62.9 us
    unnamed x109, local copies, waits for them, and re-layouts  51.6 us
    dot_general x2, matrix products, transform(): jnp.dot(flat, forward, precision=lax.Precision.HIGH).reshape(weighted.shape)  44.1 us
    convert_element_type x6, local copies, waits for them, and re-layouts, feed_forward(): values = mixed_grid.astype(jnp.float32)  40.8 us
    all_to_all x6, local copies, waits for them, and re-layouts, body(): lax.all_to_all(current, 'lon', split_axis=2, concat_axis=3, tiled=True)  31.2 us
    convert_element_type x2, other arithmetic, body(): mixed_out = (swapped.astype(jnp.float32) + jax.nn.gelu(convolved, approxi...  29 us
  transfers between devices with their start and end apart: 8, of which 4 were waited for; matrix products, arithmetic and copies ran while one was open for 7% of the time, Pallas kernels for 0%

commit v1 on v0

v1 whole, which is shorter than its diff:
```python
import functools
import math

import jax
import jax.numpy as jnp
import numpy as np
from jax import lax
from jax.experimental import pallas as pl
from jax.experimental.pallas import tpu as pltpu
from jax.sharding import PartitionSpec as P

LANES = 128


def round_up(value, step):
    return -(-value // step) * step


def plan(width, taps):
    half = taps // 2
    padded = round_up(width, LANES)
    length = round_up(width + taps, 2 * LANES)
    return half, padded, length


def bases(width, taps):
    half, padded, length = plan(width, taps)
    places = np.full(2 * half + padded, -1)
    places[:half] = np.arange(half)
    places[half : half + width] = half + np.arange(width)
    places[half + padded :] = half + width + np.arange(half)
    odd = 2 * np.arange(length // 2) + 1

    def wave(points):
        angle = np.pi / length * (points[:, None] * odd[None, :] % (2 * length))
        return np.concatenate([np.cos(angle), -np.sin(angle)], axis=1)

    forward = np.where(places[:, None] >= 0, wave(places), 0.0)
    inverse = 2.0 / length * wave(2 * half + np.arange(width)).T
    tap_basis = wave(np.arange(taps))
    return tuple(jnp.asarray(a, jnp.bfloat16) for a in (forward, inverse, tap_basis))


def gelu(values):
    return 0.5 * values * (1.0 + lax.erf(values * math.sqrt(0.5)))


def conv_kernel(
    quad, left, mid, right, low, high, factors, forward, inverse, out, ext, spectra, mixed, *, half, padded, rim
):
    rows, channels, width = mid.shape
    freqs = forward.shape[1] // 2
    every = rows + 2 * rim
    taps_r = 2 * rim + 1
    inner = slice(rim, rim + rows)
    ext[:rim] = low[...]
    ext[rim + rows :] = high[...]
    ext[inner, :, :half] = left[...]
    ext[inner, :, half : half + width] = mid[...]
    if padded > width:
        ext[inner, :, half + width : half + padded] = jnp.zeros((rows, channels, padded - width), ext.dtype)
    ext[inner, :, half + padded :] = right[...]
    group = 8 if every % 8 == 0 else 1
    for g in range(0, every, group):
        flat = ext[g : g + group].reshape(group * channels, ext.shape[2])
        result = jnp.dot(flat, forward[...], preferred_element_type=jnp.float32)
        for j in range(group):
            spectra[g + j] = result[j * channels : (j + 1) * channels] * quad[g + j]

    def block(c, carry):
        c = pl.ds(pl.multiple_of(c * 16, 16), 16)
        for f in range(0, freqs, LANES):
            re = slice(f, f + LANES)
            im = slice(freqs + f, freqs + f + LANES)
            fr = [factors[r, c, re] for r in range(taps_r)]
            fi = [factors[r, c, im] for r in range(taps_r)]
            xr = [spectra[g, c, re] for g in range(taps_r - 1)]
            xi = [spectra[g, c, im] for g in range(taps_r - 1)]
            for h in range(rows):
                xr.append(spectra[h + taps_r - 1, c, re])
                xi.append(spectra[h + taps_r - 1, c, im])
                yr = xr[0] * fr[0] - xi[0] * fi[0]
                yi = xr[0] * fi[0] + xi[0] * fr[0]
                for r in range(1, taps_r):
                    yr = yr + (xr[r] * fr[r] - xi[r] * fi[r])
                    yi = yi + (xr[r] * fi[r] + xi[r] * fr[r])
                mixed[h, c, re] = yr.astype(mixed.dtype)
                mixed[h, c, im] = yi.astype(mixed.dtype)
                xr.pop(0)
                xi.pop(0)
        return carry

    lax.fori_loop(0, channels // 16, block, 0)
    group = 4 if rows % 4 == 0 else 1
    for h in range(0, rows, group):
        flat = mixed[h : h + group].reshape(group * channels, mixed.shape[2])
        conv = jnp.dot(flat, inverse[...], preferred_element_type=jnp.float32)
        conv = conv.reshape(group, channels, width)
        out[h : h + group] = (mid[h : h + group].astype(jnp.float32) + gelu(conv)).astype(out.dtype)


def convolve(quad, left, mid, right, low, high, factors, forward, inverse, half, padded, rim):
    rows, channels, width = mid.shape
    every = rows + 2 * rim
    block = math.gcd(channels, 64)
    length = forward.shape[1]
    wide = forward.shape[0]

    def rows_of(count, last):
        return pl.BlockSpec((count, block, last), lambda i: (0, i, 0))

    def whole(array):
        return pl.BlockSpec(array.shape, lambda i: (0,) * array.ndim)

    kernel = functools.partial(conv_kernel, half=half, padded=padded, rim=rim)
    return pl.pallas_call(
        kernel,
        grid=(channels // block,),
        out_shape=jax.ShapeDtypeStruct(mid.shape, jnp.bfloat16),
        in_specs=[
            pl.BlockSpec(memory_space=pltpu.SMEM),
            rows_of(rows, half),
            rows_of(rows, width),
            rows_of(rows, half),
            rows_of(rim, wide),
            rows_of(rim, wide),
            rows_of(factors.shape[0], length),
            whole(forward),
            whole(inverse),
        ],
        out_specs=rows_of(rows, width),
        scratch_shapes=[
            pltpu.VMEM((every, block, wide), jnp.bfloat16),
            pltpu.VMEM((every, block, length), jnp.float32),
            pltpu.VMEM((rows, block, length), jnp.bfloat16),
        ],
        compiler_params=pltpu.CompilerParams(vmem_limit_bytes=56 << 20),
        cost_estimate=pl.CostEstimate(
            flops=2 * channels * length * (every * wide + rows * width),
            bytes_accessed=4 * channels * (every * wide + factors.shape[0] * length),
            transcendentals=rows * channels * width,
        ),
        name="zonal_conv",
    )(quad, left, mid, right, low, high, factors, forward, inverse)


def mlp_kernel(gain, w_in, w_out, mixed, out, *edges, half):
    values = mixed[0].astype(jnp.float32)
    average = jnp.mean(values, axis=0, keepdims=True)
    centred = values - average
    variance = jnp.mean(jnp.square(centred), axis=0, keepdims=True)
    normed = (centred * lax.rsqrt(variance + 1e-05) * gain[...]).astype(jnp.bfloat16)
    total = values
    hidden_units = w_in.shape[0]
    step = math.gcd(hidden_units, 256)
    for f in range(0, hidden_units, step):
        hidden = jnp.dot(w_in[f : f + step], normed, preferred_element_type=jnp.float32)
        hidden = gelu(hidden).astype(jnp.bfloat16)
        total = total + jnp.dot(w_out[:, f : f + step], hidden, preferred_element_type=jnp.float32)
    result = total.astype(jnp.bfloat16)
    out[0] = result
    if edges:
        edges[0][0] = result[:, :half]
        edges[1][0] = result[:, result.shape[1] - half :]


def mlp(gain, w_in, w_out, mixed, edge):
    rows, channels, width = mixed.shape
    hidden_units = w_in.shape[0]

    def whole(array):
        return pl.BlockSpec(array.shape, lambda i: (0,) * array.ndim)

    def row(last):
        return pl.BlockSpec((1, channels, last), lambda i: (i, 0, 0))

    lasts = [width] + ([edge, edge] if edge else [])
    return pl.pallas_call(
        functools.partial(mlp_kernel, half=edge),
        grid=(rows,),
        out_shape=[jax.ShapeDtypeStruct((rows, channels, last), jnp.bfloat16) for last in lasts],
        in_specs=[whole(gain), whole(w_in), whole(w_out), row(width)],
        out_specs=[row(last) for last in lasts],
        compiler_params=pltpu.CompilerParams(vmem_limit_bytes=56 << 20),
        cost_estimate=pl.CostEstimate(
            flops=4 * rows * width * channels * hidden_units,
            bytes_accessed=4 * rows * width * channels,
            transcendentals=rows * width * hidden_units,
        ),
        name="channel_mlp",
    )(gain, w_in, w_out, mixed)


def rotate(block, axis, hops):
    count = lax.axis_size(axis)
    return lax.ppermute(block, axis, [(i, (i + hops) % count) for i in range(count)])


def zonal_halos(first, last, width, half):
    if half <= width:
        return rotate(last, "lon", 1), rotate(first, "lon", -1)
    lefts, rights, hops, missing = [], [], 1, half
    while missing > 0:
        take = min(width, missing)
        lefts.insert(0, rotate(last[..., last.shape[2] - take :], "lon", hops))
        rights.append(rotate(first[..., :take], "lon", -hops))
        missing -= take
        hops += 1
    return jnp.concatenate(lefts, axis=2), jnp.concatenate(rights, axis=2)


def step_rows(block, hops):
    count = lax.axis_size("lat")
    pairs = [(i, i + hops) for i in range(count) if 0 <= i + hops < count]
    return lax.ppermute(block, "lat", pairs)


def body(ocean_state, zonal_kernel, norm_gain, input_weight, output_weight):
    blocks, kernel_rows, taps, channels = zonal_kernel.shape
    _, rows, _, width = ocean_state.shape
    rim = kernel_rows // 2
    half, padded, length = plan(width, taps)
    edge = min(half, width)
    forward, inverse, tap_basis = bases(width, taps)
    total_rows = rows * lax.axis_size("lat")
    index = lax.axis_index("lat") * rows - rim + jnp.arange(rows + 2 * rim, dtype=jnp.int32)
    quad = jnp.sin(jnp.pi * (index.astype(jnp.float32) + 0.5) / total_rows)
    quad = jnp.where((index >= 0) & (index < total_rows), quad, 0.0)
    factors = jnp.einsum("lrtc,tk->lrck", zonal_kernel, tap_basis, preferred_element_type=jnp.float32)
    w_in = jnp.swapaxes(input_weight, 1, 2)
    w_out = jnp.swapaxes(output_weight, 1, 2)
    gains = norm_gain.astype(jnp.float32)[:, :, None]

    current = ocean_state[0]
    first, last = current[..., :edge], current[..., width - edge :]
    for layer in range(blocks):
        left, right = zonal_halos(first, last, width, half)

        def extended(rows_slice):
            pieces = [left[rows_slice], current[rows_slice]]
            if padded > width:
                pieces.append(jnp.zeros((rim, channels, padded - width), current.dtype))
            return jnp.concatenate(pieces + [right[rows_slice]], axis=2)

        low = step_rows(extended(slice(rows - rim, rows)), 1)
        high = step_rows(extended(slice(0, rim)), -1)
        mixed = convolve(
            quad, left, current, right, low, high, factors[layer], forward, inverse, half, padded, rim
        )
        outs = mlp(gains[layer], w_in[layer], w_out[layer], mixed, edge if layer + 1 < blocks else 0)
        current = outs[0]
        if layer + 1 < blocks:
            first, last = outs[1], outs[2]
    return current[None]


def solution(mesh):
    in_specs = (P(None, "lat", None, "lon"), P(), P(), P(), P())
    out_specs = P(None, "lat", None, "lon")
    return jax.shard_map(body, mesh=mesh, in_specs=in_specs, out_specs=out_specs, check_vma=False)
```

time: 856 us -> 371 us (0.43)
  waiting for transfers between devices: 346 us -> 179 us
  matrix products: 167 us -> 6.64 us
  local copies, waits for them, and re-layouts: 201 us -> 56.1 us
  Pallas kernels: 0 us -> 102 us
  other arithmetic: 100 us -> 4.57 us
  starting transfers between devices: 29.7 us -> 18.9 us
    all_to_all x4 -> x0, waiting for transfers between devices: 346 us -> none  [the longest x2 213 us: body(): lax.all_to_all(current, 'lon', split_axis=2, concat_axis=3, tiled=True)]
    ppermute x4 -> x8, waiting for transfers between devices: 0.01 us -> 179 us  [the longest x4 145 us: rotate(): lax.ppermute(block, axis, [(i, (i + hops) % count) for i in range(count)])]
    dot_general x10 -> x1, matrix products: 167 us -> 6.64 us  [body(): jnp.einsum('lrtc,tk->lrck', zonal_kernel, tap_basis, preferred_element_ty...]
    pallas_call x0 -> x4, Pallas kernels: none -> 102 us  [the longest x2 52.2 us: convolve(): pl.pallas_call(kernel, grid=(channels // block,), out_shape=jax.ShapeDtyp...]
    convert_element_type x15 -> x0, local copies, waits for them, and re-layouts: 76.5 us -> none  [the longest x6 40.8 us: feed_forward(): values = mixed_grid.astype(jnp.float32)]
    all_to_all x8 -> x0, local copies, waits for them, and re-layouts: 45.6 us -> none  [the longest x6 31.2 us: body(): lax.all_to_all(current, 'lon', split_axis=2, concat_axis=3, tiled=True)]
    convert_element_type x7 -> x1, other arithmetic: 34.6 us -> 0.01 us  [body(): gains = norm_gain.astype(jnp.float32)[:, :, None]]
    unnamed x109 -> x21, local copies, waits for them, and re-layouts: 51.6 us -> 20.8 us
  transfers between devices with their start and end apart: 8 -> 8, of which waited for: 4 -> 7; matrix products, arithmetic and copies ran while one was open for 7% -> 11% of each run, Pallas kernels for 0% -> 0%
where the time goes in v1:
time: 371 us; the launch traced here: 367 us
  waiting for transfers between devices  179 us (48%)
  Pallas kernels  102 us (27%)
  local copies, waits for them, and re-layouts  56.1 us (15%)
  starting transfers between devices  18.9 us (5%)
  matrix products  6.64 us (2%)
  other arithmetic  4.57 us (1%)
    ppermute x4, waiting for transfers between devices, rotate(): lax.ppermute(block, axis, [(i, (i + hops) % count) for i in range(count)])  145 us
    pallas_call x2, Pallas kernels, convolve(): pl.pallas_call(kernel, grid=(channels // block,), out_shape=jax.ShapeDtyp...  52.2 us
    pallas_call x2, Pallas kernels, mlp(): pl.pallas_call(functools.partial(mlp_kernel, half=edge), grid=(rows,), ou...  50.1 us
    ppermute x4, waiting for transfers between devices, step_rows(): return lax.ppermute(block, 'lat', pairs)  33.5 us
    unnamed x21, local copies, waits for them, and re-layouts  20.8 us
    ppermute x4, starting transfers between devices, step_rows(): return lax.ppermute(block, 'lat', pairs)  11.3 us
    squeeze x1, local copies, waits for them, and re-layouts, body(): factors[layer]  11.1 us
    ppermute x4, starting transfers between devices, rotate(): lax.ppermute(block, axis, [(i, (i + hops) % count) for i in range(count)])  7.65 us
  transfers between devices with their start and end apart: 8, of which 7 were waited for; matrix products, arithmetic and copies ran while one was open for 11% of the time, Pallas kernels for 0%

profile of v1, /device:TPU:2, one launch (start us, length us, event | category | flops | bytes accessed | tf_op | source)
XLA Modules:
  0.0 367.3 jit_solution(179380306830387770)
XLA Ops:
  0.0 0.0 copy-start
  0.0 5.9 %copy.18 = bf16[1,12,640,192]{3,2,1,0:T(8,128)(2,1)} copy(bf16[1,12,640,192]{2,3,1,0:T(8,128)(2,1)} %param.8) | data formatting | bytes 5898240 | tf_op args[0]
  5.9 0.0 copy-start.6
  5.9 5.5 %fusion.1 = (bf16[12,640,128]{2,1,0:T(8,128)(2,1)}, bf16[12,640,128]{2,1,0:T(8,128)(2,1)}) fusion(bf16[12,640,192]{2,1,0:T(8,128)(2,1)} %bitcast.31), kind=kLoop, calls=%fused_computation.17 | loop fusion | bytes 7864320 | tf_op jit(solution)/shard_map/slice | solution.py:235
  11.4 1.6 collective-permute-start
  12.9 2.2 collective-permute-start.1
  15.2 0.0 copy-done.6
  15.2 5.6 %copy.17 = bf16[2,1280,640]{1,2,0:T(8,128)(2,1)} copy(bf16[2,1280,640]{2,1,0:T(8,128)(2,1)} %param.12) | data formatting | bytes 6553600 | tf_op args[4]
  20.8 5.6 %copy.16 = bf16[2,640,1280]{1,2,0:T(8,128)(2,1)} copy(bf16[2,640,1280]{2,1,0:T(8,128)(2,1)} %param.11) | data formatting | bytes 6553600 | tf_op args[3]
  26.5 0.9 copy.22.gain
  27.4 0.1 pad.14.clone
  27.5 0.6 and_select_fusion.quad
  28.0 1.4 slice_bitcast_fusion.6
  29.4 0.0 copy-start.2
  29.4 3.9 %slice_bitcast_fusion.2 = (bf16[640,1280]{1,0:T(8,128)(2,1)}, bf16[640,1280]{1,0:T(8,128)(2,1)}) fusion(bf16[2,640,1280]{2,1,0:T(8,128)(2,1)} %bitcast.34), kind=kLoop, calls=%fused_computation.3 | loop fusion | bytes 6553600 | tf_op jit(solution)/shard_map/squeeze | solution.py:250
  33.3 0.0 copy-done.2
  33.4 2.0 slice_bitcast_fusion.3
  35.3 23.9 %collective-permute-done.left = bf16[12,640,128]{2,1,0:T(8,128)(2,1)} collective-permute-done((bf16[12,640,128]{2,1,0:T(8,128)(2,1)}, bf16[12,640,128]{2,1,0:T(8,128)(2,1)}, u32[]{:S(2)}, u32[]{:S(2)}) %collective-permute-start) | collective-permute-done | bytes 1966112 | tf_op jit(solution)/shard_map/ppermute | solution.py:196
  59.2 1.1 fusion.4
  60.3 39.3 %collective-permute-done.1.right = bf16[12,640,128]{2,1,0:T(8,128)(2,1)} collective-permute-done((bf16[12,640,128]{2,1,0:T(8,128)(2,1)}, bf16[12,640,128]{2,1,0:T(8,128)(2,1)}, u32[]{:S(2)}, u32[]{:S(2)}) %collective-permute-start.1) | collective-permute-done | bytes 1966112 | tf_op jit(solution)/shard_map/ppermute | solution.py:196
  99.7 1.1 fusion.5
  100.8 0.0 copy-start.3
  100.8 2.0 pad_maximum_fusion.1
  102.8 1.9 collective-permute-start.2
  104.7 3.6 collective-permute-start.3
  108.4 0.0 copy-done
  108.4 0.0 copy-done.3
  108.4 6.6 %convolution_bitcast_fusion = f32[2,5,640,512]{3,2,1,0:T(8,128)} fusion(bf16[256,512,1,1]{0,1,3,2:T(8,128)(2,1)S(1)} %copy-done.3, bf16[2,5,256,640]{3,2,1,0:T(8,128)(2,1)S(1)} %copy-done), kind=kOutput, calls=%fused_computation.2 | convolution fusion | flops 1677721600 | bytes 16646144 | tf_op jit(solution)/shard_map/lrtc,tk->lrck/dot_general | solution.py:229
  115.0 11.1 %slice_bitcast_fusion = (f32[5,640,512]{2,1,0:T(8,128)}, f32[5,640,512]{2,1,0:T(8,128)}) fusion(f32[2,5,640,512]{3,2,1,0:T(8,128)} %convolution_bitcast_fusion), kind=kLoop, calls=%fused_computation | loop fusion | bytes 26214400 | tf_op jit(solution)/shard_map/squeeze | solution.py:248
  126.1 0.0 collective-permute-done.2.low
  126.1 9.0 %collective-permute-done.3.high = bf16[2,640,512]{2,1,0:T(8,128)(2,1)} collective-permute-done((bf16[2,640,512]{2,1,0:T(8,128)(2,1)}, bf16[2,640,512]{2,1,0:T(8,128)(2,1)}, u32[]{:S(2)}, u32[]{:S(2)}) %collective-permute-start.3) | collective-permute-done | bytes 1310752 | tf_op jit(solution)/shard_map/ppermute | solution.py:215
  135.1 26.1 %zonal_conv.2.mixed = bf16[12,640,192]{2,1,0:T(8,128)(2,1)} custom-call(f32[16]{0:T(128)} %and_select_fusion.quad, bf16[12,640,128]{2,1,0:T(8,128)(2,1)} %collective-permute-done.left, bf16[12,640,192]{2,1,0:T(8,128)(2,1)} %bitcast.32, bf16[12,640,128]{2,1,0:T(8,128)(2,1)} %collective-permute-done.1.right, bf16[2,640,512]{2,1,0:T(8,128)(2,1)} %collective-permute-done.2.low, ...), custom_call_target="tpu_custom_call" | custom-call | flops 6878658560 | bytes 27525120 | tf_op jit(solution)/shard_map/zonal_conv/pallas_call | solution.py:116
  161.2 25.5 %channel_mlp.2 = (bf16[12,640,192]{2,1,0:T(8,128)(2,1)}, bf16[12,640,128]{2,1,0:T(8,128)(2,1)}, bf16[12,640,128]{2,1,0:T(8,128)(2,1)}) custom-call(f32[640,1]{1,0:T(8,128)} %copy.22.gain, bf16[1280,640]{1,0:T(8,128)(2,1)} %get-tuple-element.21.w_in, bf16[640,1280]{1,0:T(8,128)(2,1)} %get-tuple-element.19.w_out, bf16[12,640,192]{2,1,0:T(8,128)(2,1)} %zonal_conv.2.mixed), custom_call_target="tpu_custom_call" | custom-call | flops 7549747200 | bytes 5898240 | tf_op jit(solution)/shard_map/channel_mlp/pallas_call | solution.py:178
  186.7 1.1 collective-permute-start.4
  187.9 2.7 collective-permute-start.5
  190.5 1.4 fusion
  191.9 41.8 %collective-permute-done.4.left = bf16[12,640,128]{2,1,0:T(8,128)(2,1)S(1)} collective-permute-done((bf16[12,640,128]{2,1,0:T(8,128)(2,1)}, bf16[12,640,128]{2,1,0:T(8,128)(2,1)S(1)}, u32[]{:S(2)}, u32[]{:S(2)}) %collective-permute-start.4) | collective-permute-done | bytes 1966112 | tf_op jit(solution)/shard_map/ppermute | solution.py:196
  233.7 0.0 copy-start.4
  233.7 1.3 copy-done.4
  235.0 40.2 %collective-permute-done.5.right = bf16[12,640,128]{2,1,0:T(8,128)(2,1)S(1)} collective-permute-done((bf16[12,640,128]{2,1,0:T(8,128)(2,1)}, bf16[12,640,128]{2,1,0:T(8,128)(2,1)S(1)}, u32[]{:S(2)}, u32[]{:S(2)}) %collective-permute-start.5) | collective-permute-done | bytes 1966112 | tf_op jit(solution)/shard_map/ppermute | solution.py:196
  275.2 0.0 copy-start.5
  275.2 1.3 copy-done.5
  276.6 2.0 pad_maximum_fusion.3
  278.5 2.4 collective-permute-start.6
  280.9 3.4 collective-permute-start.7
  284.3 0.9 copy.23.gain
  285.2 12.4 %collective-permute-done.6.low = bf16[2,640,512]{2,1,0:T(8,128)(2,1)S(1)} collective-permute-done((bf16[2,640,512]{2,1,0:T(8,128)(2,1)}, bf16[2,640,512]{2,1,0:T(8,128)(2,1)S(1)}, u32[]{:S(2)}, u32[]{:S(2)}) %collective-permute-start.6) | collective-permute-done | bytes 1310752 | tf_op jit(solution)/shard_map/ppermute | solution.py:215
  297.7 0.0 copy-start.7
  297.7 12.0 %collective-permute-done.7.high = bf16[2,640,512]{2,1,0:T(8,128)(2,1)S(1)} collective-permute-done((bf16[2,640,512]{2,1,0:T(8,128)(2,1)}, bf16[2,640,512]{2,1,0:T(8,128)(2,1)S(1)}, u32[]{:S(2)}, u32[]{:S(2)}) %collective-permute-start.7) | collective-permute-done | bytes 1310752 | tf_op jit(solution)/shard_map/ppermute | solution.py:215
  309.7 0.0 copy-start.8
  309.7 0.0 copy-done.7
  309.7 1.1 copy-done.8
  310.8 26.1 %zonal_conv.3.mixed = bf16[12,640,192]{2,1,0:T(8,128)(2,1)} custom-call(f32[16]{0:T(128)} %and_select_fusion.quad, bf16[12,640,128]{2,1,0:T(8,128)(2,1)} %copy-done.4, bf16[12,640,192]{2,1,0:T(8,128)(2,1)} %get-tuple-element.9.mid, bf16[12,640,128]{2,1,0:T(8,128)(2,1)} %copy-done.5, bf16[2,640,512]{2,1,0:T(8,128)(2,1)} %copy-done.7, ...), custom_call_target="tpu_custom_call" | custom-call | flops 6878658560 | bytes 27525120 | tf_op jit(solution)/shard_map/zonal_conv/pallas_call | solution.py:116
  336.9 24.6 %channel_mlp.3 = bf16[12,640,192]{2,1,0:T(8,128)(2,1)} custom-call(f32[640,1]{1,0:T(8,128)} %copy.23.gain, bf16[1280,640]{1,0:T(8,128)(2,1)} %get-tuple-element.22.w_in, bf16[640,1280]{1,0:T(8,128)(2,1)} %get-tuple-element.20.w_out, bf16[12,640,192]{2,1,0:T(8,128)(2,1)} %zonal_conv.3.mixed), custom_call_target="tpu_custom_call" | custom-call | flops 7549747200 | bytes 5898240 | tf_op jit(solution)/shard_map/channel_mlp/pallas_call | solution.py:178
  361.5 0.0 copy-start.1
  361.5 5.9 %copy.24 = bf16[1,12,640,192]{2,3,1,0:T(8,128)(2,1)} copy(bf16[1,12,640,192]{3,2,1,0:T(8,128)(2,1)} %bitcast.35) | data formatting | bytes 5898240 | tf_op jit(solution)/shard_map/broadcast_in_dim | solution.py:254
  367.3 0.0 copy-done.1
  (5 shorter events, 0.1 us)
Async XLA Ops:
  0.0 108.4 %copy-start = (bf16[2,5,256,640]{3,2,1,0:T(8,128)(2,1)S(1)}, bf16[2,5,256,640]{3,2,1,0:T(8,128)(2,1)}, u32[]{:S(2)}) copy-start(bf16[2,5,256,640]{3,2,1,0:T(8,128)(2,1)} %param.9) | copy-start | bytes 9830404
  5.9 9.3 %copy-start.6 = (bf16[2,640]{1,0:T(2,128)(2,1)S(1)}, bf16[2,640]{1,0:T(2,128)(2,1)}, u32[]{:S(2)}) copy-start(bf16[2,640]{1,0:T(2,128)(2,1)} %param.10) | copy-start | bytes 7684
  11.4 47.9 %collective-permute-start = (bf16[12,640,128]{2,1,0:T(8,128)(2,1)}, bf16[12,640,128]{2,1,0:T(8,128)(2,1)}, u32[]{:S(2)}, u32[]{:S(2)}) collective-permute-start(bf16[12,640,128]{2,1,0:T(8,128)(2,1)} %get-tuple-element.18), channel_id=1, source_target_pairs={{0,1},{1,2},{2,3},{3,0},{4,5},{5,6},{6,7},{7,4},{8,9},{9,10},{10,1... | collective-permute-start | bytes 5898248 | tf_op jit(solution)/shard_map/ppermute | solution.py:196
  12.9 86.7 %collective-permute-start.1 = (bf16[12,640,128]{2,1,0:T(8,128)(2,1)}, bf16[12,640,128]{2,1,0:T(8,128)(2,1)}, u32[]{:S(2)}, u32[]{:S(2)}) collective-permute-start(bf16[12,640,128]{2,1,0:T(8,128)(2,1)} %get-tuple-element.17), channel_id=1, source_target_pairs={{0,3},{1,0},{2,1},{3,2},{4,7},{5,4},{6,5},{7,6},{8,11},{9,8},{10,9... | collective-permute-start | bytes 5898248 | tf_op jit(solution)/shard_map/ppermute | solution.py:196
  29.4 3.9 %copy-start.2 = (bf16[2,640,1280]{1,2,0:T(8,128)(2,1)S(1)}, bf16[2,640,1280]{1,2,0:T(8,128)(2,1)}, u32[]{:S(2)}) copy-start(bf16[2,640,1280]{1,2,0:T(8,128)(2,1)} %copy.16) | copy-start | bytes 9830404
  100.8 7.6 %copy-start.3 = (bf16[256,512,1,1]{0,1,3,2:T(8,128)(2,1)S(1)}, bf16[256,512,1,1]{0,1,3,2:T(8,128)(2,1)}, u32[]{:S(2)}) copy-start(bf16[256,512,1,1]{0,1,3,2:T(8,128)(2,1)} %constant.36) | copy-start | bytes 786436
  102.8 23.3 %collective-permute-start.2 = (bf16[2,640,512]{2,1,0:T(8,128)(2,1)}, bf16[2,640,512]{2,1,0:T(8,128)(2,1)}, u32[]{:S(2)}, u32[]{:S(2)}) collective-permute-start(bf16[2,640,512]{2,1,0:T(8,128)(2,1)} %get-tuple-element.36), channel_id=1, source_target_pairs={{0,4},{4,8},{8,12},{12,16},{16,20},{20,24},{24,28},{1,5},{5,9},{9,... | collective-permute-start | bytes 3932168 | tf_op jit(solution)/shard_map/ppermute | solution.py:215
  104.7 30.4 %collective-permute-start.3 = (bf16[2,640,512]{2,1,0:T(8,128)(2,1)}, bf16[2,640,512]{2,1,0:T(8,128)(2,1)}, u32[]{:S(2)}, u32[]{:S(2)}) collective-permute-start(bf16[2,640,512]{2,1,0:T(8,128)(2,1)} %get-tuple-element.35), channel_id=1, source_target_pairs={{4,0},{8,4},{12,8},{16,12},{20,16},{24,20},{28,24},{5,1},{9,5},{13... | collective-permute-start | bytes 3932168 | tf_op jit(solution)/shard_map/ppermute | solution.py:215
  186.7 47.0 %collective-permute-start.4 = (bf16[12,640,128]{2,1,0:T(8,128)(2,1)}, bf16[12,640,128]{2,1,0:T(8,128)(2,1)S(1)}, u32[]{:S(2)}, u32[]{:S(2)}) collective-permute-start(bf16[12,640,128]{2,1,0:T(8,128)(2,1)} %get-tuple-element.8), channel_id=1, source_target_pairs={{0,1},{1,2},{2,3},{3,0},{4,5},{5,6},{6,7},{7,4},{8,9},{9,10},{10,1... | collective-permute-start | bytes 5898248 | tf_op jit(solution)/shard_map/ppermute | solution.py:196
  187.9 87.4 %collective-permute-start.5 = (bf16[12,640,128]{2,1,0:T(8,128)(2,1)}, bf16[12,640,128]{2,1,0:T(8,128)(2,1)S(1)}, u32[]{:S(2)}, u32[]{:S(2)}) collective-permute-start(bf16[12,640,128]{2,1,0:T(8,128)(2,1)} %get-tuple-element.10), channel_id=1, source_target_pairs={{0,3},{1,0},{2,1},{3,2},{4,7},{5,4},{6,5},{7,6},{8,11},{9,8},{10,9... | collective-permute-start | bytes 5898248 | tf_op jit(solution)/shard_map/ppermute | solution.py:196
  233.7 1.3 copy-start.4
  275.2 1.3 copy-start.5
  278.5 19.1 %collective-permute-start.6 = (bf16[2,640,512]{2,1,0:T(8,128)(2,1)}, bf16[2,640,512]{2,1,0:T(8,128)(2,1)S(1)}, u32[]{:S(2)}, u32[]{:S(2)}) collective-permute-start(bf16[2,640,512]{2,1,0:T(8,128)(2,1)} %get-tuple-element.34), channel_id=1, source_target_pairs={{0,4},{4,8},{8,12},{12,16},{16,20},{20,24},{24,28},{1,5},{5,9},{9,... | collective-permute-start | bytes 3932168 | tf_op jit(solution)/shard_map/ppermute | solution.py:215
  280.9 28.8 %collective-permute-start.7 = (bf16[2,640,512]{2,1,0:T(8,128)(2,1)}, bf16[2,640,512]{2,1,0:T(8,128)(2,1)S(1)}, u32[]{:S(2)}, u32[]{:S(2)}) collective-permute-start(bf16[2,640,512]{2,1,0:T(8,128)(2,1)} %get-tuple-element.33), channel_id=1, source_target_pairs={{4,0},{8,4},{12,8},{16,12},{20,16},{24,20},{28,24},{5,1},{9,5},{13... | collective-permute-start | bytes 3932168 | tf_op jit(solution)/shard_map/ppermute | solution.py:215
  297.7 12.0 %copy-start.7 = (bf16[2,640,512]{2,1,0:T(8,128)(2,1)}, bf16[2,640,512]{2,1,0:T(8,128)(2,1)S(1)}, u32[]{:S(2)}) copy-start(bf16[2,640,512]{2,1,0:T(8,128)(2,1)S(1)} %collective-permute-done.6.low) | copy-start | bytes 3932164
  309.7 1.1 copy-start.8
  361.5 5.9 %copy-start.1 = (bf16[2,5,256,640]{3,2,1,0:T(8,128)(2,1)S(1)}, bf16[2,5,256,640]{3,2,1,0:T(8,128)(2,1)}, u32[]{:S(2)}) copy-start(bf16[2,5,256,640]{3,2,1,0:T(8,128)(2,1)} %param.9) | copy-start | bytes 9830404

commit v2 on v1

v2 whole, which is shorter than its diff:
```python
import functools
import math

import jax
import jax.numpy as jnp
import numpy as np
from jax import lax
from jax.experimental import pallas as pl
from jax.experimental.pallas import tpu as pltpu
from jax.sharding import PartitionSpec as P

LANES = 128
PACK = 16


def bases(width, taps):
    length = -(-(width + taps) // (2 * PACK)) * 2 * PACK
    odd = 2 * np.arange(length // 2) + 1

    def wave(points):
        angle = np.pi / length * (points[:, None] * odd[None, :] % (2 * length))
        return np.concatenate([np.cos(angle), -np.sin(angle)], axis=1)

    forward = wave(np.arange(width + taps)).T
    inverse = 2.0 / length * wave(taps + np.arange(width))
    tap_basis = wave(np.arange(taps)).T
    return tuple(jnp.asarray(a, jnp.bfloat16) for a in (forward, inverse, tap_basis))


def gelu(values):
    return 0.5 * values * (1.0 + lax.erf(values * math.sqrt(0.5)))


def conv_kernel(*refs, windows, row_refs, counts):
    quad, forward, inverse, factors = refs[:4]
    sources = refs[4 : 4 + counts]
    out, ext, spectra, product = refs[4 + counts :]
    lanes = out.shape[2]
    width = out.shape[1]
    freqs = forward.shape[0] // 2
    every = len(row_refs)
    taps_r = factors.shape[0]
    for g, (_, pieces) in enumerate(row_refs):
        start = 0
        for source, at in pieces:
            size = sources[source].shape[1]
            ext[start : start + size, g * lanes : (g + 1) * lanes] = sources[source][at]
            start += size
    for g in range(0, every, 2):
        two = slice(g * lanes, (g + 2) * lanes)
        result = jnp.dot(forward[...], ext[:, two], preferred_element_type=jnp.float32)
        for j in range(2):
            spectra[g + j] = result[:, j * lanes : (j + 1) * lanes] * quad[row_refs[g + j][0]]

    def block(f, carry):
        start = pl.multiple_of(f * PACK, PACK)
        re = pl.ds(start, PACK)
        im = pl.ds(pl.multiple_of(freqs + start, PACK), PACK)
        fr = [factors[r, re] for r in range(taps_r)]
        fi = [factors[r, im] for r in range(taps_r)]
        h = 0
        for first, count in windows:
            xr = [spectra[first + g, re] for g in range(taps_r - 1)]
            xi = [spectra[first + g, im] for g in range(taps_r - 1)]
            for k in range(count):
                xr.append(spectra[first + k + taps_r - 1, re])
                xi.append(spectra[first + k + taps_r - 1, im])
                yr = xr[0] * fr[0] - xi[0] * fi[0]
                yi = xr[0] * fi[0] + xi[0] * fr[0]
                for r in range(1, taps_r):
                    yr = yr + (xr[r] * fr[r] - xi[r] * fi[r])
                    yi = yi + (xr[r] * fi[r] + xi[r] * fr[r])
                here = slice(h * lanes, (h + 1) * lanes)
                product[re, here] = yr.astype(product.dtype)
                product[im, here] = yi.astype(product.dtype)
                xr.pop(0)
                xi.pop(0)
                h += 1
        return carry

    lax.fori_loop(0, freqs // PACK, block, 0)
    own = [row_refs[first + taps_r // 2 + k][1] for first, count in windows for k in range(count)]
    for h in range(0, len(own), 2):
        two = slice(h * lanes, (h + 2) * lanes)
        conv = jnp.dot(inverse[...], product[:, two], preferred_element_type=jnp.float32)
        for j in range(2):
            source, at = own[h + j][1]
            value = sources[source][at].astype(jnp.float32)
            out[h + j] = (value + gelu(conv[:, j * lanes : (j + 1) * lanes])).astype(out.dtype)


def convolve(quad, tables, factors, sources, rows, windows):
    forward, inverse = tables
    taps_r, length, channels = factors.shape
    out_rows = sum(count for _, count in windows)
    width = inverse.shape[0]

    def block(array):
        return pl.BlockSpec((array.shape[0], array.shape[1], LANES), lambda i: (0, 0, i))

    def whole(array):
        return pl.BlockSpec(array.shape, lambda i: (0,) * array.ndim)

    out = jax.ShapeDtypeStruct((out_rows, width, channels), jnp.bfloat16)
    kernel = functools.partial(conv_kernel, windows=windows, row_refs=rows, counts=len(sources))
    return pl.pallas_call(
        kernel,
        grid=(channels // LANES,),
        out_shape=out,
        in_specs=[pl.BlockSpec(memory_space=pltpu.SMEM), whole(forward), whole(inverse), block(factors)]
        + [block(a) for a in sources],
        out_specs=block(out),
        scratch_shapes=[
            pltpu.VMEM((forward.shape[1], len(rows) * LANES), jnp.bfloat16),
            pltpu.VMEM((len(rows), length, LANES), jnp.float32),
            pltpu.VMEM((length, out_rows * LANES), jnp.bfloat16),
        ],
        compiler_params=pltpu.CompilerParams(vmem_limit_bytes=48 << 20),
        cost_estimate=pl.CostEstimate(
            flops=2 * channels * length * (len(rows) * forward.shape[1] + out_rows * width),
            bytes_accessed=2 * channels * (len(rows) * forward.shape[1] + 2 * taps_r * length),
            transcendentals=out_rows * channels * width,
        ),
        name="zonal_conv",
    )(quad, forward, inverse, factors, *sources)


def mlp_kernel(gain, w_in, w_out, mixed, *refs, half, kept):
    refs = refs[kept:]
    count, width, channels = mixed.shape
    values = mixed[...].reshape(count * width, channels).astype(jnp.float32)
    average = jnp.mean(values, axis=1, keepdims=True)
    centred = values - average
    variance = jnp.mean(jnp.square(centred), axis=1, keepdims=True)
    normed = (centred * lax.rsqrt(variance + 1e-05) * gain[...]).astype(jnp.bfloat16)
    total = values
    hidden_units = w_in.shape[1]
    step = math.gcd(hidden_units, 256)
    for f in range(0, hidden_units, step):
        hidden = jnp.dot(normed, w_in[:, f : f + step], preferred_element_type=jnp.float32)
        hidden = gelu(hidden).astype(jnp.bfloat16)
        total = total + jnp.dot(hidden, w_out[f : f + step], preferred_element_type=jnp.float32)
    result = total.astype(jnp.bfloat16).reshape(count, width, channels)
    refs[0][...] = result
    if half:
        refs[1][...] = result[:, :half]
        refs[2][...] = result[:, width - half :]


def mlp(gain, w_in, w_out, mixed, places, out_rows, edge, kept=None):
    _, width, channels = mixed.shape
    hidden_units = w_in.shape[1]
    steps = len(places)

    def place(kind):
        def index(i):
            at = places[0][kind]
            for k in range(1, steps):
                at = at + (places[k][kind] - places[k - 1][kind]) * (i >= k).astype(jnp.int32)
            return (at, 0, 0)

        return index

    def whole(array):
        return pl.BlockSpec(array.shape, lambda i: (0,) * array.ndim)

    def pair(lon, kind):
        return pl.BlockSpec((2, lon, channels), place(kind))

    lasts = [width] + ([edge, edge] if edge else [])
    extra = [] if kept is None else [kept]
    return pl.pallas_call(
        functools.partial(mlp_kernel, half=edge, kept=len(extra)),
        grid=(steps,),
        out_shape=[jax.ShapeDtypeStruct((out_rows, last, channels), jnp.bfloat16) for last in lasts],
        in_specs=[whole(gain), whole(w_in), whole(w_out), pair(width, 0)]
        + [pl.BlockSpec(memory_space=pl.ANY) for _ in extra],
        out_specs=[pair(last, 1) for last in lasts],
        input_output_aliases={4: 0} if extra else {},
        compiler_params=pltpu.CompilerParams(vmem_limit_bytes=48 << 20),
        cost_estimate=pl.CostEstimate(
            flops=8 * steps * width * channels * hidden_units,
            bytes_accessed=8 * steps * width * channels + 4 * channels * hidden_units,
            transcendentals=2 * steps * width * hidden_units,
        ),
        name="channel_mlp",
    )(gain, w_in, w_out, mixed, *extra)


def rotate(block, axis, hops):
    count = lax.axis_size(axis)
    return lax.ppermute(block, axis, [(i, (i + hops) % count) for i in range(count)])


def zonal_halos(first, last, half):
    width = first.shape[1]
    if half <= width:
        return rotate(last, "lon", 1), rotate(first, "lon", -1)
    lefts, rights, hops, missing = [], [], 1, half
    while missing > 0:
        take = min(width, missing)
        lefts.insert(0, rotate(last[:, width - take :], "lon", hops))
        rights.append(rotate(first[:, :take], "lon", -hops))
        missing -= take
        hops += 1
    return jnp.concatenate(lefts, axis=1), jnp.concatenate(rights, axis=1)


def step_rows(block, hops):
    count = lax.axis_size("lat")
    pairs = [(i, i + hops) for i in range(count) if 0 <= i + hops < count]
    return lax.ppermute(block, "lat", pairs)


def body(ocean_state, zonal_kernel, norm_gain, input_weight, output_weight):
    blocks, kernel_rows, taps, channels = zonal_kernel.shape
    _, rows, _, width = ocean_state.shape
    rim = kernel_rows // 2
    half = taps // 2
    edge = min(half, width)
    forward, inverse, tap_basis = bases(width, taps)
    total_rows = rows * lax.axis_size("lat")
    index = lax.axis_index("lat") * rows - rim + jnp.arange(rows + 2 * rim, dtype=jnp.int32)
    quad = jnp.sin(jnp.pi * (index.astype(jnp.float32) + 0.5) / total_rows)
    quad = jnp.where((index >= 0) & (index < total_rows), quad, 0.0)
    factors = [
        jnp.einsum("kt,rtc->rkc", tap_basis, zonal_kernel[layer], preferred_element_type=jnp.float32)
        for layer in range(blocks)
    ]
    gains = norm_gain.astype(jnp.float32)[:, None, :]

    groups = [
        list(range(rim)) + list(range(rows - rim, rows)),
        list(range(rim, 2 * rim)) + list(range(rows - 2 * rim, rows - rim)),
        list(range(2 * rim, rows - 2 * rim)),
    ]
    group_of = {row: (k, at) for k, members in enumerate(groups) for at, row in enumerate(members)}
    state = jnp.swapaxes(ocean_state[0], 1, 2)
    mids = [state]
    mid_of = {row: (0, row) for row in range(rows)}

    def pick(members):
        low = members[: len(members) // 2]
        high = members[len(members) // 2 :]
        return jnp.concatenate([state[low[0] : low[-1] + 1], state[high[0] : high[-1] + 1]], axis=0)

    firsts = [pick(members)[:, :edge] for members in groups]
    lasts = [pick(members)[:, width - edge :] for members in groups]
    out = None
    for layer in range(blocks):
        final = layer + 1 == blocks
        halos = [zonal_halos(firsts[k], lasts[k], half) for k in range(3)]
        left = [pair[0] for pair in halos]
        right = [pair[1] for pair in halos]

        def extended(start, stop):
            at = group_of[start][1]
            source, row = mid_of[start]
            count = stop - start
            return jnp.concatenate(
                [left[0][at : at + count], mids[source][row : row + count], right[0][at : at + count]], axis=1
            )

        low = step_rows(extended(rows - rim, rows), 1)
        high = step_rows(extended(0, rim), -1)

        def own(row, used_mids, used):
            k, at = group_of[row]
            source, mid_row = mid_of[row]
            n = len(used_mids)
            j = used.index(k)
            return (row + rim, [(n + j, at), (used_mids.index(source), mid_row), (n + len(used) + j, at)])

        def lat(number, at, place):
            return (place, [(number, at)])

        used = [0, 1]
        used_mids = sorted({mid_of[row][0] for k in used for row in groups[k]})
        sources = [mids[s] for s in used_mids] + [left[k] for k in used] + [right[k] for k in used] + [low, high]
        n = len(sources)
        outer = (
            [lat(n - 2, r, r) for r in range(rim)]
            + [own(row, used_mids, used) for row in range(2 * rim)]
            + [own(row, used_mids, used) for row in range(rows - 2 * rim, rows)]
            + [lat(n - 1, r, rows + rim + r) for r in range(rim)]
        )
        windows = [(0, rim), (3 * rim, rim)]
        mixed_outer = convolve(quad, (forward, inverse), factors[layer], sources, outer, windows)
        used = [0, 1, 2]
        used_mids = sorted({source for source, _ in mid_of.values()})
        sources = [mids[s] for s in used_mids] + left + right
        inner = [own(row, used_mids, used) for row in range(rows)]
        weights = (gains[layer], input_weight[layer], output_weight[layer])
        pairs = rows // 2
        if final:
            places = [(0, 0), (1, pairs - 1)]
            (out,) = mlp(*weights, mixed_outer, places, rows, 0)
            mixed_inner = convolve(quad, (forward, inverse), factors[layer], sources, inner, [(0, rows - 2 * rim)])
            places = [(p, p + 1) for p in range(pairs - 2)]
            (out,) = mlp(*weights, mixed_inner, places, rows, 0, kept=out)
        else:
            outs = [mlp(*weights, mixed_outer, [(0, 0), (1, 1)], 2 * rim, edge)]
            mixed_inner = convolve(quad, (forward, inverse), factors[layer], sources, inner, [(0, rows - 2 * rim)])
            outs.append(mlp(*weights, mixed_inner, [(0, 0), (pairs - 3, 1)], 2 * rim, edge))
            places = [(p + 1, p) for p in range(pairs - 4)]
            outs.append(mlp(*weights, mixed_inner, places, rows - 4 * rim, edge))
            mids = [o[0] for o in outs]
            mid_of = group_of
            firsts = [o[1] for o in outs]
            lasts = [o[2] for o in outs]
    return jnp.swapaxes(out, 1, 2)[None]


def solution(mesh):
    in_specs = (P(None, "lat", None, "lon"), P(), P(), P(), P())
    out_specs = P(None, "lat", None, "lon")
    return jax.shard_map(body, mesh=mesh, in_specs=in_specs, out_specs=out_specs, check_vma=False)
```

time: 371 us -> 264 us (0.71)
  waiting for transfers between devices: 179 us -> 109 us
  local copies, waits for them, and re-layouts: 56.1 us -> 9.98 us
  starting transfers between devices: 18.9 us -> 40.2 us
  Pallas kernels: 102 us -> 90.9 us
    ppermute x4 -> x12, waiting for transfers between devices: 145 us -> 95.6 us  [rotate(): lax.ppermute(block, axis, [(i, (i + hops) % count) for i in range(count)])]
    unnamed x21 -> x26, local copies, waits for them, and re-layouts: 20.8 us -> 0.07 us
    ppermute x4, waiting for transfers between devices: 33.5 us -> 13.3 us  [step_rows(): return lax.ppermute(block, 'lat', pairs)]
    squeeze x6 -> x2, local copies, waits for them, and re-layouts: 18.8 us -> 5.45 us  [body(): weights = (gains[layer], input_weight[layer], output_weight[layer])]
    ppermute x4 -> x12, starting transfers between devices: 7.65 us -> 20.9 us  [rotate(): lax.ppermute(block, axis, [(i, (i + hops) % count) for i in range(count)])]
    pallas_call x4 -> x9, Pallas kernels: 102 us -> 90.9 us  [the longest x4 58.7 us: convolve(): pl.pallas_call(kernel, grid=(channels // LANES,), out_shape=out, in_specs...]
    ppermute x4, starting transfers between devices: 11.3 us -> 19.2 us  [step_rows(): return lax.ppermute(block, 'lat', pairs)]
    slice x7 -> x8, local copies, waits for them, and re-layouts: 10.5 us -> 4.46 us  [the longest x1 2.5 us: body(): firsts = [pick(members)[:, :edge] for members in groups]]
  transfers between devices with their start and end apart: 8 -> 16, of which waited for: 7 -> 7; matrix products, arithmetic and copies ran while one was open for 11% -> 7% of each run, Pallas kernels for 0% -> 24%
where the time goes in v2:
time: 264 us; the launch traced here: 262 us
  waiting for transfers between devices  109 us (41%)
  Pallas kernels  90.9 us (34%)
  starting transfers between devices  40.2 us (15%)
  local copies, waits for them, and re-layouts  9.98 us (4%)
  matrix products  8.29 us (3%)
  other arithmetic  3.84 us (1%)
    ppermute x12, waiting for transfers between devices, rotate(): lax.ppermute(block, axis, [(i, (i + hops) % count) for i in range(count)])  95.6 us
    pallas_call x4, Pallas kernels, convolve(): pl.pallas_call(kernel, grid=(channels // LANES,), out_shape=out, in_specs...  58.7 us
    pallas_call x5, Pallas kernels, mlp(): pl.pallas_call(functools.partial(mlp_kernel, half=edge, kept=len(extra)),...  32.2 us
    ppermute x12, starting transfers between devices, rotate(): lax.ppermute(block, axis, [(i, (i + hops) % count) for i in range(count)])  20.9 us
    ppermute x4, starting transfers between devices, step_rows(): return lax.ppermute(block, 'lat', pairs)  19.2 us
    ppermute x4, waiting for transfers between devices, step_rows(): return lax.ppermute(block, 'lat', pairs)  13.3 us
    dot_general x2, matrix products, body(): jnp.einsum('kt,rtc->rkc', tap_basis, zonal_kernel[layer], preferred_eleme...  8.29 us
    squeeze x2, local copies, waits for them, and re-layouts, body(): weights = (gains[layer], input_weight[layer], output_weight[layer])  5.45 us
  transfers between devices with their start and end apart: 16, of which 7 were waited for; matrix products, arithmetic and copies ran while one was open for 7% of the time, Pallas kernels for 24%

profile of v2, /device:TPU:2, one launch (start us, length us, event | category | flops | bytes accessed | tf_op | source)
XLA Modules:
  0.0 262.3 jit_solution(17928070238971240602)
XLA Ops:
  0.0 2.5 fusion.6
  2.5 3.6 %collective-permute-start.7 = (bf16[4,128,640]{2,1,0:T(8,128)(2,1)}, bf16[4,128,640]{2,1,0:T(8,128)(2,1)S(1)}, u32[]{:S(2)}, u32[]{:S(2)}) collective-permute-start(bf16[4,128,640]{2,1,0:T(8,128)(2,1)} %get-tuple-element.27), channel_id=1, source_target_pairs={{0,3},{1,0},{2,1},{3,2},{4,7},{5,4},{6,5},{7,6},{8,11},{9,8},{10,9... | collective-permute-start | bytes 1966088 | tf_op jit(solution)/shard_map/ppermute | solution.py:192
  6.1 1.6 fusion.7
  7.7 0.0 copy-start.8
  7.8 0.1 pad_maximum_fusion.5
  7.9 0.5 collective-permute-start.2
  8.4 1.2 pad_maximum_fusion.4
  9.6 0.4 collective-permute-start.3
  10.0 1.6 collective-permute-start.1
  11.6 1.6 collective-permute-start
  13.2 1.9 slice_bitcast_fusion.1
  15.1 20.4 %collective-permute-done.2.refs_7_.refs_8_ = bf16[4,128,640]{2,1,0:T(8,128)(2,1)S(1)} collective-permute-done((bf16[4,128,640]{2,1,0:T(8,128)(2,1)S(1)}, bf16[4,128,640]{2,1,0:T(8,128)(2,1)S(1)}, u32[]{:S(2)}, u32[]{:S(2)}) %collective-permute-start.2) | collective-permute-done | bytes 655392 | tf_op jit(solution)/shard_map/ppermute | solution.py:192
  35.5 0.1 fusion.12
  35.6 41.8 %collective-permute-done.refs_5_ = bf16[4,128,640]{2,1,0:T(8,128)(2,1)S(1)} collective-permute-done((bf16[4,128,640]{2,1,0:T(8,128)(2,1)S(1)}, bf16[4,128,640]{2,1,0:T(8,128)(2,1)S(1)}, u32[]{:S(2)}, u32[]{:S(2)}) %collective-permute-start) | collective-permute-done | bytes 655392 | tf_op jit(solution)/shard_map/ppermute | solution.py:192
  77.4 0.1 fusion.11
  77.4 0.0 copy-start.9
  77.5 1.2 pad_maximum_fusion
  78.6 2.0 collective-permute-start.4
  80.7 1.1 pad_maximum_fusion.1
  81.8 3.8 %collective-permute-start.5 = (bf16[2,448,640]{2,1,0:T(8,128)(2,1)}, bf16[2,448,640]{2,1,0:T(8,128)(2,1)}, u32[]{:S(2)}, u32[]{:S(2)}) collective-permute-start(bf16[2,448,640]{2,1,0:T(8,128)(2,1)} %pad_maximum_fusion.1), channel_id=1, source_target_pairs={{4,0},{8,4},{12,8},{16,12},{20,16},{24,20},{28,24},{5,1},{9,5},{13... | collective-permute-start | bytes 3440648 | tf_op jit(solution)/shard_map/ppermute | solution.py:212
  85.6 3.4 %convolution_bitcast_fusion.refs_3_ = f32[5,448,640]{2,1,0:T(8,128)} fusion(bf16[448,256,1]{1,0,2:T(8,128)(2,1)S(1)} %copy-done.10, bf16[2,5,256,640]{3,2,1,0:T(8,128)(2,1)S(1)} %copy-done.9), kind=kOutput, calls=%fused_computation | convolution fusion | flops 734003200 | bytes 7602176 | tf_op jit(solution)/shard_map/kt,rtc->rkc/dot_general | solution.py:227
  89.0 0.0 copy-start
  89.0 0.0 copy-start.2
  89.0 3.5 %slice_bitcast_fusion = (bf16[1280,640]{1,0:T(8,128)(2,1)}, bf16[1280,640]{1,0:T(8,128)(2,1)S(1)}) fusion(bf16[2,1280,640]{2,1,0:T(8,128)(2,1)} %param.12), kind=kLoop, calls=%fused_computation.5 | loop fusion | bytes 6553600 | tf_op jit(solution)/shard_map/squeeze | solution.py:293
  92.6 0.0 collective-permute-done.3.refs_8_.refs_9_
  92.6 1.6 collective-permute-start.6
  94.2 0.0 copy-start.5
  94.2 0.0 collective-permute-done.1.refs_6_
  94.2 2.0 collective-permute-done.4.refs_9_
  96.2 11.3 %collective-permute-done.5.refs_10_ = bf16[2,448,640]{2,1,0:T(8,128)(2,1)} collective-permute-done((bf16[2,448,640]{2,1,0:T(8,128)(2,1)}, bf16[2,448,640]{2,1,0:T(8,128)(2,1)}, u32[]{:S(2)}, u32[]{:S(2)}) %collective-permute-start.5) | collective-permute-done | bytes 1146912 | tf_op jit(solution)/shard_map/ppermute | solution.py:212
  107.5 12.5 %zonal_conv.4.mixed = bf16[4,192,640]{2,1,0:T(8,128)(2,1)S(1)} custom-call(f32[16]{0:T(128)S(1)} %and_select_fusion.refs_0_, bf16[448,448]{1,0:T(8,128)(2,1)S(1)} %copy-done, bf16[192,448]{1,0:T(8,128)(2,1)S(1)} %copy-done.2, f32[5,448,640]{2,1,0:T(8,128)} %convolution_bitcast_fusion.refs_3_, bf16[12,192,640]{2,1,0:T(8,128)(2,1)} %bitcast.29, ...), custom_call_target="tpu_custom_call" | custom-call | flops 3523215360 | bytes 12615680 | tf_op jit(solution)/shard_map/zonal_conv/pallas_call | solution.py:106
  120.1 6.0 %channel_mlp.5 = (bf16[4,192,640]{2,1,0:T(8,128)(2,1)S(1)}, bf16[4,128,640]{2,1,0:T(8,128)(2,1)S(1)}, bf16[4,128,640]{2,1,0:T(8,128)(2,1)S(1)}) custom-call(f32[1,640]{1,0:T(1,128)S(1)} %get-tuple-element.47.gain, bf16[640,1280]{1,0:T(8,128)(2,1)S(1)} %copy-done.5, bf16[1280,640]{1,0:T(8,128)(2,1)} %get-tuple-element.23.w_out, ...), custom_call_target="tpu_custom_call" | custom-call | flops 2516582400 | bytes 5242880 | tf_op jit(solution)/shard_map/channel_mlp/pallas_call | solution.py:172
  126.0 1.7 collective-permute-start.8
  127.7 0.0 collective-permute-done.7.refs_10_
  127.7 0.0 collective-permute-done.6.refs_7_
  127.7 16.7 %zonal_conv.5.mixed = bf16[8,192,640]{2,1,0:T(8,128)(2,1)} custom-call(f32[16]{0:T(128)S(1)} %and_select_fusion.refs_0_, bf16[448,448]{1,0:T(8,128)(2,1)S(1)} %copy-done, bf16[192,448]{1,0:T(8,128)(2,1)S(1)} %copy-done.2, f32[5,448,640]{2,1,0:T(8,128)} %convolution_bitcast_fusion.refs_3_, bf16[12,192,640]{2,1,0:T(8,128)(2,1)} %bitcast.30, ...), custom_call_target="tpu_custom_call" | custom-call | flops 3963617280 | bytes 12615680 | tf_op jit(solution)/shard_map/zonal_conv/pallas_call | solution.py:106
  144.4 2.2 collective-permute-start.11
  146.6 5.6 %channel_mlp.7 = (bf16[4,192,640]{2,1,0:T(8,128)(2,1)S(1)}, bf16[4,128,640]{2,1,0:T(8,128)(2,1)S(1)}, bf16[4,128,640]{2,1,0:T(8,128)(2,1)S(1)}) custom-call(f32[1,640]{1,0:T(1,128)S(1)} %get-tuple-element.47.gain, bf16[640,1280]{1,0:T(8,128)(2,1)S(1)} %copy-done.5, bf16[1280,640]{1,0:T(8,128)(2,1)S(1)} %copy-done.6, bf16[8,192,640]{2,1,0:T(8,128)(2,1)} %zonal_conv.5.mixed), custom_call_target="tpu_custom_call" | custom-call | flops 2516582400 | bytes 5242880 | tf_op jit(solution)/shard_map/channel_mlp/pallas_call | solution.py:172
  152.2 0.1 collective-permute-start.10
  152.2 3.8 %collective-permute-start.13 = (bf16[4,128,640]{2,1,0:T(8,128)(2,1)S(1)}, bf16[4,128,640]{2,1,0:T(8,128)(2,1)S(1)}, u32[]{:S(2)}, u32[]{:S(2)}) collective-permute-start(bf16[4,128,640]{2,1,0:T(8,128)(2,1)S(1)} %get-tuple-element.22), channel_id=1, source_target_pairs={{0,3},{1,0},{2,1},{3,2},{4,7},{5,4},{6,5},{7,6},{8,11},{9,8},{10,9... | collective-permute-start | bytes 1966088 | tf_op jit(solution)/shard_map/ppermute | solution.py:192
  156.1 0.1 fusion.8
  156.1 0.0 collective-permute-done.8.refs_7_.refs_6_
  156.2 0.1 fusion.9
  156.2 5.2 %collective-permute-done.11.refs_10_.refs_8_ = bf16[4,128,640]{2,1,0:T(8,128)(2,1)S(1)} collective-permute-done((bf16[4,128,640]{2,1,0:T(8,128)(2,1)S(1)}, bf16[4,128,640]{2,1,0:T(8,128)(2,1)S(1)}, u32[]{:S(2)}, u32[]{:S(2)}) %collective-permute-start.11) | collective-permute-done | bytes 655392 | tf_op jit(solution)/shard_map/ppermute | solution.py:192
  161.5 0.1 fusion.10
  161.5 0.1 pad_maximum_fusion.2
  161.6 3.1 %collective-permute-start.14 = (bf16[2,448,640]{2,1,0:T(8,128)(2,1)S(1)}, bf16[2,448,640]{2,1,0:T(8,128)(2,1)}, u32[]{:S(2)}, u32[]{:S(2)}) collective-permute-start(bf16[2,448,640]{2,1,0:T(8,128)(2,1)S(1)} %pad_maximum_fusion.2), channel_id=1, source_target_pairs={{0,4},{4,8},{8,12},{12,16},{16,20},{20,24},{24,28},{1,5},{5,9},{9,... | collective-permute-start | bytes 3440648 | tf_op jit(solution)/shard_map/ppermute | solution.py:212
  164.8 0.1 pad_maximum_fusion.3
  164.9 10.3 %collective-permute-start.15 = (bf16[2,448,640]{2,1,0:T(8,128)(2,1)S(1)}, bf16[2,448,640]{2,1,0:T(8,128)(2,1)}, u32[]{:S(2)}, u32[]{:S(2)}) collective-permute-start(bf16[2,448,640]{2,1,0:T(8,128)(2,1)S(1)} %pad_maximum_fusion.3), channel_id=1, source_target_pairs={{4,0},{8,4},{12,8},{16,12},{20,16},{24,20},{28,24},{5,1},{9,5},{13... | collective-permute-start | bytes 3440648 | tf_op jit(solution)/shard_map/ppermute | solution.py:212
  175.2 5.6 %channel_mlp.6 = (bf16[4,192,640]{2,1,0:T(8,128)(2,1)S(1)}, bf16[4,128,640]{2,1,0:T(8,128)(2,1)S(1)}, bf16[4,128,640]{2,1,0:T(8,128)(2,1)S(1)}) custom-call(f32[1,640]{1,0:T(1,128)S(1)} %get-tuple-element.47.gain, bf16[640,1280]{1,0:T(8,128)(2,1)S(1)} %copy-done.5, bf16[1280,640]{1,0:T(8,128)(2,1)S(1)} %copy-done.6, bf16[8,192,640]{2,1,0:T(8,128)(2,1)} %zonal_conv.5.mixed), custom_call_target="tpu_custom_call" | custom-call | flops 2516582400 | bytes 5242880 | tf_op jit(solution)/shard_map/channel_mlp/pallas_call | solution.py:172
  180.8 0.0 copy-start.1
  180.8 1.0 collective-permute-start.9
  181.8 0.0 collective-permute-done.10.refs_9_
  181.8 2.9 %collective-permute-start.12 = (bf16[4,128,640]{2,1,0:T(8,128)(2,1)S(1)}, bf16[4,128,640]{2,1,0:T(8,128)(2,1)S(1)}, u32[]{:S(2)}, u32[]{:S(2)}) collective-permute-start(bf16[4,128,640]{2,1,0:T(8,128)(2,1)S(1)} %get-tuple-element.21), channel_id=1, source_target_pairs={{0,3},{1,0},{2,1},{3,2},{4,7},{5,4},{6,5},{7,6},{8,11},{9,8},{10,9... | collective-permute-start | bytes 1966088 | tf_op jit(solution)/shard_map/ppermute | solution.py:192
  184.7 4.9 %convolution_bitcast_fusion.1.refs_3_ = f32[5,448,640]{2,1,0:T(8,128)} fusion(bf16[448,256,1]{1,0,2:T(8,128)(2,1)S(1)} %copy-done.10, bf16[2,5,256,640]{3,2,1,0:T(8,128)(2,1)} %param.9), kind=kOutput, calls=%fused_computation.1 | convolution fusion | flops 734003200 | bytes 7602176 | tf_op jit(solution)/shard_map/kt,rtc->rkc/dot_general | solution.py:227
  189.5 0.0 collective-permute-done.13.refs_12_
  189.6 16.0 %collective-permute-done.9.refs_8_.refs_7_ = bf16[4,128,640]{2,1,0:T(8,128)(2,1)S(1)} collective-permute-done((bf16[4,128,640]{2,1,0:T(8,128)(2,1)S(1)}, bf16[4,128,640]{2,1,0:T(8,128)(2,1)S(1)}, u32[]{:S(2)}, u32[]{:S(2)}) %collective-permute-start.9) | collective-permute-done | bytes 655392 | tf_op jit(solution)/shard_map/ppermute | solution.py:192
  205.5 12.1 %collective-permute-done.12.refs_11_.refs_9_ = bf16[4,128,640]{2,1,0:T(8,128)(2,1)S(1)} collective-permute-done((bf16[4,128,640]{2,1,0:T(8,128)(2,1)S(1)}, bf16[4,128,640]{2,1,0:T(8,128)(2,1)S(1)}, u32[]{:S(2)}, u32[]{:S(2)}) %collective-permute-start.12) | collective-permute-done | bytes 655392 | tf_op jit(solution)/shard_map/ppermute | solution.py:192
  217.7 16.8 %zonal_conv.6.mixed = bf16[8,192,640]{2,1,0:T(8,128)(2,1)} custom-call(f32[16]{0:T(128)S(1)} %and_select_fusion.refs_0_, bf16[448,448]{1,0:T(8,128)(2,1)S(1)} %copy-done, bf16[192,448]{1,0:T(8,128)(2,1)S(1)} %copy-done.2, f32[5,448,640]{2,1,0:T(8,128)} %convolution_bitcast_fusion.1.refs_3_, bf16[4,192,640]{2,1,0:T(8,128)(2,1)S(1)} %get-tuple-element.14.refs_4_, ...), custom_call_target="tpu_custom_call" | custom-call | flops 3963617280 | bytes 12615680 | tf_op jit(solution)/shard_map/zonal_conv/pallas_call | solution.py:106
  234.4 0.0 collective-permute-done.14.refs_10_
  234.4 0.0 collective-permute-done.15.refs_11_
  234.5 12.7 %zonal_conv.7.mixed = bf16[4,192,640]{2,1,0:T(8,128)(2,1)S(1)} custom-call(f32[16]{0:T(128)S(1)} %and_select_fusion.refs_0_, bf16[448,448]{1,0:T(8,128)(2,1)S(1)} %copy-done, bf16[192,448]{1,0:T(8,128)(2,1)S(1)} %copy-done.2, f32[5,448,640]{2,1,0:T(8,128)} %convolution_bitcast_fusion.1.refs_3_, bf16[4,192,640]{2,1,0:T(8,128)(2,1)S(1)} %get-tuple-element.14.refs_4_, ...), custom_call_target="tpu_custom_call" | custom-call | flops 3523215360 | bytes 12615680 | tf_op jit(solution)/shard_map/zonal_conv/pallas_call | solution.py:106
  247.2 5.3 %channel_mlp.8.refs_0_ = bf16[12,192,640]{2,1,0:T(8,128)(2,1)} custom-call(f32[1,640]{1,0:T(1,128)S(1)} %get-tuple-element.48.gain, bf16[640,1280]{1,0:T(8,128)(2,1)S(1)} %copy-done.4, bf16[1280,640]{1,0:T(8,128)(2,1)S(1)} %get-tuple-element.24.w_out, bf16[4,192,640]{2,1,0:T(8,128)(2,1)S(1)} %zonal_conv.7.mixed), custom_call_target="tpu_custom_call" | custom-call | flops 2516582400 | bytes 5242880 | tf_op jit(solution)/shard_map/channel_mlp/pallas_call | solution.py:172
  252.5 9.8 %channel_mlp.9 = bf16[12,192,640]{2,1,0:T(8,128)(2,1)} custom-call(f32[1,640]{1,0:T(1,128)S(1)} %get-tuple-element.48.gain, bf16[640,1280]{1,0:T(8,128)(2,1)S(1)} %copy-done.4, bf16[1280,640]{1,0:T(8,128)(2,1)S(1)} %get-tuple-element.24.w_out, bf16[8,192,640]{2,1,0:T(8,128)(2,1)S(1)} %copy-done.3, ...), custom_call_target="tpu_custom_call", output_to_operand_aliasing={{}: (4, {})} | custom-call | flops 5033164800 | bytes 7208960 | tf_op jit(solution)/shard_map/channel_mlp/pallas_call | solution.py:172
  (22 shorter events, 0.1 us)
Async XLA Ops:
  2.5 125.2 %collective-permute-start.7 = (bf16[4,128,640]{2,1,0:T(8,128)(2,1)}, bf16[4,128,640]{2,1,0:T(8,128)(2,1)S(1)}, u32[]{:S(2)}, u32[]{:S(2)}) collective-permute-start(bf16[4,128,640]{2,1,0:T(8,128)(2,1)} %get-tuple-element.27), channel_id=1, source_target_pairs={{0,3},{1,0},{2,1},{3,2},{4,7},{5,4},{6,5},{7,6},{8,11},{9,8},{10,9... | collective-permute-start | bytes 1966088 | tf_op jit(solution)/shard_map/ppermute | solution.py:192
  7.7 5.4 %copy-start.8 = (bf16[2,640,1280]{2,1,0:T(8,128)(2,1)S(1)}, bf16[2,640,1280]{2,1,0:T(8,128)(2,1)}, u32[]{:S(2)}) copy-start(bf16[2,640,1280]{2,1,0:T(8,128)(2,1)} %param.11) | copy-start | bytes 9830404
  7.9 27.6 %collective-permute-start.2 = (bf16[4,128,640]{2,1,0:T(8,128)(2,1)S(1)}, bf16[4,128,640]{2,1,0:T(8,128)(2,1)S(1)}, u32[]{:S(2)}, u32[]{:S(2)}) collective-permute-start(bf16[4,128,640]{2,1,0:T(8,128)(2,1)S(1)} %get-tuple-element.37), channel_id=1, source_target_pairs={{0,3},{1,0},{2,1},{3,2},{4,7},{5,4},{6,5},{7,6},{8,11},{9,8},{10,9... | collective-permute-start | bytes 1966088 | tf_op jit(solution)/shard_map/ppermute | solution.py:192
  9.6 83.0 %collective-permute-start.3 = (bf16[4,128,640]{2,1,0:T(8,128)(2,1)}, bf16[4,128,640]{2,1,0:T(8,128)(2,1)S(1)}, u32[]{:S(2)}, u32[]{:S(2)}) collective-permute-start(bf16[4,128,640]{2,1,0:T(8,128)(2,1)} %get-tuple-element.35), channel_id=1, source_target_pairs={{0,3},{1,0},{2,1},{3,2},{4,7},{5,4},{6,5},{7,6},{8,11},{9,8},{10,9... | collective-permute-start | bytes 1966088 | tf_op jit(solution)/shard_map/ppermute | solution.py:192
  10.0 84.2 %collective-permute-start.1 = (bf16[4,128,640]{2,1,0:T(8,128)(2,1)}, bf16[4,128,640]{2,1,0:T(8,128)(2,1)S(1)}, u32[]{:S(2)}, u32[]{:S(2)}) collective-permute-start(bf16[4,128,640]{2,1,0:T(8,128)(2,1)} %get-tuple-element.36), channel_id=1, source_target_pairs={{0,1},{1,2},{2,3},{3,0},{4,5},{5,6},{6,7},{7,4},{8,9},{9,10},{10,1... | collective-permute-start | bytes 1966088 | tf_op jit(solution)/shard_map/ppermute | solution.py:192
  11.6 65.8 %collective-permute-start = (bf16[4,128,640]{2,1,0:T(8,128)(2,1)S(1)}, bf16[4,128,640]{2,1,0:T(8,128)(2,1)S(1)}, u32[]{:S(2)}, u32[]{:S(2)}) collective-permute-start(bf16[4,128,640]{2,1,0:T(8,128)(2,1)S(1)} %get-tuple-element.38), channel_id=1, source_target_pairs={{0,1},{1,2},{2,3},{3,0},{4,5},{5,6},{6,7},{7,4},{8,9},{9,10},{10,1... | collective-permute-start | bytes 1966088 | tf_op jit(solution)/shard_map/ppermute | solution.py:192
  77.4 8.1 %copy-start.9 = (bf16[2,5,256,640]{3,2,1,0:T(8,128)(2,1)S(1)}, bf16[2,5,256,640]{3,2,1,0:T(8,128)(2,1)}, u32[]{:S(2)}) copy-start(bf16[2,5,256,640]{3,2,1,0:T(8,128)(2,1)} %param.9) | copy-start | bytes 9830404
  78.6 6.9 %copy-start.10 = (bf16[448,256,1]{1,0,2:T(8,128)(2,1)S(1)}, bf16[448,256,1]{1,0,2:T(8,128)(2,1)}, u32[]{:S(2)}) copy-start(bf16[448,256,1]{1,0,2:T(8,128)(2,1)} %constant.34) | copy-start | bytes 688132
  78.6 17.6 %collective-permute-start.4 = (bf16[2,448,640]{2,1,0:T(8,128)(2,1)}, bf16[2,448,640]{2,1,0:T(8,128)(2,1)}, u32[]{:S(2)}, u32[]{:S(2)}) collective-permute-start(bf16[2,448,640]{2,1,0:T(8,128)(2,1)} %pad_maximum_fusion), channel_id=1, source_target_pairs={{0,4},{4,8},{8,12},{12,16},{16,20},{20,24},{24,28},{1,5},{5,9},{9,... | collective-permute-start | bytes 3440648 | tf_op jit(solution)/shard_map/ppermute | solution.py:212
  81.8 7.2 %copy-start.12 = (bf16[2,640]{1,0:T(2,128)(2,1)S(1)}, bf16[2,640]{1,0:T(2,128)(2,1)}, u32[]{:S(2)}) copy-start(bf16[2,640]{1,0:T(2,128)(2,1)} %param.10) | copy-start | bytes 7684
  81.8 25.8 %collective-permute-start.5 = (bf16[2,448,640]{2,1,0:T(8,128)(2,1)}, bf16[2,448,640]{2,1,0:T(8,128)(2,1)}, u32[]{:S(2)}, u32[]{:S(2)}) collective-permute-start(bf16[2,448,640]{2,1,0:T(8,128)(2,1)} %pad_maximum_fusion.1), channel_id=1, source_target_pairs={{4,0},{8,4},{12,8},{16,12},{20,16},{24,20},{28,24},{5,1},{9,5},{13... | collective-permute-start | bytes 3440648 | tf_op jit(solution)/shard_map/ppermute | solution.py:212
  89.0 3.5 %copy-start.11 = (bf16[4,128,640]{2,1,0:T(8,128)(2,1)S(1)}, bf16[4,128,640]{2,1,0:T(8,128)(2,1)}, u32[]{:S(2)}) copy-start(bf16[4,128,640]{2,1,0:T(8,128)(2,1)} %get-tuple-element.28) | copy-start | bytes 1966084
  89.0 18.5 %copy-start = (bf16[448,448]{1,0:T(8,128)(2,1)S(1)}, bf16[448,448]{1,0:T(8,128)(2,1)}, u32[]{:S(2)}) copy-start(bf16[448,448]{1,0:T(8,128)(2,1)} %constant.30.clone.refs_1_) | copy-start | bytes 1204228
  89.0 18.5 %copy-start.2 = (bf16[192,448]{1,0:T(8,128)(2,1)S(1)}, bf16[192,448]{1,0:T(8,128)(2,1)}, u32[]{:S(2)}) copy-start(bf16[192,448]{1,0:T(8,128)(2,1)} %constant.31.clone.refs_2_) | copy-start | bytes 516100
  92.6 35.2 %collective-permute-start.6 = (bf16[4,128,640]{2,1,0:T(8,128)(2,1)S(1)}, bf16[4,128,640]{2,1,0:T(8,128)(2,1)S(1)}, u32[]{:S(2)}, u32[]{:S(2)}) collective-permute-start(bf16[4,128,640]{2,1,0:T(8,128)(2,1)S(1)} %copy-done.11), channel_id=1, source_target_pairs={{0,1},{1,2},{2,3},{3,0},{4,5},{5,6},{6,7},{7,4},{8,9},{9,10},{10,1... | collective-permute-start | bytes 1966088 | tf_op jit(solution)/shard_map/ppermute | solution.py:192
  94.2 25.8 %copy-start.5 = (bf16[640,1280]{1,0:T(8,128)(2,1)S(1)}, bf16[640,1280]{1,0:T(8,128)(2,1)}, u32[]{:S(2)}) copy-start(bf16[640,1280]{1,0:T(8,128)(2,1)} %get-tuple-element.25.w_in) | copy-start | bytes 4915204
  126.0 20.6 %copy-start.6 = (bf16[1280,640]{1,0:T(8,128)(2,1)S(1)}, bf16[1280,640]{1,0:T(8,128)(2,1)}, u32[]{:S(2)}) copy-start(bf16[1280,640]{1,0:T(8,128)(2,1)} %get-tuple-element.23.w_out) | copy-start | bytes 4915204
  126.0 30.1 %collective-permute-start.8 = (bf16[4,128,640]{2,1,0:T(8,128)(2,1)S(1)}, bf16[4,128,640]{2,1,0:T(8,128)(2,1)S(1)}, u32[]{:S(2)}, u32[]{:S(2)}) collective-permute-start(bf16[4,128,640]{2,1,0:T(8,128)(2,1)S(1)} %get-tuple-element.17), channel_id=1, source_target_pairs={{0,1},{1,2},{2,3},{3,0},{4,5},{5,6},{6,7},{7,4},{8,9},{9,10},{10,1... | collective-permute-start | bytes 1966088 | tf_op jit(solution)/shard_map/ppermute | solution.py:192
  144.4 17.1 %collective-permute-start.11 = (bf16[4,128,640]{2,1,0:T(8,128)(2,1)S(1)}, bf16[4,128,640]{2,1,0:T(8,128)(2,1)S(1)}, u32[]{:S(2)}, u32[]{:S(2)}) collective-permute-start(bf16[4,128,640]{2,1,0:T(8,128)(2,1)S(1)} %get-tuple-element.20), channel_id=1, source_target_pairs={{0,3},{1,0},{2,1},{3,2},{4,7},{5,4},{6,5},{7,6},{8,11},{9,8},{10,9... | collective-permute-start | bytes 1966088 | tf_op jit(solution)/shard_map/ppermute | solution.py:192
  152.2 4.1 %copy-start.7 = (bf16[4,192,640]{2,1,0:T(8,128)(2,1)}, bf16[4,192,640]{2,1,0:T(8,128)(2,1)S(1)}, u32[]{:S(2)}) copy-start(bf16[4,192,640]{2,1,0:T(8,128)(2,1)S(1)} %get-tuple-element.16.refs_6_) | copy-start | bytes 2949124
  152.2 29.6 %collective-permute-start.10 = (bf16[4,128,640]{2,1,0:T(8,128)(2,1)S(1)}, bf16[4,128,640]{2,1,0:T(8,128)(2,1)S(1)}, u32[]{:S(2)}, u32[]{:S(2)}) collective-permute-start(bf16[4,128,640]{2,1,0:T(8,128)(2,1)S(1)} %get-tuple-element.19), channel_id=1, source_target_pairs={{0,1},{1,2},{2,3},{3,0},{4,5},{5,6},{6,7},{7,4},{8,9},{9,10},{10,1... | collective-permute-start | bytes 1966088 | tf_op jit(solution)/shard_map/ppermute | solution.py:192
  152.2 37.3 %collective-permute-start.13 = (bf16[4,128,640]{2,1,0:T(8,128)(2,1)S(1)}, bf16[4,128,640]{2,1,0:T(8,128)(2,1)S(1)}, u32[]{:S(2)}, u32[]{:S(2)}) collective-permute-start(bf16[4,128,640]{2,1,0:T(8,128)(2,1)S(1)} %get-tuple-element.22), channel_id=1, source_target_pairs={{0,3},{1,0},{2,1},{3,2},{4,7},{5,4},{6,5},{7,6},{8,11},{9,8},{10,9... | collective-permute-start | bytes 1966088 | tf_op jit(solution)/shard_map/ppermute | solution.py:192
  161.6 72.8 %collective-permute-start.14 = (bf16[2,448,640]{2,1,0:T(8,128)(2,1)S(1)}, bf16[2,448,640]{2,1,0:T(8,128)(2,1)}, u32[]{:S(2)}, u32[]{:S(2)}) collective-permute-start(bf16[2,448,640]{2,1,0:T(8,128)(2,1)S(1)} %pad_maximum_fusion.2), channel_id=1, source_target_pairs={{0,4},{4,8},{8,12},{12,16},{16,20},{20,24},{24,28},{1,5},{5,9},{9,... | collective-permute-start | bytes 3440648 | tf_op jit(solution)/shard_map/ppermute | solution.py:212
  164.9 69.6 %collective-permute-start.15 = (bf16[2,448,640]{2,1,0:T(8,128)(2,1)S(1)}, bf16[2,448,640]{2,1,0:T(8,128)(2,1)}, u32[]{:S(2)}, u32[]{:S(2)}) collective-permute-start(bf16[2,448,640]{2,1,0:T(8,128)(2,1)S(1)} %pad_maximum_fusion.3), channel_id=1, source_target_pairs={{4,0},{8,4},{12,8},{16,12},{20,16},{24,20},{28,24},{5,1},{9,5},{13... | collective-permute-start | bytes 3440648 | tf_op jit(solution)/shard_map/ppermute | solution.py:212
  180.8 8.8 %copy-start.1 = (bf16[4,192,640]{2,1,0:T(8,128)(2,1)}, bf16[4,192,640]{2,1,0:T(8,128)(2,1)S(1)}, u32[]{:S(2)}) copy-start(bf16[4,192,640]{2,1,0:T(8,128)(2,1)S(1)} %get-tuple-element.15.refs_5_) | copy-start | bytes 2949124
  180.8 24.8 %collective-permute-start.9 = (bf16[4,128,640]{2,1,0:T(8,128)(2,1)S(1)}, bf16[4,128,640]{2,1,0:T(8,128)(2,1)S(1)}, u32[]{:S(2)}, u32[]{:S(2)}) collective-permute-start(bf16[4,128,640]{2,1,0:T(8,128)(2,1)S(1)} %get-tuple-element.18), channel_id=1, source_target_pairs={{0,1},{1,2},{2,3},{3,0},{4,5},{5,6},{6,7},{7,4},{8,9},{9,10},{10,1... | collective-permute-start | bytes 1966088 | tf_op jit(solution)/shard_map/ppermute | solution.py:192
  181.8 35.9 %collective-permute-start.12 = (bf16[4,128,640]{2,1,0:T(8,128)(2,1)S(1)}, bf16[4,128,640]{2,1,0:T(8,128)(2,1)S(1)}, u32[]{:S(2)}, u32[]{:S(2)}) collective-permute-start(bf16[4,128,640]{2,1,0:T(8,128)(2,1)S(1)} %get-tuple-element.21), channel_id=1, source_target_pairs={{0,3},{1,0},{2,1},{3,2},{4,7},{5,4},{6,5},{7,6},{8,11},{9,8},{10,9... | collective-permute-start | bytes 1966088 | tf_op jit(solution)/shard_map/ppermute | solution.py:192
  234.4 12.7 %copy-start.4 = (bf16[640,1280]{1,0:T(8,128)(2,1)S(1)}, bf16[640,1280]{1,0:T(8,128)(2,1)}, u32[]{:S(2)}) copy-start(bf16[640,1280]{1,0:T(8,128)(2,1)} %get-tuple-element.26.w_in) | copy-start | bytes 4915204
  247.2 5.3 %copy-start.3 = (bf16[8,192,640]{2,1,0:T(8,128)(2,1)S(1)}, bf16[8,192,640]{2,1,0:T(8,128)(2,1)}, u32[]{:S(2)}) copy-start(bf16[8,192,640]{2,1,0:T(8,128)(2,1)} %zonal_conv.6.mixed) | copy-start | bytes 5898244

commit v3 on v2

--- a/solution.py
+++ b/solution.py
@@ -9,6 +9,7 @@
 from jax.experimental.pallas import tpu as pltpu
 from jax.sharding import PartitionSpec as P
 
+
 LANES = 128
 PACK = 16
 
@@ -36,7 +37,6 @@
     sources = refs[4 : 4 + counts]
     out, ext, spectra, product = refs[4 + counts :]
     lanes = out.shape[2]
-    width = out.shape[1]
     freqs = forward.shape[0] // 2
     every = len(row_refs)
     taps_r = factors.shape[0]
@@ -194,8 +194,6 @@
 
 def zonal_halos(first, last, half):
     width = first.shape[1]
-    if half <= width:
-        return rotate(last, "lon", 1), rotate(first, "lon", -1)
     lefts, rights, hops, missing = [], [], 1, half
     while missing > 0:
         take = min(width, missing)
@@ -203,6 +201,8 @@
         rights.append(rotate(first[:, :take], "lon", -hops))
         missing -= take
         hops += 1
+    if len(lefts) == 1:
+        return lefts[0], rights[0]
     return jnp.concatenate(lefts, axis=1), jnp.concatenate(rights, axis=1)
 
 
@@ -213,7 +213,7 @@
 
 
 def body(ocean_state, zonal_kernel, norm_gain, input_weight, output_weight):
-    blocks, kernel_rows, taps, channels = zonal_kernel.shape
+    blocks, kernel_rows, taps, _ = zonal_kernel.shape
     _, rows, _, width = ocean_state.shape
     rim = kernel_rows // 2
     half = taps // 2
@@ -285,22 +285,22 @@
             + [lat(n - 1, r, rows + rim + r) for r in range(rim)]
         )
         windows = [(0, rim), (3 * rim, rim)]
-        mixed_outer = convolve(quad, (forward, inverse), factors[layer], sources, outer, windows)
+        tables = (forward, inverse)
+        mixed_outer = convolve(quad, tables, factors[layer], sources, outer, windows)
         used = [0, 1, 2]
         used_mids = sorted({source for source, _ in mid_of.values()})
         sources = [mids[s] for s in used_mids] + left + right
         inner = [own(row, used_mids, used) for row in range(rows)]
         weights = (gains[layer], input_weight[layer], output_weight[layer])
         pairs = rows // 2
+        mixed_inner = convolve(quad, tables, factors[layer], sources, inner, [(0, rows - 2 * rim)])
         if final:
             places = [(0, 0), (1, pairs - 1)]
             (out,) = mlp(*weights, mixed_outer, places, rows, 0)
-            mixed_inner = convolve(quad, (forward, inverse), factors[layer], sources, inner, [(0, rows - 2 * rim)])
             places = [(p, p + 1) for p in range(pairs - 2)]
             (out,) = mlp(*weights, mixed_inner, places, rows, 0, kept=out)
         else:
             outs = [mlp(*weights, mixed_outer, [(0, 0), (1, 1)], 2 * rim, edge)]
-            mixed_inner = convolve(quad, (forward, inverse), factors[layer], sources, inner, [(0, rows - 2 * rim)])
             outs.append(mlp(*weights, mixed_inner, [(0, 0), (pairs - 3, 1)], 2 * rim, edge))
             places = [(p + 1, p) for p in range(pairs - 4)]
             outs.append(mlp(*weights, mixed_inner, places, rows - 4 * rim, edge))

time: 264 us -> 264 us (level)
  no operation moved by 1% of the time
where the time goes in v3:
time: 264 us; the launch traced here: 262 us
  waiting for transfers between devices  109 us (41%)
  Pallas kernels  90.9 us (34%)
  starting transfers between devices  40.2 us (15%)
  local copies, waits for them, and re-layouts  9.98 us (4%)
  matrix products  8.29 us (3%)
  other arithmetic  3.84 us (1%)
    ppermute x12, waiting for transfers between devices, rotate(): lax.ppermute(block, axis, [(i, (i + hops) % count) for i in range(count)])  95.6 us
    pallas_call x4, Pallas kernels, convolve(): pl.pallas_call(kernel, grid=(channels // LANES,), out_shape=out, in_specs...  58.7 us
    pallas_call x5, Pallas kernels, mlp(): pl.pallas_call(functools.partial(mlp_kernel, half=edge, kept=len(extra)),...  32.2 us
    ppermute x12, starting transfers between devices, rotate(): lax.ppermute(block, axis, [(i, (i + hops) % count) for i in range(count)])  20.9 us
    ppermute x4, starting transfers between devices, step_rows(): return lax.ppermute(block, 'lat', pairs)  19.2 us
    ppermute x4, waiting for transfers between devices, step_rows(): return lax.ppermute(block, 'lat', pairs)  13.3 us
    dot_general x2, matrix products, body(): jnp.einsum('kt,rtc->rkc', tap_basis, zonal_kernel[layer], preferred_eleme...  8.29 us
    squeeze x2, local copies, waits for them, and re-layouts, body(): weights = (gains[layer], input_weight[layer], output_weight[layer])  5.45 us
  transfers between devices with their start and end apart: 16, of which 7 were waited for; matrix products, arithmetic and copies ran while one was open for 7% of the time, Pallas kernels for 24%

profile of v3, /device:TPU:2, one launch (start us, length us, event | category | flops | bytes accessed | tf_op | source)
XLA Modules:
  0.0 262.3 jit_solution(17928070238971240602)
XLA Ops:
  0.0 2.5 fusion.6
  2.5 3.6 %collective-permute-start.7 = (bf16[4,128,640]{2,1,0:T(8,128)(2,1)}, bf16[4,128,640]{2,1,0:T(8,128)(2,1)S(1)}, u32[]{:S(2)}, u32[]{:S(2)}) collective-permute-start(bf16[4,128,640]{2,1,0:T(8,128)(2,1)} %get-tuple-element.27), channel_id=1, source_target_pairs={{0,3},{1,0},{2,1},{3,2},{4,7},{5,4},{6,5},{7,6},{8,11},{9,8},{10,9... | collective-permute-start | bytes 1966088 | tf_op jit(solution)/shard_map/ppermute | solution.py:192
  6.1 1.6 fusion.7
  7.7 0.0 copy-start.8
  7.8 0.1 pad_maximum_fusion.5
  7.9 0.5 collective-permute-start.2
  8.4 1.2 pad_maximum_fusion.4
  9.6 0.4 collective-permute-start.3
  10.0 1.6 collective-permute-start.1
  11.6 1.6 collective-permute-start
  13.2 1.9 slice_bitcast_fusion.1
  15.1 20.4 %collective-permute-done.2.refs_7_.refs_8_ = bf16[4,128,640]{2,1,0:T(8,128)(2,1)S(1)} collective-permute-done((bf16[4,128,640]{2,1,0:T(8,128)(2,1)S(1)}, bf16[4,128,640]{2,1,0:T(8,128)(2,1)S(1)}, u32[]{:S(2)}, u32[]{:S(2)}) %collective-permute-start.2) | collective-permute-done | bytes 655392 | tf_op jit(solution)/shard_map/ppermute | solution.py:192
  35.5 0.1 fusion.12
  35.6 41.8 %collective-permute-done.refs_5_ = bf16[4,128,640]{2,1,0:T(8,128)(2,1)S(1)} collective-permute-done((bf16[4,128,640]{2,1,0:T(8,128)(2,1)S(1)}, bf16[4,128,640]{2,1,0:T(8,128)(2,1)S(1)}, u32[]{:S(2)}, u32[]{:S(2)}) %collective-permute-start) | collective-permute-done | bytes 655392 | tf_op jit(solution)/shard_map/ppermute | solution.py:192
  77.4 0.1 fusion.11
  77.4 0.0 copy-start.9
  77.5 1.2 pad_maximum_fusion
  78.6 2.0 collective-permute-start.4
  80.7 1.1 pad_maximum_fusion.1
  81.8 3.8 %collective-permute-start.5 = (bf16[2,448,640]{2,1,0:T(8,128)(2,1)}, bf16[2,448,640]{2,1,0:T(8,128)(2,1)}, u32[]{:S(2)}, u32[]{:S(2)}) collective-permute-start(bf16[2,448,640]{2,1,0:T(8,128)(2,1)} %pad_maximum_fusion.1), channel_id=1, source_target_pairs={{4,0},{8,4},{12,8},{16,12},{20,16},{24,20},{28,24},{5,1},{9,5},{13... | collective-permute-start | bytes 3440648 | tf_op jit(solution)/shard_map/ppermute | solution.py:212
  85.6 3.4 %convolution_bitcast_fusion.refs_3_ = f32[5,448,640]{2,1,0:T(8,128)} fusion(bf16[448,256,1]{1,0,2:T(8,128)(2,1)S(1)} %copy-done.10, bf16[2,5,256,640]{3,2,1,0:T(8,128)(2,1)S(1)} %copy-done.9), kind=kOutput, calls=%fused_computation | convolution fusion | flops 734003200 | bytes 7602176 | tf_op jit(solution)/shard_map/kt,rtc->rkc/dot_general | solution.py:227
  89.0 0.0 copy-start
  89.0 0.0 copy-start.2
  89.0 3.5 %slice_bitcast_fusion = (bf16[1280,640]{1,0:T(8,128)(2,1)}, bf16[1280,640]{1,0:T(8,128)(2,1)S(1)}) fusion(bf16[2,1280,640]{2,1,0:T(8,128)(2,1)} %param.12), kind=kLoop, calls=%fused_computation.5 | loop fusion | bytes 6553600 | tf_op jit(solution)/shard_map/squeeze | solution.py:294
  92.6 0.0 collective-permute-done.3.refs_8_.refs_9_
  92.6 1.6 collective-permute-start.6
  94.2 0.0 copy-start.5
  94.2 0.0 collective-permute-done.1.refs_6_
  94.2 2.0 collective-permute-done.4.refs_9_
  96.2 11.3 %collective-permute-done.5.refs_10_ = bf16[2,448,640]{2,1,0:T(8,128)(2,1)} collective-permute-done((bf16[2,448,640]{2,1,0:T(8,128)(2,1)}, bf16[2,448,640]{2,1,0:T(8,128)(2,1)}, u32[]{:S(2)}, u32[]{:S(2)}) %collective-permute-start.5) | collective-permute-done | bytes 1146912 | tf_op jit(solution)/shard_map/ppermute | solution.py:212
  107.5 12.5 %zonal_conv.4.mixed = bf16[4,192,640]{2,1,0:T(8,128)(2,1)S(1)} custom-call(f32[16]{0:T(128)S(1)} %and_select_fusion.refs_0_, bf16[448,448]{1,0:T(8,128)(2,1)S(1)} %copy-done, bf16[192,448]{1,0:T(8,128)(2,1)S(1)} %copy-done.2, f32[5,448,640]{2,1,0:T(8,128)} %convolution_bitcast_fusion.refs_3_, bf16[12,192,640]{2,1,0:T(8,128)(2,1)} %bitcast.29, ...), custom_call_target="tpu_custom_call" | custom-call | flops 3523215360 | bytes 12615680 | tf_op jit(solution)/shard_map/zonal_conv/pallas_call | solution.py:106
  120.1 6.0 %channel_mlp.5 = (bf16[4,192,640]{2,1,0:T(8,128)(2,1)S(1)}, bf16[4,128,640]{2,1,0:T(8,128)(2,1)S(1)}, bf16[4,128,640]{2,1,0:T(8,128)(2,1)S(1)}) custom-call(f32[1,640]{1,0:T(1,128)S(1)} %get-tuple-element.47.gain, bf16[640,1280]{1,0:T(8,128)(2,1)S(1)} %copy-done.5, bf16[1280,640]{1,0:T(8,128)(2,1)} %get-tuple-element.23.w_out, ...), custom_call_target="tpu_custom_call" | custom-call | flops 2516582400 | bytes 5242880 | tf_op jit(solution)/shard_map/channel_mlp/pallas_call | solution.py:172
  126.0 1.7 collective-permute-start.8
  127.7 0.0 collective-permute-done.7.refs_10_
  127.7 0.0 collective-permute-done.6.refs_7_
  127.7 16.7 %zonal_conv.5.mixed = bf16[8,192,640]{2,1,0:T(8,128)(2,1)} custom-call(f32[16]{0:T(128)S(1)} %and_select_fusion.refs_0_, bf16[448,448]{1,0:T(8,128)(2,1)S(1)} %copy-done, bf16[192,448]{1,0:T(8,128)(2,1)S(1)} %copy-done.2, f32[5,448,640]{2,1,0:T(8,128)} %convolution_bitcast_fusion.refs_3_, bf16[12,192,640]{2,1,0:T(8,128)(2,1)} %bitcast.30, ...), custom_call_target="tpu_custom_call" | custom-call | flops 3963617280 | bytes 12615680 | tf_op jit(solution)/shard_map/zonal_conv/pallas_call | solution.py:106
  144.4 2.2 collective-permute-start.11
  146.6 5.6 %channel_mlp.7 = (bf16[4,192,640]{2,1,0:T(8,128)(2,1)S(1)}, bf16[4,128,640]{2,1,0:T(8,128)(2,1)S(1)}, bf16[4,128,640]{2,1,0:T(8,128)(2,1)S(1)}) custom-call(f32[1,640]{1,0:T(1,128)S(1)} %get-tuple-element.47.gain, bf16[640,1280]{1,0:T(8,128)(2,1)S(1)} %copy-done.5, bf16[1280,640]{1,0:T(8,128)(2,1)S(1)} %copy-done.6, bf16[8,192,640]{2,1,0:T(8,128)(2,1)} %zonal_conv.5.mixed), custom_call_target="tpu_custom_call" | custom-call | flops 2516582400 | bytes 5242880 | tf_op jit(solution)/shard_map/channel_mlp/pallas_call | solution.py:172
  152.2 0.1 collective-permute-start.10
  152.2 3.8 %collective-permute-start.13 = (bf16[4,128,640]{2,1,0:T(8,128)(2,1)S(1)}, bf16[4,128,640]{2,1,0:T(8,128)(2,1)S(1)}, u32[]{:S(2)}, u32[]{:S(2)}) collective-permute-start(bf16[4,128,640]{2,1,0:T(8,128)(2,1)S(1)} %get-tuple-element.22), channel_id=1, source_target_pairs={{0,3},{1,0},{2,1},{3,2},{4,7},{5,4},{6,5},{7,6},{8,11},{9,8},{10,9... | collective-permute-start | bytes 1966088 | tf_op jit(solution)/shard_map/ppermute | solution.py:192
  156.1 0.1 fusion.8
  156.1 0.0 collective-permute-done.8.refs_7_.refs_6_
  156.2 0.1 fusion.9
  156.2 5.2 %collective-permute-done.11.refs_10_.refs_8_ = bf16[4,128,640]{2,1,0:T(8,128)(2,1)S(1)} collective-permute-done((bf16[4,128,640]{2,1,0:T(8,128)(2,1)S(1)}, bf16[4,128,640]{2,1,0:T(8,128)(2,1)S(1)}, u32[]{:S(2)}, u32[]{:S(2)}) %collective-permute-start.11) | collective-permute-done | bytes 655392 | tf_op jit(solution)/shard_map/ppermute | solution.py:192
  161.5 0.1 fusion.10
  161.5 0.1 pad_maximum_fusion.2
  161.6 3.1 %collective-permute-start.14 = (bf16[2,448,640]{2,1,0:T(8,128)(2,1)S(1)}, bf16[2,448,640]{2,1,0:T(8,128)(2,1)}, u32[]{:S(2)}, u32[]{:S(2)}) collective-permute-start(bf16[2,448,640]{2,1,0:T(8,128)(2,1)S(1)} %pad_maximum_fusion.2), channel_id=1, source_target_pairs={{0,4},{4,8},{8,12},{12,16},{16,20},{20,24},{24,28},{1,5},{5,9},{9,... | collective-permute-start | bytes 3440648 | tf_op jit(solution)/shard_map/ppermute | solution.py:212
  164.8 0.1 pad_maximum_fusion.3
  164.9 10.3 %collective-permute-start.15 = (bf16[2,448,640]{2,1,0:T(8,128)(2,1)S(1)}, bf16[2,448,640]{2,1,0:T(8,128)(2,1)}, u32[]{:S(2)}, u32[]{:S(2)}) collective-permute-start(bf16[2,448,640]{2,1,0:T(8,128)(2,1)S(1)} %pad_maximum_fusion.3), channel_id=1, source_target_pairs={{4,0},{8,4},{12,8},{16,12},{20,16},{24,20},{28,24},{5,1},{9,5},{13... | collective-permute-start | bytes 3440648 | tf_op jit(solution)/shard_map/ppermute | solution.py:212
  175.2 5.6 %channel_mlp.6 = (bf16[4,192,640]{2,1,0:T(8,128)(2,1)S(1)}, bf16[4,128,640]{2,1,0:T(8,128)(2,1)S(1)}, bf16[4,128,640]{2,1,0:T(8,128)(2,1)S(1)}) custom-call(f32[1,640]{1,0:T(1,128)S(1)} %get-tuple-element.47.gain, bf16[640,1280]{1,0:T(8,128)(2,1)S(1)} %copy-done.5, bf16[1280,640]{1,0:T(8,128)(2,1)S(1)} %copy-done.6, bf16[8,192,640]{2,1,0:T(8,128)(2,1)} %zonal_conv.5.mixed), custom_call_target="tpu_custom_call" | custom-call | flops 2516582400 | bytes 5242880 | tf_op jit(solution)/shard_map/channel_mlp/pallas_call | solution.py:172
  180.8 0.0 copy-start.1
  180.8 1.0 collective-permute-start.9
  181.8 0.0 collective-permute-done.10.refs_9_
  181.8 2.9 %collective-permute-start.12 = (bf16[4,128,640]{2,1,0:T(8,128)(2,1)S(1)}, bf16[4,128,640]{2,1,0:T(8,128)(2,1)S(1)}, u32[]{:S(2)}, u32[]{:S(2)}) collective-permute-start(bf16[4,128,640]{2,1,0:T(8,128)(2,1)S(1)} %get-tuple-element.21), channel_id=1, source_target_pairs={{0,3},{1,0},{2,1},{3,2},{4,7},{5,4},{6,5},{7,6},{8,11},{9,8},{10,9... | collective-permute-start | bytes 1966088 | tf_op jit(solution)/shard_map/ppermute | solution.py:192
  184.7 4.9 %convolution_bitcast_fusion.1.refs_3_ = f32[5,448,640]{2,1,0:T(8,128)} fusion(bf16[448,256,1]{1,0,2:T(8,128)(2,1)S(1)} %copy-done.10, bf16[2,5,256,640]{3,2,1,0:T(8,128)(2,1)} %param.9), kind=kOutput, calls=%fused_computation.1 | convolution fusion | flops 734003200 | bytes 7602176 | tf_op jit(solution)/shard_map/kt,rtc->rkc/dot_general | solution.py:227
  189.5 0.0 collective-permute-done.13.refs_12_
  189.6 16.0 %collective-permute-done.9.refs_8_.refs_7_ = bf16[4,128,640]{2,1,0:T(8,128)(2,1)S(1)} collective-permute-done((bf16[4,128,640]{2,1,0:T(8,128)(2,1)S(1)}, bf16[4,128,640]{2,1,0:T(8,128)(2,1)S(1)}, u32[]{:S(2)}, u32[]{:S(2)}) %collective-permute-start.9) | collective-permute-done | bytes 655392 | tf_op jit(solution)/shard_map/ppermute | solution.py:192
  205.5 12.1 %collective-permute-done.12.refs_11_.refs_9_ = bf16[4,128,640]{2,1,0:T(8,128)(2,1)S(1)} collective-permute-done((bf16[4,128,640]{2,1,0:T(8,128)(2,1)S(1)}, bf16[4,128,640]{2,1,0:T(8,128)(2,1)S(1)}, u32[]{:S(2)}, u32[]{:S(2)}) %collective-permute-start.12) | collective-permute-done | bytes 655392 | tf_op jit(solution)/shard_map/ppermute | solution.py:192
  217.7 16.8 %zonal_conv.6.mixed = bf16[8,192,640]{2,1,0:T(8,128)(2,1)} custom-call(f32[16]{0:T(128)S(1)} %and_select_fusion.refs_0_, bf16[448,448]{1,0:T(8,128)(2,1)S(1)} %copy-done, bf16[192,448]{1,0:T(8,128)(2,1)S(1)} %copy-done.2, f32[5,448,640]{2,1,0:T(8,128)} %convolution_bitcast_fusion.1.refs_3_, bf16[4,192,640]{2,1,0:T(8,128)(2,1)S(1)} %get-tuple-element.14.refs_4_, ...), custom_call_target="tpu_custom_call" | custom-call | flops 3963617280 | bytes 12615680 | tf_op jit(solution)/shard_map/zonal_conv/pallas_call | solution.py:106
  234.4 0.0 collective-permute-done.14.refs_10_
  234.4 0.0 collective-permute-done.15.refs_11_
  234.5 12.7 %zonal_conv.7.mixed = bf16[4,192,640]{2,1,0:T(8,128)(2,1)S(1)} custom-call(f32[16]{0:T(128)S(1)} %and_select_fusion.refs_0_, bf16[448,448]{1,0:T(8,128)(2,1)S(1)} %copy-done, bf16[192,448]{1,0:T(8,128)(2,1)S(1)} %copy-done.2, f32[5,448,640]{2,1,0:T(8,128)} %convolution_bitcast_fusion.1.refs_3_, bf16[4,192,640]{2,1,0:T(8,128)(2,1)S(1)} %get-tuple-element.14.refs_4_, ...), custom_call_target="tpu_custom_call" | custom-call | flops 3523215360 | bytes 12615680 | tf_op jit(solution)/shard_map/zonal_conv/pallas_call | solution.py:106
  247.2 5.3 %channel_mlp.8.refs_0_ = bf16[12,192,640]{2,1,0:T(8,128)(2,1)} custom-call(f32[1,640]{1,0:T(1,128)S(1)} %get-tuple-element.48.gain, bf16[640,1280]{1,0:T(8,128)(2,1)S(1)} %copy-done.4, bf16[1280,640]{1,0:T(8,128)(2,1)S(1)} %get-tuple-element.24.w_out, bf16[4,192,640]{2,1,0:T(8,128)(2,1)S(1)} %zonal_conv.7.mixed), custom_call_target="tpu_custom_call" | custom-call | flops 2516582400 | bytes 5242880 | tf_op jit(solution)/shard_map/channel_mlp/pallas_call | solution.py:172
  252.5 9.8 %channel_mlp.9 = bf16[12,192,640]{2,1,0:T(8,128)(2,1)} custom-call(f32[1,640]{1,0:T(1,128)S(1)} %get-tuple-element.48.gain, bf16[640,1280]{1,0:T(8,128)(2,1)S(1)} %copy-done.4, bf16[1280,640]{1,0:T(8,128)(2,1)S(1)} %get-tuple-element.24.w_out, bf16[8,192,640]{2,1,0:T(8,128)(2,1)S(1)} %copy-done.3, ...), custom_call_target="tpu_custom_call", output_to_operand_aliasing={{}: (4, {})} | custom-call | flops 5033164800 | bytes 7208960 | tf_op jit(solution)/shard_map/channel_mlp/pallas_call | solution.py:172
  (22 shorter events, 0.1 us)
Async XLA Ops:
  2.5 125.2 %collective-permute-start.7 = (bf16[4,128,640]{2,1,0:T(8,128)(2,1)}, bf16[4,128,640]{2,1,0:T(8,128)(2,1)S(1)}, u32[]{:S(2)}, u32[]{:S(2)}) collective-permute-start(bf16[4,128,640]{2,1,0:T(8,128)(2,1)} %get-tuple-element.27), channel_id=1, source_target_pairs={{0,3},{1,0},{2,1},{3,2},{4,7},{5,4},{6,5},{7,6},{8,11},{9,8},{10,9... | collective-permute-start | bytes 1966088 | tf_op jit(solution)/shard_map/ppermute | solution.py:192
  7.7 5.4 %copy-start.8 = (bf16[2,640,1280]{2,1,0:T(8,128)(2,1)S(1)}, bf16[2,640,1280]{2,1,0:T(8,128)(2,1)}, u32[]{:S(2)}) copy-start(bf16[2,640,1280]{2,1,0:T(8,128)(2,1)} %param.11) | copy-start | bytes 9830404
  7.9 27.6 %collective-permute-start.2 = (bf16[4,128,640]{2,1,0:T(8,128)(2,1)S(1)}, bf16[4,128,640]{2,1,0:T(8,128)(2,1)S(1)}, u32[]{:S(2)}, u32[]{:S(2)}) collective-permute-start(bf16[4,128,640]{2,1,0:T(8,128)(2,1)S(1)} %get-tuple-element.37), channel_id=1, source_target_pairs={{0,3},{1,0},{2,1},{3,2},{4,7},{5,4},{6,5},{7,6},{8,11},{9,8},{10,9... | collective-permute-start | bytes 1966088 | tf_op jit(solution)/shard_map/ppermute | solution.py:192
  9.6 83.0 %collective-permute-start.3 = (bf16[4,128,640]{2,1,0:T(8,128)(2,1)}, bf16[4,128,640]{2,1,0:T(8,128)(2,1)S(1)}, u32[]{:S(2)}, u32[]{:S(2)}) collective-permute-start(bf16[4,128,640]{2,1,0:T(8,128)(2,1)} %get-tuple-element.35), channel_id=1, source_target_pairs={{0,3},{1,0},{2,1},{3,2},{4,7},{5,4},{6,5},{7,6},{8,11},{9,8},{10,9... | collective-permute-start | bytes 1966088 | tf_op jit(solution)/shard_map/ppermute | solution.py:192
  10.0 84.2 %collective-permute-start.1 = (bf16[4,128,640]{2,1,0:T(8,128)(2,1)}, bf16[4,128,640]{2,1,0:T(8,128)(2,1)S(1)}, u32[]{:S(2)}, u32[]{:S(2)}) collective-permute-start(bf16[4,128,640]{2,1,0:T(8,128)(2,1)} %get-tuple-element.36), channel_id=1, source_target_pairs={{0,1},{1,2},{2,3},{3,0},{4,5},{5,6},{6,7},{7,4},{8,9},{9,10},{10,1... | collective-permute-start | bytes 1966088 | tf_op jit(solution)/shard_map/ppermute | solution.py:192
  11.6 65.8 %collective-permute-start = (bf16[4,128,640]{2,1,0:T(8,128)(2,1)S(1)}, bf16[4,128,640]{2,1,0:T(8,128)(2,1)S(1)}, u32[]{:S(2)}, u32[]{:S(2)}) collective-permute-start(bf16[4,128,640]{2,1,0:T(8,128)(2,1)S(1)} %get-tuple-element.38), channel_id=1, source_target_pairs={{0,1},{1,2},{2,3},{3,0},{4,5},{5,6},{6,7},{7,4},{8,9},{9,10},{10,1... | collective-permute-start | bytes 1966088 | tf_op jit(solution)/shard_map/ppermute | solution.py:192
  77.4 8.1 %copy-start.9 = (bf16[2,5,256,640]{3,2,1,0:T(8,128)(2,1)S(1)}, bf16[2,5,256,640]{3,2,1,0:T(8,128)(2,1)}, u32[]{:S(2)}) copy-start(bf16[2,5,256,640]{3,2,1,0:T(8,128)(2,1)} %param.9) | copy-start | bytes 9830404
  78.6 6.9 %copy-start.10 = (bf16[448,256,1]{1,0,2:T(8,128)(2,1)S(1)}, bf16[448,256,1]{1,0,2:T(8,128)(2,1)}, u32[]{:S(2)}) copy-start(bf16[448,256,1]{1,0,2:T(8,128)(2,1)} %constant.34) | copy-start | bytes 688132
  78.6 17.6 %collective-permute-start.4 = (bf16[2,448,640]{2,1,0:T(8,128)(2,1)}, bf16[2,448,640]{2,1,0:T(8,128)(2,1)}, u32[]{:S(2)}, u32[]{:S(2)}) collective-permute-start(bf16[2,448,640]{2,1,0:T(8,128)(2,1)} %pad_maximum_fusion), channel_id=1, source_target_pairs={{0,4},{4,8},{8,12},{12,16},{16,20},{20,24},{24,28},{1,5},{5,9},{9,... | collective-permute-start | bytes 3440648 | tf_op jit(solution)/shard_map/ppermute | solution.py:212
  81.8 7.2 %copy-start.12 = (bf16[2,640]{1,0:T(2,128)(2,1)S(1)}, bf16[2,640]{1,0:T(2,128)(2,1)}, u32[]{:S(2)}) copy-start(bf16[2,640]{1,0:T(2,128)(2,1)} %param.10) | copy-start | bytes 7684
  81.8 25.8 %collective-permute-start.5 = (bf16[2,448,640]{2,1,0:T(8,128)(2,1)}, bf16[2,448,640]{2,1,0:T(8,128)(2,1)}, u32[]{:S(2)}, u32[]{:S(2)}) collective-permute-start(bf16[2,448,640]{2,1,0:T(8,128)(2,1)} %pad_maximum_fusion.1), channel_id=1, source_target_pairs={{4,0},{8,4},{12,8},{16,12},{20,16},{24,20},{28,24},{5,1},{9,5},{13... | collective-permute-start | bytes 3440648 | tf_op jit(solution)/shard_map/ppermute | solution.py:212
  89.0 3.5 %copy-start.11 = (bf16[4,128,640]{2,1,0:T(8,128)(2,1)S(1)}, bf16[4,128,640]{2,1,0:T(8,128)(2,1)}, u32[]{:S(2)}) copy-start(bf16[4,128,640]{2,1,0:T(8,128)(2,1)} %get-tuple-element.28) | copy-start | bytes 1966084
  89.0 18.5 %copy-start = (bf16[448,448]{1,0:T(8,128)(2,1)S(1)}, bf16[448,448]{1,0:T(8,128)(2,1)}, u32[]{:S(2)}) copy-start(bf16[448,448]{1,0:T(8,128)(2,1)} %constant.30.clone.refs_1_) | copy-start | bytes 1204228
  89.0 18.5 %copy-start.2 = (bf16[192,448]{1,0:T(8,128)(2,1)S(1)}, bf16[192,448]{1,0:T(8,128)(2,1)}, u32[]{:S(2)}) copy-start(bf16[192,448]{1,0:T(8,128)(2,1)} %constant.31.clone.refs_2_) | copy-start | bytes 516100
  92.6 35.2 %collective-permute-start.6 = (bf16[4,128,640]{2,1,0:T(8,128)(2,1)S(1)}, bf16[4,128,640]{2,1,0:T(8,128)(2,1)S(1)}, u32[]{:S(2)}, u32[]{:S(2)}) collective-permute-start(bf16[4,128,640]{2,1,0:T(8,128)(2,1)S(1)} %copy-done.11), channel_id=1, source_target_pairs={{0,1},{1,2},{2,3},{3,0},{4,5},{5,6},{6,7},{7,4},{8,9},{9,10},{10,1... | collective-permute-start | bytes 1966088 | tf_op jit(solution)/shard_map/ppermute | solution.py:192
  94.2 25.8 %copy-start.5 = (bf16[640,1280]{1,0:T(8,128)(2,1)S(1)}, bf16[640,1280]{1,0:T(8,128)(2,1)}, u32[]{:S(2)}) copy-start(bf16[640,1280]{1,0:T(8,128)(2,1)} %get-tuple-element.25.w_in) | copy-start | bytes 4915204
  126.0 20.6 %copy-start.6 = (bf16[1280,640]{1,0:T(8,128)(2,1)S(1)}, bf16[1280,640]{1,0:T(8,128)(2,1)}, u32[]{:S(2)}) copy-start(bf16[1280,640]{1,0:T(8,128)(2,1)} %get-tuple-element.23.w_out) | copy-start | bytes 4915204
  126.0 30.1 %collective-permute-start.8 = (bf16[4,128,640]{2,1,0:T(8,128)(2,1)S(1)}, bf16[4,128,640]{2,1,0:T(8,128)(2,1)S(1)}, u32[]{:S(2)}, u32[]{:S(2)}) collective-permute-start(bf16[4,128,640]{2,1,0:T(8,128)(2,1)S(1)} %get-tuple-element.17), channel_id=1, source_target_pairs={{0,1},{1,2},{2,3},{3,0},{4,5},{5,6},{6,7},{7,4},{8,9},{9,10},{10,1... | collective-permute-start | bytes 1966088 | tf_op jit(solution)/shard_map/ppermute | solution.py:192
  144.4 17.1 %collective-permute-start.11 = (bf16[4,128,640]{2,1,0:T(8,128)(2,1)S(1)}, bf16[4,128,640]{2,1,0:T(8,128)(2,1)S(1)}, u32[]{:S(2)}, u32[]{:S(2)}) collective-permute-start(bf16[4,128,640]{2,1,0:T(8,128)(2,1)S(1)} %get-tuple-element.20), channel_id=1, source_target_pairs={{0,3},{1,0},{2,1},{3,2},{4,7},{5,4},{6,5},{7,6},{8,11},{9,8},{10,9... | collective-permute-start | bytes 1966088 | tf_op jit(solution)/shard_map/ppermute | solution.py:192
  152.2 4.1 %copy-start.7 = (bf16[4,192,640]{2,1,0:T(8,128)(2,1)}, bf16[4,192,640]{2,1,0:T(8,128)(2,1)S(1)}, u32[]{:S(2)}) copy-start(bf16[4,192,640]{2,1,0:T(8,128)(2,1)S(1)} %get-tuple-element.16.refs_6_) | copy-start | bytes 2949124
  152.2 29.6 %collective-permute-start.10 = (bf16[4,128,640]{2,1,0:T(8,128)(2,1)S(1)}, bf16[4,128,640]{2,1,0:T(8,128)(2,1)S(1)}, u32[]{:S(2)}, u32[]{:S(2)}) collective-permute-start(bf16[4,128,640]{2,1,0:T(8,128)(2,1)S(1)} %get-tuple-element.19), channel_id=1, source_target_pairs={{0,1},{1,2},{2,3},{3,0},{4,5},{5,6},{6,7},{7,4},{8,9},{9,10},{10,1... | collective-permute-start | bytes 1966088 | tf_op jit(solution)/shard_map/ppermute | solution.py:192
  152.2 37.3 %collective-permute-start.13 = (bf16[4,128,640]{2,1,0:T(8,128)(2,1)S(1)}, bf16[4,128,640]{2,1,0:T(8,128)(2,1)S(1)}, u32[]{:S(2)}, u32[]{:S(2)}) collective-permute-start(bf16[4,128,640]{2,1,0:T(8,128)(2,1)S(1)} %get-tuple-element.22), channel_id=1, source_target_pairs={{0,3},{1,0},{2,1},{3,2},{4,7},{5,4},{6,5},{7,6},{8,11},{9,8},{10,9... | collective-permute-start | bytes 1966088 | tf_op jit(solution)/shard_map/ppermute | solution.py:192
  161.6 72.8 %collective-permute-start.14 = (bf16[2,448,640]{2,1,0:T(8,128)(2,1)S(1)}, bf16[2,448,640]{2,1,0:T(8,128)(2,1)}, u32[]{:S(2)}, u32[]{:S(2)}) collective-permute-start(bf16[2,448,640]{2,1,0:T(8,128)(2,1)S(1)} %pad_maximum_fusion.2), channel_id=1, source_target_pairs={{0,4},{4,8},{8,12},{12,16},{16,20},{20,24},{24,28},{1,5},{5,9},{9,... | collective-permute-start | bytes 3440648 | tf_op jit(solution)/shard_map/ppermute | solution.py:212
  164.9 69.6 %collective-permute-start.15 = (bf16[2,448,640]{2,1,0:T(8,128)(2,1)S(1)}, bf16[2,448,640]{2,1,0:T(8,128)(2,1)}, u32[]{:S(2)}, u32[]{:S(2)}) collective-permute-start(bf16[2,448,640]{2,1,0:T(8,128)(2,1)S(1)} %pad_maximum_fusion.3), channel_id=1, source_target_pairs={{4,0},{8,4},{12,8},{16,12},{20,16},{24,20},{28,24},{5,1},{9,5},{13... | collective-permute-start | bytes 3440648 | tf_op jit(solution)/shard_map/ppermute | solution.py:212
  180.8 8.8 %copy-start.1 = (bf16[4,192,640]{2,1,0:T(8,128)(2,1)}, bf16[4,192,640]{2,1,0:T(8,128)(2,1)S(1)}, u32[]{:S(2)}) copy-start(bf16[4,192,640]{2,1,0:T(8,128)(2,1)S(1)} %get-tuple-element.15.refs_5_) | copy-start | bytes 2949124
  180.8 24.8 %collective-permute-start.9 = (bf16[4,128,640]{2,1,0:T(8,128)(2,1)S(1)}, bf16[4,128,640]{2,1,0:T(8,128)(2,1)S(1)}, u32[]{:S(2)}, u32[]{:S(2)}) collective-permute-start(bf16[4,128,640]{2,1,0:T(8,128)(2,1)S(1)} %get-tuple-element.18), channel_id=1, source_target_pairs={{0,1},{1,2},{2,3},{3,0},{4,5},{5,6},{6,7},{7,4},{8,9},{9,10},{10,1... | collective-permute-start | bytes 1966088 | tf_op jit(solution)/shard_map/ppermute | solution.py:192
  181.8 35.9 %collective-permute-start.12 = (bf16[4,128,640]{2,1,0:T(8,128)(2,1)S(1)}, bf16[4,128,640]{2,1,0:T(8,128)(2,1)S(1)}, u32[]{:S(2)}, u32[]{:S(2)}) collective-permute-start(bf16[4,128,640]{2,1,0:T(8,128)(2,1)S(1)} %get-tuple-element.21), channel_id=1, source_target_pairs={{0,3},{1,0},{2,1},{3,2},{4,7},{5,4},{6,5},{7,6},{8,11},{9,8},{10,9... | collective-permute-start | bytes 1966088 | tf_op jit(solution)/shard_map/ppermute | solution.py:192
  234.4 12.7 %copy-start.4 = (bf16[640,1280]{1,0:T(8,128)(2,1)S(1)}, bf16[640,1280]{1,0:T(8,128)(2,1)}, u32[]{:S(2)}) copy-start(bf16[640,1280]{1,0:T(8,128)(2,1)} %get-tuple-element.26.w_in) | copy-start | bytes 4915204
  247.2 5.3 %copy-start.3 = (bf16[8,192,640]{2,1,0:T(8,128)(2,1)S(1)}, bf16[8,192,640]{2,1,0:T(8,128)(2,1)}, u32[]{:S(2)}) copy-start(bf16[8,192,640]{2,1,0:T(8,128)(2,1)} %zonal_conv.6.mixed) | copy-start | bytes 5898244

commit v4 on v3

--- a/solution.py
+++ b/solution.py
@@ -89,23 +89,26 @@
             out[h + j] = (value + gelu(conv[:, j * lanes : (j + 1) * lanes])).astype(out.dtype)
 
 
-def convolve(quad, tables, factors, sources, rows, windows):
+def convolve(quad, tables, factors, sources, rows, windows, part):
     forward, inverse = tables
-    taps_r, length, channels = factors.shape
+    taps_r, length, _ = factors.shape
+    start, blocks = part
     out_rows = sum(count for _, count in windows)
     width = inverse.shape[0]
+    lanes = blocks * LANES
 
     def block(array):
-        return pl.BlockSpec((array.shape[0], array.shape[1], LANES), lambda i: (0, 0, i))
+        offset = 0 if array.shape[2] == lanes else start
+        return pl.BlockSpec((array.shape[0], array.shape[1], LANES), lambda i: (0, 0, i + offset))
 
     def whole(array):
         return pl.BlockSpec(array.shape, lambda i: (0,) * array.ndim)
 
-    out = jax.ShapeDtypeStruct((out_rows, width, channels), jnp.bfloat16)
+    out = jax.ShapeDtypeStruct((out_rows, width, lanes), jnp.bfloat16)
     kernel = functools.partial(conv_kernel, windows=windows, row_refs=rows, counts=len(sources))
     return pl.pallas_call(
         kernel,
-        grid=(channels // LANES,),
+        grid=(blocks,),
         out_shape=out,
         in_specs=[pl.BlockSpec(memory_space=pltpu.SMEM), whole(forward), whole(inverse), block(factors)]
         + [block(a) for a in sources],
@@ -117,18 +120,21 @@
         ],
         compiler_params=pltpu.CompilerParams(vmem_limit_bytes=48 << 20),
         cost_estimate=pl.CostEstimate(
-            flops=2 * channels * length * (len(rows) * forward.shape[1] + out_rows * width),
-            bytes_accessed=2 * channels * (len(rows) * forward.shape[1] + 2 * taps_r * length),
-            transcendentals=out_rows * channels * width,
+            flops=2 * lanes * length * (len(rows) * forward.shape[1] + out_rows * width),
+            bytes_accessed=2 * lanes * (len(rows) * forward.shape[1] + 2 * taps_r * length),
+            transcendentals=out_rows * lanes * width,
         ),
         name="zonal_conv",
     )(quad, forward, inverse, factors, *sources)
 
 
-def mlp_kernel(gain, w_in, w_out, mixed, *refs, half, kept):
-    refs = refs[kept:]
-    count, width, channels = mixed.shape
-    values = mixed[...].reshape(count * width, channels).astype(jnp.float32)
+def mlp_kernel(gain, w_in, w_out, *refs, half, kept, parts):
+    mixed = refs[:parts]
+    refs = refs[parts + kept :]
+    count, width, _ = mixed[0].shape
+    channels = w_in.shape[0]
+    values = [m[...].reshape(count * width, m.shape[2]).astype(jnp.float32) for m in mixed]
+    values = values[0] if parts == 1 else jnp.concatenate(values, axis=1)
     average = jnp.mean(values, axis=1, keepdims=True)
     centred = values - average
     variance = jnp.mean(jnp.square(centred), axis=1, keepdims=True)
@@ -142,14 +148,17 @@
         total = total + jnp.dot(hidden, w_out[f : f + step], preferred_element_type=jnp.float32)
     result = total.astype(jnp.bfloat16).reshape(count, width, channels)
     refs[0][...] = result
-    if half:
-        refs[1][...] = result[:, :half]
-        refs[2][...] = result[:, width - half :]
-
-
-def mlp(gain, w_in, w_out, mixed, places, out_rows, edge, kept=None):
-    _, width, channels = mixed.shape
-    hidden_units = w_in.shape[1]
+    start = 0
+    for first, last in zip(refs[1::2], refs[2::2]):
+        here = slice(start, start + first.shape[2])
+        first[...] = result[:, :half, here]
+        last[...] = result[:, width - half :, here]
+        start += first.shape[2]
+
+
+def mlp(gain, w_in, w_out, mixed, places, out_rows, edge, cuts=(), kept=None):
+    width = mixed[0].shape[1]
+    channels, hidden_units = w_in.shape
     steps = len(places)
 
     def place(kind):
@@ -164,19 +173,20 @@
     def whole(array):
         return pl.BlockSpec(array.shape, lambda i: (0,) * array.ndim)
 
-    def pair(lon, kind):
-        return pl.BlockSpec((2, lon, channels), place(kind))
-
-    lasts = [width] + ([edge, edge] if edge else [])
+    def pair(lon, lanes, kind):
+        return pl.BlockSpec((2, lon, lanes), place(kind))
+
+    lasts = [(width, channels)] + [(edge, cut) for cut in cuts for _ in range(2)]
     extra = [] if kept is None else [kept]
     return pl.pallas_call(
-        functools.partial(mlp_kernel, half=edge, kept=len(extra)),
+        functools.partial(mlp_kernel, half=edge, kept=len(extra), parts=len(mixed)),
         grid=(steps,),
-        out_shape=[jax.ShapeDtypeStruct((out_rows, last, channels), jnp.bfloat16) for last in lasts],
-        in_specs=[whole(gain), whole(w_in), whole(w_out), pair(width, 0)]
+        out_shape=[jax.ShapeDtypeStruct((out_rows, *last), jnp.bfloat16) for last in lasts],
+        in_specs=[whole(gain), whole(w_in), whole(w_out)]
+        + [pair(*m.shape[1:], 0) for m in mixed]
         + [pl.BlockSpec(memory_space=pl.ANY) for _ in extra],
-        out_specs=[pair(last, 1) for last in lasts],
-        input_output_aliases={4: 0} if extra else {},
+        out_specs=[pair(*last, 1) for last in lasts],
+        input_output_aliases={3 + len(mixed): 0} if extra else {},
         compiler_params=pltpu.CompilerParams(vmem_limit_bytes=48 << 20),
         cost_estimate=pl.CostEstimate(
             flops=8 * steps * width * channels * hidden_units,
@@ -184,7 +194,7 @@
             transcendentals=2 * steps * width * hidden_units,
         ),
         name="channel_mlp",
-    )(gain, w_in, w_out, mixed, *extra)
+    )(gain, w_in, w_out, *mixed, *extra)
 
 
 def rotate(block, axis, hops):
@@ -212,8 +222,15 @@
     return lax.ppermute(block, "lat", pairs)
 
 
+def lane_parts(channels):
+    units = channels // LANES
+    least = max(1, units // 5)
+    sizes = [(units - least + 1) // 2, (units - least) // 2, least]
+    return [(sum(sizes[:k]), size) for k, size in enumerate(sizes) if size]
+
+
 def body(ocean_state, zonal_kernel, norm_gain, input_weight, output_weight):
-    blocks, kernel_rows, taps, _ = zonal_kernel.shape
+    blocks, kernel_rows, taps, channels = zonal_kernel.shape
     _, rows, _, width = ocean_state.shape
     rim = kernel_rows // 2
     half = taps // 2
@@ -244,21 +261,26 @@
         high = members[len(members) // 2 :]
         return jnp.concatenate([state[low[0] : low[-1] + 1], state[high[0] : high[-1] + 1]], axis=0)
 
-    firsts = [pick(members)[:, :edge] for members in groups]
-    lasts = [pick(members)[:, width - edge :] for members in groups]
+    parts = lane_parts(channels)
+    pieces = [slice(start * LANES, (start + count) * LANES) for start, count in parts]
+    cuts = [count * LANES for _, count in parts]
+    lanes = [slice(None), slice(None)] + pieces
+    groups_of = [groups[0], groups[1]] + [groups[2]] * len(parts)
+    firsts = [pick(members)[:, :edge, cut] for members, cut in zip(groups_of, lanes)]
+    lasts = [pick(members)[:, width - edge :, cut] for members, cut in zip(groups_of, lanes)]
+    tables = (forward, inverse)
     out = None
     for layer in range(blocks):
         final = layer + 1 == blocks
-        halos = [zonal_halos(firsts[k], lasts[k], half) for k in range(3)]
-        left = [pair[0] for pair in halos]
-        right = [pair[1] for pair in halos]
+        halos = [zonal_halos(f, b, half) for f, b in zip(firsts, lasts)]
 
         def extended(start, stop):
             at = group_of[start][1]
             source, row = mid_of[start]
             count = stop - start
+            left, right = halos[0]
             return jnp.concatenate(
-                [left[0][at : at + count], mids[source][row : row + count], right[0][at : at + count]], axis=1
+                [left[at : at + count], mids[source][row : row + count], right[at : at + count]], axis=1
             )
 
         low = step_rows(extended(rows - rim, rows), 1)
@@ -276,7 +298,7 @@
 
         used = [0, 1]
         used_mids = sorted({mid_of[row][0] for k in used for row in groups[k]})
-        sources = [mids[s] for s in used_mids] + [left[k] for k in used] + [right[k] for k in used] + [low, high]
+        sources = [mids[s] for s in used_mids] + [halos[k][side] for side in (0, 1) for k in used] + [low, high]
         n = len(sources)
         outer = (
             [lat(n - 2, r, r) for r in range(rim)]
@@ -285,29 +307,36 @@
             + [lat(n - 1, r, rows + rim + r) for r in range(rim)]
         )
         windows = [(0, rim), (3 * rim, rim)]
-        tables = (forward, inverse)
-        mixed_outer = convolve(quad, tables, factors[layer], sources, outer, windows)
+        mixed_outer = [
+            convolve(quad, tables, factors[layer], sources, outer, windows, (0, channels // LANES))
+        ]
         used = [0, 1, 2]
         used_mids = sorted({source for source, _ in mid_of.values()})
-        sources = [mids[s] for s in used_mids] + left + right
         inner = [own(row, used_mids, used) for row in range(rows)]
+        mixed_inner = []
+        for k, part in enumerate(parts):
+            chosen = [halos[0], halos[1], halos[2 + k]]
+            sources = [mids[s] for s in used_mids] + [pair[side] for side in (0, 1) for pair in chosen]
+            mixed_inner.append(
+                convolve(quad, tables, factors[layer], sources, inner, [(0, rows - 2 * rim)], part)
+            )
         weights = (gains[layer], input_weight[layer], output_weight[layer])
         pairs = rows // 2
-        mixed_inner = convolve(quad, tables, factors[layer], sources, inner, [(0, rows - 2 * rim)])
         if final:
             places = [(0, 0), (1, pairs - 1)]
             (out,) = mlp(*weights, mixed_outer, places, rows, 0)
             places = [(p, p + 1) for p in range(pairs - 2)]
             (out,) = mlp(*weights, mixed_inner, places, rows, 0, kept=out)
         else:
-            outs = [mlp(*weights, mixed_outer, [(0, 0), (1, 1)], 2 * rim, edge)]
-            outs.append(mlp(*weights, mixed_inner, [(0, 0), (pairs - 3, 1)], 2 * rim, edge))
+            outs = [mlp(*weights, mixed_outer, [(0, 0), (1, 1)], 2 * rim, edge, [channels])]
+            places = [(0, 0), (pairs - 3, 1)]
+            outs.append(mlp(*weights, mixed_inner, places, 2 * rim, edge, [channels]))
             places = [(p + 1, p) for p in range(pairs - 4)]
-            outs.append(mlp(*weights, mixed_inner, places, rows - 4 * rim, edge))
+            outs.append(mlp(*weights, mixed_inner, places, rows - 4 * rim, edge, cuts))
             mids = [o[0] for o in outs]
             mid_of = group_of
-            firsts = [o[1] for o in outs]
-            lasts = [o[2] for o in outs]
+            firsts = [f for o in outs for f in o[1::2]]
+            lasts = [b for o in outs for b in o[2::2]]
     return jnp.swapaxes(out, 1, 2)[None]
 
 

time: 264 us -> 254 us (0.962)
  waiting for transfers between devices: 109 us -> 88.7 us
  Pallas kernels: 90.9 us -> 94.9 us
    ppermute x4, waiting for transfers between devices: 13.3 us -> 0.01 us  [step_rows(): return lax.ppermute(block, 'lat', pairs)]
    ppermute x12 -> x20, starting transfers between devices: 20.9 us -> 30.3 us  [rotate(): lax.ppermute(block, axis, [(i, (i + hops) % count) for i in range(count)])]
    ppermute x4, starting transfers between devices: 19.2 us -> 11.3 us  [step_rows(): return lax.ppermute(block, 'lat', pairs)]
    ppermute x12 -> x20, waiting for transfers between devices: 95.6 us -> 88.7 us  [rotate(): lax.ppermute(block, axis, [(i, (i + hops) % count) for i in range(count)])]
    pallas_call x9 -> x13, Pallas kernels: 90.9 us -> 94.9 us  [the longest x8 61.9 us: convolve(): pl.pallas_call(kernel, grid=(blocks,), out_shape=out, in_specs=[pl.BlockS...]
    unnamed x26 -> x36, local copies, waits for them, and re-layouts: 0.07 us -> 3.06 us
  transfers between devices with their start and end apart: 16 -> 24, of which waited for: 7 -> 9; matrix products, arithmetic and copies ran while one was open for 7% -> 8% of each run, Pallas kernels for 24% -> 19%
where the time goes in v4:
time: 254 us; the launch traced here: 251 us
  Pallas kernels  94.9 us (37%)
  waiting for transfers between devices  88.7 us (35%)
  starting transfers between devices  41.6 us (16%)
  local copies, waits for them, and re-layouts  12.2 us (5%)
  matrix products  6.86 us (3%)
  other arithmetic  5.92 us (2%)
    ppermute x20, waiting for transfers between devices, rotate(): lax.ppermute(block, axis, [(i, (i + hops) % count) for i in range(count)])  88.7 us
    pallas_call x8, Pallas kernels, convolve(): pl.pallas_call(kernel, grid=(blocks,), out_shape=out, in_specs=[pl.BlockS...  61.9 us
    pallas_call x5, Pallas kernels, mlp(): pl.pallas_call(functools.partial(mlp_kernel, half=edge, kept=len(extra),...  33 us
    ppermute x20, starting transfers between devices, rotate(): lax.ppermute(block, axis, [(i, (i + hops) % count) for i in range(count)])  30.3 us
    ppermute x4, starting transfers between devices, step_rows(): return lax.ppermute(block, 'lat', pairs)  11.3 us
    dot_general x2, matrix products, body(): jnp.einsum('kt,rtc->rkc', tap_basis, zonal_kernel[layer], preferred_eleme...  6.86 us
  transfers between devices with their start and end apart: 24, of which 9 were waited for; matrix products, arithmetic and copies ran while one was open for 8% of the time, Pallas kernels for 19%

profile of v4, /device:TPU:2, one launch (start us, length us, event | category | flops | bytes accessed | tf_op | source)
XLA Modules:
  0.0 250.6 jit_solution(17391377707898025148)
XLA Ops:
  0.0 1.0 fusion.6
  1.0 3.7 %collective-permute-start.11 = (bf16[4,128,128]{2,1,0:T(8,128)(2,1)S(1)}, bf16[4,128,128]{2,1,0:T(8,128)(2,1)S(1)}, u32[]{:S(2)}, u32[]{:S(2)}) collective-permute-start(bf16[4,128,128]{2,1,0:T(8,128)(2,1)S(1)} %get-tuple-element.35), channel_id=1, source_target_pairs={{0,3},{1,0},{2,1},{3,2},{4,7},{5,4},{6,5},{7,6},{8,11},{9,8},{10,9... | collective-permute-start | bytes 393224 | tf_op jit(solution)/shard_map/ppermute | solution.py:202
  4.7 1.6 fusion.8
  6.3 1.2 pad_maximum_fusion.4
  7.5 3.8 %collective-permute-start.3 = (bf16[4,128,640]{2,1,0:T(8,128)(2,1)}, bf16[4,128,640]{2,1,0:T(8,128)(2,1)S(1)}, u32[]{:S(2)}, u32[]{:S(2)}) collective-permute-start(bf16[4,128,640]{2,1,0:T(8,128)(2,1)} %get-tuple-element.47), channel_id=1, source_target_pairs={{0,3},{1,0},{2,1},{3,2},{4,7},{5,4},{6,5},{7,6},{8,11},{9,8},{10,9... | collective-permute-start | bytes 1966088 | tf_op jit(solution)/shard_map/ppermute | solution.py:202
  11.3 0.1 pad_maximum_fusion.5
  11.5 0.1 collective-permute-start.2
  11.5 2.0 collective-permute-start
  13.6 1.9 slice_bitcast_fusion.1
  15.5 1.2 copy-done.12
  16.7 2.1 slice_bitcast_fusion
  18.7 22.1 %collective-permute-done.2.refs_7_.refs_8_ = bf16[4,128,640]{2,1,0:T(8,128)(2,1)S(1)} collective-permute-done((bf16[4,128,640]{2,1,0:T(8,128)(2,1)S(1)}, bf16[4,128,640]{2,1,0:T(8,128)(2,1)S(1)}, u32[]{:S(2)}, u32[]{:S(2)}) %collective-permute-start.2) | collective-permute-done | bytes 655392 | tf_op jit(solution)/shard_map/ppermute | solution.py:202
  40.8 0.4 collective-permute-start.1
  41.2 0.1 fusion.13
  41.3 13.9 %collective-permute-done.refs_5_ = bf16[4,128,640]{2,1,0:T(8,128)(2,1)S(1)} collective-permute-done((bf16[4,128,640]{2,1,0:T(8,128)(2,1)S(1)}, bf16[4,128,640]{2,1,0:T(8,128)(2,1)S(1)}, u32[]{:S(2)}, u32[]{:S(2)}) %collective-permute-start) | collective-permute-done | bytes 655392 | tf_op jit(solution)/shard_map/ppermute | solution.py:202
  55.2 0.1 fusion.12
  55.3 1.2 pad_maximum_fusion
  56.4 1.9 collective-permute-start.4
  58.4 1.1 pad_maximum_fusion.1
  59.5 3.8 %collective-permute-start.5 = (bf16[2,448,640]{2,1,0:T(8,128)(2,1)}, bf16[2,448,640]{2,1,0:T(8,128)(2,1)}, u32[]{:S(2)}, u32[]{:S(2)}) collective-permute-start(bf16[2,448,640]{2,1,0:T(8,128)(2,1)} %pad_maximum_fusion.1), channel_id=1, source_target_pairs={{4,0},{8,4},{12,8},{16,12},{20,16},{24,20},{28,24},{5,1},{9,5},{13... | collective-permute-start | bytes 3440648 | tf_op jit(solution)/shard_map/ppermute | solution.py:222
  63.3 2.1 fusion.7
  65.5 2.1 collective-permute-start.9
  67.6 3.4 %convolution_bitcast_fusion.refs_3_ = f32[5,448,640]{2,1,0:T(8,128)} fusion(bf16[448,256,1]{1,0,2:T(8,128)(2,1)S(1)} %copy-done.15, bf16[2,5,256,640]{3,2,1,0:T(8,128)(2,1)S(1)} %copy-done.13), kind=kOutput, calls=%fused_computation | convolution fusion | flops 734003200 | bytes 7602176 | tf_op jit(solution)/shard_map/kt,rtc->rkc/dot_general | solution.py:244
  71.0 2.9 %collective-permute-done.9.refs_10_ = bf16[4,128,256]{2,1,0:T(8,128)(2,1)S(1)} collective-permute-done((bf16[4,128,256]{2,1,0:T(8,128)(2,1)S(1)}, bf16[4,128,256]{2,1,0:T(8,128)(2,1)S(1)}, u32[]{:S(2)}, u32[]{:S(2)}) %collective-permute-start.9) | collective-permute-done | bytes 262176 | tf_op jit(solution)/shard_map/ppermute | solution.py:202
  73.9 1.7 collective-permute-start.8
  75.7 2.1 collective-permute-start.7
  77.9 0.9 copy-done.8
  78.8 0.9 copy-done.10
  79.7 4.2 %zonal_conv.11.refs_2_ = bf16[8,192,128]{2,1,0:T(8,128)(2,1)S(1)} custom-call(f32[16]{0:T(128)S(1)} %and_select_fusion.refs_0_, bf16[448,448]{1,0:T(8,128)(2,1)S(1)} %copy-done, bf16[192,448]{1,0:T(8,128)(2,1)S(1)} %copy-done.2, f32[5,448,640]{2,1,0:T(8,128)} %convolution_bitcast_fusion.refs_3_, bf16[12,192,640]{2,1,0:T(8,128)(2,1)} %bitcast.30, ...), custom_call_target="tpu_custom_call" | custom-call | flops 792723456 | bytes 2523136 | tf_op jit(solution)/shard_map/zonal_conv/pallas_call | solution.py:109
  83.9 1.3 collective-permute-done.8.refs_7_
  85.2 7.2 %zonal_conv.10.refs_1_ = bf16[8,192,256]{2,1,0:T(8,128)(2,1)S(1)} custom-call(f32[16]{0:T(128)S(1)} %and_select_fusion.refs_0_, bf16[448,448]{1,0:T(8,128)(2,1)S(1)} %copy-done, bf16[192,448]{1,0:T(8,128)(2,1)S(1)} %copy-done.2, f32[5,448,640]{2,1,0:T(8,128)} %convolution_bitcast_fusion.refs_3_, bf16[12,192,640]{2,1,0:T(8,128)(2,1)} %bitcast.31, ...), custom_call_target="tpu_custom_call" | custom-call | flops 1585446912 | bytes 5046272 | tf_op jit(solution)/shard_map/zonal_conv/pallas_call | solution.py:109
  92.4 2.4 collective-permute-done.6.refs_7_
  94.8 7.1 %zonal_conv.9.refs_0_ = bf16[8,192,256]{2,1,0:T(8,128)(2,1)S(1)} custom-call(f32[16]{0:T(128)S(1)} %and_select_fusion.refs_0_, bf16[448,448]{1,0:T(8,128)(2,1)S(1)} %copy-done, bf16[192,448]{1,0:T(8,128)(2,1)S(1)} %copy-done.2, f32[5,448,640]{2,1,0:T(8,128)} %convolution_bitcast_fusion.refs_3_, bf16[12,192,640]{2,1,0:T(8,128)(2,1)} %bitcast.32, ...), custom_call_target="tpu_custom_call" | custom-call | flops 1585446912 | bytes 5046272 | tf_op jit(solution)/shard_map/zonal_conv/pallas_call | solution.py:109
  102.0 12.5 %zonal_conv.8.refs_0_ = bf16[4,192,640]{2,1,0:T(8,128)(2,1)S(1)} custom-call(f32[16]{0:T(128)S(1)} %and_select_fusion.refs_0_, bf16[448,448]{1,0:T(8,128)(2,1)S(1)} %copy-done, bf16[192,448]{1,0:T(8,128)(2,1)S(1)} %copy-done.2, f32[5,448,640]{2,1,0:T(8,128)} %convolution_bitcast_fusion.refs_3_, bf16[12,192,640]{2,1,0:T(8,128)(2,1)} %bitcast.33, ...), custom_call_target="tpu_custom_call" | custom-call | flops 3523215360 | bytes 12615680 | tf_op jit(solution)/shard_map/zonal_conv/pallas_call | solution.py:109
  114.6 6.0 %channel_mlp.5 = (bf16[4,192,640]{2,1,0:T(8,128)(2,1)S(1)}, bf16[4,128,640]{2,1,0:T(8,128)(2,1)S(1)}, bf16[4,128,640]{2,1,0:T(8,128)(2,1)S(1)}) custom-call(f32[1,640]{1,0:T(1,128)S(1)} %get-tuple-element.59.gain, bf16[640,1280]{1,0:T(8,128)(2,1)S(1)} %copy-done.6, bf16[1280,640]{1,0:T(8,128)(2,1)} %get-tuple-element.31.w_out, ...), custom_call_target="tpu_custom_call" | custom-call | flops 2516582400 | bytes 5242880 | tf_op jit(solution)/shard_map/channel_mlp/pallas_call | solution.py:181
  120.5 0.2 collective-permute-start.12
  120.8 6.0 %channel_mlp.7 = (bf16[4,192,640]{2,1,0:T(8,128)(2,1)S(1)}, bf16[4,128,256]{2,1,0:T(8,128)(2,1)S(1)}, bf16[4,128,256]{2,1,0:T(8,128)(2,1)S(1)}, bf16[4,128,256]{...) custom-call(f32[1,640]{1,0:T(1,128)S(1)} %get-tuple-element.59.gain,, ...), custom_call_target="tpu_custom_call" | custom-call | flops 2516582400 | bytes 5242880 | tf_op jit(solution)/shard_map/channel_mlp/pallas_call | solution.py:181
  126.8 3.1 %collective-permute-start.20 = (bf16[4,128,128]{2,1,0:T(8,128)(2,1)S(1)}, bf16[4,128,128]{2,1,0:T(8,128)(2,1)S(1)}, u32[]{:S(2)}, u32[]{:S(2)}) collective-permute-start(bf16[4,128,128]{2,1,0:T(8,128)(2,1)S(1)} %get-tuple-element.29), channel_id=1, source_target_pairs={{0,1},{1,2},{2,3},{3,0},{4,5},{5,6},{6,7},{7,4},{8,9},{9,10},{10,1... | collective-permute-start | bytes 393224 | tf_op jit(solution)/shard_map/ppermute | solution.py:202
  129.9 2.0 collective-permute-start.21
  131.8 2.0 collective-permute-start.15
  133.8 5.9 %channel_mlp.6 = (bf16[4,192,640]{2,1,0:T(8,128)(2,1)S(1)}, bf16[4,128,640]{2,1,0:T(8,128)(2,1)S(1)}, bf16[4,128,640]{2,1,0:T(8,128)(2,1)S(1)}) custom-call(f32[1,640]{1,0:T(1,128)S(1)} %get-tuple-element.59.gain, bf16[640,1280]{1,0:T(8,128)(2,1)S(1)} %copy-done.6, bf16[1280,640]{1,0:T(8,128)(2,1)} %get-tuple-element.31.w_out, ...), custom_call_target="tpu_custom_call" | custom-call | flops 2516582400 | bytes 5242880 | tf_op jit(solution)/shard_map/channel_mlp/pallas_call | solution.py:181
  139.8 0.1 collective-permute-start.13
  139.9 0.1 fusion.9
  140.0 1.4 collective-permute-done.12.refs_7_.refs_6_
  141.4 2.4 collective-permute-start.16
  143.8 0.1 fusion.10
  143.9 17.2 %collective-permute-done.15.refs_10_.refs_8_ = bf16[4,128,640]{2,1,0:T(8,128)(2,1)S(1)} collective-permute-done((bf16[4,128,640]{2,1,0:T(8,128)(2,1)S(1)}, bf16[4,128,640]{2,1,0:T(8,128)(2,1)S(1)}, u32[]{:S(2)}, u32[]{:S(2)}) %collective-permute-start.15) | collective-permute-done | bytes 655392 | tf_op jit(solution)/shard_map/ppermute | solution.py:202
  161.1 0.1 fusion.11
  161.2 1.1 pad_maximum_fusion.2
  162.3 2.0 collective-permute-start.22
  164.4 1.2 pad_maximum_fusion.3
  165.5 3.6 %collective-permute-start.23 = (bf16[2,448,640]{2,1,0:T(8,128)(2,1)}, bf16[2,448,640]{2,1,0:T(8,128)(2,1)}, u32[]{:S(2)}, u32[]{:S(2)}) collective-permute-start(bf16[2,448,640]{2,1,0:T(8,128)(2,1)} %pad_maximum_fusion.3), channel_id=1, source_target_pairs={{4,0},{8,4},{12,8},{16,12},{20,16},{24,20},{28,24},{5,1},{9,5},{13... | collective-permute-start | bytes 3440648 | tf_op jit(solution)/shard_map/ppermute | solution.py:222
  169.2 0.6 collective-permute-start.18
  169.8 21.5 %collective-permute-done.18.refs_9_ = bf16[4,128,256]{2,1,0:T(8,128)(2,1)S(1)} collective-permute-done((bf16[4,128,256]{2,1,0:T(8,128)(2,1)S(1)}, bf16[4,128,256]{2,1,0:T(8,128)(2,1)S(1)}, u32[]{:S(2)}, u32[]{:S(2)}) %collective-permute-start.18) | collective-permute-done | bytes 262176 | tf_op jit(solution)/shard_map/ppermute | solution.py:202
  191.3 3.8 %collective-permute-start.17 = (bf16[4,128,256]{2,1,0:T(8,128)(2,1)S(1)}, bf16[4,128,256]{2,1,0:T(8,128)(2,1)S(1)}, u32[]{:S(2)}, u32[]{:S(2)}) collective-permute-start(bf16[4,128,256]{2,1,0:T(8,128)(2,1)S(1)} %get-tuple-element.26), channel_id=1, source_target_pairs={{0,3},{1,0},{2,1},{3,2},{4,7},{5,4},{6,5},{7,6},{8,11},{9,8},{10,9... | collective-permute-start | bytes 786440 | tf_op jit(solution)/shard_map/ppermute | solution.py:202
  195.1 0.1 collective-permute-start.19
  195.2 3.4 %convolution_bitcast_fusion.1.refs_3_ = f32[5,448,640]{2,1,0:T(8,128)} fusion(bf16[448,256,1]{1,0,2:T(8,128)(2,1)S(1)} %copy-done.16, bf16[2,5,256,640]{3,2,1,0:T(8,128)(2,1)S(1)} %copy-done.14), kind=kOutput, calls=%fused_computation.1 | convolution fusion | flops 734003200 | bytes 7602176 | tf_op jit(solution)/shard_map/kt,rtc->rkc/dot_general | solution.py:244
  198.6 4.1 %zonal_conv.14.refs_2_ = bf16[8,192,128]{2,1,0:T(8,128)(2,1)S(1)} custom-call(f32[16]{0:T(128)S(1)} %and_select_fusion.refs_0_, bf16[448,448]{1,0:T(8,128)(2,1)S(1)} %copy-done, bf16[192,448]{1,0:T(8,128)(2,1)S(1)} %copy-done.2, f32[5,448,640]{2,1,0:T(8,128)} %convolution_bitcast_fusion.1.refs_3_, bf16[4,192,640]{2,1,0:T(8,128)(2,1)S(1)} %get-tuple-element.18.refs_4_, ...), custom_call_target="tpu_custom_call" | custom-call | flops 792723456 | bytes 2523136 | tf_op jit(solution)/shard_map/zonal_conv/pallas_call | solution.py:109
  202.7 5.9 %collective-permute-done.19.refs_12_ = bf16[4,128,256]{2,1,0:T(8,128)(2,1)S(1)} collective-permute-done((bf16[4,128,256]{2,1,0:T(8,128)(2,1)S(1)}, bf16[4,128,256]{2,1,0:T(8,128)(2,1)S(1)}, u32[]{:S(2)}, u32[]{:S(2)}) %collective-permute-start.19) | collective-permute-done | bytes 262176 | tf_op jit(solution)/shard_map/ppermute | solution.py:202
  208.6 7.1 %zonal_conv.13.refs_1_ = bf16[8,192,256]{2,1,0:T(8,128)(2,1)S(1)} custom-call(f32[16]{0:T(128)S(1)} %and_select_fusion.refs_0_, bf16[448,448]{1,0:T(8,128)(2,1)S(1)} %copy-done, bf16[192,448]{1,0:T(8,128)(2,1)S(1)} %copy-done.2, f32[5,448,640]{2,1,0:T(8,128)} %convolution_bitcast_fusion.1.refs_3_, bf16[4,192,640]{2,1,0:T(8,128)(2,1)S(1)} %get-tuple-element.18.refs_4_, ...), custom_call_target="tpu_custom_call" | custom-call | flops 1585446912 | bytes 5046272 | tf_op jit(solution)/shard_map/zonal_conv/pallas_call | solution.py:109
  215.7 7.1 %zonal_conv.12.refs_0_ = bf16[8,192,256]{2,1,0:T(8,128)(2,1)S(1)} custom-call(f32[16]{0:T(128)S(1)} %and_select_fusion.refs_0_, bf16[448,448]{1,0:T(8,128)(2,1)S(1)} %copy-done, bf16[192,448]{1,0:T(8,128)(2,1)S(1)} %copy-done.2, f32[5,448,640]{2,1,0:T(8,128)} %convolution_bitcast_fusion.1.refs_3_, bf16[4,192,640]{2,1,0:T(8,128)(2,1)S(1)} %get-tuple-element.18.refs_4_, ...), custom_call_target="tpu_custom_call" | custom-call | flops 1585446912 | bytes 5046272 | tf_op jit(solution)/shard_map/zonal_conv/pallas_call | solution.py:109
  222.9 12.6 %zonal_conv.15.refs_0_ = bf16[4,192,640]{2,1,0:T(8,128)(2,1)S(1)} custom-call(f32[16]{0:T(128)S(1)} %and_select_fusion.refs_0_, bf16[448,448]{1,0:T(8,128)(2,1)S(1)} %copy-done, bf16[192,448]{1,0:T(8,128)(2,1)S(1)} %copy-done.2, f32[5,448,640]{2,1,0:T(8,128)} %convolution_bitcast_fusion.1.refs_3_, bf16[4,192,640]{2,1,0:T(8,128)(2,1)S(1)} %get-tuple-element.18.refs_4_, ...), custom_call_target="tpu_custom_call" | custom-call | flops 3523215360 | bytes 12615680 | tf_op jit(solution)/shard_map/zonal_conv/pallas_call | solution.py:109
  235.5 5.3 %channel_mlp.8.refs_3_ = bf16[12,192,640]{2,1,0:T(8,128)(2,1)} custom-call(f32[1,640]{1,0:T(1,128)S(1)} %get-tuple-element.60.gain, bf16[640,1280]{1,0:T(8,128)(2,1)S(1)} %copy-done.4, bf16[1280,640]{1,0:T(8,128)(2,1)S(1)} %copy-done.5, bf16[4,192,640]{2,1,0:T(8,128)(2,1)S(1)} %zonal_conv.15.refs_0_), custom_call_target="tpu_custom_call" | custom-call | flops 2516582400 | bytes 5242880 | tf_op jit(solution)/shard_map/channel_mlp/pallas_call | solution.py:181
  240.8 9.8 %channel_mlp.9 = bf16[12,192,640]{2,1,0:T(8,128)(2,1)} custom-call(f32[1,640]{1,0:T(1,128)S(1)} %get-tuple-element.60.gain, bf16[640,1280]{1,0:T(8,128)(2,1)S(1)} %copy-done.4, bf16[1280,640]{1,0:T(8,128)(2,1)S(1)} %copy-done.5, bf16[8,192,256]{2,1,0:T(8,128)(2,1)S(1)} %zonal_conv.12.refs_0_, ...), custom_call_target="tpu_custom_call", output_to_operand_aliasing={{}: (6, {})} | custom-call | flops 5033164800 | bytes 7208960 | tf_op jit(solution)/shard_map/channel_mlp/pallas_call | solution.py:181
  (53 shorter events, 0.2 us)
Async XLA Ops:
  1.0 58.5 %collective-permute-start.11 = (bf16[4,128,128]{2,1,0:T(8,128)(2,1)S(1)}, bf16[4,128,128]{2,1,0:T(8,128)(2,1)S(1)}, u32[]{:S(2)}, u32[]{:S(2)}) collective-permute-start(bf16[4,128,128]{2,1,0:T(8,128)(2,1)S(1)} %get-tuple-element.35), channel_id=1, source_target_pairs={{0,3},{1,0},{2,1},{3,2},{4,7},{5,4},{6,5},{7,6},{8,11},{9,8},{10,9... | collective-permute-start | bytes 393224 | tf_op jit(solution)/shard_map/ppermute | solution.py:202
  4.7 60.8 %collective-permute-start.10 = (bf16[4,128,128]{2,1,0:T(8,128)(2,1)S(1)}, bf16[4,128,128]{2,1,0:T(8,128)(2,1)S(1)}, u32[]{:S(2)}, u32[]{:S(2)}) collective-permute-start(bf16[4,128,128]{2,1,0:T(8,128)(2,1)S(1)} %get-tuple-element.36), channel_id=1, source_target_pairs={{0,1},{1,2},{2,3},{3,0},{4,5},{5,6},{6,7},{7,4},{8,9},{9,10},{10,1... | collective-permute-start | bytes 393224 | tf_op jit(solution)/shard_map/ppermute | solution.py:202
  6.3 7.2 %copy-start.11 = (bf16[2,640,1280]{2,1,0:T(8,128)(2,1)S(1)}, bf16[2,640,1280]{2,1,0:T(8,128)(2,1)}, u32[]{:S(2)}) copy-start(bf16[2,640,1280]{2,1,0:T(8,128)(2,1)} %param.11) | copy-start | bytes 9830404
  7.5 68.2 %collective-permute-start.3 = (bf16[4,128,640]{2,1,0:T(8,128)(2,1)}, bf16[4,128,640]{2,1,0:T(8,128)(2,1)S(1)}, u32[]{:S(2)}, u32[]{:S(2)}) collective-permute-start(bf16[4,128,640]{2,1,0:T(8,128)(2,1)} %get-tuple-element.47), channel_id=1, source_target_pairs={{0,3},{1,0},{2,1},{3,2},{4,7},{5,4},{6,5},{7,6},{8,11},{9,8},{10,9... | collective-permute-start | bytes 1966088 | tf_op jit(solution)/shard_map/ppermute | solution.py:202
  11.5 29.4 %collective-permute-start.2 = (bf16[4,128,640]{2,1,0:T(8,128)(2,1)S(1)}, bf16[4,128,640]{2,1,0:T(8,128)(2,1)S(1)}, u32[]{:S(2)}, u32[]{:S(2)}) collective-permute-start(bf16[4,128,640]{2,1,0:T(8,128)(2,1)S(1)} %get-tuple-element.49), channel_id=1, source_target_pairs={{0,3},{1,0},{2,1},{3,2},{4,7},{5,4},{6,5},{7,6},{8,11},{9,8},{10,9... | collective-permute-start | bytes 1966088 | tf_op jit(solution)/shard_map/ppermute | solution.py:202
  11.5 43.7 %collective-permute-start = (bf16[4,128,640]{2,1,0:T(8,128)(2,1)S(1)}, bf16[4,128,640]{2,1,0:T(8,128)(2,1)S(1)}, u32[]{:S(2)}, u32[]{:S(2)}) collective-permute-start(bf16[4,128,640]{2,1,0:T(8,128)(2,1)S(1)} %get-tuple-element.50), channel_id=1, source_target_pairs={{0,1},{1,2},{2,3},{3,0},{4,5},{5,6},{6,7},{7,4},{8,9},{9,10},{10,1... | collective-permute-start | bytes 1966088 | tf_op jit(solution)/shard_map/ppermute | solution.py:202
  13.6 3.1 %copy-start.12 = (bf16[2,1280,640]{2,1,0:T(8,128)(2,1)S(1)}, bf16[2,1280,640]{2,1,0:T(8,128)(2,1)}, u32[]{:S(2)}) copy-start(bf16[2,1280,640]{2,1,0:T(8,128)(2,1)} %param.12) | copy-start | bytes 9830404
  40.8 37.0 %collective-permute-start.1 = (bf16[4,128,640]{2,1,0:T(8,128)(2,1)}, bf16[4,128,640]{2,1,0:T(8,128)(2,1)S(1)}, u32[]{:S(2)}, u32[]{:S(2)}) collective-permute-start(bf16[4,128,640]{2,1,0:T(8,128)(2,1)} %get-tuple-element.48), channel_id=1, source_target_pairs={{0,1},{1,2},{2,3},{3,0},{4,5},{5,6},{6,7},{7,4},{8,9},{9,10},{10,1... | collective-permute-start | bytes 1966088 | tf_op jit(solution)/shard_map/ppermute | solution.py:202
  56.4 45.6 %collective-permute-start.4 = (bf16[2,448,640]{2,1,0:T(8,128)(2,1)}, bf16[2,448,640]{2,1,0:T(8,128)(2,1)}, u32[]{:S(2)}, u32[]{:S(2)}) collective-permute-start(bf16[2,448,640]{2,1,0:T(8,128)(2,1)} %pad_maximum_fusion), channel_id=1, source_target_pairs={{0,4},{4,8},{8,12},{12,16},{16,20},{20,24},{24,28},{1,5},{5,9},{9,... | collective-permute-start | bytes 3440648 | tf_op jit(solution)/shard_map/ppermute | solution.py:222
  58.4 9.2 %copy-start.13 = (bf16[2,5,256,640]{3,2,1,0:T(8,128)(2,1)S(1)}, bf16[2,5,256,640]{3,2,1,0:T(8,128)(2,1)}, u32[]{:S(2)}) copy-start(bf16[2,5,256,640]{3,2,1,0:T(8,128)(2,1)} %param.9) | copy-start | bytes 9830404
  58.4 9.2 %copy-start.15 = (bf16[448,256,1]{1,0,2:T(8,128)(2,1)S(1)}, bf16[448,256,1]{1,0,2:T(8,128)(2,1)}, u32[]{:S(2)}) copy-start(bf16[448,256,1]{1,0,2:T(8,128)(2,1)} %constant.34) | copy-start | bytes 688132
  59.5 5.9 %copy-start.7 = (bf16[4,128,128]{2,1,0:T(8,128)(2,1)}, bf16[4,128,128]{2,1,0:T(8,128)(2,1)S(1)}, u32[]{:S(2)}) copy-start(bf16[4,128,128]{2,1,0:T(8,128)(2,1)S(1)} %collective-permute-done.11.refs_10_) | copy-start | bytes 393220
  59.5 42.5 %collective-permute-start.5 = (bf16[2,448,640]{2,1,0:T(8,128)(2,1)}, bf16[2,448,640]{2,1,0:T(8,128)(2,1)}, u32[]{:S(2)}, u32[]{:S(2)}) collective-permute-start(bf16[2,448,640]{2,1,0:T(8,128)(2,1)} %pad_maximum_fusion.1), channel_id=1, source_target_pairs={{4,0},{8,4},{12,8},{16,12},{20,16},{24,20},{28,24},{5,1},{9,5},{13... | collective-permute-start | bytes 3440648 | tf_op jit(solution)/shard_map/ppermute | solution.py:222
  65.4 5.6 %copy-start.9 = (bf16[4,128,128]{2,1,0:T(8,128)(2,1)}, bf16[4,128,128]{2,1,0:T(8,128)(2,1)S(1)}, u32[]{:S(2)}) copy-start(bf16[4,128,128]{2,1,0:T(8,128)(2,1)S(1)} %collective-permute-done.10.refs_7_) | copy-start | bytes 393220
  65.4 10.2 %copy-start.17 = (bf16[2,640]{1,0:T(2,128)(2,1)S(1)}, bf16[2,640]{1,0:T(2,128)(2,1)}, u32[]{:S(2)}) copy-start(bf16[2,640]{1,0:T(2,128)(2,1)} %param.10) | copy-start | bytes 7684
  65.4 12.5 %copy-start = (bf16[448,448]{1,0:T(8,128)(2,1)S(1)}, bf16[448,448]{1,0:T(8,128)(2,1)}, u32[]{:S(2)}) copy-start(bf16[448,448]{1,0:T(8,128)(2,1)} %constant.30.clone.refs_1_) | copy-start | bytes 1204228
  65.5 12.5 %copy-start.2 = (bf16[192,448]{1,0:T(8,128)(2,1)S(1)}, bf16[192,448]{1,0:T(8,128)(2,1)}, u32[]{:S(2)}) copy-start(bf16[192,448]{1,0:T(8,128)(2,1)} %constant.31.clone.refs_2_) | copy-start | bytes 516100
  65.5 8.5 %collective-permute-start.9 = (bf16[4,128,256]{2,1,0:T(8,128)(2,1)S(1)}, bf16[4,128,256]{2,1,0:T(8,128)(2,1)S(1)}, u32[]{:S(2)}, u32[]{:S(2)}) collective-permute-start(bf16[4,128,256]{2,1,0:T(8,128)(2,1)S(1)} %get-tuple-element.37), channel_id=1, source_target_pairs={{0,3},{1,0},{2,1},{3,2},{4,7},{5,4},{6,5},{7,6},{8,11},{9,8},{10,9... | collective-permute-start | bytes 786440 | tf_op jit(solution)/shard_map/ppermute | solution.py:202
  73.9 11.3 %collective-permute-start.8 = (bf16[4,128,256]{2,1,0:T(8,128)(2,1)}, bf16[4,128,256]{2,1,0:T(8,128)(2,1)}, u32[]{:S(2)}, u32[]{:S(2)}) collective-permute-start(bf16[4,128,256]{2,1,0:T(8,128)(2,1)} %get-tuple-element.38), channel_id=1, source_target_pairs={{0,1},{1,2},{2,3},{3,0},{4,5},{5,6},{6,7},{7,4},{8,9},{9,10},{10,1... | collective-permute-start | bytes 786440 | tf_op jit(solution)/shard_map/ppermute | solution.py:202
  75.7 16.7 %collective-permute-start.7 = (bf16[4,128,256]{2,1,0:T(8,128)(2,1)}, bf16[4,128,256]{2,1,0:T(8,128)(2,1)S(1)}, u32[]{:S(2)}, u32[]{:S(2)}) collective-permute-start(bf16[4,128,256]{2,1,0:T(8,128)(2,1)} %get-tuple-element.39), channel_id=1, source_target_pairs={{0,3},{1,0},{2,1},{3,2},{4,7},{5,4},{6,5},{7,6},{8,11},{9,8},{10,9... | collective-permute-start | bytes 786440 | tf_op jit(solution)/shard_map/ppermute | solution.py:202
  77.8 17.0 %collective-permute-start.6 = (bf16[4,128,256]{2,1,0:T(8,128)(2,1)}, bf16[4,128,256]{2,1,0:T(8,128)(2,1)S(1)}, u32[]{:S(2)}, u32[]{:S(2)}) collective-permute-start(bf16[4,128,256]{2,1,0:T(8,128)(2,1)} %get-tuple-element.40), channel_id=1, source_target_pairs={{0,1},{1,2},{2,3},{3,0},{4,5},{5,6},{6,7},{7,4},{8,9},{9,10},{10,1... | collective-permute-start | bytes 786440 | tf_op jit(solution)/shard_map/ppermute | solution.py:202
  77.9 0.9 copy-start.8
  78.8 0.9 copy-start.10
  102.0 12.6 %copy-start.6 = (bf16[640,1280]{1,0:T(8,128)(2,1)S(1)}, bf16[640,1280]{1,0:T(8,128)(2,1)}, u32[]{:S(2)}) copy-start(bf16[640,1280]{1,0:T(8,128)(2,1)} %get-tuple-element.33.w_in) | copy-start | bytes 4915204
  120.5 20.9 %collective-permute-start.12 = (bf16[4,128,640]{2,1,0:T(8,128)(2,1)S(1)}, bf16[4,128,640]{2,1,0:T(8,128)(2,1)S(1)}, u32[]{:S(2)}, u32[]{:S(2)}) collective-permute-start(bf16[4,128,640]{2,1,0:T(8,128)(2,1)S(1)} %get-tuple-element.21), channel_id=1, source_target_pairs={{0,1},{1,2},{2,3},{3,0},{4,5},{5,6},{6,7},{7,4},{8,9},{9,10},{10,1... | collective-permute-start | bytes 1966088 | tf_op jit(solution)/shard_map/ppermute | solution.py:202
  126.8 13.0 %copy-start.3 = (bf16[4,192,640]{2,1,0:T(8,128)(2,1)}, bf16[4,192,640]{2,1,0:T(8,128)(2,1)S(1)}, u32[]{:S(2)}) copy-start(bf16[4,192,640]{2,1,0:T(8,128)(2,1)S(1)} %get-tuple-element.20.refs_6_) | copy-start | bytes 2949124
  126.8 38.7 %collective-permute-start.20 = (bf16[4,128,128]{2,1,0:T(8,128)(2,1)S(1)}, bf16[4,128,128]{2,1,0:T(8,128)(2,1)S(1)}, u32[]{:S(2)}, u32[]{:S(2)}) collective-permute-start(bf16[4,128,128]{2,1,0:T(8,128)(2,1)S(1)} %get-tuple-element.29), channel_id=1, source_target_pairs={{0,1},{1,2},{2,3},{3,0},{4,5},{5,6},{6,7},{7,4},{8,9},{9,10},{10,1... | collective-permute-start | bytes 393224 | tf_op jit(solution)/shard_map/ppermute | solution.py:202
  129.9 39.3 %collective-permute-start.21 = (bf16[4,128,128]{2,1,0:T(8,128)(2,1)S(1)}, bf16[4,128,128]{2,1,0:T(8,128)(2,1)S(1)}, u32[]{:S(2)}, u32[]{:S(2)}) collective-permute-start(bf16[4,128,128]{2,1,0:T(8,128)(2,1)S(1)} %get-tuple-element.30), channel_id=1, source_target_pairs={{0,3},{1,0},{2,1},{3,2},{4,7},{5,4},{6,5},{7,6},{8,11},{9,8},{10,9... | collective-permute-start | bytes 393224 | tf_op jit(solution)/shard_map/ppermute | solution.py:202
  131.8 29.3 %collective-permute-start.15 = (bf16[4,128,640]{2,1,0:T(8,128)(2,1)S(1)}, bf16[4,128,640]{2,1,0:T(8,128)(2,1)S(1)}, u32[]{:S(2)}, u32[]{:S(2)}) collective-permute-start(bf16[4,128,640]{2,1,0:T(8,128)(2,1)S(1)} %get-tuple-element.24), channel_id=1, source_target_pairs={{0,3},{1,0},{2,1},{3,2},{4,7},{5,4},{6,5},{7,6},{8,11},{9,8},{10,9... | collective-permute-start | bytes 1966088 | tf_op jit(solution)/shard_map/ppermute | solution.py:202
  139.8 58.8 %copy-start.1 = (bf16[4,192,640]{2,1,0:T(8,128)(2,1)}, bf16[4,192,640]{2,1,0:T(8,128)(2,1)S(1)}, u32[]{:S(2)}) copy-start(bf16[4,192,640]{2,1,0:T(8,128)(2,1)S(1)} %get-tuple-element.19.refs_5_) | copy-start | bytes 2949124
  139.8 51.5 %collective-permute-start.13 = (bf16[4,128,640]{2,1,0:T(8,128)(2,1)S(1)}, bf16[4,128,640]{2,1,0:T(8,128)(2,1)S(1)}, u32[]{:S(2)}, u32[]{:S(2)}) collective-permute-start(bf16[4,128,640]{2,1,0:T(8,128)(2,1)S(1)} %get-tuple-element.22), channel_id=1, source_target_pairs={{0,1},{1,2},{2,3},{3,0},{4,5},{5,6},{6,7},{7,4},{8,9},{9,10},{10,1... | collective-permute-start | bytes 1966088 | tf_op jit(solution)/shard_map/ppermute | solution.py:202
  141.4 53.7 %collective-permute-start.16 = (bf16[4,128,640]{2,1,0:T(8,128)(2,1)S(1)}, bf16[4,128,640]{2,1,0:T(8,128)(2,1)S(1)}, u32[]{:S(2)}, u32[]{:S(2)}) collective-permute-start(bf16[4,128,640]{2,1,0:T(8,128)(2,1)S(1)} %get-tuple-element.25), channel_id=1, source_target_pairs={{0,3},{1,0},{2,1},{3,2},{4,7},{5,4},{6,5},{7,6},{8,11},{9,8},{10,9... | collective-permute-start | bytes 1966088 | tf_op jit(solution)/shard_map/ppermute | solution.py:202
  161.2 34.0 %copy-start.14 = (bf16[2,5,256,640]{3,2,1,0:T(8,128)(2,1)S(1)}, bf16[2,5,256,640]{3,2,1,0:T(8,128)(2,1)}, u32[]{:S(2)}) copy-start(bf16[2,5,256,640]{3,2,1,0:T(8,128)(2,1)} %param.9) | copy-start | bytes 9830404
  162.3 32.9 %copy-start.16 = (bf16[448,256,1]{1,0,2:T(8,128)(2,1)S(1)}, bf16[448,256,1]{1,0,2:T(8,128)(2,1)}, u32[]{:S(2)}) copy-start(bf16[448,256,1]{1,0,2:T(8,128)(2,1)} %constant.34) | copy-start | bytes 688132
  162.3 60.5 %collective-permute-start.22 = (bf16[2,448,640]{2,1,0:T(8,128)(2,1)}, bf16[2,448,640]{2,1,0:T(8,128)(2,1)}, u32[]{:S(2)}, u32[]{:S(2)}) collective-permute-start(bf16[2,448,640]{2,1,0:T(8,128)(2,1)} %pad_maximum_fusion.2), channel_id=1, source_target_pairs={{0,4},{4,8},{8,12},{12,16},{16,20},{20,24},{24,28},{1,5},{5,9},{9,... | collective-permute-start | bytes 3440648 | tf_op jit(solution)/shard_map/ppermute | solution.py:222
  165.5 57.3 %collective-permute-start.23 = (bf16[2,448,640]{2,1,0:T(8,128)(2,1)}, bf16[2,448,640]{2,1,0:T(8,128)(2,1)}, u32[]{:S(2)}, u32[]{:S(2)}) collective-permute-start(bf16[2,448,640]{2,1,0:T(8,128)(2,1)} %pad_maximum_fusion.3), channel_id=1, source_target_pairs={{4,0},{8,4},{12,8},{16,12},{20,16},{24,20},{28,24},{5,1},{9,5},{13... | collective-permute-start | bytes 3440648 | tf_op jit(solution)/shard_map/ppermute | solution.py:222
  169.2 22.1 %collective-permute-start.18 = (bf16[4,128,256]{2,1,0:T(8,128)(2,1)S(1)}, bf16[4,128,256]{2,1,0:T(8,128)(2,1)S(1)}, u32[]{:S(2)}, u32[]{:S(2)}) collective-permute-start(bf16[4,128,256]{2,1,0:T(8,128)(2,1)S(1)} %get-tuple-element.27), channel_id=1, source_target_pairs={{0,1},{1,2},{2,3},{3,0},{4,5},{5,6},{6,7},{7,4},{8,9},{9,10},{10,1... | collective-permute-start | bytes 786440 | tf_op jit(solution)/shard_map/ppermute | solution.py:202
  191.3 24.4 %collective-permute-start.14 = (bf16[4,128,256]{2,1,0:T(8,128)(2,1)S(1)}, bf16[4,128,256]{2,1,0:T(8,128)(2,1)S(1)}, u32[]{:S(2)}, u32[]{:S(2)}) collective-permute-start(bf16[4,128,256]{2,1,0:T(8,128)(2,1)S(1)} %get-tuple-element.23), channel_id=1, source_target_pairs={{0,1},{1,2},{2,3},{3,0},{4,5},{5,6},{6,7},{7,4},{8,9},{9,10},{10,1... | collective-permute-start | bytes 786440 | tf_op jit(solution)/shard_map/ppermute | solution.py:202
  191.3 24.4 %collective-permute-start.17 = (bf16[4,128,256]{2,1,0:T(8,128)(2,1)S(1)}, bf16[4,128,256]{2,1,0:T(8,128)(2,1)S(1)}, u32[]{:S(2)}, u32[]{:S(2)}) collective-permute-start(bf16[4,128,256]{2,1,0:T(8,128)(2,1)S(1)} %get-tuple-element.26), channel_id=1, source_target_pairs={{0,3},{1,0},{2,1},{3,2},{4,7},{5,4},{6,5},{7,6},{8,11},{9,8},{10,9... | collective-permute-start | bytes 786440 | tf_op jit(solution)/shard_map/ppermute | solution.py:202
  195.1 13.5 %collective-permute-start.19 = (bf16[4,128,256]{2,1,0:T(8,128)(2,1)S(1)}, bf16[4,128,256]{2,1,0:T(8,128)(2,1)S(1)}, u32[]{:S(2)}, u32[]{:S(2)}) collective-permute-start(bf16[4,128,256]{2,1,0:T(8,128)(2,1)S(1)} %get-tuple-element.28), channel_id=1, source_target_pairs={{0,3},{1,0},{2,1},{3,2},{4,7},{5,4},{6,5},{7,6},{8,11},{9,8},{10,9... | collective-permute-start | bytes 786440 | tf_op jit(solution)/shard_map/ppermute | solution.py:202
  222.8 12.7 %copy-start.4 = (bf16[640,1280]{1,0:T(8,128)(2,1)S(1)}, bf16[640,1280]{1,0:T(8,128)(2,1)}, u32[]{:S(2)}) copy-start(bf16[640,1280]{1,0:T(8,128)(2,1)} %get-tuple-element.34.w_in) | copy-start | bytes 4915204
  222.8 12.7 %copy-start.5 = (bf16[1280,640]{1,0:T(8,128)(2,1)S(1)}, bf16[1280,640]{1,0:T(8,128)(2,1)}, u32[]{:S(2)}) copy-start(bf16[1280,640]{1,0:T(8,128)(2,1)} %get-tuple-element.32.w_out) | copy-start | bytes 4915204

commit v5 on v4

--- a/solution.py
+++ b/solution.py
@@ -12,6 +12,7 @@
 
 LANES = 128
 PACK = 16
+SUBLANES = 8
 
 
 def bases(width, taps):
@@ -35,56 +36,56 @@
 def conv_kernel(*refs, windows, row_refs, counts):
     quad, forward, inverse, factors = refs[:4]
     sources = refs[4 : 4 + counts]
-    out, ext, spectra, product = refs[4 + counts :]
+    out, spectra, product = refs[4 + counts :]
     lanes = out.shape[2]
     freqs = forward.shape[0] // 2
     every = len(row_refs)
     taps_r = factors.shape[0]
-    for g, (_, pieces) in enumerate(row_refs):
-        start = 0
-        for source, at in pieces:
-            size = sources[source].shape[1]
-            ext[start : start + size, g * lanes : (g + 1) * lanes] = sources[source][at]
-            start += size
+
+    def row(g):
+        return jnp.concatenate([sources[source][at, lon] for source, at, lon in row_refs[g][1]], axis=0)
+
     for g in range(0, every, 2):
-        two = slice(g * lanes, (g + 2) * lanes)
-        result = jnp.dot(forward[...], ext[:, two], preferred_element_type=jnp.float32)
+        two = jnp.concatenate([row(g), row(g + 1)], axis=1)
+        result = jnp.dot(forward[...], two, preferred_element_type=jnp.float32)
         for j in range(2):
             spectra[g + j] = result[:, j * lanes : (j + 1) * lanes] * quad[row_refs[g + j][0]]
 
     def block(f, carry):
-        start = pl.multiple_of(f * PACK, PACK)
-        re = pl.ds(start, PACK)
-        im = pl.ds(pl.multiple_of(freqs + start, PACK), PACK)
+        start = pl.multiple_of(f * SUBLANES, SUBLANES)
+        re = pl.ds(start, SUBLANES)
+        im = pl.ds(pl.multiple_of(freqs + start, SUBLANES), SUBLANES)
         fr = [factors[r, re] for r in range(taps_r)]
         fi = [factors[r, im] for r in range(taps_r)]
+        fd = [b - a for a, b in zip(fr, fi)]
+        fs = [b + a for a, b in zip(fr, fi)]
         h = 0
         for first, count in windows:
             xr = [spectra[first + g, re] for g in range(taps_r - 1)]
             xi = [spectra[first + g, im] for g in range(taps_r - 1)]
+            xs = [a + b for a, b in zip(xr, xi)]
             for k in range(count):
                 xr.append(spectra[first + k + taps_r - 1, re])
                 xi.append(spectra[first + k + taps_r - 1, im])
-                yr = xr[0] * fr[0] - xi[0] * fi[0]
-                yi = xr[0] * fi[0] + xi[0] * fr[0]
+                xs.append(xr[-1] + xi[-1])
+                both, up, down = xs[0] * fr[0], xr[0] * fd[0], xi[0] * fs[0]
                 for r in range(1, taps_r):
-                    yr = yr + (xr[r] * fr[r] - xi[r] * fi[r])
-                    yi = yi + (xr[r] * fi[r] + xi[r] * fr[r])
+                    both, up, down = both + xs[r] * fr[r], up + xr[r] * fd[r], down + xi[r] * fs[r]
                 here = slice(h * lanes, (h + 1) * lanes)
-                product[re, here] = yr.astype(product.dtype)
-                product[im, here] = yi.astype(product.dtype)
-                xr.pop(0)
-                xi.pop(0)
+                product[re, here] = both - down
+                product[im, here] = both + up
+                for window in (xr, xi, xs):
+                    window.pop(0)
                 h += 1
         return carry
 
-    lax.fori_loop(0, freqs // PACK, block, 0)
+    lax.fori_loop(0, freqs // SUBLANES, block, 0, unroll=4)
     own = [row_refs[first + taps_r // 2 + k][1] for first, count in windows for k in range(count)]
     for h in range(0, len(own), 2):
         two = slice(h * lanes, (h + 2) * lanes)
-        conv = jnp.dot(inverse[...], product[:, two], preferred_element_type=jnp.float32)
+        conv = jnp.dot(inverse[...], product[:, two].astype(jnp.bfloat16), preferred_element_type=jnp.float32)
         for j in range(2):
-            source, at = own[h + j][1]
+            source, at, _ = own[h + j][1]
             value = sources[source][at].astype(jnp.float32)
             out[h + j] = (value + gelu(conv[:, j * lanes : (j + 1) * lanes])).astype(out.dtype)
 
@@ -114,9 +115,8 @@
         + [block(a) for a in sources],
         out_specs=block(out),
         scratch_shapes=[
-            pltpu.VMEM((forward.shape[1], len(rows) * LANES), jnp.bfloat16),
             pltpu.VMEM((len(rows), length, LANES), jnp.float32),
-            pltpu.VMEM((length, out_rows * LANES), jnp.bfloat16),
+            pltpu.VMEM((length, out_rows * LANES), jnp.float32),
         ],
         compiler_params=pltpu.CompilerParams(vmem_limit_bytes=48 << 20),
         cost_estimate=pl.CostEstimate(
@@ -128,25 +128,29 @@
     )(quad, forward, inverse, factors, *sources)
 
 
-def mlp_kernel(gain, w_in, w_out, *refs, half, kept, parts):
-    mixed = refs[:parts]
-    refs = refs[parts + kept :]
+def mlp_kernel(gain, w_in, w_out, *refs, half, kept, parts, together):
+    mixed = refs[: parts * together]
+    refs = refs[parts * together + kept :]
     count, width, _ = mixed[0].shape
-    channels = w_in.shape[0]
-    values = [m[...].reshape(count * width, m.shape[2]).astype(jnp.float32) for m in mixed]
-    values = values[0] if parts == 1 else jnp.concatenate(values, axis=1)
-    average = jnp.mean(values, axis=1, keepdims=True)
-    centred = values - average
-    variance = jnp.mean(jnp.square(centred), axis=1, keepdims=True)
-    normed = (centred * lax.rsqrt(variance + 1e-05) * gain[...]).astype(jnp.bfloat16)
-    total = values
-    hidden_units = w_in.shape[1]
-    step = math.gcd(hidden_units, 256)
+    channels, hidden_units = w_in.shape
+    totals, normed = [], []
+    for t in range(together):
+        pieces = mixed[t * parts : (t + 1) * parts]
+        values = [m[...].reshape(count * width, m.shape[2]).astype(jnp.float32) for m in pieces]
+        values = values[0] if parts == 1 else jnp.concatenate(values, axis=1)
+        average = jnp.mean(values, axis=1, keepdims=True)
+        centred = values - average
+        variance = jnp.mean(jnp.square(centred), axis=1, keepdims=True)
+        normed.append((centred * lax.rsqrt(variance + 1e-05) * gain[...]).astype(jnp.bfloat16))
+        totals.append(values)
+    normed = jnp.concatenate(normed, axis=0)
+    total = jnp.concatenate(totals, axis=0)
+    step = hidden_units
     for f in range(0, hidden_units, step):
         hidden = jnp.dot(normed, w_in[:, f : f + step], preferred_element_type=jnp.float32)
         hidden = gelu(hidden).astype(jnp.bfloat16)
         total = total + jnp.dot(hidden, w_out[f : f + step], preferred_element_type=jnp.float32)
-    result = total.astype(jnp.bfloat16).reshape(count, width, channels)
+    result = total.astype(jnp.bfloat16).reshape(together * count, width, channels)
     refs[0][...] = result
     start = 0
     for first, last in zip(refs[1::2], refs[2::2]):
@@ -156,16 +160,16 @@
         start += first.shape[2]
 
 
-def mlp(gain, w_in, w_out, mixed, places, out_rows, edge, cuts=(), kept=None):
+def mlp(gain, w_in, w_out, mixed, steps, out_rows, edge, cuts=(), kept=None):
     width = mixed[0].shape[1]
     channels, hidden_units = w_in.shape
-    steps = len(places)
-
-    def place(kind):
+    together = len(steps[0][0])
+
+    def chosen(values):
         def index(i):
-            at = places[0][kind]
-            for k in range(1, steps):
-                at = at + (places[k][kind] - places[k - 1][kind]) * (i >= k).astype(jnp.int32)
+            at = values[0]
+            for k in range(1, len(values)):
+                at = at + (values[k] - values[k - 1]) * (i >= k).astype(jnp.int32)
             return (at, 0, 0)
 
         return index
@@ -173,28 +177,33 @@
     def whole(array):
         return pl.BlockSpec(array.shape, lambda i: (0,) * array.ndim)
 
-    def pair(lon, lanes, kind):
-        return pl.BlockSpec((2, lon, lanes), place(kind))
+    def given(lon, lanes):
+        sizes = (pl.Element(2 * together), pl.Element(lon), pl.Element(lanes))
+        return pl.BlockSpec(sizes, chosen([row for _, row in steps]))
 
     lasts = [(width, channels)] + [(edge, cut) for cut in cuts for _ in range(2)]
     extra = [] if kept is None else [kept]
     return pl.pallas_call(
-        functools.partial(mlp_kernel, half=edge, kept=len(extra), parts=len(mixed)),
-        grid=(steps,),
+        functools.partial(mlp_kernel, half=edge, kept=len(extra), parts=len(mixed), together=together),
+        grid=(len(steps),),
         out_shape=[jax.ShapeDtypeStruct((out_rows, *last), jnp.bfloat16) for last in lasts],
         in_specs=[whole(gain), whole(w_in), whole(w_out)]
-        + [pair(*m.shape[1:], 0) for m in mixed]
+        + [
+            pl.BlockSpec((2, *m.shape[1:]), chosen([pairs[t] for pairs, _ in steps]))
+            for t in range(together)
+            for m in mixed
+        ]
         + [pl.BlockSpec(memory_space=pl.ANY) for _ in extra],
-        out_specs=[pair(*last, 1) for last in lasts],
-        input_output_aliases={3 + len(mixed): 0} if extra else {},
+        out_specs=[given(*last) for last in lasts],
+        input_output_aliases={3 + together * len(mixed): 0} if extra else {},
         compiler_params=pltpu.CompilerParams(vmem_limit_bytes=48 << 20),
         cost_estimate=pl.CostEstimate(
-            flops=8 * steps * width * channels * hidden_units,
-            bytes_accessed=8 * steps * width * channels + 4 * channels * hidden_units,
-            transcendentals=2 * steps * width * hidden_units,
+            flops=8 * len(steps) * together * width * channels * hidden_units,
+            bytes_accessed=8 * len(steps) * together * width * channels + 4 * channels * hidden_units,
+            transcendentals=2 * len(steps) * together * width * hidden_units,
         ),
         name="channel_mlp",
-    )(gain, w_in, w_out, *mixed, *extra)
+    )(gain, w_in, w_out, *(list(mixed) * together), *extra)
 
 
 def rotate(block, axis, hops):
@@ -274,37 +283,46 @@
         final = layer + 1 == blocks
         halos = [zonal_halos(f, b, half) for f, b in zip(firsts, lasts)]
 
-        def extended(start, stop):
+        def near(start):
+            source, row = mid_of[start]
+            return mids[source][row : row + rim]
+
+        def far(start):
             at = group_of[start][1]
-            source, row = mid_of[start]
-            count = stop - start
-            left, right = halos[0]
-            return jnp.concatenate(
-                [left[at : at + count], mids[source][row : row + count], right[at : at + count]], axis=1
-            )
-
-        low = step_rows(extended(rows - rim, rows), 1)
-        high = step_rows(extended(0, rim), -1)
+            return jnp.concatenate([halo[at : at + rim] for halo in halos[0]], axis=1)
+
+        low = [step_rows(near(rows - rim), 1), step_rows(far(rows - rim), 1)]
+        high = [step_rows(near(0), -1), step_rows(far(0), -1)]
 
         def own(row, used_mids, used):
             k, at = group_of[row]
             source, mid_row = mid_of[row]
             n = len(used_mids)
             j = used.index(k)
-            return (row + rim, [(n + j, at), (used_mids.index(source), mid_row), (n + len(used) + j, at)])
+            every = slice(None)
+            middle = (used_mids.index(source), mid_row, every)
+            return (row + rim, [(n + j, at, every), middle, (n + len(used) + j, at, every)])
 
         def lat(number, at, place):
-            return (place, [(number, at)])
+            return (
+                place,
+                [
+                    (number + 1, at, slice(0, half)),
+                    (number, at, slice(None)),
+                    (number + 1, at, slice(half, 2 * half)),
+                ],
+            )
 
         used = [0, 1]
         used_mids = sorted({mid_of[row][0] for k in used for row in groups[k]})
-        sources = [mids[s] for s in used_mids] + [halos[k][side] for side in (0, 1) for k in used] + [low, high]
+        sources = [mids[s] for s in used_mids] + [halos[k][side] for side in (0, 1) for k in used]
+        sources = sources + low + high
         n = len(sources)
         outer = (
-            [lat(n - 2, r, r) for r in range(rim)]
+            [lat(n - 4, r, r) for r in range(rim)]
             + [own(row, used_mids, used) for row in range(2 * rim)]
             + [own(row, used_mids, used) for row in range(rows - 2 * rim, rows)]
-            + [lat(n - 1, r, rows + rim + r) for r in range(rim)]
+            + [lat(n - 2, r, rows + rim + r) for r in range(rim)]
         )
         windows = [(0, rim), (3 * rim, rim)]
         mixed_outer = [
@@ -323,16 +341,14 @@
         weights = (gains[layer], input_weight[layer], output_weight[layer])
         pairs = rows // 2
         if final:
-            places = [(0, 0), (1, pairs - 1)]
-            (out,) = mlp(*weights, mixed_outer, places, rows, 0)
-            places = [(p, p + 1) for p in range(pairs - 2)]
-            (out,) = mlp(*weights, mixed_inner, places, rows, 0, kept=out)
+            (out,) = mlp(*weights, mixed_outer, [([0], 0), ([1], rows - 2)], rows, 0)
+            steps = [([p], 2 * p + rim) for p in range(pairs - 2)]
+            (out,) = mlp(*weights, mixed_inner, steps, rows, 0, kept=out)
         else:
-            outs = [mlp(*weights, mixed_outer, [(0, 0), (1, 1)], 2 * rim, edge, [channels])]
-            places = [(0, 0), (pairs - 3, 1)]
-            outs.append(mlp(*weights, mixed_inner, places, 2 * rim, edge, [channels]))
-            places = [(p + 1, p) for p in range(pairs - 4)]
-            outs.append(mlp(*weights, mixed_inner, places, rows - 4 * rim, edge, cuts))
+            outs = [mlp(*weights, mixed_outer, [([0], 0), ([1], 2)], 2 * rim, edge, [channels])]
+            outs.append(mlp(*weights, mixed_inner, [([0], 0), ([pairs - 3], 2)], 2 * rim, edge, [channels]))
+            steps = [([p + 1], 2 * p) for p in range(pairs - 4)]
+            outs.append(mlp(*weights, mixed_inner, steps, rows - 4 * rim, edge, cuts))
             mids = [o[0] for o in outs]
             mid_of = group_of
             firsts = [f for o in outs for f in o[1::2]]

time: 254 us -> 261 us (1.028)
  starting transfers between devices: 41.6 us -> 67.6 us
  waiting for transfers between devices: 88.7 us -> 74.9 us
  Pallas kernels: 94.9 us -> 86.3 us
  local copies, waits for them, and re-layouts: 12.2 us -> 18.5 us
    ppermute x20, starting transfers between devices: 30.3 us -> 48.8 us  [rotate(): lax.ppermute(block, axis, [(i, (i + hops) % count) for i in range(count)])]
    ppermute x20, waiting for transfers between devices: 88.7 us -> 74.9 us  [rotate(): lax.ppermute(block, axis, [(i, (i + hops) % count) for i in range(count)])]
    ppermute x4 -> x8, starting transfers between devices: 11.3 us -> 18.8 us  [step_rows(): return lax.ppermute(block, 'lat', pairs)]
    pallas_call x8, Pallas kernels: 61.9 us -> 56.2 us  [convolve(): pl.pallas_call(kernel, grid=(blocks,), out_shape=out, in_specs=[pl.BlockS...]
    unnamed x36 -> x50, local copies, waits for them, and re-layouts: 3.06 us -> 7.57 us
    pallas_call x5, Pallas kernels: 33 us -> 30 us  [mlp(): pl.pallas_call(functools.partial(mlp_kernel, half=edge, kept=len(extra),...]
    concatenate x4, other arithmetic: 4.56 us -> 1.9 us  [far(): return jnp.concatenate([halo[at:at + rim] for halo in halos[0]], axis=1)]
  transfers between devices with their start and end apart: 24 -> 28, of which waited for: 9 -> 10; matrix products, arithmetic and copies ran while one was open for 8% -> 8% of each run, Pallas kernels for 19% -> 17%
where the time goes in v5:
time: 261 us; the launch traced here: 259 us
  Pallas kernels  86.3 us (33%)
  waiting for transfers between devices  74.9 us (29%)
  starting transfers between devices  67.6 us (26%)
  local copies, waits for them, and re-layouts  18.5 us (7%)
  matrix products  6.75 us (3%)
  other arithmetic  4.31 us (2%)
    ppermute x20, waiting for transfers between devices, rotate(): lax.ppermute(block, axis, [(i, (i + hops) % count) for i in range(count)])  74.9 us
    pallas_call x8, Pallas kernels, convolve(): pl.pallas_call(kernel, grid=(blocks,), out_shape=out, in_specs=[pl.BlockS...  56.2 us
    ppermute x20, starting transfers between devices, rotate(): lax.ppermute(block, axis, [(i, (i + hops) % count) for i in range(count)])  48.8 us
    pallas_call x5, Pallas kernels, mlp(): pl.pallas_call(functools.partial(mlp_kernel, half=edge, kept=len(extra),...  30 us
    ppermute x8, starting transfers between devices, step_rows(): return lax.ppermute(block, 'lat', pairs)  18.8 us
    unnamed x50, local copies, waits for them, and re-layouts  7.57 us
    dot_general x2, matrix products, body(): jnp.einsum('kt,rtc->rkc', tap_basis, zonal_kernel[layer], preferred_eleme...  6.75 us
  transfers between devices with their start and end apart: 28, of which 10 were waited for; matrix products, arithmetic and copies ran while one was open for 8% of the time, Pallas kernels for 17%

profile of v5, /device:TPU:2, one launch (start us, length us, event | category | flops | bytes accessed | tf_op | source)
XLA Modules:
  0.0 258.9 jit_solution(5708266577926478618)
XLA Ops:
  0.0 1.0 fusion.6
  1.0 3.7 %collective-permute-start.13 = (bf16[4,128,128]{2,1,0:T(8,128)(2,1)S(1)}, bf16[4,128,128]{2,1,0:T(8,128)(2,1)S(1)}, u32[]{:S(2)}, u32[]{:S(2)}) collective-permute-start(bf16[4,128,128]{2,1,0:T(8,128)(2,1)S(1)} %get-tuple-element.35), channel_id=1, source_target_pairs={{0,3},{1,0},{2,1},{3,2},{4,7},{5,4},{6,5},{7,6},{8,11},{9,8},{10,9... | collective-permute-start | bytes 393224 | tf_op jit(solution)/shard_map/ppermute | solution.py:211
  4.7 2.0 fusion.7
  6.6 3.8 %collective-permute-start.11 = (bf16[4,128,256]{2,1,0:T(8,128)(2,1)S(1)}, bf16[4,128,256]{2,1,0:T(8,128)(2,1)S(1)}, u32[]{:S(2)}, u32[]{:S(2)}) collective-permute-start(bf16[4,128,256]{2,1,0:T(8,128)(2,1)S(1)} %get-tuple-element.37), channel_id=1, source_target_pairs={{0,3},{1,0},{2,1},{3,2},{4,7},{5,4},{6,5},{7,6},{8,11},{9,8},{10,9... | collective-permute-start | bytes 786440 | tf_op jit(solution)/shard_map/ppermute | solution.py:211
  10.5 2.8 %fusion.8 = (bf16[2,192,640]{2,1,0:T(8,128)(2,1)S(1)}, bf16[2,192,640]{2,1,0:T(8,128)(2,1)S(1)}, bf16[2,192,640]{2,1,0:T(8,128)(2,1)}, bf16[2,192,640]{2,1,0:T(8,128)(2,1)}) fusion(bf16[12,192,640]{2,1,0:T(8,128)(2,1)} %bitcast.29), kind=kLoop, calls=%fused_computation.25 | loop fusion | bytes 3932160 | tf_op jit(solution)/shard_map/slice | solution.py:271
  13.2 1.4 pad_maximum_fusion.1
  14.7 2.0 collective-permute-start
  16.7 2.0 slice_bitcast_fusion.1
  18.7 2.0 slice_bitcast_fusion
  20.7 1.0 pad_maximum_fusion
  22.2 3.4 %convolution_bitcast_fusion.refs_3_ = f32[5,448,640]{2,1,0:T(8,128)} fusion(bf16[448,256,1]{1,0,2:T(8,128)(2,1)S(1)} %copy-done.22, bf16[2,5,256,640]{3,2,1,0:T(8,128)(2,1)S(1)} %copy-done.20), kind=kOutput, calls=%fused_computation | convolution fusion | flops 734003200 | bytes 7602176 | tf_op jit(solution)/shard_map/kt,rtc->rkc/dot_general | solution.py:253
  25.6 6.5 %collective-permute-done.2.refs_7_.refs_8_ = bf16[4,128,640]{2,1,0:T(8,128)(2,1)S(1)} collective-permute-done((bf16[4,128,640]{2,1,0:T(8,128)(2,1)S(1)}, bf16[4,128,640]{2,1,0:T(8,128)(2,1)S(1)}, u32[]{:S(2)}, u32[]{:S(2)}) %collective-permute-start.2) | collective-permute-done | bytes 655392 | tf_op jit(solution)/shard_map/ppermute | solution.py:211
  32.1 3.5 %collective-permute-start.3 = (bf16[4,128,640]{2,1,0:T(8,128)(2,1)S(1)}, bf16[4,128,640]{2,1,0:T(8,128)(2,1)S(1)}, u32[]{:S(2)}, u32[]{:S(2)}) collective-permute-start(bf16[4,128,640]{2,1,0:T(8,128)(2,1)S(1)} %get-tuple-element.47), channel_id=1, source_target_pairs={{0,3},{1,0},{2,1},{3,2},{4,7},{5,4},{6,5},{7,6},{8,11},{9,8},{10,9... | collective-permute-start | bytes 1966088 | tf_op jit(solution)/shard_map/ppermute | solution.py:211
  36.3 0.7 copy-done.16
  37.0 3.8 %collective-permute-start.9 = (bf16[4,128,256]{2,1,0:T(8,128)(2,1)S(1)}, bf16[4,128,256]{2,1,0:T(8,128)(2,1)S(1)}, u32[]{:S(2)}, u32[]{:S(2)}) collective-permute-start(bf16[4,128,256]{2,1,0:T(8,128)(2,1)S(1)} %get-tuple-element.39), channel_id=1, source_target_pairs={{0,3},{1,0},{2,1},{3,2},{4,7},{5,4},{6,5},{7,6},{8,11},{9,8},{10,9... | collective-permute-start | bytes 786440 | tf_op jit(solution)/shard_map/ppermute | solution.py:211
  40.8 5.3 %collective-permute-done.refs_5_ = bf16[4,128,640]{2,1,0:T(8,128)(2,1)S(1)} collective-permute-done((bf16[4,128,640]{2,1,0:T(8,128)(2,1)S(1)}, bf16[4,128,640]{2,1,0:T(8,128)(2,1)S(1)}, u32[]{:S(2)}, u32[]{:S(2)}) %collective-permute-start) | collective-permute-done | bytes 655392 | tf_op jit(solution)/shard_map/ppermute | solution.py:211
  46.1 1.7 collective-permute-start.1
  47.9 0.9 pad_maximum_fusion.3
  48.8 0.9 pad_maximum_fusion.2
  49.7 1.9 collective-permute-start.4
  51.6 14.2 %collective-permute-done.10.refs_7_ = bf16[4,128,256]{2,1,0:T(8,128)(2,1)S(1)} collective-permute-done((bf16[4,128,256]{2,1,0:T(8,128)(2,1)S(1)}, bf16[4,128,256]{2,1,0:T(8,128)(2,1)S(1)}, u32[]{:S(2)}, u32[]{:S(2)}) %collective-permute-start.10) | collective-permute-done | bytes 262176 | tf_op jit(solution)/shard_map/ppermute | solution.py:211
  65.8 0.7 copy-done.10
  66.5 1.9 collective-permute-start.6
  68.4 2.9 %collective-permute-done.9.refs_10_ = bf16[4,128,256]{2,1,0:T(8,128)(2,1)S(1)} collective-permute-done((bf16[4,128,256]{2,1,0:T(8,128)(2,1)S(1)}, bf16[4,128,256]{2,1,0:T(8,128)(2,1)S(1)}, u32[]{:S(2)}, u32[]{:S(2)}) %collective-permute-start.9) | collective-permute-done | bytes 262176 | tf_op jit(solution)/shard_map/ppermute | solution.py:211
  71.3 0.7 copy-done.12
  72.1 1.9 collective-permute-start.5
  74.0 3.6 %collective-permute-start.7 = (bf16[2,256,640]{2,1,0:T(8,128)(2,1)}, bf16[2,256,640]{2,1,0:T(8,128)(2,1)}, u32[]{:S(2)}, u32[]{:S(2)}) collective-permute-start(bf16[2,256,640]{2,1,0:T(8,128)(2,1)} %pad_maximum_fusion.3), channel_id=1, source_target_pairs={{4,0},{8,4},{12,8},{16,12},{20,16},{24,20},{28,24},{5,1},{9,5},{13... | collective-permute-start | bytes 1966088 | tf_op jit(solution)/shard_map/ppermute | solution.py:231
  77.7 6.9 %collective-permute-done.1.refs_6_ = bf16[4,128,640]{2,1,0:T(8,128)(2,1)S(1)} collective-permute-done((bf16[4,128,640]{2,1,0:T(8,128)(2,1)}, bf16[4,128,640]{2,1,0:T(8,128)(2,1)S(1)}, u32[]{:S(2)}, u32[]{:S(2)}) %collective-permute-start.1) | collective-permute-done | bytes 655392 | tf_op jit(solution)/shard_map/ppermute | solution.py:211
  84.6 1.4 collective-permute-start.8
  86.0 0.9 copy-done.15
  86.9 0.9 copy-done.17
  87.8 3.8 %zonal_conv.11.refs_2_ = bf16[8,192,128]{2,1,0:T(8,128)(2,1)S(1)} custom-call(f32[16]{0:T(128)S(1)} %and_select_fusion.refs_0_, bf16[448,448]{1,0:T(8,128)(2,1)S(1)} %copy-done, bf16[192,448]{1,0:T(8,128)(2,1)S(1)} %copy-done.3, f32[5,448,640]{2,1,0:T(8,128)} %convolution_bitcast_fusion.refs_3_, bf16[12,192,640]{2,1,0:T(8,128)(2,1)} %bitcast.30, ...), custom_call_target="tpu_custom_call" | custom-call | flops 792723456 | bytes 2523136 | tf_op jit(solution)/shard_map/zonal_conv/pallas_call | solution.py:110
  91.7 6.3 %zonal_conv.10.refs_1_ = bf16[8,192,256]{2,1,0:T(8,128)(2,1)S(1)} custom-call(f32[16]{0:T(128)S(1)} %and_select_fusion.refs_0_, bf16[448,448]{1,0:T(8,128)(2,1)S(1)} %copy-done, bf16[192,448]{1,0:T(8,128)(2,1)S(1)} %copy-done.3, f32[5,448,640]{2,1,0:T(8,128)} %convolution_bitcast_fusion.refs_3_, bf16[12,192,640]{2,1,0:T(8,128)(2,1)} %bitcast.31, ...), custom_call_target="tpu_custom_call" | custom-call | flops 1585446912 | bytes 5046272 | tf_op jit(solution)/shard_map/zonal_conv/pallas_call | solution.py:110
  98.0 6.3 %zonal_conv.9.refs_0_ = bf16[8,192,256]{2,1,0:T(8,128)(2,1)S(1)} custom-call(f32[16]{0:T(128)S(1)} %and_select_fusion.refs_0_, bf16[448,448]{1,0:T(8,128)(2,1)S(1)} %copy-done, bf16[192,448]{1,0:T(8,128)(2,1)S(1)} %copy-done.3, f32[5,448,640]{2,1,0:T(8,128)} %convolution_bitcast_fusion.refs_3_, bf16[12,192,640]{2,1,0:T(8,128)(2,1)} %bitcast.32, ...), custom_call_target="tpu_custom_call" | custom-call | flops 1585446912 | bytes 5046272 | tf_op jit(solution)/shard_map/zonal_conv/pallas_call | solution.py:110
  104.3 11.9 %zonal_conv.8.refs_0_ = bf16[4,192,640]{2,1,0:T(8,128)(2,1)} custom-call(f32[16]{0:T(128)S(1)} %and_select_fusion.refs_0_, bf16[448,448]{1,0:T(8,128)(2,1)S(1)} %copy-done, bf16[192,448]{1,0:T(8,128)(2,1)S(1)} %copy-done.3, f32[5,448,640]{2,1,0:T(8,128)} %convolution_bitcast_fusion.refs_3_, bf16[12,192,640]{2,1,0:T(8,128)(2,1)} %bitcast.33, ...), custom_call_target="tpu_custom_call" | custom-call | flops 3523215360 | bytes 12615680 | tf_op jit(solution)/shard_map/zonal_conv/pallas_call | solution.py:110
  116.2 1.2 copy-done.8
  117.4 5.5 %channel_mlp.5 = (bf16[4,192,640]{2,1,0:T(8,128)(2,1)S(1)}, bf16[4,128,640]{2,1,0:T(8,128)(2,1)S(1)}, bf16[4,128,640]{2,1,0:T(8,128)(2,1)S(1)}) custom-call(f32[1,640]{1,0:T(1,128)S(1)} %get-tuple-element.59.gain, bf16[640,1280]{1,0:T(8,128)(2,1)S(1)} %copy-done.7, bf16[1280,640]{1,0:T(8,128)(2,1)} %get-tuple-element.31.w_out, bf16[4,192,640]{2,1,0:T(8,128)(2,1)S(1)} %copy-done.8), custom_call_target="tpu_custom_call" | custom-call | flops 2516582400 | bytes 5242880 | tf_op jit(solution)/shard_map/channel_mlp/pallas_call | solution.py:186
  122.9 1.6 collective-permute-start.14
  124.4 5.5 %channel_mlp.7 = (bf16[4,192,640]{2,1,0:T(8,128)(2,1)S(1)}, bf16[4,128,256]{2,1,0:T(8,128)(2,1)S(1)}, bf16[4,128,256]{2,1,0:T(8,128)(2,1)S(1)}, bf16[4,128,256]{...) custom-call(f32[1,640]{1,0:T(1,128)S(1)} %get-tuple-element.59.gain,, ...), custom_call_target="tpu_custom_call" | custom-call | flops 2516582400 | bytes 5242880 | tf_op jit(solution)/shard_map/channel_mlp/pallas_call | solution.py:186
  129.9 1.5 collective-permute-start.22
  131.4 2.4 collective-permute-start.23
  133.8 0.7 collective-permute-start.17
  134.5 5.5 %channel_mlp.6 = (bf16[4,192,640]{2,1,0:T(8,128)(2,1)S(1)}, bf16[4,128,640]{2,1,0:T(8,128)(2,1)S(1)}, bf16[4,128,640]{2,1,0:T(8,128)(2,1)S(1)}) custom-call(f32[1,640]{1,0:T(1,128)S(1)} %get-tuple-element.59.gain, bf16[640,1280]{1,0:T(8,128)(2,1)S(1)} %copy-done.7, bf16[1280,640]{1,0:T(8,128)(2,1)} %get-tuple-element.31.w_out, ...), custom_call_target="tpu_custom_call" | custom-call | flops 2516582400 | bytes 5242880 | tf_op jit(solution)/shard_map/channel_mlp/pallas_call | solution.py:186
  140.0 1.4 collective-permute-start.15
  141.4 1.0 fusion.9
  142.6 2.3 collective-permute-start.18
  145.4 14.7 %collective-permute-start.16 = (bf16[4,128,256]{2,1,0:T(8,128)(2,1)S(1)}, bf16[4,128,256]{2,1,0:T(8,128)(2,1)S(1)}, u32[]{:S(2)}, u32[]{:S(2)}) collective-permute-start(bf16[4,128,256]{2,1,0:T(8,128)(2,1)S(1)} %get-tuple-element.23), channel_id=1, source_target_pairs={{0,1},{1,2},{2,3},{3,0},{4,5},{5,6},{6,7},{7,4},{8,9},{9,10},{10,1... | collective-permute-start | bytes 786440 | tf_op jit(solution)/shard_map/ppermute | solution.py:211
  160.1 3.0 %collective-permute-start.20 = (bf16[4,128,256]{2,1,0:T(8,128)(2,1)S(1)}, bf16[4,128,256]{2,1,0:T(8,128)(2,1)S(1)}, u32[]{:S(2)}, u32[]{:S(2)}) collective-permute-start(bf16[4,128,256]{2,1,0:T(8,128)(2,1)S(1)} %get-tuple-element.27), channel_id=1, source_target_pairs={{0,1},{1,2},{2,3},{3,0},{4,5},{5,6},{6,7},{7,4},{8,9},{9,10},{10,1... | collective-permute-start | bytes 786440 | tf_op jit(solution)/shard_map/ppermute | solution.py:211
  163.0 0.8 collective-permute-start.21
  164.1 32.0 %collective-permute-done.16.refs_9_ = bf16[4,128,256]{2,1,0:T(8,128)(2,1)S(1)} collective-permute-done((bf16[4,128,256]{2,1,0:T(8,128)(2,1)S(1)}, bf16[4,128,256]{2,1,0:T(8,128)(2,1)S(1)}, u32[]{:S(2)}, u32[]{:S(2)}) %collective-permute-start.16) | collective-permute-done | bytes 262176 | tf_op jit(solution)/shard_map/ppermute | solution.py:211
  196.5 5.1 %collective-permute-done.20.refs_9_ = bf16[4,128,256]{2,1,0:T(8,128)(2,1)S(1)} collective-permute-done((bf16[4,128,256]{2,1,0:T(8,128)(2,1)S(1)}, bf16[4,128,256]{2,1,0:T(8,128)(2,1)S(1)}, u32[]{:S(2)}, u32[]{:S(2)}) %collective-permute-start.20) | collective-permute-done | bytes 262176 | tf_op jit(solution)/shard_map/ppermute | solution.py:211
  201.6 1.9 collective-permute-start.26
  203.5 1.4 collective-permute-done.21.refs_12_
  205.0 1.9 collective-permute-start.24
  206.9 3.5 %collective-permute-start.25 = (bf16[2,256,640]{2,1,0:T(8,128)(2,1)S(1)}, bf16[2,256,640]{2,1,0:T(8,128)(2,1)S(1)}, u32[]{:S(2)}, u32[]{:S(2)}) collective-permute-start(bf16[2,256,640]{2,1,0:T(8,128)(2,1)S(1)} %pad_maximum_fusion.4), channel_id=1, source_target_pairs={{0,4},{4,8},{8,12},{12,16},{16,20},{20,24},{24,28},{1,5},{5,9},{9,... | collective-permute-start | bytes 1966088 | tf_op jit(solution)/shard_map/ppermute | solution.py:231
  210.4 2.1 collective-permute-start.27
  212.5 3.4 %convolution_bitcast_fusion.1.refs_3_ = f32[5,448,640]{2,1,0:T(8,128)} fusion(bf16[448,256,1]{1,0,2:T(8,128)(2,1)S(1)} %copy-done.23, bf16[2,5,256,640]{3,2,1,0:T(8,128)(2,1)S(1)} %copy-done.21), kind=kOutput, calls=%fused_computation.1 | convolution fusion | flops 734003200 | bytes 7602176 | tf_op jit(solution)/shard_map/kt,rtc->rkc/dot_general | solution.py:253
  215.9 3.6 %zonal_conv.14.refs_2_ = bf16[8,192,128]{2,1,0:T(8,128)(2,1)S(1)} custom-call(f32[16]{0:T(128)S(1)} %and_select_fusion.refs_0_, bf16[448,448]{1,0:T(8,128)(2,1)S(1)} %copy-done, bf16[192,448]{1,0:T(8,128)(2,1)S(1)} %copy-done.3, f32[5,448,640]{2,1,0:T(8,128)} %convolution_bitcast_fusion.1.refs_3_, bf16[4,192,640]{2,1,0:T(8,128)(2,1)S(1)} %get-tuple-element.18.refs_4_, ...), custom_call_target="tpu_custom_call" | custom-call | flops 792723456 | bytes 2523136 | tf_op jit(solution)/shard_map/zonal_conv/pallas_call | solution.py:110
  219.5 6.2 %zonal_conv.13.refs_1_ = bf16[8,192,256]{2,1,0:T(8,128)(2,1)S(1)} custom-call(f32[16]{0:T(128)S(1)} %and_select_fusion.refs_0_, bf16[448,448]{1,0:T(8,128)(2,1)S(1)} %copy-done, bf16[192,448]{1,0:T(8,128)(2,1)S(1)} %copy-done.3, f32[5,448,640]{2,1,0:T(8,128)} %convolution_bitcast_fusion.1.refs_3_, bf16[4,192,640]{2,1,0:T(8,128)(2,1)S(1)} %get-tuple-element.18.refs_4_, ...), custom_call_target="tpu_custom_call" | custom-call | flops 1585446912 | bytes 5046272 | tf_op jit(solution)/shard_map/zonal_conv/pallas_call | solution.py:110
  225.7 6.2 %zonal_conv.12.refs_0_ = bf16[8,192,256]{2,1,0:T(8,128)(2,1)S(1)} custom-call(f32[16]{0:T(128)S(1)} %and_select_fusion.refs_0_, bf16[448,448]{1,0:T(8,128)(2,1)S(1)} %copy-done, bf16[192,448]{1,0:T(8,128)(2,1)S(1)} %copy-done.3, f32[5,448,640]{2,1,0:T(8,128)} %convolution_bitcast_fusion.1.refs_3_, bf16[4,192,640]{2,1,0:T(8,128)(2,1)S(1)} %get-tuple-element.18.refs_4_, ...), custom_call_target="tpu_custom_call" | custom-call | flops 1585446912 | bytes 5046272 | tf_op jit(solution)/shard_map/zonal_conv/pallas_call | solution.py:110
  232.0 12.0 %zonal_conv.15.refs_0_ = bf16[4,192,640]{2,1,0:T(8,128)(2,1)} custom-call(f32[16]{0:T(128)S(1)} %and_select_fusion.refs_0_, bf16[448,448]{1,0:T(8,128)(2,1)S(1)} %copy-done, bf16[192,448]{1,0:T(8,128)(2,1)S(1)} %copy-done.3, f32[5,448,640]{2,1,0:T(8,128)} %convolution_bitcast_fusion.1.refs_3_, bf16[4,192,640]{2,1,0:T(8,128)(2,1)} %copy-done.1, ...), custom_call_target="tpu_custom_call" | custom-call | flops 3523215360 | bytes 12615680 | tf_op jit(solution)/shard_map/zonal_conv/pallas_call | solution.py:110
  244.0 1.2 copy-done.9
  245.2 4.8 %channel_mlp.8.refs_3_ = bf16[12,192,640]{2,1,0:T(8,128)(2,1)} custom-call(f32[1,640]{1,0:T(1,128)S(1)} %get-tuple-element.60.gain, bf16[640,1280]{1,0:T(8,128)(2,1)S(1)} %copy-done.5, bf16[1280,640]{1,0:T(8,128)(2,1)S(1)} %copy-done.6, bf16[4,192,640]{2,1,0:T(8,128)(2,1)S(1)} %copy-done.9), custom_call_target="tpu_custom_call" | custom-call | flops 2516582400 | bytes 5242880 | tf_op jit(solution)/shard_map/channel_mlp/pallas_call | solution.py:186
  250.0 8.9 %channel_mlp.9 = bf16[12,192,640]{2,1,0:T(8,128)(2,1)} custom-call(f32[1,640]{1,0:T(1,128)S(1)} %get-tuple-element.60.gain, bf16[640,1280]{1,0:T(8,128)(2,1)S(1)} %copy-done.5, bf16[1280,640]{1,0:T(8,128)(2,1)S(1)} %copy-done.6, bf16[8,192,256]{2,1,0:T(8,128)(2,1)S(1)} %zonal_conv.12.refs_0_, ...), custom_call_target="tpu_custom_call", output_to_operand_aliasing={{}: (6, {})} | custom-call | flops 5033164800 | bytes 7208960 | tf_op jit(solution)/shard_map/channel_mlp/pallas_call | solution.py:186
  (75 shorter events, 2.9 us)
Async XLA Ops:
  1.0 34.6 %collective-permute-start.13 = (bf16[4,128,128]{2,1,0:T(8,128)(2,1)S(1)}, bf16[4,128,128]{2,1,0:T(8,128)(2,1)S(1)}, u32[]{:S(2)}, u32[]{:S(2)}) collective-permute-start(bf16[4,128,128]{2,1,0:T(8,128)(2,1)S(1)} %get-tuple-element.35), channel_id=1, source_target_pairs={{0,3},{1,0},{2,1},{3,2},{4,7},{5,4},{6,5},{7,6},{8,11},{9,8},{10,9... | collective-permute-start | bytes 393224 | tf_op jit(solution)/shard_map/ppermute | solution.py:211
  4.7 31.6 %collective-permute-start.12 = (bf16[4,128,128]{2,1,0:T(8,128)(2,1)S(1)}, bf16[4,128,128]{2,1,0:T(8,128)(2,1)S(1)}, u32[]{:S(2)}, u32[]{:S(2)}) collective-permute-start(bf16[4,128,128]{2,1,0:T(8,128)(2,1)S(1)} %get-tuple-element.36), channel_id=1, source_target_pairs={{0,1},{1,2},{2,3},{3,0},{4,5},{5,6},{6,7},{7,4},{8,9},{9,10},{10,1... | collective-permute-start | bytes 393224 | tf_op jit(solution)/shard_map/ppermute | solution.py:211
  6.6 43.1 %collective-permute-start.11 = (bf16[4,128,256]{2,1,0:T(8,128)(2,1)S(1)}, bf16[4,128,256]{2,1,0:T(8,128)(2,1)S(1)}, u32[]{:S(2)}, u32[]{:S(2)}) collective-permute-start(bf16[4,128,256]{2,1,0:T(8,128)(2,1)S(1)} %get-tuple-element.37), channel_id=1, source_target_pairs={{0,3},{1,0},{2,1},{3,2},{4,7},{5,4},{6,5},{7,6},{8,11},{9,8},{10,9... | collective-permute-start | bytes 786440 | tf_op jit(solution)/shard_map/ppermute | solution.py:211
  10.5 6.2 %copy-start.18 = (bf16[2,640,1280]{2,1,0:T(8,128)(2,1)S(1)}, bf16[2,640,1280]{2,1,0:T(8,128)(2,1)}, u32[]{:S(2)}) copy-start(bf16[2,640,1280]{2,1,0:T(8,128)(2,1)} %param.11) | copy-start | bytes 9830404
  14.6 17.4 %collective-permute-start.2 = (bf16[4,128,640]{2,1,0:T(8,128)(2,1)S(1)}, bf16[4,128,640]{2,1,0:T(8,128)(2,1)S(1)}, u32[]{:S(2)}, u32[]{:S(2)}) collective-permute-start(bf16[4,128,640]{2,1,0:T(8,128)(2,1)S(1)} %get-tuple-element.49), channel_id=1, source_target_pairs={{0,3},{1,0},{2,1},{3,2},{4,7},{5,4},{6,5},{7,6},{8,11},{9,8},{10,9... | collective-permute-start | bytes 1966088 | tf_op jit(solution)/shard_map/ppermute | solution.py:211
  14.7 4.0 %copy-start.19 = (bf16[2,1280,640]{2,1,0:T(8,128)(2,1)S(1)}, bf16[2,1280,640]{2,1,0:T(8,128)(2,1)}, u32[]{:S(2)}) copy-start(bf16[2,1280,640]{2,1,0:T(8,128)(2,1)} %param.12) | copy-start | bytes 9830404
  14.7 31.4 %collective-permute-start = (bf16[4,128,640]{2,1,0:T(8,128)(2,1)S(1)}, bf16[4,128,640]{2,1,0:T(8,128)(2,1)S(1)}, u32[]{:S(2)}, u32[]{:S(2)}) collective-permute-start(bf16[4,128,640]{2,1,0:T(8,128)(2,1)S(1)} %get-tuple-element.50), channel_id=1, source_target_pairs={{0,1},{1,2},{2,3},{3,0},{4,5},{5,6},{6,7},{7,4},{8,9},{9,10},{10,1... | collective-permute-start | bytes 1966088 | tf_op jit(solution)/shard_map/ppermute | solution.py:211
  18.7 3.2 %copy-start.20 = (bf16[2,5,256,640]{3,2,1,0:T(8,128)(2,1)S(1)}, bf16[2,5,256,640]{3,2,1,0:T(8,128)(2,1)}, u32[]{:S(2)}) copy-start(bf16[2,5,256,640]{3,2,1,0:T(8,128)(2,1)} %param.9) | copy-start | bytes 9830404
  20.7 1.5 copy-start.22
  32.1 41.9 %collective-permute-start.3 = (bf16[4,128,640]{2,1,0:T(8,128)(2,1)S(1)}, bf16[4,128,640]{2,1,0:T(8,128)(2,1)S(1)}, u32[]{:S(2)}, u32[]{:S(2)}) collective-permute-start(bf16[4,128,640]{2,1,0:T(8,128)(2,1)S(1)} %get-tuple-element.47), channel_id=1, source_target_pairs={{0,3},{1,0},{2,1},{3,2},{4,7},{5,4},{6,5},{7,6},{8,11},{9,8},{10,9... | collective-permute-start | bytes 1966088 | tf_op jit(solution)/shard_map/ppermute | solution.py:211
  35.6 0.6 copy-start.14
  36.3 29.5 %collective-permute-start.10 = (bf16[4,128,256]{2,1,0:T(8,128)(2,1)S(1)}, bf16[4,128,256]{2,1,0:T(8,128)(2,1)S(1)}, u32[]{:S(2)}, u32[]{:S(2)}) collective-permute-start(bf16[4,128,256]{2,1,0:T(8,128)(2,1)S(1)} %get-tuple-element.38), channel_id=1, source_target_pairs={{0,1},{1,2},{2,3},{3,0},{4,5},{5,6},{6,7},{7,4},{8,9},{9,10},{10,1... | collective-permute-start | bytes 786440 | tf_op jit(solution)/shard_map/ppermute | solution.py:211
  36.3 0.7 copy-start.16
  37.0 34.4 %collective-permute-start.9 = (bf16[4,128,256]{2,1,0:T(8,128)(2,1)S(1)}, bf16[4,128,256]{2,1,0:T(8,128)(2,1)S(1)}, u32[]{:S(2)}, u32[]{:S(2)}) collective-permute-start(bf16[4,128,256]{2,1,0:T(8,128)(2,1)S(1)} %get-tuple-element.39), channel_id=1, source_target_pairs={{0,3},{1,0},{2,1},{3,2},{4,7},{5,4},{6,5},{7,6},{8,11},{9,8},{10,9... | collective-permute-start | bytes 786440 | tf_op jit(solution)/shard_map/ppermute | solution.py:211
  46.1 38.5 %collective-permute-start.1 = (bf16[4,128,640]{2,1,0:T(8,128)(2,1)}, bf16[4,128,640]{2,1,0:T(8,128)(2,1)S(1)}, u32[]{:S(2)}, u32[]{:S(2)}) collective-permute-start(bf16[4,128,640]{2,1,0:T(8,128)(2,1)} %get-tuple-element.48), channel_id=1, source_target_pairs={{0,1},{1,2},{2,3},{3,0},{4,5},{5,6},{6,7},{7,4},{8,9},{9,10},{10,1... | collective-permute-start | bytes 1966088 | tf_op jit(solution)/shard_map/ppermute | solution.py:211
  47.9 29.8 %copy-start.24 = (bf16[2,640]{1,0:T(2,128)(2,1)S(1)}, bf16[2,640]{1,0:T(2,128)(2,1)}, u32[]{:S(2)}) copy-start(bf16[2,640]{1,0:T(2,128)(2,1)} %param.10) | copy-start | bytes 7684
  47.9 38.1 %copy-start = (bf16[448,448]{1,0:T(8,128)(2,1)S(1)}, bf16[448,448]{1,0:T(8,128)(2,1)}, u32[]{:S(2)}) copy-start(bf16[448,448]{1,0:T(8,128)(2,1)} %constant.30.clone.refs_1_) | copy-start | bytes 1204228
  47.9 38.1 %copy-start.3 = (bf16[192,448]{1,0:T(8,128)(2,1)S(1)}, bf16[192,448]{1,0:T(8,128)(2,1)}, u32[]{:S(2)}) copy-start(bf16[192,448]{1,0:T(8,128)(2,1)} %constant.31.clone.refs_2_) | copy-start | bytes 516100
  49.7 54.6 %collective-permute-start.4 = (bf16[2,192,640]{2,1,0:T(8,128)(2,1)}, bf16[2,192,640]{2,1,0:T(8,128)(2,1)}, u32[]{:S(2)}, u32[]{:S(2)}) collective-permute-start(bf16[2,192,640]{2,1,0:T(8,128)(2,1)} %get-tuple-element.43), channel_id=1, source_target_pairs={{0,4},{4,8},{8,12},{12,16},{16,20},{20,24},{24,28},{1,5},{5,9},{9,... | collective-permute-start | bytes 1474568 | tf_op jit(solution)/shard_map/ppermute | solution.py:231
  65.8 0.7 copy-start.10
  66.5 37.8 %collective-permute-start.6 = (bf16[2,192,640]{2,1,0:T(8,128)(2,1)}, bf16[2,192,640]{2,1,0:T(8,128)(2,1)}, u32[]{:S(2)}, u32[]{:S(2)}) collective-permute-start(bf16[2,192,640]{2,1,0:T(8,128)(2,1)} %get-tuple-element.44), channel_id=1, source_target_pairs={{4,0},{8,4},{12,8},{16,12},{20,16},{24,20},{28,24},{5,1},{9,5},{13... | collective-permute-start | bytes 1474568 | tf_op jit(solution)/shard_map/ppermute | solution.py:231
  71.3 0.7 copy-start.12
  72.1 32.3 %collective-permute-start.5 = (bf16[2,256,640]{2,1,0:T(8,128)(2,1)}, bf16[2,256,640]{2,1,0:T(8,128)(2,1)}, u32[]{:S(2)}, u32[]{:S(2)}) collective-permute-start(bf16[2,256,640]{2,1,0:T(8,128)(2,1)} %pad_maximum_fusion.2), channel_id=1, source_target_pairs={{0,4},{4,8},{8,12},{12,16},{16,20},{20,24},{24,28},{1,5},{5,9},{9,... | collective-permute-start | bytes 1966088 | tf_op jit(solution)/shard_map/ppermute | solution.py:231
  74.0 30.3 %collective-permute-start.7 = (bf16[2,256,640]{2,1,0:T(8,128)(2,1)}, bf16[2,256,640]{2,1,0:T(8,128)(2,1)}, u32[]{:S(2)}, u32[]{:S(2)}) collective-permute-start(bf16[2,256,640]{2,1,0:T(8,128)(2,1)} %pad_maximum_fusion.3), channel_id=1, source_target_pairs={{4,0},{8,4},{12,8},{16,12},{20,16},{24,20},{28,24},{5,1},{9,5},{13... | collective-permute-start | bytes 1966088 | tf_op jit(solution)/shard_map/ppermute | solution.py:231
  84.6 13.4 %collective-permute-start.8 = (bf16[4,128,256]{2,1,0:T(8,128)(2,1)}, bf16[4,128,256]{2,1,0:T(8,128)(2,1)S(1)}, u32[]{:S(2)}, u32[]{:S(2)}) collective-permute-start(bf16[4,128,256]{2,1,0:T(8,128)(2,1)} %get-tuple-element.40), channel_id=1, source_target_pairs={{0,1},{1,2},{2,3},{3,0},{4,5},{5,6},{6,7},{7,4},{8,9},{9,10},{10,1... | collective-permute-start | bytes 786440 | tf_op jit(solution)/shard_map/ppermute | solution.py:211
  86.0 0.9 copy-start.15
  86.9 0.9 copy-start.17
  87.8 3.8 %copy-start.11 = (bf16[4,128,256]{2,1,0:T(8,128)(2,1)S(1)}, bf16[4,128,256]{2,1,0:T(8,128)(2,1)}, u32[]{:S(2)}) copy-start(bf16[4,128,256]{2,1,0:T(8,128)(2,1)} %copy-done.10) | copy-start | bytes 786436
  91.7 6.4 %copy-start.13 = (bf16[4,128,256]{2,1,0:T(8,128)(2,1)S(1)}, bf16[4,128,256]{2,1,0:T(8,128)(2,1)}, u32[]{:S(2)}) copy-start(bf16[4,128,256]{2,1,0:T(8,128)(2,1)} %copy-done.12) | copy-start | bytes 786436
  104.3 11.9 %copy-start.7 = (bf16[640,1280]{1,0:T(8,128)(2,1)S(1)}, bf16[640,1280]{1,0:T(8,128)(2,1)}, u32[]{:S(2)}) copy-start(bf16[640,1280]{1,0:T(8,128)(2,1)} %get-tuple-element.33.w_in) | copy-start | bytes 4915204
  116.2 1.2 copy-start.8
  122.9 102.9 %copy-start.1 = (bf16[4,192,640]{2,1,0:T(8,128)(2,1)}, bf16[4,192,640]{2,1,0:T(8,128)(2,1)S(1)}, u32[]{:S(2)}) copy-start(bf16[4,192,640]{2,1,0:T(8,128)(2,1)S(1)} %get-tuple-element.18.refs_4_) | copy-start | bytes 2949124
  122.9 19.7 %collective-permute-start.14 = (bf16[4,128,640]{2,1,0:T(8,128)(2,1)S(1)}, bf16[4,128,640]{2,1,0:T(8,128)(2,1)S(1)}, u32[]{:S(2)}, u32[]{:S(2)}) collective-permute-start(bf16[4,128,640]{2,1,0:T(8,128)(2,1)S(1)} %get-tuple-element.21), channel_id=1, source_target_pairs={{0,1},{1,2},{2,3},{3,0},{4,5},{5,6},{6,7},{7,4},{8,9},{9,10},{10,1... | collective-permute-start | bytes 1966088 | tf_op jit(solution)/shard_map/ppermute | solution.py:211
  129.9 10.0 %copy-start.4 = (bf16[4,192,640]{2,1,0:T(8,128)(2,1)}, bf16[4,192,640]{2,1,0:T(8,128)(2,1)S(1)}, u32[]{:S(2)}) copy-start(bf16[4,192,640]{2,1,0:T(8,128)(2,1)S(1)} %get-tuple-element.20.refs_6_) | copy-start | bytes 2949124
  129.9 15.5 %collective-permute-start.22 = (bf16[4,128,128]{2,1,0:T(8,128)(2,1)S(1)}, bf16[4,128,128]{2,1,0:T(8,128)(2,1)S(1)}, u32[]{:S(2)}, u32[]{:S(2)}) collective-permute-start(bf16[4,128,128]{2,1,0:T(8,128)(2,1)S(1)} %get-tuple-element.29), channel_id=1, source_target_pairs={{0,1},{1,2},{2,3},{3,0},{4,5},{5,6},{6,7},{7,4},{8,9},{9,10},{10,1... | collective-permute-start | bytes 393224 | tf_op jit(solution)/shard_map/ppermute | solution.py:211
  131.4 28.7 %collective-permute-start.23 = (bf16[4,128,128]{2,1,0:T(8,128)(2,1)S(1)}, bf16[4,128,128]{2,1,0:T(8,128)(2,1)S(1)}, u32[]{:S(2)}, u32[]{:S(2)}) collective-permute-start(bf16[4,128,128]{2,1,0:T(8,128)(2,1)S(1)} %get-tuple-element.30), channel_id=1, source_target_pairs={{0,3},{1,0},{2,1},{3,2},{4,7},{5,4},{6,5},{7,6},{8,11},{9,8},{10,9... | collective-permute-start | bytes 393224 | tf_op jit(solution)/shard_map/ppermute | solution.py:211
  133.8 29.3 %collective-permute-start.17 = (bf16[4,128,640]{2,1,0:T(8,128)(2,1)S(1)}, bf16[4,128,640]{2,1,0:T(8,128)(2,1)S(1)}, u32[]{:S(2)}, u32[]{:S(2)}) collective-permute-start(bf16[4,128,640]{2,1,0:T(8,128)(2,1)S(1)} %get-tuple-element.24), channel_id=1, source_target_pairs={{0,3},{1,0},{2,1},{3,2},{4,7},{5,4},{6,5},{7,6},{8,11},{9,8},{10,9... | collective-permute-start | bytes 1966088 | tf_op jit(solution)/shard_map/ppermute | solution.py:211
  140.0 75.9 %copy-start.2 = (bf16[4,192,640]{2,1,0:T(8,128)(2,1)}, bf16[4,192,640]{2,1,0:T(8,128)(2,1)S(1)}, u32[]{:S(2)}) copy-start(bf16[4,192,640]{2,1,0:T(8,128)(2,1)S(1)} %get-tuple-element.19.refs_5_) | copy-start | bytes 2949124
  140.0 66.9 %collective-permute-start.15 = (bf16[4,128,640]{2,1,0:T(8,128)(2,1)S(1)}, bf16[4,128,640]{2,1,0:T(8,128)(2,1)S(1)}, u32[]{:S(2)}, u32[]{:S(2)}) collective-permute-start(bf16[4,128,640]{2,1,0:T(8,128)(2,1)S(1)} %get-tuple-element.22), channel_id=1, source_target_pairs={{0,1},{1,2},{2,3},{3,0},{4,5},{5,6},{6,7},{7,4},{8,9},{9,10},{10,1... | collective-permute-start | bytes 1966088 | tf_op jit(solution)/shard_map/ppermute | solution.py:211
  142.6 67.8 %collective-permute-start.18 = (bf16[4,128,640]{2,1,0:T(8,128)(2,1)S(1)}, bf16[4,128,640]{2,1,0:T(8,128)(2,1)S(1)}, u32[]{:S(2)}, u32[]{:S(2)}) collective-permute-start(bf16[4,128,640]{2,1,0:T(8,128)(2,1)S(1)} %get-tuple-element.25), channel_id=1, source_target_pairs={{0,3},{1,0},{2,1},{3,2},{4,7},{5,4},{6,5},{7,6},{8,11},{9,8},{10,9... | collective-permute-start | bytes 1966088 | tf_op jit(solution)/shard_map/ppermute | solution.py:211
  145.4 50.7 %collective-permute-start.16 = (bf16[4,128,256]{2,1,0:T(8,128)(2,1)S(1)}, bf16[4,128,256]{2,1,0:T(8,128)(2,1)S(1)}, u32[]{:S(2)}, u32[]{:S(2)}) collective-permute-start(bf16[4,128,256]{2,1,0:T(8,128)(2,1)S(1)} %get-tuple-element.23), channel_id=1, source_target_pairs={{0,1},{1,2},{2,3},{3,0},{4,5},{5,6},{6,7},{7,4},{8,9},{9,10},{10,1... | collective-permute-start | bytes 786440 | tf_op jit(solution)/shard_map/ppermute | solution.py:211
  160.1 41.6 %collective-permute-start.20 = (bf16[4,128,256]{2,1,0:T(8,128)(2,1)S(1)}, bf16[4,128,256]{2,1,0:T(8,128)(2,1)S(1)}, u32[]{:S(2)}, u32[]{:S(2)}) collective-permute-start(bf16[4,128,256]{2,1,0:T(8,128)(2,1)S(1)} %get-tuple-element.27), channel_id=1, source_target_pairs={{0,1},{1,2},{2,3},{3,0},{4,5},{5,6},{6,7},{7,4},{8,9},{9,10},{10,1... | collective-permute-start | bytes 786440 | tf_op jit(solution)/shard_map/ppermute | solution.py:211
  163.0 41.9 %collective-permute-start.21 = (bf16[4,128,256]{2,1,0:T(8,128)(2,1)S(1)}, bf16[4,128,256]{2,1,0:T(8,128)(2,1)S(1)}, u32[]{:S(2)}, u32[]{:S(2)}) collective-permute-start(bf16[4,128,256]{2,1,0:T(8,128)(2,1)S(1)} %get-tuple-element.28), channel_id=1, source_target_pairs={{0,3},{1,0},{2,1},{3,2},{4,7},{5,4},{6,5},{7,6},{8,11},{9,8},{10,9... | collective-permute-start | bytes 786440 | tf_op jit(solution)/shard_map/ppermute | solution.py:211
  163.9 48.6 %copy-start.21 = (bf16[2,5,256,640]{3,2,1,0:T(8,128)(2,1)S(1)}, bf16[2,5,256,640]{3,2,1,0:T(8,128)(2,1)}, u32[]{:S(2)}) copy-start(bf16[2,5,256,640]{3,2,1,0:T(8,128)(2,1)} %param.9) | copy-start | bytes 9830404
  164.0 48.5 %copy-start.23 = (bf16[448,256,1]{1,0,2:T(8,128)(2,1)S(1)}, bf16[448,256,1]{1,0,2:T(8,128)(2,1)}, u32[]{:S(2)}) copy-start(bf16[448,256,1]{1,0,2:T(8,128)(2,1)} %constant.34) | copy-start | bytes 688132
  196.1 29.7 %collective-permute-start.19 = (bf16[4,128,256]{2,1,0:T(8,128)(2,1)S(1)}, bf16[4,128,256]{2,1,0:T(8,128)(2,1)S(1)}, u32[]{:S(2)}, u32[]{:S(2)}) collective-permute-start(bf16[4,128,256]{2,1,0:T(8,128)(2,1)S(1)} %get-tuple-element.26), channel_id=1, source_target_pairs={{0,3},{1,0},{2,1},{3,2},{4,7},{5,4},{6,5},{7,6},{8,11},{9,8},{10,9... | collective-permute-start | bytes 786440 | tf_op jit(solution)/shard_map/ppermute | solution.py:211
  201.6 30.3 %collective-permute-start.26 = (bf16[2,192,640]{2,1,0:T(8,128)(2,1)}, bf16[2,192,640]{2,1,0:T(8,128)(2,1)S(1)}, u32[]{:S(2)}, u32[]{:S(2)}) collective-permute-start(bf16[2,192,640]{2,1,0:T(8,128)(2,1)} %get-tuple-element.45), channel_id=1, source_target_pairs={{4,0},{8,4},{12,8},{16,12},{20,16},{24,20},{28,24},{5,1},{9,5},{13... | collective-permute-start | bytes 1474568 | tf_op jit(solution)/shard_map/ppermute | solution.py:231
  205.0 27.0 %collective-permute-start.24 = (bf16[2,192,640]{2,1,0:T(8,128)(2,1)}, bf16[2,192,640]{2,1,0:T(8,128)(2,1)S(1)}, u32[]{:S(2)}, u32[]{:S(2)}) collective-permute-start(bf16[2,192,640]{2,1,0:T(8,128)(2,1)} %get-tuple-element.46), channel_id=1, source_target_pairs={{0,4},{4,8},{8,12},{12,16},{16,20},{20,24},{24,28},{1,5},{5,9},{9,... | collective-permute-start | bytes 1474568 | tf_op jit(solution)/shard_map/ppermute | solution.py:231
  206.9 25.1 %collective-permute-start.25 = (bf16[2,256,640]{2,1,0:T(8,128)(2,1)S(1)}, bf16[2,256,640]{2,1,0:T(8,128)(2,1)S(1)}, u32[]{:S(2)}, u32[]{:S(2)}) collective-permute-start(bf16[2,256,640]{2,1,0:T(8,128)(2,1)S(1)} %pad_maximum_fusion.4), channel_id=1, source_target_pairs={{0,4},{4,8},{8,12},{12,16},{16,20},{20,24},{24,28},{1,5},{5,9},{9,... | collective-permute-start | bytes 1966088 | tf_op jit(solution)/shard_map/ppermute | solution.py:231
  210.4 21.6 %collective-permute-start.27 = (bf16[2,256,640]{2,1,0:T(8,128)(2,1)S(1)}, bf16[2,256,640]{2,1,0:T(8,128)(2,1)S(1)}, u32[]{:S(2)}, u32[]{:S(2)}) collective-permute-start(bf16[2,256,640]{2,1,0:T(8,128)(2,1)S(1)} %pad_maximum_fusion.5), channel_id=1, source_target_pairs={{4,0},{8,4},{12,8},{16,12},{20,16},{24,20},{28,24},{5,1},{9,5},{13... | collective-permute-start | bytes 1966088 | tf_op jit(solution)/shard_map/ppermute | solution.py:231
  231.9 12.0 %copy-start.5 = (bf16[640,1280]{1,0:T(8,128)(2,1)S(1)}, bf16[640,1280]{1,0:T(8,128)(2,1)}, u32[]{:S(2)}) copy-start(bf16[640,1280]{1,0:T(8,128)(2,1)} %get-tuple-element.34.w_in) | copy-start | bytes 4915204
  232.0 12.0 %copy-start.6 = (bf16[1280,640]{1,0:T(8,128)(2,1)S(1)}, bf16[1280,640]{1,0:T(8,128)(2,1)}, u32[]{:S(2)}) copy-start(bf16[1280,640]{1,0:T(8,128)(2,1)} %get-tuple-element.32.w_out) | copy-start | bytes 4915204
  244.0 1.2 copy-start.9

commit v6 on v5

--- a/solution.py
+++ b/solution.py
@@ -118,7 +118,7 @@
             pltpu.VMEM((len(rows), length, LANES), jnp.float32),
             pltpu.VMEM((length, out_rows * LANES), jnp.float32),
         ],
-        compiler_params=pltpu.CompilerParams(vmem_limit_bytes=48 << 20),
+        compiler_params=pltpu.CompilerParams(vmem_limit_bytes=20 << 20),
         cost_estimate=pl.CostEstimate(
             flops=2 * lanes * length * (len(rows) * forward.shape[1] + out_rows * width),
             bytes_accessed=2 * lanes * (len(rows) * forward.shape[1] + 2 * taps_r * length),
@@ -196,7 +196,7 @@
         + [pl.BlockSpec(memory_space=pl.ANY) for _ in extra],
         out_specs=[given(*last) for last in lasts],
         input_output_aliases={3 + together * len(mixed): 0} if extra else {},
-        compiler_params=pltpu.CompilerParams(vmem_limit_bytes=48 << 20),
+        compiler_params=pltpu.CompilerParams(vmem_limit_bytes=20 << 20),
         cost_estimate=pl.CostEstimate(
             flops=8 * len(steps) * together * width * channels * hidden_units,
             bytes_accessed=8 * len(steps) * together * width * channels + 4 * channels * hidden_units,
@@ -249,10 +249,10 @@
     index = lax.axis_index("lat") * rows - rim + jnp.arange(rows + 2 * rim, dtype=jnp.int32)
     quad = jnp.sin(jnp.pi * (index.astype(jnp.float32) + 0.5) / total_rows)
     quad = jnp.where((index >= 0) & (index < total_rows), quad, 0.0)
-    factors = [
-        jnp.einsum("kt,rtc->rkc", tap_basis, zonal_kernel[layer], preferred_element_type=jnp.float32)
-        for layer in range(blocks)
-    ]
+    factors = []
+    for layer in range(blocks):
+        taps_of = zonal_kernel[layer]
+        factors.append(jnp.einsum("kt,rtc->rkc", tap_basis, taps_of, preferred_element_type=jnp.float32))
     gains = norm_gain.astype(jnp.float32)[:, None, :]
 
     groups = [
@@ -265,18 +265,20 @@
     mids = [state]
     mid_of = {row: (0, row) for row in range(rows)}
 
-    def pick(members):
-        low = members[: len(members) // 2]
-        high = members[len(members) // 2 :]
-        return jnp.concatenate([state[low[0] : low[-1] + 1], state[high[0] : high[-1] + 1]], axis=0)
+    pairs = state.reshape(rows // rim, rim, width, channels)
+
+    def pick(members, lon, cut):
+        first, last = members[0] // rim, members[-1] // rim
+        chosen = pairs[first : last + 1 : max(1, (last - first) // (len(members) // rim - 1))]
+        return chosen[:, :, lon, cut].reshape(len(members), -1, chosen[..., cut].shape[-1])
 
     parts = lane_parts(channels)
     pieces = [slice(start * LANES, (start + count) * LANES) for start, count in parts]
     cuts = [count * LANES for _, count in parts]
-    lanes = [slice(None), slice(None)] + pieces
+    lanes = [slice(0, channels)] * 2 + pieces
     groups_of = [groups[0], groups[1]] + [groups[2]] * len(parts)
-    firsts = [pick(members)[:, :edge, cut] for members, cut in zip(groups_of, lanes)]
-    lasts = [pick(members)[:, width - edge :, cut] for members, cut in zip(groups_of, lanes)]
+    firsts = [pick(members, slice(0, edge), cut) for members, cut in zip(groups_of, lanes)]
+    lasts = [pick(members, slice(width - edge, width), cut) for members, cut in zip(groups_of, lanes)]
     tables = (forward, inverse)
     out = None
     for layer in range(blocks):
@@ -339,15 +341,15 @@
                 convolve(quad, tables, factors[layer], sources, inner, [(0, rows - 2 * rim)], part)
             )
         weights = (gains[layer], input_weight[layer], output_weight[layer])
-        pairs = rows // 2
+        count = rows // 2
         if final:
             (out,) = mlp(*weights, mixed_outer, [([0], 0), ([1], rows - 2)], rows, 0)
-            steps = [([p], 2 * p + rim) for p in range(pairs - 2)]
+            steps = [([p], 2 * p + rim) for p in range(count - 2)]
             (out,) = mlp(*weights, mixed_inner, steps, rows, 0, kept=out)
         else:
             outs = [mlp(*weights, mixed_outer, [([0], 0), ([1], 2)], 2 * rim, edge, [channels])]
-            outs.append(mlp(*weights, mixed_inner, [([0], 0), ([pairs - 3], 2)], 2 * rim, edge, [channels]))
-            steps = [([p + 1], 2 * p) for p in range(pairs - 4)]
+            outs.append(mlp(*weights, mixed_inner, [([0], 0), ([count - 3], 2)], 2 * rim, edge, [channels]))
+            steps = [([p + 1], 2 * p) for p in range(count - 4)]
             outs.append(mlp(*weights, mixed_inner, steps, rows - 4 * rim, edge, cuts))
             mids = [o[0] for o in outs]
             mid_of = group_of

time: 261 us -> 269 us (1.031)
  the two profiles are of different devices: /device:TPU:2 before, /device:TPU:20 now
where the time goes in v6:
time: 269 us; the launch traced here: 268 us
  waiting for transfers between devices  105 us (39%)
  Pallas kernels  78.9 us (29%)
  starting transfers between devices  55.2 us (21%)
  local copies, waits for them, and re-layouts  22.1 us (8%)
  matrix products  4.36 us (2%)
    ppermute x20, waiting for transfers between devices, rotate(): lax.ppermute(block, axis, [(i, (i + hops) % count) for i in range(count)])  102 us
    pallas_call x8, Pallas kernels, convolve(): pl.pallas_call(kernel, grid=(blocks,), out_shape=out, in_specs=[pl.BlockS...  53.1 us
    ppermute x20, starting transfers between devices, rotate(): lax.ppermute(block, axis, [(i, (i + hops) % count) for i in range(count)])  34 us
    pallas_call x5, Pallas kernels, mlp(): pl.pallas_call(functools.partial(mlp_kernel, half=edge, kept=len(extra),...  25.8 us
    ppermute x8, starting transfers between devices, step_rows(): return lax.ppermute(block, 'lat', pairs)  21.2 us
    unnamed x60, local copies, waits for them, and re-layouts  13 us
  transfers between devices with their start and end apart: 28, of which 9 were waited for; matrix products, arithmetic and copies ran while one was open for 5% of the time, Pallas kernels for 14%

profile of v6, /device:TPU:20, one launch (start us, length us, event | category | flops | bytes accessed | tf_op | source)
XLA Modules:
  0.0 268.4 jit_solution(5636524258805459740)
XLA Ops:
  0.0 1.4 slice.157
  1.5 1.6 collective-permute-start.12
  3.1 0.4 collective-permute-start.13
  3.6 0.8 fusion.8
  4.4 1.6 collective-permute-start.10
  6.2 1.2 fusion.9
  7.4 2.0 collective-permute-start
  9.4 1.9 slice_bitcast_fusion.1
  11.4 1.2 copy-done.24
  12.5 2.0 slice_bitcast_fusion
  14.6 1.1 fusion.4
  15.7 0.4 copy-done.27
  16.1 3.4 %convolution_bitcast_fusion.refs_3_ = f32[5,448,640]{2,1,0:T(8,128)} fusion(bf16[448,256,1]{1,0,2:T(8,128)(2,1)S(1)} %copy-done.27, bf16[2,5,256,640]{3,2,1,0:T(8,128)(2,1)S(1)} %copy-done.25), kind=kOutput, calls=%fused_computation | convolution fusion | flops 734003200 | bytes 7602176 | tf_op jit(solution)/shard_map/kt,rtc->rkc/dot_general | solution.py:255
  19.5 10.4 %collective-permute-done.refs_5_ = bf16[4,128,640]{2,1,0:T(8,128)(2,1)S(1)} collective-permute-done((bf16[4,128,640]{2,1,0:T(8,128)(2,1)S(1)}, bf16[4,128,640]{2,1,0:T(8,128)(2,1)S(1)}, u32[]{:S(2)}, u32[]{:S(2)}) %collective-permute-start) | collective-permute-done | bytes 655392 | tf_op jit(solution)/shard_map/ppermute | solution.py:211
  30.0 14.5 %collective-permute-start.1 = (bf16[4,128,640]{2,1,0:T(8,128)(2,1)S(1)}, bf16[4,128,640]{2,1,0:T(8,128)(2,1)S(1)}, u32[]{:S(2)}, u32[]{:S(2)}) collective-permute-start(bf16[4,128,640]{2,1,0:T(8,128)(2,1)S(1)} %bitcast.49), channel_id=1, source_target_pairs={{0,1},{1,2},{2,3},{3,0},{4,5},{5,6},{6,7},{7,4},{8,9},{9,10},{10,1... | collective-permute-start | bytes 1966088 | tf_op jit(solution)/shard_map/ppermute | solution.py:211
  44.6 0.6 copy-done.21
  45.3 2.9 %collective-permute-start.3 = (bf16[4,128,640]{2,1,0:T(8,128)(2,1)}, bf16[4,128,640]{2,1,0:T(8,128)(2,1)}, u32[]{:S(2)}, u32[]{:S(2)}) collective-permute-start(bf16[4,128,640]{2,1,0:T(8,128)(2,1)} %bitcast.17), channel_id=1, source_target_pairs={{0,3},{1,0},{2,1},{3,2},{4,7},{5,4},{6,5},{7,6},{8,11},{9,8},{10,9... | collective-permute-start | bytes 1966088 | tf_op jit(solution)/shard_map/ppermute | solution.py:211
  48.3 0.9 pad_maximum_fusion.1
  49.2 0.9 pad_maximum_fusion
  50.1 0.7 copy-done.15
  50.8 1.9 collective-permute-start.6
  52.7 12.9 %collective-permute-done.11.refs_10_ = bf16[4,128,256]{2,1,0:T(8,128)(2,1)S(1)} collective-permute-done((bf16[4,128,256]{2,1,0:T(8,128)(2,1)S(1)}, bf16[4,128,256]{2,1,0:T(8,128)(2,1)S(1)}, u32[]{:S(2)}, u32[]{:S(2)}) %collective-permute-start.11) | collective-permute-done | bytes 262176 | tf_op jit(solution)/shard_map/ppermute | solution.py:211
  65.7 0.7 copy-done.17
  66.3 1.9 collective-permute-start.4
  68.3 3.0 %collective-permute-done.9.refs_10_ = bf16[4,128,256]{2,1,0:T(8,128)(2,1)S(1)} collective-permute-done((bf16[4,128,256]{2,1,0:T(8,128)(2,1)S(1)}, bf16[4,128,256]{2,1,0:T(8,128)(2,1)S(1)}, u32[]{:S(2)}, u32[]{:S(2)}) %collective-permute-start.9) | collective-permute-done | bytes 262176 | tf_op jit(solution)/shard_map/ppermute | solution.py:211
  71.3 0.7 copy-done.19
  72.0 1.9 collective-permute-start.5
  73.9 0.8 copy-done.9
  74.8 4.5 %collective-permute-start.7 = (bf16[2,256,640]{2,1,0:T(8,128)(2,1)}, bf16[2,256,640]{2,1,0:T(8,128)(2,1)}, u32[]{:S(2)}, u32[]{:S(2)}) collective-permute-start(bf16[2,256,640]{2,1,0:T(8,128)(2,1)} %pad_maximum_fusion.1), channel_id=1, source_target_pairs={{4,0},{8,4},{12,8},{16,12},{20,16},{24,20},{28,24},{5,1},{9,5},{13... | collective-permute-start | bytes 1966088 | tf_op jit(solution)/shard_map/ppermute | solution.py:231
  79.3 3.3 %collective-permute-done.3.refs_8_.refs_9_ = bf16[4,128,640]{2,1,0:T(8,128)(2,1)} collective-permute-done((bf16[4,128,640]{2,1,0:T(8,128)(2,1)}, bf16[4,128,640]{2,1,0:T(8,128)(2,1)}, u32[]{:S(2)}, u32[]{:S(2)}) %collective-permute-start.3) | collective-permute-done | bytes 655392 | tf_op jit(solution)/shard_map/ppermute | solution.py:211
  82.7 4.4 %collective-permute-start.8 = (bf16[4,128,256]{2,1,0:T(8,128)(2,1)}, bf16[4,128,256]{2,1,0:T(8,128)(2,1)S(1)}, u32[]{:S(2)}, u32[]{:S(2)}) collective-permute-start(bf16[4,128,256]{2,1,0:T(8,128)(2,1)} %bitcast.52), channel_id=1, source_target_pairs={{0,1},{1,2},{2,3},{3,0},{4,5},{5,6},{6,7},{7,4},{8,9},{9,10},{10,1... | collective-permute-start | bytes 786440 | tf_op jit(solution)/shard_map/ppermute | solution.py:211
  87.1 2.6 copy-done
  89.8 1.1 copy-done.4
  90.8 1.1 copy-done.6
  91.9 0.9 copy-done.7
  92.9 1.1 copy-done.10
  93.9 0.9 copy-done.22
  94.8 3.5 %zonal_conv.11.refs_2_ = bf16[8,192,128]{2,1,0:T(8,128)(2,1)S(1)} custom-call(f32[16]{0:T(128)S(1)} %and_select_fusion.refs_0_, bf16[448,448]{1,0:T(8,128)(2,1)S(1)} %copy-done.2, bf16[192,448]{1,0:T(8,128)(2,1)S(1)} %copy-done.7, f32[5,448,640]{2,1,0:T(8,128)S(1)} %copy-done, bf16[12,192,640]{2,1,0:T(8,128)(2,1)S(1)} %bitcast.43, ...), custom_call_target="tpu_custom_call" | custom-call | flops 792723456 | bytes 2523136 | tf_op jit(solution)/shard_map/zonal_conv/pallas_call | solution.py:110
  98.4 6.0 %zonal_conv.10.refs_1_ = bf16[8,192,256]{2,1,0:T(8,128)(2,1)S(1)} custom-call(f32[16]{0:T(128)S(1)} %and_select_fusion.refs_0_, bf16[448,448]{1,0:T(8,128)(2,1)S(1)} %copy-done.2, bf16[192,448]{1,0:T(8,128)(2,1)S(1)} %copy-done.7, f32[5,448,640]{2,1,0:T(8,128)S(1)} %copy-done, bf16[12,192,640]{2,1,0:T(8,128)(2,1)S(1)} %bitcast.44, ...), custom_call_target="tpu_custom_call" | custom-call | flops 1585446912 | bytes 5046272 | tf_op jit(solution)/shard_map/zonal_conv/pallas_call | solution.py:110
  104.4 6.0 %zonal_conv.9.refs_0_ = bf16[8,192,256]{2,1,0:T(8,128)(2,1)S(1)} custom-call(f32[16]{0:T(128)S(1)} %and_select_fusion.refs_0_, bf16[448,448]{1,0:T(8,128)(2,1)S(1)} %copy-done.2, bf16[192,448]{1,0:T(8,128)(2,1)S(1)} %copy-done.7, f32[5,448,640]{2,1,0:T(8,128)S(1)} %copy-done, bf16[12,192,640]{2,1,0:T(8,128)(2,1)S(1)} %bitcast.45, ...), custom_call_target="tpu_custom_call" | custom-call | flops 1585446912 | bytes 5046272 | tf_op jit(solution)/shard_map/zonal_conv/pallas_call | solution.py:110
  110.5 12.1 %zonal_conv.8.refs_0_ = bf16[4,192,640]{2,1,0:T(8,128)(2,1)S(1)} custom-call(f32[16]{0:T(128)S(1)} %and_select_fusion.refs_0_, bf16[448,448]{1,0:T(8,128)(2,1)S(1)} %copy-done.2, bf16[192,448]{1,0:T(8,128)(2,1)S(1)} %copy-done.7, f32[5,448,640]{2,1,0:T(8,128)S(1)} %copy-done, bf16[12,192,640]{2,1,0:T(8,128)(2,1)S(1)} %bitcast.46, ...), custom_call_target="tpu_custom_call" | custom-call | flops 3523215360 | bytes 12615680 | tf_op jit(solution)/shard_map/zonal_conv/pallas_call | solution.py:110
  122.7 4.1 %channel_mlp.5 = (bf16[4,192,640]{2,1,0:T(8,128)(2,1)S(1)}, bf16[4,128,640]{2,1,0:T(8,128)(2,1)S(1)}, bf16[4,128,640]{2,1,0:T(8,128)(2,1)S(1)}) custom-call(f32[1,640]{1,0:T(1,128)S(1)} %get-tuple-element.59.gain, bf16[640,1280]{1,0:T(8,128)(2,1)S(1)} %copy-done.13, bf16[1280,640]{1,0:T(8,128)(2,1)S(1)} %copy-done.14, bf16[4,192,640]{2,1,0:T(8,128)(2,1)S(1)} %zonal_conv.8.refs_0_), custom_call_target="tpu_custom_call" | custom-call | flops 2516582400 | bytes 5242880 | tf_op jit(solution)/shard_map/channel_mlp/pallas_call | solution.py:186
  126.7 0.2 collective-permute-start.14
  127.0 4.1 %channel_mlp.7 = (bf16[4,192,640]{2,1,0:T(8,128)(2,1)S(1)}, bf16[4,128,256]{2,1,0:T(8,128)(2,1)S(1)}, bf16[4,128,256]{2,1,0:T(8,128)(2,1)S(1)}, bf16[4,128,256]{...) custom-call(f32[1,640]{1,0:T(1,128)S(1)} %get-tuple-element.59.gain,, ...), custom_call_target="tpu_custom_call" | custom-call | flops 2516582400 | bytes 5242880 | tf_op jit(solution)/shard_map/channel_mlp/pallas_call | solution.py:186
  131.1 2.0 collective-permute-start.23
  133.1 2.0 collective-permute-start.17
  135.1 4.0 %channel_mlp.6 = (bf16[4,192,640]{2,1,0:T(8,128)(2,1)S(1)}, bf16[4,128,640]{2,1,0:T(8,128)(2,1)S(1)}, bf16[4,128,640]{2,1,0:T(8,128)(2,1)S(1)}) custom-call(f32[1,640]{1,0:T(1,128)S(1)} %get-tuple-element.59.gain, bf16[640,1280]{1,0:T(8,128)(2,1)S(1)} %copy-done.13, bf16[1280,640]{1,0:T(8,128)(2,1)S(1)} %copy-done.14, ...), custom_call_target="tpu_custom_call" | custom-call | flops 2516582400 | bytes 5242880 | tf_op jit(solution)/shard_map/channel_mlp/pallas_call | solution.py:186
  139.4 22.1 %collective-permute-done.14.refs_7_.refs_6_ = bf16[4,128,640]{2,1,0:T(8,128)(2,1)S(1)} collective-permute-done((bf16[4,128,640]{2,1,0:T(8,128)(2,1)S(1)}, bf16[4,128,640]{2,1,0:T(8,128)(2,1)S(1)}, u32[]{:S(2)}, u32[]{:S(2)}) %collective-permute-start.14) | collective-permute-done | bytes 655392 | tf_op jit(solution)/shard_map/ppermute | solution.py:211
  161.5 2.7 %collective-permute-done.22.refs_9_ = bf16[4,128,128]{2,1,0:T(8,128)(2,1)S(1)} collective-permute-done((bf16[4,128,128]{2,1,0:T(8,128)(2,1)S(1)}, bf16[4,128,128]{2,1,0:T(8,128)(2,1)S(1)}, u32[]{:S(2)}, u32[]{:S(2)}) %collective-permute-start.22) | collective-permute-done | bytes 131104 | tf_op jit(solution)/shard_map/ppermute | solution.py:211
  164.3 2.0 collective-permute-start.21
  166.5 31.9 %collective-permute-done.16.refs_9_ = bf16[4,128,256]{2,1,0:T(8,128)(2,1)S(1)} collective-permute-done((bf16[4,128,256]{2,1,0:T(8,128)(2,1)S(1)}, bf16[4,128,256]{2,1,0:T(8,128)(2,1)S(1)}, u32[]{:S(2)}, u32[]{:S(2)}) %collective-permute-start.16) | collective-permute-done | bytes 262176 | tf_op jit(solution)/shard_map/ppermute | solution.py:211
  198.5 15.6 %collective-permute-done.20.refs_9_ = bf16[4,128,256]{2,1,0:T(8,128)(2,1)S(1)} collective-permute-done((bf16[4,128,256]{2,1,0:T(8,128)(2,1)S(1)}, bf16[4,128,256]{2,1,0:T(8,128)(2,1)S(1)}, u32[]{:S(2)}, u32[]{:S(2)}) %collective-permute-start.20) | collective-permute-done | bytes 262176 | tf_op jit(solution)/shard_map/ppermute | solution.py:211
  214.0 2.3 collective-permute-start.26
  216.4 2.1 collective-permute-start.24
  218.5 3.7 %collective-permute-start.25 = (bf16[2,256,640]{2,1,0:T(8,128)(2,1)S(1)}, bf16[2,256,640]{2,1,0:T(8,128)(2,1)S(1)}, u32[]{:S(2)}, u32[]{:S(2)}) collective-permute-start(bf16[2,256,640]{2,1,0:T(8,128)(2,1)S(1)} %pad_maximum_fusion.2), channel_id=1, source_target_pairs={{0,4},{4,8},{8,12},{12,16},{16,20},{20,24},{24,28},{1,5},{5,9},{9,... | collective-permute-start | bytes 1966088 | tf_op jit(solution)/shard_map/ppermute | solution.py:231
  222.2 2.8 %collective-permute-start.27 = (bf16[2,256,640]{2,1,0:T(8,128)(2,1)S(1)}, bf16[2,256,640]{2,1,0:T(8,128)(2,1)S(1)}, u32[]{:S(2)}, u32[]{:S(2)}) collective-permute-start(bf16[2,256,640]{2,1,0:T(8,128)(2,1)S(1)} %pad_maximum_fusion.3), channel_id=1, source_target_pairs={{4,0},{8,4},{12,8},{16,12},{20,16},{24,20},{28,24},{5,1},{9,5},{13... | collective-permute-start | bytes 1966088 | tf_op jit(solution)/shard_map/ppermute | solution.py:231
  225.0 0.9 convolution_bitcast_fusion.1.refs_3_
  226.0 2.9 %zonal_conv.14.refs_2_ = bf16[8,192,128]{2,1,0:T(8,128)(2,1)S(1)} custom-call(f32[16]{0:T(128)S(1)} %and_select_fusion.refs_0_, bf16[448,448]{1,0:T(8,128)(2,1)S(1)} %copy-done.2, bf16[192,448]{1,0:T(8,128)(2,1)S(1)} %copy-done.8, f32[5,448,640]{2,1,0:T(8,128)S(1)} %convolution_bitcast_fusion.1.refs_3_, bf16[4,192,640]{2,1,0:T(8,128)(2,1)S(1)} %get-tuple-element.18.refs_4_, ...), custom_call_target="tpu_custom_call" | custom-call | flops 792723456 | bytes 2523136 | tf_op jit(solution)/shard_map/zonal_conv/pallas_call | solution.py:110
  228.9 5.7 %zonal_conv.13.refs_1_ = bf16[8,192,256]{2,1,0:T(8,128)(2,1)S(1)} custom-call(f32[16]{0:T(128)S(1)} %and_select_fusion.refs_0_, bf16[448,448]{1,0:T(8,128)(2,1)S(1)} %copy-done.2, bf16[192,448]{1,0:T(8,128)(2,1)S(1)} %copy-done.8, f32[5,448,640]{2,1,0:T(8,128)S(1)} %convolution_bitcast_fusion.1.refs_3_, bf16[4,192,640]{2,1,0:T(8,128)(2,1)S(1)} %get-tuple-element.18.refs_4_, ...), custom_call_target="tpu_custom_call" | custom-call | flops 1585446912 | bytes 5046272 | tf_op jit(solution)/shard_map/zonal_conv/pallas_call | solution.py:110
  234.6 5.7 %zonal_conv.12.refs_0_ = bf16[8,192,256]{2,1,0:T(8,128)(2,1)S(1)} custom-call(f32[16]{0:T(128)S(1)} %and_select_fusion.refs_0_, bf16[448,448]{1,0:T(8,128)(2,1)S(1)} %copy-done.2, bf16[192,448]{1,0:T(8,128)(2,1)S(1)} %copy-done.8, f32[5,448,640]{2,1,0:T(8,128)S(1)} %convolution_bitcast_fusion.1.refs_3_, bf16[4,192,640]{2,1,0:T(8,128)(2,1)S(1)} %get-tuple-element.18.refs_4_, ...), custom_call_target="tpu_custom_call" | custom-call | flops 1585446912 | bytes 5046272 | tf_op jit(solution)/shard_map/zonal_conv/pallas_call | solution.py:110
  240.4 3.2 %collective-permute-done.25.refs_11_ = bf16[2,256,640]{2,1,0:T(8,128)(2,1)S(1)} collective-permute-done((bf16[2,256,640]{2,1,0:T(8,128)(2,1)S(1)}, bf16[2,256,640]{2,1,0:T(8,128)(2,1)S(1)}, u32[]{:S(2)}, u32[]{:S(2)}) %collective-permute-start.25) | collective-permute-done | bytes 655392 | tf_op jit(solution)/shard_map/ppermute | solution.py:231
  243.6 11.1 %zonal_conv.15.refs_0_ = bf16[4,192,640]{2,1,0:T(8,128)(2,1)S(1)} custom-call(f32[16]{0:T(128)S(1)} %and_select_fusion.refs_0_, bf16[448,448]{1,0:T(8,128)(2,1)S(1)} %copy-done.2, bf16[192,448]{1,0:T(8,128)(2,1)S(1)} %copy-done.8, f32[5,448,640]{2,1,0:T(8,128)S(1)} %convolution_bitcast_fusion.1.refs_3_, bf16[4,192,640]{2,1,0:T(8,128)(2,1)S(1)} %get-tuple-element.18.refs_4_, ...), custom_call_target="tpu_custom_call" | custom-call | flops 3523215360 | bytes 12615680 | tf_op jit(solution)/shard_map/zonal_conv/pallas_call | solution.py:110
  254.7 4.8 %channel_mlp.8.refs_3_ = bf16[12,192,640]{2,1,0:T(8,128)(2,1)} custom-call(f32[1,640]{1,0:T(1,128)S(1)} %get-tuple-element.60.gain, bf16[640,1280]{1,0:T(8,128)(2,1)S(1)} %copy-done.11, bf16[1280,640]{1,0:T(8,128)(2,1)S(1)} %copy-done.12, bf16[4,192,640]{2,1,0:T(8,128)(2,1)S(1)} %zonal_conv.15.refs_0_), custom_call_target="tpu_custom_call" | custom-call | flops 2516582400 | bytes 5242880 | tf_op jit(solution)/shard_map/channel_mlp/pallas_call | solution.py:186
  259.6 8.9 %channel_mlp.9 = bf16[12,192,640]{2,1,0:T(8,128)(2,1)} custom-call(f32[1,640]{1,0:T(1,128)S(1)} %get-tuple-element.60.gain, bf16[640,1280]{1,0:T(8,128)(2,1)S(1)} %copy-done.11, bf16[1280,640]{1,0:T(8,128)(2,1)S(1)} %copy-done.12, bf16[8,192,256]{2,1,0:T(8,128)(2,1)S(1)} %zonal_conv.12.refs_0_, ...), custom_call_target="tpu_custom_call", output_to_operand_aliasing={{}: (6, {})} | custom-call | flops 5033164800 | bytes 7208960 | tf_op jit(solution)/shard_map/channel_mlp/pallas_call | solution.py:186
  (86 shorter events, 1.3 us)
Async XLA Ops:
  0.0 6.0 %copy-start.1 = (bf16[1,12,640,192]{2,3,1,0:T(8,128)(2,1)S(1)}, bf16[1,12,640,192]{2,3,1,0:T(8,128)(2,1)}, u32[]{:S(2)}) copy-start(bf16[1,12,640,192]{2,3,1,0:T(8,128)(2,1)} %param.8) | copy-start | bytes 8847364
  1.5 43.0 %collective-permute-start.12 = (bf16[4,128,128]{2,1,0:T(8,128)(2,1)S(1)}, bf16[4,128,128]{2,1,0:T(8,128)(2,1)S(1)}, u32[]{:S(2)}, u32[]{:S(2)}) collective-permute-start(bf16[4,128,128]{2,1,0:T(8,128)(2,1)S(1)} %bitcast.57), channel_id=1, source_target_pairs={{0,1},{1,2},{2,3},{3,0},{4,5},{5,6},{6,7},{7,4},{8,9},{9,10},{10,1... | collective-permute-start | bytes 393224 | tf_op jit(solution)/shard_map/ppermute | solution.py:211
  3.1 41.5 %collective-permute-start.13 = (bf16[4,128,128]{2,1,0:T(8,128)(2,1)S(1)}, bf16[4,128,128]{2,1,0:T(8,128)(2,1)S(1)}, u32[]{:S(2)}, u32[]{:S(2)}) collective-permute-start(bf16[4,128,128]{2,1,0:T(8,128)(2,1)S(1)} %bitcast.56), channel_id=1, source_target_pairs={{0,3},{1,0},{2,1},{3,2},{4,7},{5,4},{6,5},{7,6},{8,11},{9,8},{10,9... | collective-permute-start | bytes 393224 | tf_op jit(solution)/shard_map/ppermute | solution.py:211
  4.4 45.7 %collective-permute-start.10 = (bf16[4,128,256]{2,1,0:T(8,128)(2,1)S(1)}, bf16[4,128,256]{2,1,0:T(8,128)(2,1)S(1)}, u32[]{:S(2)}, u32[]{:S(2)}) collective-permute-start(bf16[4,128,256]{2,1,0:T(8,128)(2,1)S(1)} %bitcast.55), channel_id=1, source_target_pairs={{0,1},{1,2},{2,3},{3,0},{4,5},{5,6},{6,7},{7,4},{8,9},{9,10},{10,1... | collective-permute-start | bytes 786440 | tf_op jit(solution)/shard_map/ppermute | solution.py:211
  6.2 3.3 %copy-start.23 = (bf16[2,640,1280]{2,1,0:T(8,128)(2,1)S(1)}, bf16[2,640,1280]{2,1,0:T(8,128)(2,1)}, u32[]{:S(2)}) copy-start(bf16[2,640,1280]{2,1,0:T(8,128)(2,1)} %param.11) | copy-start | bytes 9830404
  7.4 22.6 %collective-permute-start = (bf16[4,128,640]{2,1,0:T(8,128)(2,1)S(1)}, bf16[4,128,640]{2,1,0:T(8,128)(2,1)S(1)}, u32[]{:S(2)}, u32[]{:S(2)}) collective-permute-start(bf16[4,128,640]{2,1,0:T(8,128)(2,1)S(1)} %bitcast.51), channel_id=1, source_target_pairs={{0,1},{1,2},{2,3},{3,0},{4,5},{5,6},{6,7},{7,4},{8,9},{9,10},{10,1... | collective-permute-start | bytes 1966088 | tf_op jit(solution)/shard_map/ppermute | solution.py:211
  9.4 3.1 %copy-start.24 = (bf16[2,1280,640]{2,1,0:T(8,128)(2,1)S(1)}, bf16[2,1280,640]{2,1,0:T(8,128)(2,1)}, u32[]{:S(2)}) copy-start(bf16[2,1280,640]{2,1,0:T(8,128)(2,1)} %param.12) | copy-start | bytes 9830404
  9.4 35.8 %collective-permute-start.2 = (bf16[4,128,640]{2,1,0:T(8,128)(2,1)S(1)}, bf16[4,128,640]{2,1,0:T(8,128)(2,1)S(1)}, u32[]{:S(2)}, u32[]{:S(2)}) collective-permute-start(bf16[4,128,640]{2,1,0:T(8,128)(2,1)S(1)} %bitcast.50), channel_id=1, source_target_pairs={{0,3},{1,0},{2,1},{3,2},{4,7},{5,4},{6,5},{7,6},{8,11},{9,8},{10,9... | collective-permute-start | bytes 1966088 | tf_op jit(solution)/shard_map/ppermute | solution.py:211
  12.5 3.2 %copy-start.25 = (bf16[2,5,256,640]{3,2,1,0:T(8,128)(2,1)S(1)}, bf16[2,5,256,640]{3,2,1,0:T(8,128)(2,1)}, u32[]{:S(2)}) copy-start(bf16[2,5,256,640]{3,2,1,0:T(8,128)(2,1)} %param.9) | copy-start | bytes 9830404
  14.6 1.6 copy-start.27
  30.0 19.2 %copy-start.3 = (bf16[4,128,640]{2,1,0:T(8,128)(2,1)}, bf16[4,128,640]{2,1,0:T(8,128)(2,1)S(1)}, u32[]{:S(2)}) copy-start(bf16[4,128,640]{2,1,0:T(8,128)(2,1)S(1)} %collective-permute-done.refs_5_) | copy-start | bytes 1966084
  30.0 43.9 %collective-permute-start.1 = (bf16[4,128,640]{2,1,0:T(8,128)(2,1)S(1)}, bf16[4,128,640]{2,1,0:T(8,128)(2,1)S(1)}, u32[]{:S(2)}, u32[]{:S(2)}) collective-permute-start(bf16[4,128,640]{2,1,0:T(8,128)(2,1)S(1)} %bitcast.49), channel_id=1, source_target_pairs={{0,1},{1,2},{2,3},{3,0},{4,5},{5,6},{6,7},{7,4},{8,9},{9,10},{10,1... | collective-permute-start | bytes 1966088 | tf_op jit(solution)/shard_map/ppermute | solution.py:211
  44.5 21.1 %collective-permute-start.11 = (bf16[4,128,256]{2,1,0:T(8,128)(2,1)S(1)}, bf16[4,128,256]{2,1,0:T(8,128)(2,1)S(1)}, u32[]{:S(2)}, u32[]{:S(2)}) collective-permute-start(bf16[4,128,256]{2,1,0:T(8,128)(2,1)S(1)} %bitcast.54), channel_id=1, source_target_pairs={{0,3},{1,0},{2,1},{3,2},{4,7},{5,4},{6,5},{7,6},{8,11},{9,8},{10,9... | collective-permute-start | bytes 786440 | tf_op jit(solution)/shard_map/ppermute | solution.py:211
  44.6 0.7 copy-start.21
  45.3 26.0 %collective-permute-start.9 = (bf16[4,128,256]{2,1,0:T(8,128)(2,1)S(1)}, bf16[4,128,256]{2,1,0:T(8,128)(2,1)S(1)}, u32[]{:S(2)}, u32[]{:S(2)}) collective-permute-start(bf16[4,128,256]{2,1,0:T(8,128)(2,1)S(1)} %bitcast.53), channel_id=1, source_target_pairs={{0,3},{1,0},{2,1},{3,2},{4,7},{5,4},{6,5},{7,6},{8,11},{9,8},{10,9... | collective-permute-start | bytes 786440 | tf_op jit(solution)/shard_map/ppermute | solution.py:211
  45.3 4.8 %copy-start.5 = (bf16[4,128,640]{2,1,0:T(8,128)(2,1)}, bf16[4,128,640]{2,1,0:T(8,128)(2,1)S(1)}, u32[]{:S(2)}) copy-start(bf16[4,128,640]{2,1,0:T(8,128)(2,1)S(1)} %collective-permute-done.2.refs_7_.refs_8_) | copy-start | bytes 1966084
  45.3 37.4 %collective-permute-start.3 = (bf16[4,128,640]{2,1,0:T(8,128)(2,1)}, bf16[4,128,640]{2,1,0:T(8,128)(2,1)}, u32[]{:S(2)}, u32[]{:S(2)}) collective-permute-start(bf16[4,128,640]{2,1,0:T(8,128)(2,1)} %bitcast.17), channel_id=1, source_target_pairs={{0,3},{1,0},{2,1},{3,2},{4,7},{5,4},{6,5},{7,6},{8,11},{9,8},{10,9... | collective-permute-start | bytes 1966088 | tf_op jit(solution)/shard_map/ppermute | solution.py:211
  48.2 31.1 %copy-start.29 = (bf16[2,640]{1,0:T(2,128)(2,1)S(1)}, bf16[2,640]{1,0:T(2,128)(2,1)}, u32[]{:S(2)}) copy-start(bf16[2,640]{1,0:T(2,128)(2,1)} %param.10) | copy-start | bytes 7684
  48.2 38.9 %copy-start.2 = (bf16[448,448]{1,0:T(8,128)(2,1)S(1)}, bf16[448,448]{1,0:T(8,128)(2,1)}, u32[]{:S(2)}) copy-start(bf16[448,448]{1,0:T(8,128)(2,1)} %constant.30.clone.refs_1_) | copy-start | bytes 1204228
  50.1 0.7 copy-start.15
  50.8 59.7 %collective-permute-start.6 = (bf16[2,192,640]{2,1,0:T(8,128)(2,1)}, bf16[2,192,640]{2,1,0:T(8,128)(2,1)}, u32[]{:S(2)}, u32[]{:S(2)}) collective-permute-start(bf16[2,192,640]{2,1,0:T(8,128)(2,1)} %get-tuple-element.35), channel_id=1, source_target_pairs={{4,0},{8,4},{12,8},{16,12},{20,16},{24,20},{28,24},{5,1},{9,5},{13... | collective-permute-start | bytes 1474568 | tf_op jit(solution)/shard_map/ppermute | solution.py:231
  65.6 0.7 copy-start.17
  66.3 44.2 %collective-permute-start.4 = (bf16[2,192,640]{2,1,0:T(8,128)(2,1)}, bf16[2,192,640]{2,1,0:T(8,128)(2,1)}, u32[]{:S(2)}, u32[]{:S(2)}) collective-permute-start(bf16[2,192,640]{2,1,0:T(8,128)(2,1)} %get-tuple-element.36), channel_id=1, source_target_pairs={{0,4},{4,8},{8,12},{12,16},{16,20},{20,24},{24,28},{1,5},{5,9},{9,... | collective-permute-start | bytes 1474568 | tf_op jit(solution)/shard_map/ppermute | solution.py:231
  71.3 0.7 copy-start.19
  72.0 38.5 %collective-permute-start.5 = (bf16[2,256,640]{2,1,0:T(8,128)(2,1)}, bf16[2,256,640]{2,1,0:T(8,128)(2,1)}, u32[]{:S(2)}, u32[]{:S(2)}) collective-permute-start(bf16[2,256,640]{2,1,0:T(8,128)(2,1)} %pad_maximum_fusion), channel_id=1, source_target_pairs={{0,4},{4,8},{8,12},{12,16},{16,20},{20,24},{24,28},{1,5},{5,9},{9,... | collective-permute-start | bytes 1966088 | tf_op jit(solution)/shard_map/ppermute | solution.py:231
  73.9 0.8 copy-start.9
  74.8 35.8 %collective-permute-start.7 = (bf16[2,256,640]{2,1,0:T(8,128)(2,1)}, bf16[2,256,640]{2,1,0:T(8,128)(2,1)}, u32[]{:S(2)}, u32[]{:S(2)}) collective-permute-start(bf16[2,256,640]{2,1,0:T(8,128)(2,1)} %pad_maximum_fusion.1), channel_id=1, source_target_pairs={{4,0},{8,4},{12,8},{16,12},{20,16},{24,20},{28,24},{5,1},{9,5},{13... | collective-permute-start | bytes 1966088 | tf_op jit(solution)/shard_map/ppermute | solution.py:231
  82.7 21.8 %collective-permute-start.8 = (bf16[4,128,256]{2,1,0:T(8,128)(2,1)}, bf16[4,128,256]{2,1,0:T(8,128)(2,1)S(1)}, u32[]{:S(2)}, u32[]{:S(2)}) collective-permute-start(bf16[4,128,256]{2,1,0:T(8,128)(2,1)} %bitcast.52), channel_id=1, source_target_pairs={{0,1},{1,2},{2,3},{3,0},{4,5},{5,6},{6,7},{7,4},{8,9},{9,10},{10,1... | collective-permute-start | bytes 786440 | tf_op jit(solution)/shard_map/ppermute | solution.py:211
  87.1 2.6 copy-start
  89.7 1.1 copy-start.4
  90.8 1.1 copy-start.6
  91.9 0.9 copy-start.7
  92.9 1.1 copy-start.10
  93.9 0.9 copy-start.22
  94.8 3.5 %copy-start.16 = (bf16[4,128,256]{2,1,0:T(8,128)(2,1)S(1)}, bf16[4,128,256]{2,1,0:T(8,128)(2,1)}, u32[]{:S(2)}) copy-start(bf16[4,128,256]{2,1,0:T(8,128)(2,1)} %copy-done.15) | copy-start | bytes 786436
  94.8 3.5 %copy-start.18 = (bf16[4,128,256]{2,1,0:T(8,128)(2,1)S(1)}, bf16[4,128,256]{2,1,0:T(8,128)(2,1)}, u32[]{:S(2)}) copy-start(bf16[4,128,256]{2,1,0:T(8,128)(2,1)} %copy-done.17) | copy-start | bytes 786436
  98.3 6.1 %copy-start.20 = (bf16[4,128,256]{2,1,0:T(8,128)(2,1)S(1)}, bf16[4,128,256]{2,1,0:T(8,128)(2,1)}, u32[]{:S(2)}) copy-start(bf16[4,128,256]{2,1,0:T(8,128)(2,1)} %copy-done.19) | copy-start | bytes 786436
  110.5 12.2 %copy-start.13 = (bf16[640,1280]{1,0:T(8,128)(2,1)S(1)}, bf16[640,1280]{1,0:T(8,128)(2,1)}, u32[]{:S(2)}) copy-start(bf16[640,1280]{1,0:T(8,128)(2,1)} %get-tuple-element.33.w_in) | copy-start | bytes 4915204
  110.5 12.2 %copy-start.14 = (bf16[1280,640]{1,0:T(8,128)(2,1)S(1)}, bf16[1280,640]{1,0:T(8,128)(2,1)}, u32[]{:S(2)}) copy-start(bf16[1280,640]{1,0:T(8,128)(2,1)} %get-tuple-element.31.w_out) | copy-start | bytes 4915204
  126.7 34.7 %collective-permute-start.14 = (bf16[4,128,640]{2,1,0:T(8,128)(2,1)S(1)}, bf16[4,128,640]{2,1,0:T(8,128)(2,1)S(1)}, u32[]{:S(2)}, u32[]{:S(2)}) collective-permute-start(bf16[4,128,640]{2,1,0:T(8,128)(2,1)S(1)} %get-tuple-element.21), channel_id=1, source_target_pairs={{0,1},{1,2},{2,3},{3,0},{4,5},{5,6},{6,7},{7,4},{8,9},{9,10},{10,1... | collective-permute-start | bytes 1966088 | tf_op jit(solution)/shard_map/ppermute | solution.py:211
  131.0 33.2 %collective-permute-start.22 = (bf16[4,128,128]{2,1,0:T(8,128)(2,1)S(1)}, bf16[4,128,128]{2,1,0:T(8,128)(2,1)S(1)}, u32[]{:S(2)}, u32[]{:S(2)}) collective-permute-start(bf16[4,128,128]{2,1,0:T(8,128)(2,1)S(1)} %get-tuple-element.29), channel_id=1, source_target_pairs={{0,1},{1,2},{2,3},{3,0},{4,5},{5,6},{6,7},{7,4},{8,9},{9,10},{10,1... | collective-permute-start | bytes 393224 | tf_op jit(solution)/shard_map/ppermute | solution.py:211
  131.1 33.1 %collective-permute-start.23 = (bf16[4,128,128]{2,1,0:T(8,128)(2,1)S(1)}, bf16[4,128,128]{2,1,0:T(8,128)(2,1)S(1)}, u32[]{:S(2)}, u32[]{:S(2)}) collective-permute-start(bf16[4,128,128]{2,1,0:T(8,128)(2,1)S(1)} %get-tuple-element.30), channel_id=1, source_target_pairs={{0,3},{1,0},{2,1},{3,2},{4,7},{5,4},{6,5},{7,6},{8,11},{9,8},{10,9... | collective-permute-start | bytes 393224 | tf_op jit(solution)/shard_map/ppermute | solution.py:211
  133.1 31.1 %collective-permute-start.17 = (bf16[4,128,640]{2,1,0:T(8,128)(2,1)S(1)}, bf16[4,128,640]{2,1,0:T(8,128)(2,1)S(1)}, u32[]{:S(2)}, u32[]{:S(2)}) collective-permute-start(bf16[4,128,640]{2,1,0:T(8,128)(2,1)S(1)} %get-tuple-element.24), channel_id=1, source_target_pairs={{0,3},{1,0},{2,1},{3,2},{4,7},{5,4},{6,5},{7,6},{8,11},{9,8},{10,9... | collective-permute-start | bytes 1966088 | tf_op jit(solution)/shard_map/ppermute | solution.py:211
  139.1 79.4 %collective-permute-start.15 = (bf16[4,128,640]{2,1,0:T(8,128)(2,1)S(1)}, bf16[4,128,640]{2,1,0:T(8,128)(2,1)S(1)}, u32[]{:S(2)}, u32[]{:S(2)}) collective-permute-start(bf16[4,128,640]{2,1,0:T(8,128)(2,1)S(1)} %get-tuple-element.22), channel_id=1, source_target_pairs={{0,1},{1,2},{2,3},{3,0},{4,5},{5,6},{6,7},{7,4},{8,9},{9,10},{10,1... | collective-permute-start | bytes 1966088 | tf_op jit(solution)/shard_map/ppermute | solution.py:211
  161.4 60.8 %collective-permute-start.18 = (bf16[4,128,640]{2,1,0:T(8,128)(2,1)S(1)}, bf16[4,128,640]{2,1,0:T(8,128)(2,1)S(1)}, u32[]{:S(2)}, u32[]{:S(2)}) collective-permute-start(bf16[4,128,640]{2,1,0:T(8,128)(2,1)S(1)} %get-tuple-element.25), channel_id=1, source_target_pairs={{0,3},{1,0},{2,1},{3,2},{4,7},{5,4},{6,5},{7,6},{8,11},{9,8},{10,9... | collective-permute-start | bytes 1966088 | tf_op jit(solution)/shard_map/ppermute | solution.py:211
  164.2 34.2 %collective-permute-start.16 = (bf16[4,128,256]{2,1,0:T(8,128)(2,1)S(1)}, bf16[4,128,256]{2,1,0:T(8,128)(2,1)S(1)}, u32[]{:S(2)}, u32[]{:S(2)}) collective-permute-start(bf16[4,128,256]{2,1,0:T(8,128)(2,1)S(1)} %get-tuple-element.23), channel_id=1, source_target_pairs={{0,1},{1,2},{2,3},{3,0},{4,5},{5,6},{6,7},{7,4},{8,9},{9,10},{10,1... | collective-permute-start | bytes 786440 | tf_op jit(solution)/shard_map/ppermute | solution.py:211
  164.2 49.8 %collective-permute-start.20 = (bf16[4,128,256]{2,1,0:T(8,128)(2,1)S(1)}, bf16[4,128,256]{2,1,0:T(8,128)(2,1)S(1)}, u32[]{:S(2)}, u32[]{:S(2)}) collective-permute-start(bf16[4,128,256]{2,1,0:T(8,128)(2,1)S(1)} %get-tuple-element.27), channel_id=1, source_target_pairs={{0,1},{1,2},{2,3},{3,0},{4,5},{5,6},{6,7},{7,4},{8,9},{9,10},{10,1... | collective-permute-start | bytes 786440 | tf_op jit(solution)/shard_map/ppermute | solution.py:211
  164.3 52.1 %collective-permute-start.21 = (bf16[4,128,256]{2,1,0:T(8,128)(2,1)S(1)}, bf16[4,128,256]{2,1,0:T(8,128)(2,1)S(1)}, u32[]{:S(2)}, u32[]{:S(2)}) collective-permute-start(bf16[4,128,256]{2,1,0:T(8,128)(2,1)S(1)} %get-tuple-element.28), channel_id=1, source_target_pairs={{0,3},{1,0},{2,1},{3,2},{4,7},{5,4},{6,5},{7,6},{8,11},{9,8},{10,9... | collective-permute-start | bytes 786440 | tf_op jit(solution)/shard_map/ppermute | solution.py:211
  166.3 58.7 %copy-start.26 = (bf16[2,5,256,640]{3,2,1,0:T(8,128)(2,1)S(1)}, bf16[2,5,256,640]{3,2,1,0:T(8,128)(2,1)}, u32[]{:S(2)}) copy-start(bf16[2,5,256,640]{3,2,1,0:T(8,128)(2,1)} %param.9) | copy-start | bytes 9830404
  166.4 58.6 %copy-start.28 = (bf16[448,256,1]{1,0,2:T(8,128)(2,1)S(1)}, bf16[448,256,1]{1,0,2:T(8,128)(2,1)}, u32[]{:S(2)}) copy-start(bf16[448,256,1]{1,0,2:T(8,128)(2,1)} %constant.34) | copy-start | bytes 688132
  198.5 36.2 %collective-permute-start.19 = (bf16[4,128,256]{2,1,0:T(8,128)(2,1)S(1)}, bf16[4,128,256]{2,1,0:T(8,128)(2,1)S(1)}, u32[]{:S(2)}, u32[]{:S(2)}) collective-permute-start(bf16[4,128,256]{2,1,0:T(8,128)(2,1)S(1)} %get-tuple-element.26), channel_id=1, source_target_pairs={{0,3},{1,0},{2,1},{3,2},{4,7},{5,4},{6,5},{7,6},{8,11},{9,8},{10,9... | collective-permute-start | bytes 786440 | tf_op jit(solution)/shard_map/ppermute | solution.py:211
  214.0 26.3 %collective-permute-start.26 = (bf16[2,192,640]{2,1,0:T(8,128)(2,1)S(1)}, bf16[2,192,640]{2,1,0:T(8,128)(2,1)S(1)}, u32[]{:S(2)}, u32[]{:S(2)}) collective-permute-start(bf16[2,192,640]{2,1,0:T(8,128)(2,1)S(1)} %get-tuple-element.39), channel_id=1, source_target_pairs={{4,0},{8,4},{12,8},{16,12},{20,16},{24,20},{28,24},{5,1},{9,5},{13... | collective-permute-start | bytes 1474568 | tf_op jit(solution)/shard_map/ppermute | solution.py:231
  216.4 9.6 %copy-start.8 = (bf16[192,448]{1,0:T(8,128)(2,1)S(1)}, bf16[192,448]{1,0:T(8,128)(2,1)}, u32[]{:S(2)}) copy-start(bf16[192,448]{1,0:T(8,128)(2,1)} %constant.31.clone.refs_2_) | copy-start | bytes 516100
  216.4 24.0 %collective-permute-start.24 = (bf16[2,192,640]{2,1,0:T(8,128)(2,1)S(1)}, bf16[2,192,640]{2,1,0:T(8,128)(2,1)S(1)}, u32[]{:S(2)}, u32[]{:S(2)}) collective-permute-start(bf16[2,192,640]{2,1,0:T(8,128)(2,1)S(1)} %get-tuple-element.40), channel_id=1, source_target_pairs={{0,4},{4,8},{8,12},{12,16},{16,20},{20,24},{24,28},{1,5},{5,9},{9,... | collective-permute-start | bytes 1474568 | tf_op jit(solution)/shard_map/ppermute | solution.py:231
  218.5 25.1 %collective-permute-start.25 = (bf16[2,256,640]{2,1,0:T(8,128)(2,1)S(1)}, bf16[2,256,640]{2,1,0:T(8,128)(2,1)S(1)}, u32[]{:S(2)}, u32[]{:S(2)}) collective-permute-start(bf16[2,256,640]{2,1,0:T(8,128)(2,1)S(1)} %pad_maximum_fusion.2), channel_id=1, source_target_pairs={{0,4},{4,8},{8,12},{12,16},{16,20},{20,24},{24,28},{1,5},{5,9},{9,... | collective-permute-start | bytes 1966088 | tf_op jit(solution)/shard_map/ppermute | solution.py:231
  222.2 21.4 %collective-permute-start.27 = (bf16[2,256,640]{2,1,0:T(8,128)(2,1)S(1)}, bf16[2,256,640]{2,1,0:T(8,128)(2,1)S(1)}, u32[]{:S(2)}, u32[]{:S(2)}) collective-permute-start(bf16[2,256,640]{2,1,0:T(8,128)(2,1)S(1)} %pad_maximum_fusion.3), channel_id=1, source_target_pairs={{4,0},{8,4},{12,8},{16,12},{20,16},{24,20},{28,24},{5,1},{9,5},{13... | collective-permute-start | bytes 1966088 | tf_op jit(solution)/shard_map/ppermute | solution.py:231
  240.3 14.4 %copy-start.11 = (bf16[640,1280]{1,0:T(8,128)(2,1)S(1)}, bf16[640,1280]{1,0:T(8,128)(2,1)}, u32[]{:S(2)}) copy-start(bf16[640,1280]{1,0:T(8,128)(2,1)} %get-tuple-element.34.w_in) | copy-start | bytes 4915204
  240.4 14.4 %copy-start.12 = (bf16[1280,640]{1,0:T(8,128)(2,1)S(1)}, bf16[1280,640]{1,0:T(8,128)(2,1)}, u32[]{:S(2)}) copy-start(bf16[1280,640]{1,0:T(8,128)(2,1)} %get-tuple-element.32.w_out) | copy-start | bytes 4915204

commit v7 on v6

--- a/solution.py
+++ b/solution.py
@@ -267,7 +267,7 @@
 
     pairs = state.reshape(rows // rim, rim, width, channels)
 
-    def pick(members, lon, cut):
+    def pick(pairs, members, lon, cut):
         first, last = members[0] // rim, members[-1] // rim
         chosen = pairs[first : last + 1 : max(1, (last - first) // (len(members) // rim - 1))]
         return chosen[:, :, lon, cut].reshape(len(members), -1, chosen[..., cut].shape[-1])
@@ -277,8 +277,12 @@
     cuts = [count * LANES for _, count in parts]
     lanes = [slice(0, channels)] * 2 + pieces
     groups_of = [groups[0], groups[1]] + [groups[2]] * len(parts)
-    firsts = [pick(members, slice(0, edge), cut) for members, cut in zip(groups_of, lanes)]
-    lasts = [pick(members, slice(width - edge, width), cut) for members, cut in zip(groups_of, lanes)]
+    head, tail = slice(0, edge), slice(width - edge, width)
+    firsts = [pick(pairs, groups[0], head, lanes[0])]
+    lasts = [pick(pairs, groups[0], tail, lanes[0])]
+    pairs, _, _ = lax.optimization_barrier((pairs, firsts[0], lasts[0]))
+    firsts += [pick(pairs, members, head, cut) for members, cut in zip(groups_of[1:], lanes[1:])]
+    lasts += [pick(pairs, members, tail, cut) for members, cut in zip(groups_of[1:], lanes[1:])]
     tables = (forward, inverse)
     out = None
     for layer in range(blocks):

time: 269 us -> 280 us (1.041)
  waiting for transfers between devices: 105 us -> 127 us
  starting transfers between devices: 55.2 us -> 43.6 us
    ppermute x20, waiting for transfers between devices: 102 us -> 124 us  [rotate(): lax.ppermute(block, axis, [(i, (i + hops) % count) for i in range(count)])]
    ppermute x20, starting transfers between devices: 34 us -> 22.5 us  [rotate(): lax.ppermute(block, axis, [(i, (i + hops) % count) for i in range(count)])]
  transfers between devices with their start and end apart: 28 -> 28, of which waited for: 9 -> 10; matrix products, arithmetic and copies ran while one was open for 5% -> 5% of each run, Pallas kernels for 14% -> 14%
where the time goes in v7:
time: 280 us; the launch traced here: 279 us
  waiting for transfers between devices  127 us (45%)
  Pallas kernels  79.1 us (28%)
  starting transfers between devices  43.6 us (16%)
  local copies, waits for them, and re-layouts  22 us (8%)
  matrix products  4.36 us (2%)
    ppermute x20, waiting for transfers between devices, rotate(): lax.ppermute(block, axis, [(i, (i + hops) % count) for i in range(count)])  124 us
    pallas_call x8, Pallas kernels, convolve(): pl.pallas_call(kernel, grid=(blocks,), out_shape=out, in_specs=[pl.BlockS...  53.2 us
    pallas_call x5, Pallas kernels, mlp(): pl.pallas_call(functools.partial(mlp_kernel, half=edge, kept=len(extra),...  25.8 us
    ppermute x20, starting transfers between devices, rotate(): lax.ppermute(block, axis, [(i, (i + hops) % count) for i in range(count)])  22.5 us
    ppermute x8, starting transfers between devices, step_rows(): return lax.ppermute(block, 'lat', pairs)  21.2 us
    unnamed x60, local copies, waits for them, and re-layouts  13.1 us
  transfers between devices with their start and end apart: 28, of which 10 were waited for; matrix products, arithmetic and copies ran while one was open for 5% of the time, Pallas kernels for 14%

profile of v7, /device:TPU:20, one launch (start us, length us, event | category | flops | bytes accessed | tf_op | source)
XLA Modules:
  0.0 278.9 jit_solution(11560196701074530773)
XLA Ops:
  0.0 1.4 slice.120
  1.6 1.6 collective-permute-start
  3.7 1.6 collective-permute-start.12
  5.9 1.0 fusion.8
  6.9 1.6 collective-permute-start.1
  8.5 1.1 fusion.6
  9.6 1.9 slice_bitcast_fusion.1
  11.5 1.2 copy-done.24
  12.7 2.0 slice_bitcast_fusion
  14.7 0.8 fusion.5
  16.1 3.4 %convolution_bitcast_fusion.refs_3_ = f32[5,448,640]{2,1,0:T(8,128)} fusion(bf16[448,256,1]{1,0,2:T(8,128)(2,1)S(1)} %copy-done.27, bf16[2,5,256,640]{3,2,1,0:T(8,128)(2,1)S(1)} %copy-done.25), kind=kOutput, calls=%fused_computation | convolution fusion | flops 734003200 | bytes 7602176 | tf_op jit(solution)/shard_map/kt,rtc->rkc/dot_general | solution.py:255
  19.5 13.8 %collective-permute-done.refs_5_ = bf16[4,128,640]{2,1,0:T(8,128)(2,1)S(1)} collective-permute-done((bf16[4,128,640]{2,1,0:T(8,128)(2,1)S(1)}, bf16[4,128,640]{2,1,0:T(8,128)(2,1)S(1)}, u32[]{:S(2)}, u32[]{:S(2)}) %collective-permute-start) | collective-permute-done | bytes 655392 | tf_op jit(solution)/shard_map/ppermute | solution.py:211
  33.3 5.5 %collective-permute-done.12.refs_7_ = bf16[4,128,128]{2,1,0:T(8,128)(2,1)S(1)} collective-permute-done((bf16[4,128,128]{2,1,0:T(8,128)(2,1)S(1)}, bf16[4,128,128]{2,1,0:T(8,128)(2,1)S(1)}, u32[]{:S(2)}, u32[]{:S(2)}) %collective-permute-start.12) | collective-permute-done | bytes 131104 | tf_op jit(solution)/shard_map/ppermute | solution.py:211
  38.9 1.6 collective-permute-start.10
  40.5 0.7 copy-done.21
  41.1 0.4 collective-permute-start.11
  41.6 0.8 collective-permute-start.9
  42.4 0.9 pad_maximum_fusion.1
  43.4 0.9 pad_maximum_fusion
  44.3 28.3 %collective-permute-done.10.refs_7_ = bf16[4,128,256]{2,1,0:T(8,128)(2,1)S(1)} collective-permute-done((bf16[4,128,256]{2,1,0:T(8,128)(2,1)S(1)}, bf16[4,128,256]{2,1,0:T(8,128)(2,1)S(1)}, u32[]{:S(2)}, u32[]{:S(2)}) %collective-permute-start.10) | collective-permute-done | bytes 262176 | tf_op jit(solution)/shard_map/ppermute | solution.py:211
  72.6 0.7 copy-done.15
  73.3 1.9 collective-permute-start.6
  75.2 2.9 %collective-permute-done.11.refs_10_ = bf16[4,128,256]{2,1,0:T(8,128)(2,1)S(1)} collective-permute-done((bf16[4,128,256]{2,1,0:T(8,128)(2,1)S(1)}, bf16[4,128,256]{2,1,0:T(8,128)(2,1)S(1)}, u32[]{:S(2)}, u32[]{:S(2)}) %collective-permute-start.11) | collective-permute-done | bytes 262176 | tf_op jit(solution)/shard_map/ppermute | solution.py:211
  78.1 0.7 copy-done.17
  78.8 1.9 collective-permute-start.4
  80.7 1.9 collective-permute-done.9.refs_10_
  82.7 0.7 copy-done.19
  83.4 1.9 collective-permute-start.5
  85.3 0.8 copy-done.9
  86.2 4.5 %collective-permute-start.7 = (bf16[2,256,640]{2,1,0:T(8,128)(2,1)}, bf16[2,256,640]{2,1,0:T(8,128)(2,1)}, u32[]{:S(2)}, u32[]{:S(2)}) collective-permute-start(bf16[2,256,640]{2,1,0:T(8,128)(2,1)} %pad_maximum_fusion.1), channel_id=1, source_target_pairs={{4,0},{8,4},{12,8},{16,12},{20,16},{24,20},{28,24},{5,1},{9,5},{13... | collective-permute-start | bytes 1966088 | tf_op jit(solution)/shard_map/ppermute | solution.py:231
  90.7 7.4 %collective-permute-start.8 = (bf16[4,128,256]{2,1,0:T(8,128)(2,1)}, bf16[4,128,256]{2,1,0:T(8,128)(2,1)S(1)}, u32[]{:S(2)}, u32[]{:S(2)}) collective-permute-start(bf16[4,128,256]{2,1,0:T(8,128)(2,1)} %bitcast.51), channel_id=1, source_target_pairs={{0,1},{1,2},{2,3},{3,0},{4,5},{5,6},{6,7},{7,4},{8,9},{9,10},{10,1... | collective-permute-start | bytes 786440 | tf_op jit(solution)/shard_map/ppermute | solution.py:211
  98.2 2.6 copy-done
  100.8 1.1 copy-done.4
  101.9 1.1 copy-done.6
  103.0 0.9 copy-done.7
  103.9 1.1 copy-done.10
  105.0 0.9 copy-done.22
  105.9 3.5 %zonal_conv.11.refs_2_ = bf16[8,192,128]{2,1,0:T(8,128)(2,1)S(1)} custom-call(f32[16]{0:T(128)S(1)} %and_select_fusion.refs_0_, bf16[448,448]{1,0:T(8,128)(2,1)S(1)} %copy-done.2, bf16[192,448]{1,0:T(8,128)(2,1)S(1)} %copy-done.7, f32[5,448,640]{2,1,0:T(8,128)S(1)} %copy-done, bf16[12,192,640]{2,1,0:T(8,128)(2,1)S(1)} %bitcast.44, ...), custom_call_target="tpu_custom_call" | custom-call | flops 792723456 | bytes 2523136 | tf_op jit(solution)/shard_map/zonal_conv/pallas_call | solution.py:110
  109.4 6.1 %zonal_conv.10.refs_1_ = bf16[8,192,256]{2,1,0:T(8,128)(2,1)S(1)} custom-call(f32[16]{0:T(128)S(1)} %and_select_fusion.refs_0_, bf16[448,448]{1,0:T(8,128)(2,1)S(1)} %copy-done.2, bf16[192,448]{1,0:T(8,128)(2,1)S(1)} %copy-done.7, f32[5,448,640]{2,1,0:T(8,128)S(1)} %copy-done, bf16[12,192,640]{2,1,0:T(8,128)(2,1)S(1)} %bitcast.45, ...), custom_call_target="tpu_custom_call" | custom-call | flops 1585446912 | bytes 5046272 | tf_op jit(solution)/shard_map/zonal_conv/pallas_call | solution.py:110
  115.5 6.0 %zonal_conv.9.refs_0_ = bf16[8,192,256]{2,1,0:T(8,128)(2,1)S(1)} custom-call(f32[16]{0:T(128)S(1)} %and_select_fusion.refs_0_, bf16[448,448]{1,0:T(8,128)(2,1)S(1)} %copy-done.2, bf16[192,448]{1,0:T(8,128)(2,1)S(1)} %copy-done.7, f32[5,448,640]{2,1,0:T(8,128)S(1)} %copy-done, bf16[12,192,640]{2,1,0:T(8,128)(2,1)S(1)} %bitcast.46, ...), custom_call_target="tpu_custom_call" | custom-call | flops 1585446912 | bytes 5046272 | tf_op jit(solution)/shard_map/zonal_conv/pallas_call | solution.py:110
  121.6 12.1 %zonal_conv.8.refs_0_ = bf16[4,192,640]{2,1,0:T(8,128)(2,1)S(1)} custom-call(f32[16]{0:T(128)S(1)} %and_select_fusion.refs_0_, bf16[448,448]{1,0:T(8,128)(2,1)S(1)} %copy-done.2, bf16[192,448]{1,0:T(8,128)(2,1)S(1)} %copy-done.7, f32[5,448,640]{2,1,0:T(8,128)S(1)} %copy-done, bf16[12,192,640]{2,1,0:T(8,128)(2,1)S(1)} %bitcast.47, ...), custom_call_target="tpu_custom_call" | custom-call | flops 3523215360 | bytes 12615680 | tf_op jit(solution)/shard_map/zonal_conv/pallas_call | solution.py:110
  133.8 4.0 %channel_mlp.5 = (bf16[4,192,640]{2,1,0:T(8,128)(2,1)S(1)}, bf16[4,128,640]{2,1,0:T(8,128)(2,1)S(1)}, bf16[4,128,640]{2,1,0:T(8,128)(2,1)S(1)}) custom-call(f32[1,640]{1,0:T(1,128)S(1)} %get-tuple-element.59.gain, bf16[640,1280]{1,0:T(8,128)(2,1)S(1)} %copy-done.13, bf16[1280,640]{1,0:T(8,128)(2,1)S(1)} %copy-done.14, bf16[4,192,640]{2,1,0:T(8,128)(2,1)S(1)} %zonal_conv.8.refs_0_), custom_call_target="tpu_custom_call" | custom-call | flops 2516582400 | bytes 5242880 | tf_op jit(solution)/shard_map/channel_mlp/pallas_call | solution.py:186
  138.1 4.0 %channel_mlp.7 = (bf16[4,192,640]{2,1,0:T(8,128)(2,1)S(1)}, bf16[4,128,256]{2,1,0:T(8,128)(2,1)S(1)}, bf16[4,128,256]{2,1,0:T(8,128)(2,1)S(1)}, bf16[4,128,256]{...) custom-call(f32[1,640]{1,0:T(1,128)S(1)} %get-tuple-element.59.gain,, ...), custom_call_target="tpu_custom_call" | custom-call | flops 2516582400 | bytes 5242880 | tf_op jit(solution)/shard_map/channel_mlp/pallas_call | solution.py:186
  142.2 2.0 collective-permute-start.23
  144.3 2.0 collective-permute-start.17
  146.2 4.0 %channel_mlp.6 = (bf16[4,192,640]{2,1,0:T(8,128)(2,1)S(1)}, bf16[4,128,640]{2,1,0:T(8,128)(2,1)S(1)}, bf16[4,128,640]{2,1,0:T(8,128)(2,1)S(1)}) custom-call(f32[1,640]{1,0:T(1,128)S(1)} %get-tuple-element.59.gain, bf16[640,1280]{1,0:T(8,128)(2,1)S(1)} %copy-done.13, bf16[1280,640]{1,0:T(8,128)(2,1)S(1)} %copy-done.14, ...), custom_call_target="tpu_custom_call" | custom-call | flops 2516582400 | bytes 5242880 | tf_op jit(solution)/shard_map/channel_mlp/pallas_call | solution.py:186
  150.5 22.1 %collective-permute-done.14.refs_7_.refs_6_ = bf16[4,128,640]{2,1,0:T(8,128)(2,1)S(1)} collective-permute-done((bf16[4,128,640]{2,1,0:T(8,128)(2,1)S(1)}, bf16[4,128,640]{2,1,0:T(8,128)(2,1)S(1)}, u32[]{:S(2)}, u32[]{:S(2)}) %collective-permute-start.14) | collective-permute-done | bytes 655392 | tf_op jit(solution)/shard_map/ppermute | solution.py:211
  172.6 2.7 collective-permute-done.22.refs_9_
  175.4 1.1 collective-permute-start.20
  176.5 0.9 collective-permute-start.21
  177.7 39.8 %collective-permute-done.16.refs_9_ = bf16[4,128,256]{2,1,0:T(8,128)(2,1)S(1)} collective-permute-done((bf16[4,128,256]{2,1,0:T(8,128)(2,1)S(1)}, bf16[4,128,256]{2,1,0:T(8,128)(2,1)S(1)}, u32[]{:S(2)}, u32[]{:S(2)}) %collective-permute-start.16) | collective-permute-done | bytes 262176 | tf_op jit(solution)/shard_map/ppermute | solution.py:211
  217.5 6.9 %collective-permute-done.20.refs_9_ = bf16[4,128,256]{2,1,0:T(8,128)(2,1)S(1)} collective-permute-done((bf16[4,128,256]{2,1,0:T(8,128)(2,1)S(1)}, bf16[4,128,256]{2,1,0:T(8,128)(2,1)S(1)}, u32[]{:S(2)}, u32[]{:S(2)}) %collective-permute-start.20) | collective-permute-done | bytes 262176 | tf_op jit(solution)/shard_map/ppermute | solution.py:211
  224.4 1.9 collective-permute-start.26
  226.4 2.5 collective-permute-start.24
  228.9 1.9 collective-permute-start.25
  230.9 4.5 %collective-permute-start.27 = (bf16[2,256,640]{2,1,0:T(8,128)(2,1)S(1)}, bf16[2,256,640]{2,1,0:T(8,128)(2,1)S(1)}, u32[]{:S(2)}, u32[]{:S(2)}) collective-permute-start(bf16[2,256,640]{2,1,0:T(8,128)(2,1)S(1)} %pad_maximum_fusion.3), channel_id=1, source_target_pairs={{4,0},{8,4},{12,8},{16,12},{20,16},{24,20},{28,24},{5,1},{9,5},{13... | collective-permute-start | bytes 1966088 | tf_op jit(solution)/shard_map/ppermute | solution.py:231
  235.4 0.9 convolution_bitcast_fusion.1.refs_3_
  236.4 2.9 %zonal_conv.14.refs_2_ = bf16[8,192,128]{2,1,0:T(8,128)(2,1)S(1)} custom-call(f32[16]{0:T(128)S(1)} %and_select_fusion.refs_0_, bf16[448,448]{1,0:T(8,128)(2,1)S(1)} %copy-done.2, bf16[192,448]{1,0:T(8,128)(2,1)S(1)} %copy-done.8, f32[5,448,640]{2,1,0:T(8,128)S(1)} %convolution_bitcast_fusion.1.refs_3_, bf16[4,192,640]{2,1,0:T(8,128)(2,1)S(1)} %get-tuple-element.20.refs_4_, ...), custom_call_target="tpu_custom_call" | custom-call | flops 792723456 | bytes 2523136 | tf_op jit(solution)/shard_map/zonal_conv/pallas_call | solution.py:110
  239.3 5.8 %zonal_conv.13.refs_1_ = bf16[8,192,256]{2,1,0:T(8,128)(2,1)S(1)} custom-call(f32[16]{0:T(128)S(1)} %and_select_fusion.refs_0_, bf16[448,448]{1,0:T(8,128)(2,1)S(1)} %copy-done.2, bf16[192,448]{1,0:T(8,128)(2,1)S(1)} %copy-done.8, f32[5,448,640]{2,1,0:T(8,128)S(1)} %convolution_bitcast_fusion.1.refs_3_, bf16[4,192,640]{2,1,0:T(8,128)(2,1)S(1)} %get-tuple-element.20.refs_4_, ...), custom_call_target="tpu_custom_call" | custom-call | flops 1585446912 | bytes 5046272 | tf_op jit(solution)/shard_map/zonal_conv/pallas_call | solution.py:110
  245.0 5.7 %zonal_conv.12.refs_0_ = bf16[8,192,256]{2,1,0:T(8,128)(2,1)S(1)} custom-call(f32[16]{0:T(128)S(1)} %and_select_fusion.refs_0_, bf16[448,448]{1,0:T(8,128)(2,1)S(1)} %copy-done.2, bf16[192,448]{1,0:T(8,128)(2,1)S(1)} %copy-done.8, f32[5,448,640]{2,1,0:T(8,128)S(1)} %convolution_bitcast_fusion.1.refs_3_, bf16[4,192,640]{2,1,0:T(8,128)(2,1)S(1)} %get-tuple-element.20.refs_4_, ...), custom_call_target="tpu_custom_call" | custom-call | flops 1585446912 | bytes 5046272 | tf_op jit(solution)/shard_map/zonal_conv/pallas_call | solution.py:110
  250.8 3.2 %collective-permute-done.25.refs_11_ = bf16[2,256,640]{2,1,0:T(8,128)(2,1)S(1)} collective-permute-done((bf16[2,256,640]{2,1,0:T(8,128)(2,1)S(1)}, bf16[2,256,640]{2,1,0:T(8,128)(2,1)S(1)}, u32[]{:S(2)}, u32[]{:S(2)}) %collective-permute-start.25) | collective-permute-done | bytes 655392 | tf_op jit(solution)/shard_map/ppermute | solution.py:231
  254.0 11.1 %zonal_conv.15.refs_0_ = bf16[4,192,640]{2,1,0:T(8,128)(2,1)S(1)} custom-call(f32[16]{0:T(128)S(1)} %and_select_fusion.refs_0_, bf16[448,448]{1,0:T(8,128)(2,1)S(1)} %copy-done.2, bf16[192,448]{1,0:T(8,128)(2,1)S(1)} %copy-done.8, f32[5,448,640]{2,1,0:T(8,128)S(1)} %convolution_bitcast_fusion.1.refs_3_, bf16[4,192,640]{2,1,0:T(8,128)(2,1)S(1)} %get-tuple-element.20.refs_4_, ...), custom_call_target="tpu_custom_call" | custom-call | flops 3523215360 | bytes 12615680 | tf_op jit(solution)/shard_map/zonal_conv/pallas_call | solution.py:110
  265.2 4.8 %channel_mlp.8.refs_3_ = bf16[12,192,640]{2,1,0:T(8,128)(2,1)} custom-call(f32[1,640]{1,0:T(1,128)S(1)} %get-tuple-element.60.gain, bf16[640,1280]{1,0:T(8,128)(2,1)S(1)} %copy-done.11, bf16[1280,640]{1,0:T(8,128)(2,1)S(1)} %copy-done.12, bf16[4,192,640]{2,1,0:T(8,128)(2,1)S(1)} %zonal_conv.15.refs_0_), custom_call_target="tpu_custom_call" | custom-call | flops 2516582400 | bytes 5242880 | tf_op jit(solution)/shard_map/channel_mlp/pallas_call | solution.py:186
  270.1 8.9 %channel_mlp.9 = bf16[12,192,640]{2,1,0:T(8,128)(2,1)} custom-call(f32[1,640]{1,0:T(1,128)S(1)} %get-tuple-element.60.gain, bf16[640,1280]{1,0:T(8,128)(2,1)S(1)} %copy-done.11, bf16[1280,640]{1,0:T(8,128)(2,1)S(1)} %copy-done.12, bf16[8,192,256]{2,1,0:T(8,128)(2,1)S(1)} %zonal_conv.12.refs_0_, ...), custom_call_target="tpu_custom_call", output_to_operand_aliasing={{}: (6, {})} | custom-call | flops 5033164800 | bytes 7208960 | tf_op jit(solution)/shard_map/channel_mlp/pallas_call | solution.py:186
  (87 shorter events, 2.8 us)
Async XLA Ops:
  0.0 3.7 %copy-start.1 = (bf16[1,12,640,192]{2,3,1,0:T(8,128)(2,1)S(1)}, bf16[1,12,640,192]{2,3,1,0:T(8,128)(2,1)}, u32[]{:S(2)}) copy-start(bf16[1,12,640,192]{2,3,1,0:T(8,128)(2,1)} %param.8) | copy-start | bytes 8847364
  1.6 31.7 %collective-permute-start = (bf16[4,128,640]{2,1,0:T(8,128)(2,1)S(1)}, bf16[4,128,640]{2,1,0:T(8,128)(2,1)S(1)}, u32[]{:S(2)}, u32[]{:S(2)}) collective-permute-start(bf16[4,128,640]{2,1,0:T(8,128)(2,1)S(1)} %bitcast.50), channel_id=1, source_target_pairs={{0,1},{1,2},{2,3},{3,0},{4,5},{5,6},{6,7},{7,4},{8,9},{9,10},{10,1... | collective-permute-start | bytes 1966088 | tf_op jit(solution)/shard_map/ppermute | solution.py:211
  3.2 38.4 %collective-permute-start.2 = (bf16[4,128,640]{2,1,0:T(8,128)(2,1)S(1)}, bf16[4,128,640]{2,1,0:T(8,128)(2,1)S(1)}, u32[]{:S(2)}, u32[]{:S(2)}) collective-permute-start(bf16[4,128,640]{2,1,0:T(8,128)(2,1)S(1)} %bitcast.49), channel_id=1, source_target_pairs={{0,3},{1,0},{2,1},{3,2},{4,7},{5,4},{6,5},{7,6},{8,11},{9,8},{10,9... | collective-permute-start | bytes 1966088 | tf_op jit(solution)/shard_map/ppermute | solution.py:211
  3.7 35.2 %collective-permute-start.12 = (bf16[4,128,128]{2,1,0:T(8,128)(2,1)S(1)}, bf16[4,128,128]{2,1,0:T(8,128)(2,1)S(1)}, u32[]{:S(2)}, u32[]{:S(2)}) collective-permute-start(bf16[4,128,128]{2,1,0:T(8,128)(2,1)S(1)} %bitcast.56), channel_id=1, source_target_pairs={{0,1},{1,2},{2,3},{3,0},{4,5},{5,6},{6,7},{7,4},{8,9},{9,10},{10,1... | collective-permute-start | bytes 393224 | tf_op jit(solution)/shard_map/ppermute | solution.py:211
  5.3 35.1 %collective-permute-start.13 = (bf16[4,128,128]{2,1,0:T(8,128)(2,1)S(1)}, bf16[4,128,128]{2,1,0:T(8,128)(2,1)S(1)}, u32[]{:S(2)}, u32[]{:S(2)}) collective-permute-start(bf16[4,128,128]{2,1,0:T(8,128)(2,1)S(1)} %bitcast.55), channel_id=1, source_target_pairs={{0,3},{1,0},{2,1},{3,2},{4,7},{5,4},{6,5},{7,6},{8,11},{9,8},{10,9... | collective-permute-start | bytes 393224 | tf_op jit(solution)/shard_map/ppermute | solution.py:211
  5.9 3.7 %copy-start.23 = (bf16[2,640,1280]{2,1,0:T(8,128)(2,1)S(1)}, bf16[2,640,1280]{2,1,0:T(8,128)(2,1)}, u32[]{:S(2)}) copy-start(bf16[2,640,1280]{2,1,0:T(8,128)(2,1)} %param.11) | copy-start | bytes 9830404
  6.9 78.4 %collective-permute-start.1 = (bf16[4,128,640]{2,1,0:T(8,128)(2,1)S(1)}, bf16[4,128,640]{2,1,0:T(8,128)(2,1)S(1)}, u32[]{:S(2)}, u32[]{:S(2)}) collective-permute-start(bf16[4,128,640]{2,1,0:T(8,128)(2,1)S(1)} %bitcast.48), channel_id=1, source_target_pairs={{0,1},{1,2},{2,3},{3,0},{4,5},{5,6},{6,7},{7,4},{8,9},{9,10},{10,1... | collective-permute-start | bytes 1966088 | tf_op jit(solution)/shard_map/ppermute | solution.py:211
  9.6 3.1 %copy-start.24 = (bf16[2,1280,640]{2,1,0:T(8,128)(2,1)S(1)}, bf16[2,1280,640]{2,1,0:T(8,128)(2,1)}, u32[]{:S(2)}) copy-start(bf16[2,1280,640]{2,1,0:T(8,128)(2,1)} %param.12) | copy-start | bytes 9830404
  12.7 3.2 %copy-start.25 = (bf16[2,5,256,640]{3,2,1,0:T(8,128)(2,1)S(1)}, bf16[2,5,256,640]{3,2,1,0:T(8,128)(2,1)}, u32[]{:S(2)}) copy-start(bf16[2,5,256,640]{3,2,1,0:T(8,128)(2,1)} %param.9) | copy-start | bytes 9830404
  14.7 1.4 copy-start.27
  33.3 10.1 %copy-start.3 = (bf16[4,128,640]{2,1,0:T(8,128)(2,1)}, bf16[4,128,640]{2,1,0:T(8,128)(2,1)S(1)}, u32[]{:S(2)}) copy-start(bf16[4,128,640]{2,1,0:T(8,128)(2,1)S(1)} %collective-permute-done.refs_5_) | copy-start | bytes 1966084
  33.3 57.5 %collective-permute-start.3 = (bf16[4,128,640]{2,1,0:T(8,128)(2,1)}, bf16[4,128,640]{2,1,0:T(8,128)(2,1)}, u32[]{:S(2)}, u32[]{:S(2)}) collective-permute-start(bf16[4,128,640]{2,1,0:T(8,128)(2,1)} %bitcast.17), channel_id=1, source_target_pairs={{0,3},{1,0},{2,1},{3,2},{4,7},{5,4},{6,5},{7,6},{8,11},{9,8},{10,9... | collective-permute-start | bytes 1966088 | tf_op jit(solution)/shard_map/ppermute | solution.py:211
  38.9 33.7 %collective-permute-start.10 = (bf16[4,128,256]{2,1,0:T(8,128)(2,1)S(1)}, bf16[4,128,256]{2,1,0:T(8,128)(2,1)S(1)}, u32[]{:S(2)}, u32[]{:S(2)}) collective-permute-start(bf16[4,128,256]{2,1,0:T(8,128)(2,1)S(1)} %bitcast.54), channel_id=1, source_target_pairs={{0,1},{1,2},{2,3},{3,0},{4,5},{5,6},{6,7},{7,4},{8,9},{9,10},{10,1... | collective-permute-start | bytes 786440 | tf_op jit(solution)/shard_map/ppermute | solution.py:211
  40.5 0.7 copy-start.21
  41.1 37.0 %collective-permute-start.11 = (bf16[4,128,256]{2,1,0:T(8,128)(2,1)S(1)}, bf16[4,128,256]{2,1,0:T(8,128)(2,1)S(1)}, u32[]{:S(2)}, u32[]{:S(2)}) collective-permute-start(bf16[4,128,256]{2,1,0:T(8,128)(2,1)S(1)} %bitcast.53), channel_id=1, source_target_pairs={{0,3},{1,0},{2,1},{3,2},{4,7},{5,4},{6,5},{7,6},{8,11},{9,8},{10,9... | collective-permute-start | bytes 786440 | tf_op jit(solution)/shard_map/ppermute | solution.py:211
  41.6 2.7 copy-start.5
  41.6 41.1 %collective-permute-start.9 = (bf16[4,128,256]{2,1,0:T(8,128)(2,1)S(1)}, bf16[4,128,256]{2,1,0:T(8,128)(2,1)S(1)}, u32[]{:S(2)}, u32[]{:S(2)}) collective-permute-start(bf16[4,128,256]{2,1,0:T(8,128)(2,1)S(1)} %bitcast.52), channel_id=1, source_target_pairs={{0,3},{1,0},{2,1},{3,2},{4,7},{5,4},{6,5},{7,6},{8,11},{9,8},{10,9... | collective-permute-start | bytes 786440 | tf_op jit(solution)/shard_map/ppermute | solution.py:211
  42.4 48.3 %copy-start.29 = (bf16[2,640]{1,0:T(2,128)(2,1)S(1)}, bf16[2,640]{1,0:T(2,128)(2,1)}, u32[]{:S(2)}) copy-start(bf16[2,640]{1,0:T(2,128)(2,1)} %param.10) | copy-start | bytes 7684
  42.4 55.7 %copy-start.2 = (bf16[448,448]{1,0:T(8,128)(2,1)S(1)}, bf16[448,448]{1,0:T(8,128)(2,1)}, u32[]{:S(2)}) copy-start(bf16[448,448]{1,0:T(8,128)(2,1)} %constant.30.clone.refs_1_) | copy-start | bytes 1204228
  72.6 0.7 copy-start.15
  73.3 48.3 %collective-permute-start.6 = (bf16[2,192,640]{2,1,0:T(8,128)(2,1)}, bf16[2,192,640]{2,1,0:T(8,128)(2,1)}, u32[]{:S(2)}, u32[]{:S(2)}) collective-permute-start(bf16[2,192,640]{2,1,0:T(8,128)(2,1)} %get-tuple-element.43), channel_id=1, source_target_pairs={{4,0},{8,4},{12,8},{16,12},{20,16},{24,20},{28,24},{5,1},{9,5},{13... | collective-permute-start | bytes 1474568 | tf_op jit(solution)/shard_map/ppermute | solution.py:231
  78.1 0.7 copy-start.17
  78.8 42.8 %collective-permute-start.4 = (bf16[2,192,640]{2,1,0:T(8,128)(2,1)}, bf16[2,192,640]{2,1,0:T(8,128)(2,1)}, u32[]{:S(2)}, u32[]{:S(2)}) collective-permute-start(bf16[2,192,640]{2,1,0:T(8,128)(2,1)} %get-tuple-element.44), channel_id=1, source_target_pairs={{0,4},{4,8},{8,12},{12,16},{16,20},{20,24},{24,28},{1,5},{5,9},{9,... | collective-permute-start | bytes 1474568 | tf_op jit(solution)/shard_map/ppermute | solution.py:231
  82.7 0.7 copy-start.19
  83.4 38.2 %collective-permute-start.5 = (bf16[2,256,640]{2,1,0:T(8,128)(2,1)}, bf16[2,256,640]{2,1,0:T(8,128)(2,1)}, u32[]{:S(2)}, u32[]{:S(2)}) collective-permute-start(bf16[2,256,640]{2,1,0:T(8,128)(2,1)} %pad_maximum_fusion), channel_id=1, source_target_pairs={{0,4},{4,8},{8,12},{12,16},{16,20},{20,24},{24,28},{1,5},{5,9},{9,... | collective-permute-start | bytes 1966088 | tf_op jit(solution)/shard_map/ppermute | solution.py:231
  85.3 0.8 copy-start.9
  86.2 35.5 %collective-permute-start.7 = (bf16[2,256,640]{2,1,0:T(8,128)(2,1)}, bf16[2,256,640]{2,1,0:T(8,128)(2,1)}, u32[]{:S(2)}, u32[]{:S(2)}) collective-permute-start(bf16[2,256,640]{2,1,0:T(8,128)(2,1)} %pad_maximum_fusion.1), channel_id=1, source_target_pairs={{4,0},{8,4},{12,8},{16,12},{20,16},{24,20},{28,24},{5,1},{9,5},{13... | collective-permute-start | bytes 1966088 | tf_op jit(solution)/shard_map/ppermute | solution.py:231
  90.7 24.8 %collective-permute-start.8 = (bf16[4,128,256]{2,1,0:T(8,128)(2,1)}, bf16[4,128,256]{2,1,0:T(8,128)(2,1)S(1)}, u32[]{:S(2)}, u32[]{:S(2)}) collective-permute-start(bf16[4,128,256]{2,1,0:T(8,128)(2,1)} %bitcast.51), channel_id=1, source_target_pairs={{0,1},{1,2},{2,3},{3,0},{4,5},{5,6},{6,7},{7,4},{8,9},{9,10},{10,1... | collective-permute-start | bytes 786440 | tf_op jit(solution)/shard_map/ppermute | solution.py:211
  98.2 2.6 copy-start
  100.8 1.1 copy-start.4
  101.9 1.1 copy-start.6
  103.0 0.9 copy-start.7
  103.9 1.1 copy-start.10
  105.0 0.9 copy-start.22
  105.9 3.5 %copy-start.16 = (bf16[4,128,256]{2,1,0:T(8,128)(2,1)S(1)}, bf16[4,128,256]{2,1,0:T(8,128)(2,1)}, u32[]{:S(2)}) copy-start(bf16[4,128,256]{2,1,0:T(8,128)(2,1)} %copy-done.15) | copy-start | bytes 786436
  105.9 3.5 %copy-start.18 = (bf16[4,128,256]{2,1,0:T(8,128)(2,1)S(1)}, bf16[4,128,256]{2,1,0:T(8,128)(2,1)}, u32[]{:S(2)}) copy-start(bf16[4,128,256]{2,1,0:T(8,128)(2,1)} %copy-done.17) | copy-start | bytes 786436
  109.4 6.1 %copy-start.20 = (bf16[4,128,256]{2,1,0:T(8,128)(2,1)S(1)}, bf16[4,128,256]{2,1,0:T(8,128)(2,1)}, u32[]{:S(2)}) copy-start(bf16[4,128,256]{2,1,0:T(8,128)(2,1)} %copy-done.19) | copy-start | bytes 786436
  121.6 12.2 %copy-start.13 = (bf16[640,1280]{1,0:T(8,128)(2,1)S(1)}, bf16[640,1280]{1,0:T(8,128)(2,1)}, u32[]{:S(2)}) copy-start(bf16[640,1280]{1,0:T(8,128)(2,1)} %get-tuple-element.35.w_in) | copy-start | bytes 4915204
  121.6 12.2 %copy-start.14 = (bf16[1280,640]{1,0:T(8,128)(2,1)S(1)}, bf16[1280,640]{1,0:T(8,128)(2,1)}, u32[]{:S(2)}) copy-start(bf16[1280,640]{1,0:T(8,128)(2,1)} %get-tuple-element.33.w_out) | copy-start | bytes 4915204
  137.9 34.7 %collective-permute-start.14 = (bf16[4,128,640]{2,1,0:T(8,128)(2,1)S(1)}, bf16[4,128,640]{2,1,0:T(8,128)(2,1)S(1)}, u32[]{:S(2)}, u32[]{:S(2)}) collective-permute-start(bf16[4,128,640]{2,1,0:T(8,128)(2,1)S(1)} %get-tuple-element.23), channel_id=1, source_target_pairs={{0,1},{1,2},{2,3},{3,0},{4,5},{5,6},{6,7},{7,4},{8,9},{9,10},{10,1... | collective-permute-start | bytes 1966088 | tf_op jit(solution)/shard_map/ppermute | solution.py:211
  142.2 33.2 %collective-permute-start.22 = (bf16[4,128,128]{2,1,0:T(8,128)(2,1)S(1)}, bf16[4,128,128]{2,1,0:T(8,128)(2,1)S(1)}, u32[]{:S(2)}, u32[]{:S(2)}) collective-permute-start(bf16[4,128,128]{2,1,0:T(8,128)(2,1)S(1)} %get-tuple-element.31), channel_id=1, source_target_pairs={{0,1},{1,2},{2,3},{3,0},{4,5},{5,6},{6,7},{7,4},{8,9},{9,10},{10,1... | collective-permute-start | bytes 393224 | tf_op jit(solution)/shard_map/ppermute | solution.py:211
  142.2 33.1 %collective-permute-start.23 = (bf16[4,128,128]{2,1,0:T(8,128)(2,1)S(1)}, bf16[4,128,128]{2,1,0:T(8,128)(2,1)S(1)}, u32[]{:S(2)}, u32[]{:S(2)}) collective-permute-start(bf16[4,128,128]{2,1,0:T(8,128)(2,1)S(1)} %get-tuple-element.32), channel_id=1, source_target_pairs={{0,3},{1,0},{2,1},{3,2},{4,7},{5,4},{6,5},{7,6},{8,11},{9,8},{10,9... | collective-permute-start | bytes 393224 | tf_op jit(solution)/shard_map/ppermute | solution.py:211
  144.3 32.2 %collective-permute-start.17 = (bf16[4,128,640]{2,1,0:T(8,128)(2,1)S(1)}, bf16[4,128,640]{2,1,0:T(8,128)(2,1)S(1)}, u32[]{:S(2)}, u32[]{:S(2)}) collective-permute-start(bf16[4,128,640]{2,1,0:T(8,128)(2,1)S(1)} %get-tuple-element.26), channel_id=1, source_target_pairs={{0,3},{1,0},{2,1},{3,2},{4,7},{5,4},{6,5},{7,6},{8,11},{9,8},{10,9... | collective-permute-start | bytes 1966088 | tf_op jit(solution)/shard_map/ppermute | solution.py:211
  150.3 78.6 %collective-permute-start.15 = (bf16[4,128,640]{2,1,0:T(8,128)(2,1)S(1)}, bf16[4,128,640]{2,1,0:T(8,128)(2,1)S(1)}, u32[]{:S(2)}, u32[]{:S(2)}) collective-permute-start(bf16[4,128,640]{2,1,0:T(8,128)(2,1)S(1)} %get-tuple-element.24), channel_id=1, source_target_pairs={{0,1},{1,2},{2,3},{3,0},{4,5},{5,6},{6,7},{7,4},{8,9},{9,10},{10,1... | collective-permute-start | bytes 1966088 | tf_op jit(solution)/shard_map/ppermute | solution.py:211
  172.6 58.3 %collective-permute-start.18 = (bf16[4,128,640]{2,1,0:T(8,128)(2,1)S(1)}, bf16[4,128,640]{2,1,0:T(8,128)(2,1)S(1)}, u32[]{:S(2)}, u32[]{:S(2)}) collective-permute-start(bf16[4,128,640]{2,1,0:T(8,128)(2,1)S(1)} %get-tuple-element.27), channel_id=1, source_target_pairs={{0,3},{1,0},{2,1},{3,2},{4,7},{5,4},{6,5},{7,6},{8,11},{9,8},{10,9... | collective-permute-start | bytes 1966088 | tf_op jit(solution)/shard_map/ppermute | solution.py:211
  175.4 42.1 %collective-permute-start.16 = (bf16[4,128,256]{2,1,0:T(8,128)(2,1)S(1)}, bf16[4,128,256]{2,1,0:T(8,128)(2,1)S(1)}, u32[]{:S(2)}, u32[]{:S(2)}) collective-permute-start(bf16[4,128,256]{2,1,0:T(8,128)(2,1)S(1)} %get-tuple-element.25), channel_id=1, source_target_pairs={{0,1},{1,2},{2,3},{3,0},{4,5},{5,6},{6,7},{7,4},{8,9},{9,10},{10,1... | collective-permute-start | bytes 786440 | tf_op jit(solution)/shard_map/ppermute | solution.py:211
  175.4 49.1 %collective-permute-start.20 = (bf16[4,128,256]{2,1,0:T(8,128)(2,1)S(1)}, bf16[4,128,256]{2,1,0:T(8,128)(2,1)S(1)}, u32[]{:S(2)}, u32[]{:S(2)}) collective-permute-start(bf16[4,128,256]{2,1,0:T(8,128)(2,1)S(1)} %get-tuple-element.29), channel_id=1, source_target_pairs={{0,1},{1,2},{2,3},{3,0},{4,5},{5,6},{6,7},{7,4},{8,9},{9,10},{10,1... | collective-permute-start | bytes 786440 | tf_op jit(solution)/shard_map/ppermute | solution.py:211
  176.5 49.8 %collective-permute-start.21 = (bf16[4,128,256]{2,1,0:T(8,128)(2,1)S(1)}, bf16[4,128,256]{2,1,0:T(8,128)(2,1)S(1)}, u32[]{:S(2)}, u32[]{:S(2)}) collective-permute-start(bf16[4,128,256]{2,1,0:T(8,128)(2,1)S(1)} %get-tuple-element.30), channel_id=1, source_target_pairs={{0,3},{1,0},{2,1},{3,2},{4,7},{5,4},{6,5},{7,6},{8,11},{9,8},{10,9... | collective-permute-start | bytes 786440 | tf_op jit(solution)/shard_map/ppermute | solution.py:211
  177.5 58.0 %copy-start.26 = (bf16[2,5,256,640]{3,2,1,0:T(8,128)(2,1)S(1)}, bf16[2,5,256,640]{3,2,1,0:T(8,128)(2,1)}, u32[]{:S(2)}) copy-start(bf16[2,5,256,640]{3,2,1,0:T(8,128)(2,1)} %param.9) | copy-start | bytes 9830404
  177.5 57.9 %copy-start.28 = (bf16[448,256,1]{1,0,2:T(8,128)(2,1)S(1)}, bf16[448,256,1]{1,0,2:T(8,128)(2,1)}, u32[]{:S(2)}) copy-start(bf16[448,256,1]{1,0,2:T(8,128)(2,1)} %constant.34) | copy-start | bytes 688132
  217.5 27.5 %collective-permute-start.19 = (bf16[4,128,256]{2,1,0:T(8,128)(2,1)S(1)}, bf16[4,128,256]{2,1,0:T(8,128)(2,1)S(1)}, u32[]{:S(2)}, u32[]{:S(2)}) collective-permute-start(bf16[4,128,256]{2,1,0:T(8,128)(2,1)S(1)} %get-tuple-element.28), channel_id=1, source_target_pairs={{0,3},{1,0},{2,1},{3,2},{4,7},{5,4},{6,5},{7,6},{8,11},{9,8},{10,9... | collective-permute-start | bytes 786440 | tf_op jit(solution)/shard_map/ppermute | solution.py:211
  224.4 26.4 %collective-permute-start.26 = (bf16[2,192,640]{2,1,0:T(8,128)(2,1)S(1)}, bf16[2,192,640]{2,1,0:T(8,128)(2,1)S(1)}, u32[]{:S(2)}, u32[]{:S(2)}) collective-permute-start(bf16[2,192,640]{2,1,0:T(8,128)(2,1)S(1)} %get-tuple-element.45), channel_id=1, source_target_pairs={{4,0},{8,4},{12,8},{16,12},{20,16},{24,20},{28,24},{5,1},{9,5},{13... | collective-permute-start | bytes 1474568 | tf_op jit(solution)/shard_map/ppermute | solution.py:231
  226.4 10.0 %copy-start.8 = (bf16[192,448]{1,0:T(8,128)(2,1)S(1)}, bf16[192,448]{1,0:T(8,128)(2,1)}, u32[]{:S(2)}) copy-start(bf16[192,448]{1,0:T(8,128)(2,1)} %constant.31.clone.refs_2_) | copy-start | bytes 516100
  226.4 24.5 %collective-permute-start.24 = (bf16[2,192,640]{2,1,0:T(8,128)(2,1)S(1)}, bf16[2,192,640]{2,1,0:T(8,128)(2,1)S(1)}, u32[]{:S(2)}, u32[]{:S(2)}) collective-permute-start(bf16[2,192,640]{2,1,0:T(8,128)(2,1)S(1)} %get-tuple-element.46), channel_id=1, source_target_pairs={{0,4},{4,8},{8,12},{12,16},{16,20},{20,24},{24,28},{1,5},{5,9},{9,... | collective-permute-start | bytes 1474568 | tf_op jit(solution)/shard_map/ppermute | solution.py:231
  228.9 25.1 %collective-permute-start.25 = (bf16[2,256,640]{2,1,0:T(8,128)(2,1)S(1)}, bf16[2,256,640]{2,1,0:T(8,128)(2,1)S(1)}, u32[]{:S(2)}, u32[]{:S(2)}) collective-permute-start(bf16[2,256,640]{2,1,0:T(8,128)(2,1)S(1)} %pad_maximum_fusion.2), channel_id=1, source_target_pairs={{0,4},{4,8},{8,12},{12,16},{16,20},{20,24},{24,28},{1,5},{5,9},{9,... | collective-permute-start | bytes 1966088 | tf_op jit(solution)/shard_map/ppermute | solution.py:231
  230.9 23.2 %collective-permute-start.27 = (bf16[2,256,640]{2,1,0:T(8,128)(2,1)S(1)}, bf16[2,256,640]{2,1,0:T(8,128)(2,1)S(1)}, u32[]{:S(2)}, u32[]{:S(2)}) collective-permute-start(bf16[2,256,640]{2,1,0:T(8,128)(2,1)S(1)} %pad_maximum_fusion.3), channel_id=1, source_target_pairs={{4,0},{8,4},{12,8},{16,12},{20,16},{24,20},{28,24},{5,1},{9,5},{13... | collective-permute-start | bytes 1966088 | tf_op jit(solution)/shard_map/ppermute | solution.py:231
  250.8 14.4 %copy-start.11 = (bf16[640,1280]{1,0:T(8,128)(2,1)S(1)}, bf16[640,1280]{1,0:T(8,128)(2,1)}, u32[]{:S(2)}) copy-start(bf16[640,1280]{1,0:T(8,128)(2,1)} %get-tuple-element.36.w_in) | copy-start | bytes 4915204
  250.8 14.4 %copy-start.12 = (bf16[1280,640]{1,0:T(8,128)(2,1)S(1)}, bf16[1280,640]{1,0:T(8,128)(2,1)}, u32[]{:S(2)}) copy-start(bf16[1280,640]{1,0:T(8,128)(2,1)} %get-tuple-element.34.w_out) | copy-start | bytes 4915204

commit v8 on v7

--- a/solution.py
+++ b/solution.py
@@ -33,17 +33,24 @@
     return 0.5 * values * (1.0 + lax.erf(values * math.sqrt(0.5)))
 
 
-def conv_kernel(*refs, windows, row_refs, counts):
+def conv_kernel(*refs, windows, row_refs, counts, begin, lanes):
     quad, forward, inverse, factors = refs[:4]
     sources = refs[4 : 4 + counts]
     out, spectra, product = refs[4 + counts :]
-    lanes = out.shape[2]
+    step = pl.program_id(0)
+    part = out.shape[2]
+
+    def block_of(ref):
+        offset = 0 if ref.shape[2] == part else begin
+        return pl.ds(pl.multiple_of((step + offset) * lanes, lanes), lanes)
+
+    ours = [block_of(ref) for ref in sources]
     freqs = forward.shape[0] // 2
     every = len(row_refs)
     taps_r = factors.shape[0]
 
     def row(g):
-        return jnp.concatenate([sources[source][at, lon] for source, at, lon in row_refs[g][1]], axis=0)
+        return jnp.concatenate([sources[s][at, lon, ours[s]] for s, at, lon in row_refs[g][1]], axis=0)
 
     for g in range(0, every, 2):
         two = jnp.concatenate([row(g), row(g + 1)], axis=1)
@@ -86,8 +93,8 @@
         conv = jnp.dot(inverse[...], product[:, two].astype(jnp.bfloat16), preferred_element_type=jnp.float32)
         for j in range(2):
             source, at, _ = own[h + j][1]
-            value = sources[source][at].astype(jnp.float32)
-            out[h + j] = (value + gelu(conv[:, j * lanes : (j + 1) * lanes])).astype(out.dtype)
+            value = sources[source][at, :, ours[source]].astype(jnp.float32)
+            out[h + j, :, block_of(out)] = (value + gelu(conv[:, j * lanes : (j + 1) * lanes])).astype(out.dtype)
 
 
 def convolve(quad, tables, factors, sources, rows, windows, part):
@@ -98,22 +105,23 @@
     width = inverse.shape[0]
     lanes = blocks * LANES
 
-    def block(array):
-        offset = 0 if array.shape[2] == lanes else start
-        return pl.BlockSpec((array.shape[0], array.shape[1], LANES), lambda i: (0, 0, i + offset))
-
-    def whole(array):
-        return pl.BlockSpec(array.shape, lambda i: (0,) * array.ndim)
-
+    held = pl.BlockSpec(memory_space=pltpu.VMEM)
     out = jax.ShapeDtypeStruct((out_rows, width, lanes), jnp.bfloat16)
-    kernel = functools.partial(conv_kernel, windows=windows, row_refs=rows, counts=len(sources))
+    kernel = functools.partial(
+        conv_kernel, windows=windows, row_refs=rows, counts=len(sources), begin=start, lanes=LANES
+    )
     return pl.pallas_call(
         kernel,
         grid=(blocks,),
         out_shape=out,
-        in_specs=[pl.BlockSpec(memory_space=pltpu.SMEM), whole(forward), whole(inverse), block(factors)]
-        + [block(a) for a in sources],
-        out_specs=block(out),
+        in_specs=[
+            pl.BlockSpec(memory_space=pltpu.SMEM),
+            held,
+            held,
+            pl.BlockSpec((taps_r, length, LANES), lambda i: (0, 0, i + start)),
+        ]
+        + [held] * len(sources),
+        out_specs=held,
         scratch_shapes=[
             pltpu.VMEM((len(rows), length, LANES), jnp.float32),
             pltpu.VMEM((length, out_rows * LANES), jnp.float32),

time: 280 us -> 278 us (level)
  transfers between devices with their start and end apart: 28 -> 28, of which waited for: 10 -> 10; matrix products, arithmetic and copies ran while one was open for 5% -> 5% of each run, Pallas kernels for 14% -> 13%
where the time goes in v8:
time: 278 us; the launch traced here: 277 us
  waiting for transfers between devices  128 us (46%)
  Pallas kernels  76.5 us (28%)
  starting transfers between devices  43.6 us (16%)
  local copies, waits for them, and re-layouts  22 us (8%)
  matrix products  4.36 us (2%)
    ppermute x20, waiting for transfers between devices, rotate(): lax.ppermute(block, axis, [(i, (i + hops) % count) for i in range(count)])  124 us
    pallas_call x8, Pallas kernels, convolve(): pl.pallas_call(kernel, grid=(blocks,), out_shape=out, in_specs=[pl.BlockS...  50.7 us
    pallas_call x5, Pallas kernels, mlp(): pl.pallas_call(functools.partial(mlp_kernel, half=edge, kept=len(extra),...  25.9 us
    ppermute x20, starting transfers between devices, rotate(): lax.ppermute(block, axis, [(i, (i + hops) % count) for i in range(count)])  22.4 us
    ppermute x8, starting transfers between devices, step_rows(): return lax.ppermute(block, 'lat', pairs)  21.2 us
    unnamed x60, local copies, waits for them, and re-layouts  13.1 us
  transfers between devices with their start and end apart: 28, of which 10 were waited for; matrix products, arithmetic and copies ran while one was open for 5% of the time, Pallas kernels for 13%

profile of v8, /device:TPU:20, one launch (start us, length us, event | category | flops | bytes accessed | tf_op | source)
XLA Modules:
  0.0 277.0 jit_solution(5784432016888230721)
XLA Ops:
  0.0 1.4 slice.120
  1.6 1.6 collective-permute-start
  3.7 1.6 collective-permute-start.12
  5.9 1.0 fusion.8
  6.9 1.6 collective-permute-start.1
  8.5 1.1 fusion.6
  9.6 1.9 slice_bitcast_fusion.1
  11.5 1.2 copy-done.24
  12.7 2.0 slice_bitcast_fusion
  14.7 0.8 fusion.5
  16.1 3.4 %convolution_bitcast_fusion.refs_3_ = f32[5,448,640]{2,1,0:T(8,128)} fusion(bf16[448,256,1]{1,0,2:T(8,128)(2,1)S(1)} %copy-done.27, bf16[2,5,256,640]{3,2,1,0:T(8,128)(2,1)S(1)} %copy-done.25), kind=kOutput, calls=%fused_computation | convolution fusion | flops 734003200 | bytes 7602176 | tf_op jit(solution)/shard_map/kt,rtc->rkc/dot_general | solution.py:263
  19.5 13.8 %collective-permute-done.refs_5_ = bf16[4,128,640]{2,1,0:T(8,128)(2,1)S(1)} collective-permute-done((bf16[4,128,640]{2,1,0:T(8,128)(2,1)S(1)}, bf16[4,128,640]{2,1,0:T(8,128)(2,1)S(1)}, u32[]{:S(2)}, u32[]{:S(2)}) %collective-permute-start) | collective-permute-done | bytes 655392 | tf_op jit(solution)/shard_map/ppermute | solution.py:219
  33.3 5.5 %collective-permute-done.12.refs_7_ = bf16[4,128,128]{2,1,0:T(8,128)(2,1)S(1)} collective-permute-done((bf16[4,128,128]{2,1,0:T(8,128)(2,1)S(1)}, bf16[4,128,128]{2,1,0:T(8,128)(2,1)S(1)}, u32[]{:S(2)}, u32[]{:S(2)}) %collective-permute-start.12) | collective-permute-done | bytes 131104 | tf_op jit(solution)/shard_map/ppermute | solution.py:219
  38.9 1.6 collective-permute-start.10
  40.5 0.7 copy-done.21
  41.1 0.4 collective-permute-start.11
  41.6 0.8 collective-permute-start.9
  42.4 0.9 pad_maximum_fusion.1
  43.4 0.9 pad_maximum_fusion
  44.3 28.3 %collective-permute-done.10.refs_7_ = bf16[4,128,256]{2,1,0:T(8,128)(2,1)S(1)} collective-permute-done((bf16[4,128,256]{2,1,0:T(8,128)(2,1)S(1)}, bf16[4,128,256]{2,1,0:T(8,128)(2,1)S(1)}, u32[]{:S(2)}, u32[]{:S(2)}) %collective-permute-start.10) | collective-permute-done | bytes 262176 | tf_op jit(solution)/shard_map/ppermute | solution.py:219
  72.6 0.7 copy-done.15
  73.3 1.9 collective-permute-start.6
  75.2 2.9 %collective-permute-done.11.refs_10_ = bf16[4,128,256]{2,1,0:T(8,128)(2,1)S(1)} collective-permute-done((bf16[4,128,256]{2,1,0:T(8,128)(2,1)S(1)}, bf16[4,128,256]{2,1,0:T(8,128)(2,1)S(1)}, u32[]{:S(2)}, u32[]{:S(2)}) %collective-permute-start.11) | collective-permute-done | bytes 262176 | tf_op jit(solution)/shard_map/ppermute | solution.py:219
  78.1 0.7 copy-done.17
  78.8 1.9 collective-permute-start.4
  80.7 1.9 collective-permute-done.9.refs_10_
  82.7 0.7 copy-done.19
  83.4 1.9 collective-permute-start.5
  85.3 0.8 copy-done.9
  86.2 4.5 %collective-permute-start.7 = (bf16[2,256,640]{2,1,0:T(8,128)(2,1)}, bf16[2,256,640]{2,1,0:T(8,128)(2,1)}, u32[]{:S(2)}, u32[]{:S(2)}) collective-permute-start(bf16[2,256,640]{2,1,0:T(8,128)(2,1)} %pad_maximum_fusion.1), channel_id=1, source_target_pairs={{4,0},{8,4},{12,8},{16,12},{20,16},{24,20},{28,24},{5,1},{9,5},{13... | collective-permute-start | bytes 1966088 | tf_op jit(solution)/shard_map/ppermute | solution.py:239
  90.7 7.4 %collective-permute-start.8 = (bf16[4,128,256]{2,1,0:T(8,128)(2,1)}, bf16[4,128,256]{2,1,0:T(8,128)(2,1)S(1)}, u32[]{:S(2)}, u32[]{:S(2)}) collective-permute-start(bf16[4,128,256]{2,1,0:T(8,128)(2,1)} %bitcast.51), channel_id=1, source_target_pairs={{0,1},{1,2},{2,3},{3,0},{4,5},{5,6},{6,7},{7,4},{8,9},{9,10},{10,1... | collective-permute-start | bytes 786440 | tf_op jit(solution)/shard_map/ppermute | solution.py:219
  98.2 2.6 copy-done
  100.8 1.1 copy-done.4
  101.9 1.1 copy-done.6
  103.0 0.9 copy-done.7
  103.9 1.1 copy-done.10
  105.0 0.9 copy-done.22
  105.9 3.5 %zonal_conv.11.refs_2_ = bf16[8,192,128]{2,1,0:T(8,128)(2,1)S(1)} custom-call(f32[16]{0:T(128)S(1)} %and_select_fusion.refs_0_, bf16[448,448]{1,0:T(8,128)(2,1)S(1)} %copy-done.2, bf16[192,448]{1,0:T(8,128)(2,1)S(1)} %copy-done.7, f32[5,448,640]{2,1,0:T(8,128)S(1)} %copy-done, bf16[12,192,640]{2,1,0:T(8,128)(2,1)S(1)} %bitcast.44, ...), custom_call_target="tpu_custom_call" | custom-call | flops 792723456 | bytes 2523136 | tf_op jit(solution)/shard_map/zonal_conv/pallas_call | solution.py:113
  109.5 6.0 %zonal_conv.10.refs_1_ = bf16[8,192,256]{2,1,0:T(8,128)(2,1)S(1)} custom-call(f32[16]{0:T(128)S(1)} %and_select_fusion.refs_0_, bf16[448,448]{1,0:T(8,128)(2,1)S(1)} %copy-done.2, bf16[192,448]{1,0:T(8,128)(2,1)S(1)} %copy-done.7, f32[5,448,640]{2,1,0:T(8,128)S(1)} %copy-done, bf16[12,192,640]{2,1,0:T(8,128)(2,1)S(1)} %bitcast.45, ...), custom_call_target="tpu_custom_call" | custom-call | flops 1585446912 | bytes 5046272 | tf_op jit(solution)/shard_map/zonal_conv/pallas_call | solution.py:113
  115.5 6.0 %zonal_conv.9.refs_0_ = bf16[8,192,256]{2,1,0:T(8,128)(2,1)S(1)} custom-call(f32[16]{0:T(128)S(1)} %and_select_fusion.refs_0_, bf16[448,448]{1,0:T(8,128)(2,1)S(1)} %copy-done.2, bf16[192,448]{1,0:T(8,128)(2,1)S(1)} %copy-done.7, f32[5,448,640]{2,1,0:T(8,128)S(1)} %copy-done, bf16[12,192,640]{2,1,0:T(8,128)(2,1)S(1)} %bitcast.46, ...), custom_call_target="tpu_custom_call" | custom-call | flops 1585446912 | bytes 5046272 | tf_op jit(solution)/shard_map/zonal_conv/pallas_call | solution.py:113
  121.5 11.5 %zonal_conv.8.refs_0_ = bf16[4,192,640]{2,1,0:T(8,128)(2,1)S(1)} custom-call(f32[16]{0:T(128)S(1)} %and_select_fusion.refs_0_, bf16[448,448]{1,0:T(8,128)(2,1)S(1)} %copy-done.2, bf16[192,448]{1,0:T(8,128)(2,1)S(1)} %copy-done.7, f32[5,448,640]{2,1,0:T(8,128)S(1)} %copy-done, bf16[12,192,640]{2,1,0:T(8,128)(2,1)S(1)} %bitcast.47, ...), custom_call_target="tpu_custom_call" | custom-call | flops 3523215360 | bytes 12615680 | tf_op jit(solution)/shard_map/zonal_conv/pallas_call | solution.py:113
  133.0 4.1 %channel_mlp.5 = (bf16[4,192,640]{2,1,0:T(8,128)(2,1)S(1)}, bf16[4,128,640]{2,1,0:T(8,128)(2,1)S(1)}, bf16[4,128,640]{2,1,0:T(8,128)(2,1)S(1)}) custom-call(f32[1,640]{1,0:T(1,128)S(1)} %get-tuple-element.59.gain, bf16[640,1280]{1,0:T(8,128)(2,1)S(1)} %copy-done.13, bf16[1280,640]{1,0:T(8,128)(2,1)S(1)} %copy-done.14, bf16[4,192,640]{2,1,0:T(8,128)(2,1)S(1)} %zonal_conv.8.refs_0_), custom_call_target="tpu_custom_call" | custom-call | flops 2516582400 | bytes 5242880 | tf_op jit(solution)/shard_map/channel_mlp/pallas_call | solution.py:194
  137.3 4.1 %channel_mlp.7 = (bf16[4,192,640]{2,1,0:T(8,128)(2,1)S(1)}, bf16[4,128,256]{2,1,0:T(8,128)(2,1)S(1)}, bf16[4,128,256]{2,1,0:T(8,128)(2,1)S(1)}, bf16[4,128,256]{...) custom-call(f32[1,640]{1,0:T(1,128)S(1)} %get-tuple-element.59.gain,, ...), custom_call_target="tpu_custom_call" | custom-call | flops 2516582400 | bytes 5242880 | tf_op jit(solution)/shard_map/channel_mlp/pallas_call | solution.py:194
  141.5 2.0 collective-permute-start.23
  143.5 2.0 collective-permute-start.17
  145.5 4.0 %channel_mlp.6 = (bf16[4,192,640]{2,1,0:T(8,128)(2,1)S(1)}, bf16[4,128,640]{2,1,0:T(8,128)(2,1)S(1)}, bf16[4,128,640]{2,1,0:T(8,128)(2,1)S(1)}) custom-call(f32[1,640]{1,0:T(1,128)S(1)} %get-tuple-element.59.gain, bf16[640,1280]{1,0:T(8,128)(2,1)S(1)} %copy-done.13, bf16[1280,640]{1,0:T(8,128)(2,1)S(1)} %copy-done.14, ...), custom_call_target="tpu_custom_call" | custom-call | flops 2516582400 | bytes 5242880 | tf_op jit(solution)/shard_map/channel_mlp/pallas_call | solution.py:194
  149.7 22.1 %collective-permute-done.14.refs_7_.refs_6_ = bf16[4,128,640]{2,1,0:T(8,128)(2,1)S(1)} collective-permute-done((bf16[4,128,640]{2,1,0:T(8,128)(2,1)S(1)}, bf16[4,128,640]{2,1,0:T(8,128)(2,1)S(1)}, u32[]{:S(2)}, u32[]{:S(2)}) %collective-permute-start.14) | collective-permute-done | bytes 655392 | tf_op jit(solution)/shard_map/ppermute | solution.py:219
  171.9 2.7 collective-permute-done.22.refs_9_
  174.6 1.1 collective-permute-start.20
  175.8 0.9 collective-permute-start.21
  176.9 39.8 %collective-permute-done.16.refs_9_ = bf16[4,128,256]{2,1,0:T(8,128)(2,1)S(1)} collective-permute-done((bf16[4,128,256]{2,1,0:T(8,128)(2,1)S(1)}, bf16[4,128,256]{2,1,0:T(8,128)(2,1)S(1)}, u32[]{:S(2)}, u32[]{:S(2)}) %collective-permute-start.16) | collective-permute-done | bytes 262176 | tf_op jit(solution)/shard_map/ppermute | solution.py:219
  216.7 6.9 %collective-permute-done.20.refs_9_ = bf16[4,128,256]{2,1,0:T(8,128)(2,1)S(1)} collective-permute-done((bf16[4,128,256]{2,1,0:T(8,128)(2,1)S(1)}, bf16[4,128,256]{2,1,0:T(8,128)(2,1)S(1)}, u32[]{:S(2)}, u32[]{:S(2)}) %collective-permute-start.20) | collective-permute-done | bytes 262176 | tf_op jit(solution)/shard_map/ppermute | solution.py:219
  223.7 1.9 collective-permute-start.26
  225.6 2.5 collective-permute-start.24
  228.2 1.9 collective-permute-start.25
  230.1 4.5 %collective-permute-start.27 = (bf16[2,256,640]{2,1,0:T(8,128)(2,1)S(1)}, bf16[2,256,640]{2,1,0:T(8,128)(2,1)S(1)}, u32[]{:S(2)}, u32[]{:S(2)}) collective-permute-start(bf16[2,256,640]{2,1,0:T(8,128)(2,1)S(1)} %pad_maximum_fusion.3), channel_id=1, source_target_pairs={{4,0},{8,4},{12,8},{16,12},{20,16},{24,20},{28,24},{5,1},{9,5},{13... | collective-permute-start | bytes 1966088 | tf_op jit(solution)/shard_map/ppermute | solution.py:239
  234.7 0.9 convolution_bitcast_fusion.1.refs_3_
  235.6 2.9 %zonal_conv.14.refs_2_ = bf16[8,192,128]{2,1,0:T(8,128)(2,1)S(1)} custom-call(f32[16]{0:T(128)S(1)} %and_select_fusion.refs_0_, bf16[448,448]{1,0:T(8,128)(2,1)S(1)} %copy-done.2, bf16[192,448]{1,0:T(8,128)(2,1)S(1)} %copy-done.8, f32[5,448,640]{2,1,0:T(8,128)S(1)} %convolution_bitcast_fusion.1.refs_3_, bf16[4,192,640]{2,1,0:T(8,128)(2,1)S(1)} %get-tuple-element.20.refs_4_, ...), custom_call_target="tpu_custom_call" | custom-call | flops 792723456 | bytes 2523136 | tf_op jit(solution)/shard_map/zonal_conv/pallas_call | solution.py:113
  238.5 5.4 %zonal_conv.13.refs_1_ = bf16[8,192,256]{2,1,0:T(8,128)(2,1)S(1)} custom-call(f32[16]{0:T(128)S(1)} %and_select_fusion.refs_0_, bf16[448,448]{1,0:T(8,128)(2,1)S(1)} %copy-done.2, bf16[192,448]{1,0:T(8,128)(2,1)S(1)} %copy-done.8, f32[5,448,640]{2,1,0:T(8,128)S(1)} %convolution_bitcast_fusion.1.refs_3_, bf16[4,192,640]{2,1,0:T(8,128)(2,1)S(1)} %get-tuple-element.20.refs_4_, ...), custom_call_target="tpu_custom_call" | custom-call | flops 1585446912 | bytes 5046272 | tf_op jit(solution)/shard_map/zonal_conv/pallas_call | solution.py:113
  243.9 5.4 %zonal_conv.12.refs_0_ = bf16[8,192,256]{2,1,0:T(8,128)(2,1)S(1)} custom-call(f32[16]{0:T(128)S(1)} %and_select_fusion.refs_0_, bf16[448,448]{1,0:T(8,128)(2,1)S(1)} %copy-done.2, bf16[192,448]{1,0:T(8,128)(2,1)S(1)} %copy-done.8, f32[5,448,640]{2,1,0:T(8,128)S(1)} %convolution_bitcast_fusion.1.refs_3_, bf16[4,192,640]{2,1,0:T(8,128)(2,1)S(1)} %get-tuple-element.20.refs_4_, ...), custom_call_target="tpu_custom_call" | custom-call | flops 1585446912 | bytes 5046272 | tf_op jit(solution)/shard_map/zonal_conv/pallas_call | solution.py:113
  249.4 3.9 %collective-permute-done.25.refs_11_ = bf16[2,256,640]{2,1,0:T(8,128)(2,1)S(1)} collective-permute-done((bf16[2,256,640]{2,1,0:T(8,128)(2,1)S(1)}, bf16[2,256,640]{2,1,0:T(8,128)(2,1)S(1)}, u32[]{:S(2)}, u32[]{:S(2)}) %collective-permute-start.25) | collective-permute-done | bytes 655392 | tf_op jit(solution)/shard_map/ppermute | solution.py:239
  253.3 10.0 %zonal_conv.15.refs_0_ = bf16[4,192,640]{2,1,0:T(8,128)(2,1)S(1)} custom-call(f32[16]{0:T(128)S(1)} %and_select_fusion.refs_0_, bf16[448,448]{1,0:T(8,128)(2,1)S(1)} %copy-done.2, bf16[192,448]{1,0:T(8,128)(2,1)S(1)} %copy-done.8, f32[5,448,640]{2,1,0:T(8,128)S(1)} %convolution_bitcast_fusion.1.refs_3_, bf16[4,192,640]{2,1,0:T(8,128)(2,1)S(1)} %get-tuple-element.20.refs_4_, ...), custom_call_target="tpu_custom_call" | custom-call | flops 3523215360 | bytes 12615680 | tf_op jit(solution)/shard_map/zonal_conv/pallas_call | solution.py:113
  263.3 4.9 %channel_mlp.8.refs_3_ = bf16[12,192,640]{2,1,0:T(8,128)(2,1)} custom-call(f32[1,640]{1,0:T(1,128)S(1)} %get-tuple-element.60.gain, bf16[640,1280]{1,0:T(8,128)(2,1)S(1)} %copy-done.11, bf16[1280,640]{1,0:T(8,128)(2,1)S(1)} %copy-done.12, bf16[4,192,640]{2,1,0:T(8,128)(2,1)S(1)} %zonal_conv.15.refs_0_), custom_call_target="tpu_custom_call" | custom-call | flops 2516582400 | bytes 5242880 | tf_op jit(solution)/shard_map/channel_mlp/pallas_call | solution.py:194
  268.2 8.9 %channel_mlp.9 = bf16[12,192,640]{2,1,0:T(8,128)(2,1)} custom-call(f32[1,640]{1,0:T(1,128)S(1)} %get-tuple-element.60.gain, bf16[640,1280]{1,0:T(8,128)(2,1)S(1)} %copy-done.11, bf16[1280,640]{1,0:T(8,128)(2,1)S(1)} %copy-done.12, bf16[8,192,256]{2,1,0:T(8,128)(2,1)S(1)} %zonal_conv.12.refs_0_, ...), custom_call_target="tpu_custom_call", output_to_operand_aliasing={{}: (6, {})} | custom-call | flops 5033164800 | bytes 7208960 | tf_op jit(solution)/shard_map/channel_mlp/pallas_call | solution.py:194
  (87 shorter events, 2.8 us)
Async XLA Ops:
  0.0 3.7 %copy-start.1 = (bf16[1,12,640,192]{2,3,1,0:T(8,128)(2,1)S(1)}, bf16[1,12,640,192]{2,3,1,0:T(8,128)(2,1)}, u32[]{:S(2)}) copy-start(bf16[1,12,640,192]{2,3,1,0:T(8,128)(2,1)} %param.8) | copy-start | bytes 8847364
  1.6 31.7 %collective-permute-start = (bf16[4,128,640]{2,1,0:T(8,128)(2,1)S(1)}, bf16[4,128,640]{2,1,0:T(8,128)(2,1)S(1)}, u32[]{:S(2)}, u32[]{:S(2)}) collective-permute-start(bf16[4,128,640]{2,1,0:T(8,128)(2,1)S(1)} %bitcast.50), channel_id=1, source_target_pairs={{0,1},{1,2},{2,3},{3,0},{4,5},{5,6},{6,7},{7,4},{8,9},{9,10},{10,1... | collective-permute-start | bytes 1966088 | tf_op jit(solution)/shard_map/ppermute | solution.py:219
  3.2 38.4 %collective-permute-start.2 = (bf16[4,128,640]{2,1,0:T(8,128)(2,1)S(1)}, bf16[4,128,640]{2,1,0:T(8,128)(2,1)S(1)}, u32[]{:S(2)}, u32[]{:S(2)}) collective-permute-start(bf16[4,128,640]{2,1,0:T(8,128)(2,1)S(1)} %bitcast.49), channel_id=1, source_target_pairs={{0,3},{1,0},{2,1},{3,2},{4,7},{5,4},{6,5},{7,6},{8,11},{9,8},{10,9... | collective-permute-start | bytes 1966088 | tf_op jit(solution)/shard_map/ppermute | solution.py:219
  3.7 35.2 %collective-permute-start.12 = (bf16[4,128,128]{2,1,0:T(8,128)(2,1)S(1)}, bf16[4,128,128]{2,1,0:T(8,128)(2,1)S(1)}, u32[]{:S(2)}, u32[]{:S(2)}) collective-permute-start(bf16[4,128,128]{2,1,0:T(8,128)(2,1)S(1)} %bitcast.56), channel_id=1, source_target_pairs={{0,1},{1,2},{2,3},{3,0},{4,5},{5,6},{6,7},{7,4},{8,9},{9,10},{10,1... | collective-permute-start | bytes 393224 | tf_op jit(solution)/shard_map/ppermute | solution.py:219
  5.3 35.1 %collective-permute-start.13 = (bf16[4,128,128]{2,1,0:T(8,128)(2,1)S(1)}, bf16[4,128,128]{2,1,0:T(8,128)(2,1)S(1)}, u32[]{:S(2)}, u32[]{:S(2)}) collective-permute-start(bf16[4,128,128]{2,1,0:T(8,128)(2,1)S(1)} %bitcast.55), channel_id=1, source_target_pairs={{0,3},{1,0},{2,1},{3,2},{4,7},{5,4},{6,5},{7,6},{8,11},{9,8},{10,9... | collective-permute-start | bytes 393224 | tf_op jit(solution)/shard_map/ppermute | solution.py:219
  5.9 3.7 %copy-start.23 = (bf16[2,640,1280]{2,1,0:T(8,128)(2,1)S(1)}, bf16[2,640,1280]{2,1,0:T(8,128)(2,1)}, u32[]{:S(2)}) copy-start(bf16[2,640,1280]{2,1,0:T(8,128)(2,1)} %param.11) | copy-start | bytes 9830404
  6.9 78.4 %collective-permute-start.1 = (bf16[4,128,640]{2,1,0:T(8,128)(2,1)S(1)}, bf16[4,128,640]{2,1,0:T(8,128)(2,1)S(1)}, u32[]{:S(2)}, u32[]{:S(2)}) collective-permute-start(bf16[4,128,640]{2,1,0:T(8,128)(2,1)S(1)} %bitcast.48), channel_id=1, source_target_pairs={{0,1},{1,2},{2,3},{3,0},{4,5},{5,6},{6,7},{7,4},{8,9},{9,10},{10,1... | collective-permute-start | bytes 1966088 | tf_op jit(solution)/shard_map/ppermute | solution.py:219
  9.6 3.1 %copy-start.24 = (bf16[2,1280,640]{2,1,0:T(8,128)(2,1)S(1)}, bf16[2,1280,640]{2,1,0:T(8,128)(2,1)}, u32[]{:S(2)}) copy-start(bf16[2,1280,640]{2,1,0:T(8,128)(2,1)} %param.12) | copy-start | bytes 9830404
  12.7 3.2 %copy-start.25 = (bf16[2,5,256,640]{3,2,1,0:T(8,128)(2,1)S(1)}, bf16[2,5,256,640]{3,2,1,0:T(8,128)(2,1)}, u32[]{:S(2)}) copy-start(bf16[2,5,256,640]{3,2,1,0:T(8,128)(2,1)} %param.9) | copy-start | bytes 9830404
  14.7 1.4 copy-start.27
  33.3 10.1 %copy-start.3 = (bf16[4,128,640]{2,1,0:T(8,128)(2,1)}, bf16[4,128,640]{2,1,0:T(8,128)(2,1)S(1)}, u32[]{:S(2)}) copy-start(bf16[4,128,640]{2,1,0:T(8,128)(2,1)S(1)} %collective-permute-done.refs_5_) | copy-start | bytes 1966084
  33.3 57.5 %collective-permute-start.3 = (bf16[4,128,640]{2,1,0:T(8,128)(2,1)}, bf16[4,128,640]{2,1,0:T(8,128)(2,1)}, u32[]{:S(2)}, u32[]{:S(2)}) collective-permute-start(bf16[4,128,640]{2,1,0:T(8,128)(2,1)} %bitcast.17), channel_id=1, source_target_pairs={{0,3},{1,0},{2,1},{3,2},{4,7},{5,4},{6,5},{7,6},{8,11},{9,8},{10,9... | collective-permute-start | bytes 1966088 | tf_op jit(solution)/shard_map/ppermute | solution.py:219
  38.9 33.7 %collective-permute-start.10 = (bf16[4,128,256]{2,1,0:T(8,128)(2,1)S(1)}, bf16[4,128,256]{2,1,0:T(8,128)(2,1)S(1)}, u32[]{:S(2)}, u32[]{:S(2)}) collective-permute-start(bf16[4,128,256]{2,1,0:T(8,128)(2,1)S(1)} %bitcast.54), channel_id=1, source_target_pairs={{0,1},{1,2},{2,3},{3,0},{4,5},{5,6},{6,7},{7,4},{8,9},{9,10},{10,1... | collective-permute-start | bytes 786440 | tf_op jit(solution)/shard_map/ppermute | solution.py:219
  40.5 0.7 copy-start.21
  41.1 37.0 %collective-permute-start.11 = (bf16[4,128,256]{2,1,0:T(8,128)(2,1)S(1)}, bf16[4,128,256]{2,1,0:T(8,128)(2,1)S(1)}, u32[]{:S(2)}, u32[]{:S(2)}) collective-permute-start(bf16[4,128,256]{2,1,0:T(8,128)(2,1)S(1)} %bitcast.53), channel_id=1, source_target_pairs={{0,3},{1,0},{2,1},{3,2},{4,7},{5,4},{6,5},{7,6},{8,11},{9,8},{10,9... | collective-permute-start | bytes 786440 | tf_op jit(solution)/shard_map/ppermute | solution.py:219
  41.6 2.7 copy-start.5
  41.6 41.1 %collective-permute-start.9 = (bf16[4,128,256]{2,1,0:T(8,128)(2,1)S(1)}, bf16[4,128,256]{2,1,0:T(8,128)(2,1)S(1)}, u32[]{:S(2)}, u32[]{:S(2)}) collective-permute-start(bf16[4,128,256]{2,1,0:T(8,128)(2,1)S(1)} %bitcast.52), channel_id=1, source_target_pairs={{0,3},{1,0},{2,1},{3,2},{4,7},{5,4},{6,5},{7,6},{8,11},{9,8},{10,9... | collective-permute-start | bytes 786440 | tf_op jit(solution)/shard_map/ppermute | solution.py:219
  42.4 48.3 %copy-start.29 = (bf16[2,640]{1,0:T(2,128)(2,1)S(1)}, bf16[2,640]{1,0:T(2,128)(2,1)}, u32[]{:S(2)}) copy-start(bf16[2,640]{1,0:T(2,128)(2,1)} %param.10) | copy-start | bytes 7684
  42.4 55.7 %copy-start.2 = (bf16[448,448]{1,0:T(8,128)(2,1)S(1)}, bf16[448,448]{1,0:T(8,128)(2,1)}, u32[]{:S(2)}) copy-start(bf16[448,448]{1,0:T(8,128)(2,1)} %constant.30.clone.refs_1_) | copy-start | bytes 1204228
  72.6 0.7 copy-start.15
  73.3 48.2 %collective-permute-start.6 = (bf16[2,192,640]{2,1,0:T(8,128)(2,1)}, bf16[2,192,640]{2,1,0:T(8,128)(2,1)}, u32[]{:S(2)}, u32[]{:S(2)}) collective-permute-start(bf16[2,192,640]{2,1,0:T(8,128)(2,1)} %get-tuple-element.43), channel_id=1, source_target_pairs={{4,0},{8,4},{12,8},{16,12},{20,16},{24,20},{28,24},{5,1},{9,5},{13... | collective-permute-start | bytes 1474568 | tf_op jit(solution)/shard_map/ppermute | solution.py:239
  78.1 0.7 copy-start.17
  78.8 42.7 %collective-permute-start.4 = (bf16[2,192,640]{2,1,0:T(8,128)(2,1)}, bf16[2,192,640]{2,1,0:T(8,128)(2,1)}, u32[]{:S(2)}, u32[]{:S(2)}) collective-permute-start(bf16[2,192,640]{2,1,0:T(8,128)(2,1)} %get-tuple-element.44), channel_id=1, source_target_pairs={{0,4},{4,8},{8,12},{12,16},{16,20},{20,24},{24,28},{1,5},{5,9},{9,... | collective-permute-start | bytes 1474568 | tf_op jit(solution)/shard_map/ppermute | solution.py:239
  82.7 0.7 copy-start.19
  83.4 38.1 %collective-permute-start.5 = (bf16[2,256,640]{2,1,0:T(8,128)(2,1)}, bf16[2,256,640]{2,1,0:T(8,128)(2,1)}, u32[]{:S(2)}, u32[]{:S(2)}) collective-permute-start(bf16[2,256,640]{2,1,0:T(8,128)(2,1)} %pad_maximum_fusion), channel_id=1, source_target_pairs={{0,4},{4,8},{8,12},{12,16},{16,20},{20,24},{24,28},{1,5},{5,9},{9,... | collective-permute-start | bytes 1966088 | tf_op jit(solution)/shard_map/ppermute | solution.py:239
  85.3 0.8 copy-start.9
  86.2 35.4 %collective-permute-start.7 = (bf16[2,256,640]{2,1,0:T(8,128)(2,1)}, bf16[2,256,640]{2,1,0:T(8,128)(2,1)}, u32[]{:S(2)}, u32[]{:S(2)}) collective-permute-start(bf16[2,256,640]{2,1,0:T(8,128)(2,1)} %pad_maximum_fusion.1), channel_id=1, source_target_pairs={{4,0},{8,4},{12,8},{16,12},{20,16},{24,20},{28,24},{5,1},{9,5},{13... | collective-permute-start | bytes 1966088 | tf_op jit(solution)/shard_map/ppermute | solution.py:239
  90.7 24.7 %collective-permute-start.8 = (bf16[4,128,256]{2,1,0:T(8,128)(2,1)}, bf16[4,128,256]{2,1,0:T(8,128)(2,1)S(1)}, u32[]{:S(2)}, u32[]{:S(2)}) collective-permute-start(bf16[4,128,256]{2,1,0:T(8,128)(2,1)} %bitcast.51), channel_id=1, source_target_pairs={{0,1},{1,2},{2,3},{3,0},{4,5},{5,6},{6,7},{7,4},{8,9},{9,10},{10,1... | collective-permute-start | bytes 786440 | tf_op jit(solution)/shard_map/ppermute | solution.py:219
  98.2 2.6 copy-start
  100.8 1.1 copy-start.4
  101.9 1.1 copy-start.6
  103.0 0.9 copy-start.7
  103.9 1.1 copy-start.10
  105.0 0.9 copy-start.22
  105.9 3.6 %copy-start.16 = (bf16[4,128,256]{2,1,0:T(8,128)(2,1)S(1)}, bf16[4,128,256]{2,1,0:T(8,128)(2,1)}, u32[]{:S(2)}) copy-start(bf16[4,128,256]{2,1,0:T(8,128)(2,1)} %copy-done.15) | copy-start | bytes 786436
  105.9 3.6 %copy-start.18 = (bf16[4,128,256]{2,1,0:T(8,128)(2,1)S(1)}, bf16[4,128,256]{2,1,0:T(8,128)(2,1)}, u32[]{:S(2)}) copy-start(bf16[4,128,256]{2,1,0:T(8,128)(2,1)} %copy-done.17) | copy-start | bytes 786436
  109.5 6.0 %copy-start.20 = (bf16[4,128,256]{2,1,0:T(8,128)(2,1)S(1)}, bf16[4,128,256]{2,1,0:T(8,128)(2,1)}, u32[]{:S(2)}) copy-start(bf16[4,128,256]{2,1,0:T(8,128)(2,1)} %copy-done.19) | copy-start | bytes 786436
  121.5 11.6 %copy-start.13 = (bf16[640,1280]{1,0:T(8,128)(2,1)S(1)}, bf16[640,1280]{1,0:T(8,128)(2,1)}, u32[]{:S(2)}) copy-start(bf16[640,1280]{1,0:T(8,128)(2,1)} %get-tuple-element.35.w_in) | copy-start | bytes 4915204
  121.5 11.6 %copy-start.14 = (bf16[1280,640]{1,0:T(8,128)(2,1)S(1)}, bf16[1280,640]{1,0:T(8,128)(2,1)}, u32[]{:S(2)}) copy-start(bf16[1280,640]{1,0:T(8,128)(2,1)} %get-tuple-element.33.w_out) | copy-start | bytes 4915204
  137.1 34.7 %collective-permute-start.14 = (bf16[4,128,640]{2,1,0:T(8,128)(2,1)S(1)}, bf16[4,128,640]{2,1,0:T(8,128)(2,1)S(1)}, u32[]{:S(2)}, u32[]{:S(2)}) collective-permute-start(bf16[4,128,640]{2,1,0:T(8,128)(2,1)S(1)} %get-tuple-element.23), channel_id=1, source_target_pairs={{0,1},{1,2},{2,3},{3,0},{4,5},{5,6},{6,7},{7,4},{8,9},{9,10},{10,1... | collective-permute-start | bytes 1966088 | tf_op jit(solution)/shard_map/ppermute | solution.py:219
  141.4 33.2 %collective-permute-start.22 = (bf16[4,128,128]{2,1,0:T(8,128)(2,1)S(1)}, bf16[4,128,128]{2,1,0:T(8,128)(2,1)S(1)}, u32[]{:S(2)}, u32[]{:S(2)}) collective-permute-start(bf16[4,128,128]{2,1,0:T(8,128)(2,1)S(1)} %get-tuple-element.31), channel_id=1, source_target_pairs={{0,1},{1,2},{2,3},{3,0},{4,5},{5,6},{6,7},{7,4},{8,9},{9,10},{10,1... | collective-permute-start | bytes 393224 | tf_op jit(solution)/shard_map/ppermute | solution.py:219
  141.5 33.1 %collective-permute-start.23 = (bf16[4,128,128]{2,1,0:T(8,128)(2,1)S(1)}, bf16[4,128,128]{2,1,0:T(8,128)(2,1)S(1)}, u32[]{:S(2)}, u32[]{:S(2)}) collective-permute-start(bf16[4,128,128]{2,1,0:T(8,128)(2,1)S(1)} %get-tuple-element.32), channel_id=1, source_target_pairs={{0,3},{1,0},{2,1},{3,2},{4,7},{5,4},{6,5},{7,6},{8,11},{9,8},{10,9... | collective-permute-start | bytes 393224 | tf_op jit(solution)/shard_map/ppermute | solution.py:219
  143.5 32.2 %collective-permute-start.17 = (bf16[4,128,640]{2,1,0:T(8,128)(2,1)S(1)}, bf16[4,128,640]{2,1,0:T(8,128)(2,1)S(1)}, u32[]{:S(2)}, u32[]{:S(2)}) collective-permute-start(bf16[4,128,640]{2,1,0:T(8,128)(2,1)S(1)} %get-tuple-element.26), channel_id=1, source_target_pairs={{0,3},{1,0},{2,1},{3,2},{4,7},{5,4},{6,5},{7,6},{8,11},{9,8},{10,9... | collective-permute-start | bytes 1966088 | tf_op jit(solution)/shard_map/ppermute | solution.py:219
  149.5 78.6 %collective-permute-start.15 = (bf16[4,128,640]{2,1,0:T(8,128)(2,1)S(1)}, bf16[4,128,640]{2,1,0:T(8,128)(2,1)S(1)}, u32[]{:S(2)}, u32[]{:S(2)}) collective-permute-start(bf16[4,128,640]{2,1,0:T(8,128)(2,1)S(1)} %get-tuple-element.24), channel_id=1, source_target_pairs={{0,1},{1,2},{2,3},{3,0},{4,5},{5,6},{6,7},{7,4},{8,9},{9,10},{10,1... | collective-permute-start | bytes 1966088 | tf_op jit(solution)/shard_map/ppermute | solution.py:219
  171.8 58.3 %collective-permute-start.18 = (bf16[4,128,640]{2,1,0:T(8,128)(2,1)S(1)}, bf16[4,128,640]{2,1,0:T(8,128)(2,1)S(1)}, u32[]{:S(2)}, u32[]{:S(2)}) collective-permute-start(bf16[4,128,640]{2,1,0:T(8,128)(2,1)S(1)} %get-tuple-element.27), channel_id=1, source_target_pairs={{0,3},{1,0},{2,1},{3,2},{4,7},{5,4},{6,5},{7,6},{8,11},{9,8},{10,9... | collective-permute-start | bytes 1966088 | tf_op jit(solution)/shard_map/ppermute | solution.py:219
  174.6 42.1 %collective-permute-start.16 = (bf16[4,128,256]{2,1,0:T(8,128)(2,1)S(1)}, bf16[4,128,256]{2,1,0:T(8,128)(2,1)S(1)}, u32[]{:S(2)}, u32[]{:S(2)}) collective-permute-start(bf16[4,128,256]{2,1,0:T(8,128)(2,1)S(1)} %get-tuple-element.25), channel_id=1, source_target_pairs={{0,1},{1,2},{2,3},{3,0},{4,5},{5,6},{6,7},{7,4},{8,9},{9,10},{10,1... | collective-permute-start | bytes 786440 | tf_op jit(solution)/shard_map/ppermute | solution.py:219
  174.6 49.1 %collective-permute-start.20 = (bf16[4,128,256]{2,1,0:T(8,128)(2,1)S(1)}, bf16[4,128,256]{2,1,0:T(8,128)(2,1)S(1)}, u32[]{:S(2)}, u32[]{:S(2)}) collective-permute-start(bf16[4,128,256]{2,1,0:T(8,128)(2,1)S(1)} %get-tuple-element.29), channel_id=1, source_target_pairs={{0,1},{1,2},{2,3},{3,0},{4,5},{5,6},{6,7},{7,4},{8,9},{9,10},{10,1... | collective-permute-start | bytes 786440 | tf_op jit(solution)/shard_map/ppermute | solution.py:219
  175.8 49.8 %collective-permute-start.21 = (bf16[4,128,256]{2,1,0:T(8,128)(2,1)S(1)}, bf16[4,128,256]{2,1,0:T(8,128)(2,1)S(1)}, u32[]{:S(2)}, u32[]{:S(2)}) collective-permute-start(bf16[4,128,256]{2,1,0:T(8,128)(2,1)S(1)} %get-tuple-element.30), channel_id=1, source_target_pairs={{0,3},{1,0},{2,1},{3,2},{4,7},{5,4},{6,5},{7,6},{8,11},{9,8},{10,9... | collective-permute-start | bytes 786440 | tf_op jit(solution)/shard_map/ppermute | solution.py:219
  176.7 58.0 %copy-start.26 = (bf16[2,5,256,640]{3,2,1,0:T(8,128)(2,1)S(1)}, bf16[2,5,256,640]{3,2,1,0:T(8,128)(2,1)}, u32[]{:S(2)}) copy-start(bf16[2,5,256,640]{3,2,1,0:T(8,128)(2,1)} %param.9) | copy-start | bytes 9830404
  176.8 57.9 %copy-start.28 = (bf16[448,256,1]{1,0,2:T(8,128)(2,1)S(1)}, bf16[448,256,1]{1,0,2:T(8,128)(2,1)}, u32[]{:S(2)}) copy-start(bf16[448,256,1]{1,0,2:T(8,128)(2,1)} %constant.34) | copy-start | bytes 688132
  216.7 27.2 %collective-permute-start.19 = (bf16[4,128,256]{2,1,0:T(8,128)(2,1)S(1)}, bf16[4,128,256]{2,1,0:T(8,128)(2,1)S(1)}, u32[]{:S(2)}, u32[]{:S(2)}) collective-permute-start(bf16[4,128,256]{2,1,0:T(8,128)(2,1)S(1)} %get-tuple-element.28), channel_id=1, source_target_pairs={{0,3},{1,0},{2,1},{3,2},{4,7},{5,4},{6,5},{7,6},{8,11},{9,8},{10,9... | collective-permute-start | bytes 786440 | tf_op jit(solution)/shard_map/ppermute | solution.py:219
  223.7 25.7 %collective-permute-start.26 = (bf16[2,192,640]{2,1,0:T(8,128)(2,1)S(1)}, bf16[2,192,640]{2,1,0:T(8,128)(2,1)S(1)}, u32[]{:S(2)}, u32[]{:S(2)}) collective-permute-start(bf16[2,192,640]{2,1,0:T(8,128)(2,1)S(1)} %get-tuple-element.45), channel_id=1, source_target_pairs={{4,0},{8,4},{12,8},{16,12},{20,16},{24,20},{28,24},{5,1},{9,5},{13... | collective-permute-start | bytes 1474568 | tf_op jit(solution)/shard_map/ppermute | solution.py:239
  225.6 10.0 %copy-start.8 = (bf16[192,448]{1,0:T(8,128)(2,1)S(1)}, bf16[192,448]{1,0:T(8,128)(2,1)}, u32[]{:S(2)}) copy-start(bf16[192,448]{1,0:T(8,128)(2,1)} %constant.31.clone.refs_2_) | copy-start | bytes 516100
  225.6 23.8 %collective-permute-start.24 = (bf16[2,192,640]{2,1,0:T(8,128)(2,1)S(1)}, bf16[2,192,640]{2,1,0:T(8,128)(2,1)S(1)}, u32[]{:S(2)}, u32[]{:S(2)}) collective-permute-start(bf16[2,192,640]{2,1,0:T(8,128)(2,1)S(1)} %get-tuple-element.46), channel_id=1, source_target_pairs={{0,4},{4,8},{8,12},{12,16},{16,20},{20,24},{24,28},{1,5},{5,9},{9,... | collective-permute-start | bytes 1474568 | tf_op jit(solution)/shard_map/ppermute | solution.py:239
  228.2 25.1 %collective-permute-start.25 = (bf16[2,256,640]{2,1,0:T(8,128)(2,1)S(1)}, bf16[2,256,640]{2,1,0:T(8,128)(2,1)S(1)}, u32[]{:S(2)}, u32[]{:S(2)}) collective-permute-start(bf16[2,256,640]{2,1,0:T(8,128)(2,1)S(1)} %pad_maximum_fusion.2), channel_id=1, source_target_pairs={{0,4},{4,8},{8,12},{12,16},{16,20},{20,24},{24,28},{1,5},{5,9},{9,... | collective-permute-start | bytes 1966088 | tf_op jit(solution)/shard_map/ppermute | solution.py:239
  230.1 23.2 %collective-permute-start.27 = (bf16[2,256,640]{2,1,0:T(8,128)(2,1)S(1)}, bf16[2,256,640]{2,1,0:T(8,128)(2,1)S(1)}, u32[]{:S(2)}, u32[]{:S(2)}) collective-permute-start(bf16[2,256,640]{2,1,0:T(8,128)(2,1)S(1)} %pad_maximum_fusion.3), channel_id=1, source_target_pairs={{4,0},{8,4},{12,8},{16,12},{20,16},{24,20},{28,24},{5,1},{9,5},{13... | collective-permute-start | bytes 1966088 | tf_op jit(solution)/shard_map/ppermute | solution.py:239
  249.4 13.9 %copy-start.11 = (bf16[640,1280]{1,0:T(8,128)(2,1)S(1)}, bf16[640,1280]{1,0:T(8,128)(2,1)}, u32[]{:S(2)}) copy-start(bf16[640,1280]{1,0:T(8,128)(2,1)} %get-tuple-element.36.w_in) | copy-start | bytes 4915204
  249.4 13.9 %copy-start.12 = (bf16[1280,640]{1,0:T(8,128)(2,1)S(1)}, bf16[1280,640]{1,0:T(8,128)(2,1)}, u32[]{:S(2)}) copy-start(bf16[1280,640]{1,0:T(8,128)(2,1)} %get-tuple-element.34.w_out) | copy-start | bytes 4915204

commit v9 on v8

--- a/solution.py
+++ b/solution.py
@@ -277,8 +277,10 @@
 
     def pick(pairs, members, lon, cut):
         first, last = members[0] // rim, members[-1] // rim
-        chosen = pairs[first : last + 1 : max(1, (last - first) // (len(members) // rim - 1))]
-        return chosen[:, :, lon, cut].reshape(len(members), -1, chosen[..., cut].shape[-1])
+        stride = max(1, (last - first) // (len(members) // rim - 1))
+        low, high = (first, 0, lon.start, cut.start), (last + 1, rim, lon.stop, cut.stop)
+        chosen = lax.slice(pairs, low, high, (stride, 1, 1, 1))
+        return chosen.reshape(len(members), *chosen.shape[2:])
 
     parts = lane_parts(channels)
     pieces = [slice(start * LANES, (start + count) * LANES) for start, count in parts]
@@ -286,9 +288,10 @@
     lanes = [slice(0, channels)] * 2 + pieces
     groups_of = [groups[0], groups[1]] + [groups[2]] * len(parts)
     head, tail = slice(0, edge), slice(width - edge, width)
+    lasts = [pick(pairs, groups[0], tail, lanes[0])]
+    pairs, _ = lax.optimization_barrier((pairs, lasts[0]))
     firsts = [pick(pairs, groups[0], head, lanes[0])]
-    lasts = [pick(pairs, groups[0], tail, lanes[0])]
-    pairs, _, _ = lax.optimization_barrier((pairs, firsts[0], lasts[0]))
+    pairs, _ = lax.optimization_barrier((pairs, firsts[0]))
     firsts += [pick(pairs, members, head, cut) for members, cut in zip(groups_of[1:], lanes[1:])]
     lasts += [pick(pairs, members, tail, cut) for members, cut in zip(groups_of[1:], lanes[1:])]
     tables = (forward, inverse)

time: 278 us -> 267 us (0.960)
  waiting for transfers between devices: 128 us -> 115 us
    ppermute x20, waiting for transfers between devices: 124 us -> 112 us  [rotate(): lax.ppermute(block, axis, [(i, (i + hops) % count) for i in range(count)])]
  transfers between devices with their start and end apart: 28 -> 28, of which waited for: 10 -> 10; matrix products, arithmetic and copies ran while one was open for 5% -> 6% of each run, Pallas kernels for 13% -> 14%
where the time goes in v9:
time: 267 us; the launch traced here: 266 us
  waiting for transfers between devices  115 us (43%)
  Pallas kernels  76.3 us (29%)
  starting transfers between devices  44 us (16%)
  local copies, waits for them, and re-layouts  23.7 us (9%)
  matrix products  4.35 us (2%)
    ppermute x20, waiting for transfers between devices, rotate(): lax.ppermute(block, axis, [(i, (i + hops) % count) for i in range(count)])  112 us
    pallas_call x8, Pallas kernels, convolve(): pl.pallas_call(kernel, grid=(blocks,), out_shape=out, in_specs=[pl.BlockS...  50.5 us
    pallas_call x5, Pallas kernels, mlp(): pl.pallas_call(functools.partial(mlp_kernel, half=edge, kept=len(extra),...  25.8 us
    ppermute x20, starting transfers between devices, rotate(): lax.ppermute(block, axis, [(i, (i + hops) % count) for i in range(count)])  22.8 us
    ppermute x8, starting transfers between devices, step_rows(): return lax.ppermute(block, 'lat', pairs)  21.2 us
    unnamed x60, local copies, waits for them, and re-layouts  13 us
  transfers between devices with their start and end apart: 28, of which 10 were waited for; matrix products, arithmetic and copies ran while one was open for 6% of the time, Pallas kernels for 14%

profile of v9, /device:TPU:20, one launch (start us, length us, event | category | flops | bytes accessed | tf_op | source)
XLA Modules:
  0.0 266.3 jit_solution(10757858745784924478)
XLA Ops:
  0.0 1.3 slice.100
  1.3 1.6 collective-permute-start
  2.9 1.1 slice.101
  4.6 1.0 fusion.4
  5.6 1.6 collective-permute-start.12
  7.7 0.8 fusion.5
  8.5 1.6 collective-permute-start.10
  10.1 1.0 fusion.7
  11.1 1.9 slice_bitcast_fusion.1
  13.1 1.2 copy-done.24
  14.2 2.0 slice_bitcast_fusion
  16.2 1.1 fusion.6
  17.8 3.4 %convolution_bitcast_fusion.refs_3_ = f32[5,448,640]{2,1,0:T(8,128)} fusion(bf16[448,256,1]{1,0,2:T(8,128)(2,1)S(1)} %copy-done.27, bf16[2,5,256,640]{3,2,1,0:T(8,128)(2,1)S(1)} %copy-done.25), kind=kOutput, calls=%fused_computation | convolution fusion | flops 734003200 | bytes 7602176 | tf_op jit(solution)/shard_map/kt,rtc->rkc/dot_general | solution.py:263
  21.2 11.6 %collective-permute-done.2.refs_7_.refs_8_ = bf16[4,128,640]{2,1,0:T(8,128)(2,1)S(1)} collective-permute-done((bf16[4,128,640]{2,1,0:T(8,128)(2,1)S(1)}, bf16[4,128,640]{2,1,0:T(8,128)(2,1)S(1)}, u32[]{:S(2)}, u32[]{:S(2)}) %collective-permute-start.2) | collective-permute-done | bytes 655392 | tf_op jit(solution)/shard_map/ppermute | solution.py:219
  32.8 1.6 collective-permute-start.1
  34.5 4.2 %collective-permute-done.12.refs_7_ = bf16[4,128,128]{2,1,0:T(8,128)(2,1)S(1)} collective-permute-done((bf16[4,128,128]{2,1,0:T(8,128)(2,1)S(1)}, bf16[4,128,128]{2,1,0:T(8,128)(2,1)S(1)}, u32[]{:S(2)}, u32[]{:S(2)}) %collective-permute-start.12) | collective-permute-done | bytes 131104 | tf_op jit(solution)/shard_map/ppermute | solution.py:219
  39.3 1.3 collective-permute-start.9
  40.6 3.2 %collective-permute-start.3 = (bf16[4,128,640]{2,1,0:T(8,128)(2,1)}, bf16[4,128,640]{2,1,0:T(8,128)(2,1)}, u32[]{:S(2)}, u32[]{:S(2)}) collective-permute-start(bf16[4,128,640]{2,1,0:T(8,128)(2,1)} %bitcast.17), channel_id=1, source_target_pairs={{0,3},{1,0},{2,1},{3,2},{4,7},{5,4},{6,5},{7,6},{8,11},{9,8},{10,9... | collective-permute-start | bytes 1966088 | tf_op jit(solution)/shard_map/ppermute | solution.py:219
  43.9 0.9 pad_maximum_fusion.1
  44.8 0.9 pad_maximum_fusion
  45.7 0.7 copy-done.15
  46.4 1.9 collective-permute-start.6
  48.4 15.4 %collective-permute-done.11.refs_10_ = bf16[4,128,256]{2,1,0:T(8,128)(2,1)S(1)} collective-permute-done((bf16[4,128,256]{2,1,0:T(8,128)(2,1)S(1)}, bf16[4,128,256]{2,1,0:T(8,128)(2,1)S(1)}, u32[]{:S(2)}, u32[]{:S(2)}) %collective-permute-start.11) | collective-permute-done | bytes 262176 | tf_op jit(solution)/shard_map/ppermute | solution.py:219
  63.8 0.7 copy-done.17
  64.5 1.9 collective-permute-start.4
  66.4 3.0 %collective-permute-done.9.refs_10_ = bf16[4,128,256]{2,1,0:T(8,128)(2,1)S(1)} collective-permute-done((bf16[4,128,256]{2,1,0:T(8,128)(2,1)S(1)}, bf16[4,128,256]{2,1,0:T(8,128)(2,1)S(1)}, u32[]{:S(2)}, u32[]{:S(2)}) %collective-permute-start.9) | collective-permute-done | bytes 262176 | tf_op jit(solution)/shard_map/ppermute | solution.py:219
  69.4 0.7 copy-done.19
  70.1 1.9 collective-permute-start.5
  72.0 0.8 copy-done.9
  72.9 4.5 %collective-permute-start.7 = (bf16[2,256,640]{2,1,0:T(8,128)(2,1)}, bf16[2,256,640]{2,1,0:T(8,128)(2,1)}, u32[]{:S(2)}, u32[]{:S(2)}) collective-permute-start(bf16[2,256,640]{2,1,0:T(8,128)(2,1)} %pad_maximum_fusion.1), channel_id=1, source_target_pairs={{4,0},{8,4},{12,8},{16,12},{20,16},{24,20},{28,24},{5,1},{9,5},{13... | collective-permute-start | bytes 1966088 | tf_op jit(solution)/shard_map/ppermute | solution.py:239
  77.4 5.0 %collective-permute-done.3.refs_8_.refs_9_ = bf16[4,128,640]{2,1,0:T(8,128)(2,1)} collective-permute-done((bf16[4,128,640]{2,1,0:T(8,128)(2,1)}, bf16[4,128,640]{2,1,0:T(8,128)(2,1)}, u32[]{:S(2)}, u32[]{:S(2)}) %collective-permute-start.3) | collective-permute-done | bytes 655392 | tf_op jit(solution)/shard_map/ppermute | solution.py:219
  82.5 4.4 %collective-permute-start.8 = (bf16[4,128,256]{2,1,0:T(8,128)(2,1)}, bf16[4,128,256]{2,1,0:T(8,128)(2,1)S(1)}, u32[]{:S(2)}, u32[]{:S(2)}) collective-permute-start(bf16[4,128,256]{2,1,0:T(8,128)(2,1)} %bitcast.52), channel_id=1, source_target_pairs={{0,1},{1,2},{2,3},{3,0},{4,5},{5,6},{6,7},{7,4},{8,9},{9,10},{10,1... | collective-permute-start | bytes 786440 | tf_op jit(solution)/shard_map/ppermute | solution.py:219
  86.9 2.6 copy-done
  89.5 1.1 copy-done.4
  90.6 1.1 copy-done.6
  91.7 0.9 copy-done.7
  92.6 1.1 copy-done.10
  93.7 0.9 copy-done.22
  94.6 3.5 %zonal_conv.11.refs_2_ = bf16[8,192,128]{2,1,0:T(8,128)(2,1)S(1)} custom-call(f32[16]{0:T(128)S(1)} %and_select_fusion.refs_0_, bf16[448,448]{1,0:T(8,128)(2,1)S(1)} %copy-done.2, bf16[192,448]{1,0:T(8,128)(2,1)S(1)} %copy-done.7, f32[5,448,640]{2,1,0:T(8,128)S(1)} %copy-done, bf16[12,192,640]{2,1,0:T(8,128)(2,1)S(1)} %bitcast.45, ...), custom_call_target="tpu_custom_call" | custom-call | flops 792723456 | bytes 2523136 | tf_op jit(solution)/shard_map/zonal_conv/pallas_call | solution.py:113
  98.2 5.9 %zonal_conv.10.refs_1_ = bf16[8,192,256]{2,1,0:T(8,128)(2,1)S(1)} custom-call(f32[16]{0:T(128)S(1)} %and_select_fusion.refs_0_, bf16[448,448]{1,0:T(8,128)(2,1)S(1)} %copy-done.2, bf16[192,448]{1,0:T(8,128)(2,1)S(1)} %copy-done.7, f32[5,448,640]{2,1,0:T(8,128)S(1)} %copy-done, bf16[12,192,640]{2,1,0:T(8,128)(2,1)S(1)} %bitcast.46, ...), custom_call_target="tpu_custom_call" | custom-call | flops 1585446912 | bytes 5046272 | tf_op jit(solution)/shard_map/zonal_conv/pallas_call | solution.py:113
  104.2 5.9 %zonal_conv.9.refs_0_ = bf16[8,192,256]{2,1,0:T(8,128)(2,1)S(1)} custom-call(f32[16]{0:T(128)S(1)} %and_select_fusion.refs_0_, bf16[448,448]{1,0:T(8,128)(2,1)S(1)} %copy-done.2, bf16[192,448]{1,0:T(8,128)(2,1)S(1)} %copy-done.7, f32[5,448,640]{2,1,0:T(8,128)S(1)} %copy-done, bf16[12,192,640]{2,1,0:T(8,128)(2,1)S(1)} %bitcast.47, ...), custom_call_target="tpu_custom_call" | custom-call | flops 1585446912 | bytes 5046272 | tf_op jit(solution)/shard_map/zonal_conv/pallas_call | solution.py:113
  110.2 11.4 %zonal_conv.8.refs_0_ = bf16[4,192,640]{2,1,0:T(8,128)(2,1)S(1)} custom-call(f32[16]{0:T(128)S(1)} %and_select_fusion.refs_0_, bf16[448,448]{1,0:T(8,128)(2,1)S(1)} %copy-done.2, bf16[192,448]{1,0:T(8,128)(2,1)S(1)} %copy-done.7, f32[5,448,640]{2,1,0:T(8,128)S(1)} %copy-done, bf16[12,192,640]{2,1,0:T(8,128)(2,1)S(1)} %bitcast.48, ...), custom_call_target="tpu_custom_call" | custom-call | flops 3523215360 | bytes 12615680 | tf_op jit(solution)/shard_map/zonal_conv/pallas_call | solution.py:113
  121.7 4.1 %channel_mlp.5 = (bf16[4,192,640]{2,1,0:T(8,128)(2,1)S(1)}, bf16[4,128,640]{2,1,0:T(8,128)(2,1)S(1)}, bf16[4,128,640]{2,1,0:T(8,128)(2,1)S(1)}) custom-call(f32[1,640]{1,0:T(1,128)S(1)} %get-tuple-element.59.gain, bf16[640,1280]{1,0:T(8,128)(2,1)S(1)} %copy-done.13, bf16[1280,640]{1,0:T(8,128)(2,1)S(1)} %copy-done.14, bf16[4,192,640]{2,1,0:T(8,128)(2,1)S(1)} %zonal_conv.8.refs_0_), custom_call_target="tpu_custom_call" | custom-call | flops 2516582400 | bytes 5242880 | tf_op jit(solution)/shard_map/channel_mlp/pallas_call | solution.py:194
  126.0 4.0 %channel_mlp.7 = (bf16[4,192,640]{2,1,0:T(8,128)(2,1)S(1)}, bf16[4,128,256]{2,1,0:T(8,128)(2,1)S(1)}, bf16[4,128,256]{2,1,0:T(8,128)(2,1)S(1)}, bf16[4,128,256]{...) custom-call(f32[1,640]{1,0:T(1,128)S(1)} %get-tuple-element.59.gain,, ...), custom_call_target="tpu_custom_call" | custom-call | flops 2516582400 | bytes 5242880 | tf_op jit(solution)/shard_map/channel_mlp/pallas_call | solution.py:194
  130.1 2.0 collective-permute-start.23
  132.2 2.0 collective-permute-start.17
  134.1 4.0 %channel_mlp.6 = (bf16[4,192,640]{2,1,0:T(8,128)(2,1)S(1)}, bf16[4,128,640]{2,1,0:T(8,128)(2,1)S(1)}, bf16[4,128,640]{2,1,0:T(8,128)(2,1)S(1)}) custom-call(f32[1,640]{1,0:T(1,128)S(1)} %get-tuple-element.59.gain, bf16[640,1280]{1,0:T(8,128)(2,1)S(1)} %copy-done.13, bf16[1280,640]{1,0:T(8,128)(2,1)S(1)} %copy-done.14, ...), custom_call_target="tpu_custom_call" | custom-call | flops 2516582400 | bytes 5242880 | tf_op jit(solution)/shard_map/channel_mlp/pallas_call | solution.py:194
  138.4 22.1 %collective-permute-done.14.refs_7_.refs_6_ = bf16[4,128,640]{2,1,0:T(8,128)(2,1)S(1)} collective-permute-done((bf16[4,128,640]{2,1,0:T(8,128)(2,1)S(1)}, bf16[4,128,640]{2,1,0:T(8,128)(2,1)S(1)}, u32[]{:S(2)}, u32[]{:S(2)}) %collective-permute-start.14) | collective-permute-done | bytes 655392 | tf_op jit(solution)/shard_map/ppermute | solution.py:219
  160.5 2.7 %collective-permute-done.22.refs_9_ = bf16[4,128,128]{2,1,0:T(8,128)(2,1)S(1)} collective-permute-done((bf16[4,128,128]{2,1,0:T(8,128)(2,1)S(1)}, bf16[4,128,128]{2,1,0:T(8,128)(2,1)S(1)}, u32[]{:S(2)}, u32[]{:S(2)}) %collective-permute-start.22) | collective-permute-done | bytes 131104 | tf_op jit(solution)/shard_map/ppermute | solution.py:219
  163.3 2.0 collective-permute-start.21
  165.5 31.9 %collective-permute-done.16.refs_9_ = bf16[4,128,256]{2,1,0:T(8,128)(2,1)S(1)} collective-permute-done((bf16[4,128,256]{2,1,0:T(8,128)(2,1)S(1)}, bf16[4,128,256]{2,1,0:T(8,128)(2,1)S(1)}, u32[]{:S(2)}, u32[]{:S(2)}) %collective-permute-start.16) | collective-permute-done | bytes 262176 | tf_op jit(solution)/shard_map/ppermute | solution.py:219
  197.5 15.6 %collective-permute-done.20.refs_9_ = bf16[4,128,256]{2,1,0:T(8,128)(2,1)S(1)} collective-permute-done((bf16[4,128,256]{2,1,0:T(8,128)(2,1)S(1)}, bf16[4,128,256]{2,1,0:T(8,128)(2,1)S(1)}, u32[]{:S(2)}, u32[]{:S(2)}) %collective-permute-start.20) | collective-permute-done | bytes 262176 | tf_op jit(solution)/shard_map/ppermute | solution.py:219
  213.1 2.3 collective-permute-start.26
  215.4 2.1 collective-permute-start.24
  217.6 3.7 %collective-permute-start.25 = (bf16[2,256,640]{2,1,0:T(8,128)(2,1)S(1)}, bf16[2,256,640]{2,1,0:T(8,128)(2,1)S(1)}, u32[]{:S(2)}, u32[]{:S(2)}) collective-permute-start(bf16[2,256,640]{2,1,0:T(8,128)(2,1)S(1)} %pad_maximum_fusion.2), channel_id=1, source_target_pairs={{0,4},{4,8},{8,12},{12,16},{16,20},{20,24},{24,28},{1,5},{5,9},{9,... | collective-permute-start | bytes 1966088 | tf_op jit(solution)/shard_map/ppermute | solution.py:239
  221.2 2.8 %collective-permute-start.27 = (bf16[2,256,640]{2,1,0:T(8,128)(2,1)S(1)}, bf16[2,256,640]{2,1,0:T(8,128)(2,1)S(1)}, u32[]{:S(2)}, u32[]{:S(2)}) collective-permute-start(bf16[2,256,640]{2,1,0:T(8,128)(2,1)S(1)} %pad_maximum_fusion.3), channel_id=1, source_target_pairs={{4,0},{8,4},{12,8},{16,12},{20,16},{24,20},{28,24},{5,1},{9,5},{13... | collective-permute-start | bytes 1966088 | tf_op jit(solution)/shard_map/ppermute | solution.py:239
  224.1 0.9 convolution_bitcast_fusion.1.refs_3_
  225.0 2.9 %zonal_conv.14.refs_2_ = bf16[8,192,128]{2,1,0:T(8,128)(2,1)S(1)} custom-call(f32[16]{0:T(128)S(1)} %and_select_fusion.refs_0_, bf16[448,448]{1,0:T(8,128)(2,1)S(1)} %copy-done.2, bf16[192,448]{1,0:T(8,128)(2,1)S(1)} %copy-done.8, f32[5,448,640]{2,1,0:T(8,128)S(1)} %convolution_bitcast_fusion.1.refs_3_, bf16[4,192,640]{2,1,0:T(8,128)(2,1)S(1)} %get-tuple-element.22.refs_4_, ...), custom_call_target="tpu_custom_call" | custom-call | flops 792723456 | bytes 2523136 | tf_op jit(solution)/shard_map/zonal_conv/pallas_call | solution.py:113
  227.9 5.4 %zonal_conv.13.refs_1_ = bf16[8,192,256]{2,1,0:T(8,128)(2,1)S(1)} custom-call(f32[16]{0:T(128)S(1)} %and_select_fusion.refs_0_, bf16[448,448]{1,0:T(8,128)(2,1)S(1)} %copy-done.2, bf16[192,448]{1,0:T(8,128)(2,1)S(1)} %copy-done.8, f32[5,448,640]{2,1,0:T(8,128)S(1)} %convolution_bitcast_fusion.1.refs_3_, bf16[4,192,640]{2,1,0:T(8,128)(2,1)S(1)} %get-tuple-element.22.refs_4_, ...), custom_call_target="tpu_custom_call" | custom-call | flops 1585446912 | bytes 5046272 | tf_op jit(solution)/shard_map/zonal_conv/pallas_call | solution.py:113
  233.3 5.4 %zonal_conv.12.refs_0_ = bf16[8,192,256]{2,1,0:T(8,128)(2,1)S(1)} custom-call(f32[16]{0:T(128)S(1)} %and_select_fusion.refs_0_, bf16[448,448]{1,0:T(8,128)(2,1)S(1)} %copy-done.2, bf16[192,448]{1,0:T(8,128)(2,1)S(1)} %copy-done.8, f32[5,448,640]{2,1,0:T(8,128)S(1)} %convolution_bitcast_fusion.1.refs_3_, bf16[4,192,640]{2,1,0:T(8,128)(2,1)S(1)} %get-tuple-element.22.refs_4_, ...), custom_call_target="tpu_custom_call" | custom-call | flops 1585446912 | bytes 5046272 | tf_op jit(solution)/shard_map/zonal_conv/pallas_call | solution.py:113
  238.8 3.8 %collective-permute-done.25.refs_11_ = bf16[2,256,640]{2,1,0:T(8,128)(2,1)S(1)} collective-permute-done((bf16[2,256,640]{2,1,0:T(8,128)(2,1)S(1)}, bf16[2,256,640]{2,1,0:T(8,128)(2,1)S(1)}, u32[]{:S(2)}, u32[]{:S(2)}) %collective-permute-start.25) | collective-permute-done | bytes 655392 | tf_op jit(solution)/shard_map/ppermute | solution.py:239
  242.6 10.0 %zonal_conv.15.refs_0_ = bf16[4,192,640]{2,1,0:T(8,128)(2,1)S(1)} custom-call(f32[16]{0:T(128)S(1)} %and_select_fusion.refs_0_, bf16[448,448]{1,0:T(8,128)(2,1)S(1)} %copy-done.2, bf16[192,448]{1,0:T(8,128)(2,1)S(1)} %copy-done.8, f32[5,448,640]{2,1,0:T(8,128)S(1)} %convolution_bitcast_fusion.1.refs_3_, bf16[4,192,640]{2,1,0:T(8,128)(2,1)S(1)} %get-tuple-element.22.refs_4_, ...), custom_call_target="tpu_custom_call" | custom-call | flops 3523215360 | bytes 12615680 | tf_op jit(solution)/shard_map/zonal_conv/pallas_call | solution.py:113
  252.6 4.8 %channel_mlp.8.refs_3_ = bf16[12,192,640]{2,1,0:T(8,128)(2,1)} custom-call(f32[1,640]{1,0:T(1,128)S(1)} %get-tuple-element.60.gain, bf16[640,1280]{1,0:T(8,128)(2,1)S(1)} %copy-done.11, bf16[1280,640]{1,0:T(8,128)(2,1)S(1)} %copy-done.12, bf16[4,192,640]{2,1,0:T(8,128)(2,1)S(1)} %zonal_conv.15.refs_0_), custom_call_target="tpu_custom_call" | custom-call | flops 2516582400 | bytes 5242880 | tf_op jit(solution)/shard_map/channel_mlp/pallas_call | solution.py:194
  257.4 8.9 %channel_mlp.9 = bf16[12,192,640]{2,1,0:T(8,128)(2,1)} custom-call(f32[1,640]{1,0:T(1,128)S(1)} %get-tuple-element.60.gain, bf16[640,1280]{1,0:T(8,128)(2,1)S(1)} %copy-done.11, bf16[1280,640]{1,0:T(8,128)(2,1)S(1)} %copy-done.12, bf16[8,192,256]{2,1,0:T(8,128)(2,1)S(1)} %zonal_conv.12.refs_0_, ...), custom_call_target="tpu_custom_call", output_to_operand_aliasing={{}: (6, {})} | custom-call | flops 5033164800 | bytes 7208960 | tf_op jit(solution)/shard_map/channel_mlp/pallas_call | solution.py:194
  (86 shorter events, 3.2 us)
Async XLA Ops:
  0.0 7.7 %copy-start.1 = (bf16[1,12,640,192]{2,3,1,0:T(8,128)(2,1)S(1)}, bf16[1,12,640,192]{2,3,1,0:T(8,128)(2,1)}, u32[]{:S(2)}) copy-start(bf16[1,12,640,192]{2,3,1,0:T(8,128)(2,1)} %param.8) | copy-start | bytes 8847364
  1.3 39.3 %collective-permute-start = (bf16[4,128,640]{2,1,0:T(8,128)(2,1)S(1)}, bf16[4,128,640]{2,1,0:T(8,128)(2,1)S(1)}, u32[]{:S(2)}, u32[]{:S(2)}) collective-permute-start(bf16[4,128,640]{2,1,0:T(8,128)(2,1)S(1)} %bitcast.50), channel_id=1, source_target_pairs={{0,1},{1,2},{2,3},{3,0},{4,5},{5,6},{6,7},{7,4},{8,9},{9,10},{10,1... | collective-permute-start | bytes 1966088 | tf_op jit(solution)/shard_map/ppermute | solution.py:219
  4.1 28.7 %collective-permute-start.2 = (bf16[4,128,640]{2,1,0:T(8,128)(2,1)S(1)}, bf16[4,128,640]{2,1,0:T(8,128)(2,1)S(1)}, u32[]{:S(2)}, u32[]{:S(2)}) collective-permute-start(bf16[4,128,640]{2,1,0:T(8,128)(2,1)S(1)} %bitcast.51), channel_id=1, source_target_pairs={{0,3},{1,0},{2,1},{3,2},{4,7},{5,4},{6,5},{7,6},{8,11},{9,8},{10,9... | collective-permute-start | bytes 1966088 | tf_op jit(solution)/shard_map/ppermute | solution.py:219
  5.6 33.0 %collective-permute-start.12 = (bf16[4,128,128]{2,1,0:T(8,128)(2,1)S(1)}, bf16[4,128,128]{2,1,0:T(8,128)(2,1)S(1)}, u32[]{:S(2)}, u32[]{:S(2)}) collective-permute-start(bf16[4,128,128]{2,1,0:T(8,128)(2,1)S(1)} %bitcast.57), channel_id=1, source_target_pairs={{0,1},{1,2},{2,3},{3,0},{4,5},{5,6},{6,7},{7,4},{8,9},{9,10},{10,1... | collective-permute-start | bytes 393224 | tf_op jit(solution)/shard_map/ppermute | solution.py:219
  7.2 31.4 %collective-permute-start.13 = (bf16[4,128,128]{2,1,0:T(8,128)(2,1)S(1)}, bf16[4,128,128]{2,1,0:T(8,128)(2,1)S(1)}, u32[]{:S(2)}, u32[]{:S(2)}) collective-permute-start(bf16[4,128,128]{2,1,0:T(8,128)(2,1)S(1)} %bitcast.56), channel_id=1, source_target_pairs={{0,3},{1,0},{2,1},{3,2},{4,7},{5,4},{6,5},{7,6},{8,11},{9,8},{10,9... | collective-permute-start | bytes 393224 | tf_op jit(solution)/shard_map/ppermute | solution.py:219
  7.7 3.4 %copy-start.23 = (bf16[2,640,1280]{2,1,0:T(8,128)(2,1)S(1)}, bf16[2,640,1280]{2,1,0:T(8,128)(2,1)}, u32[]{:S(2)}) copy-start(bf16[2,640,1280]{2,1,0:T(8,128)(2,1)} %param.11) | copy-start | bytes 9830404
  8.5 37.2 %collective-permute-start.10 = (bf16[4,128,256]{2,1,0:T(8,128)(2,1)S(1)}, bf16[4,128,256]{2,1,0:T(8,128)(2,1)S(1)}, u32[]{:S(2)}, u32[]{:S(2)}) collective-permute-start(bf16[4,128,256]{2,1,0:T(8,128)(2,1)S(1)} %bitcast.55), channel_id=1, source_target_pairs={{0,1},{1,2},{2,3},{3,0},{4,5},{5,6},{6,7},{7,4},{8,9},{9,10},{10,1... | collective-permute-start | bytes 786440 | tf_op jit(solution)/shard_map/ppermute | solution.py:219
  11.1 3.1 %copy-start.24 = (bf16[2,1280,640]{2,1,0:T(8,128)(2,1)S(1)}, bf16[2,1280,640]{2,1,0:T(8,128)(2,1)}, u32[]{:S(2)}) copy-start(bf16[2,1280,640]{2,1,0:T(8,128)(2,1)} %param.12) | copy-start | bytes 9830404
  14.2 3.2 %copy-start.25 = (bf16[2,5,256,640]{3,2,1,0:T(8,128)(2,1)S(1)}, bf16[2,5,256,640]{3,2,1,0:T(8,128)(2,1)}, u32[]{:S(2)}) copy-start(bf16[2,5,256,640]{3,2,1,0:T(8,128)(2,1)} %param.9) | copy-start | bytes 9830404
  16.2 1.6 copy-start.27
  32.8 12.0 %copy-start.5 = (bf16[4,128,640]{2,1,0:T(8,128)(2,1)}, bf16[4,128,640]{2,1,0:T(8,128)(2,1)S(1)}, u32[]{:S(2)}) copy-start(bf16[4,128,640]{2,1,0:T(8,128)(2,1)S(1)} %collective-permute-done.2.refs_7_.refs_8_) | copy-start | bytes 1966084
  32.8 39.2 %collective-permute-start.1 = (bf16[4,128,640]{2,1,0:T(8,128)(2,1)S(1)}, bf16[4,128,640]{2,1,0:T(8,128)(2,1)S(1)}, u32[]{:S(2)}, u32[]{:S(2)}) collective-permute-start(bf16[4,128,640]{2,1,0:T(8,128)(2,1)S(1)} %bitcast.49), channel_id=1, source_target_pairs={{0,1},{1,2},{2,3},{3,0},{4,5},{5,6},{6,7},{7,4},{8,9},{9,10},{10,1... | collective-permute-start | bytes 1966088 | tf_op jit(solution)/shard_map/ppermute | solution.py:219
  38.6 25.1 %collective-permute-start.11 = (bf16[4,128,256]{2,1,0:T(8,128)(2,1)S(1)}, bf16[4,128,256]{2,1,0:T(8,128)(2,1)S(1)}, u32[]{:S(2)}, u32[]{:S(2)}) collective-permute-start(bf16[4,128,256]{2,1,0:T(8,128)(2,1)S(1)} %bitcast.54), channel_id=1, source_target_pairs={{0,3},{1,0},{2,1},{3,2},{4,7},{5,4},{6,5},{7,6},{8,11},{9,8},{10,9... | collective-permute-start | bytes 786440 | tf_op jit(solution)/shard_map/ppermute | solution.py:219
  38.6 0.7 copy-start.21
  39.3 30.1 %collective-permute-start.9 = (bf16[4,128,256]{2,1,0:T(8,128)(2,1)S(1)}, bf16[4,128,256]{2,1,0:T(8,128)(2,1)S(1)}, u32[]{:S(2)}, u32[]{:S(2)}) collective-permute-start(bf16[4,128,256]{2,1,0:T(8,128)(2,1)S(1)} %bitcast.53), channel_id=1, source_target_pairs={{0,3},{1,0},{2,1},{3,2},{4,7},{5,4},{6,5},{7,6},{8,11},{9,8},{10,9... | collective-permute-start | bytes 786440 | tf_op jit(solution)/shard_map/ppermute | solution.py:219
  40.6 5.1 %copy-start.3 = (bf16[4,128,640]{2,1,0:T(8,128)(2,1)}, bf16[4,128,640]{2,1,0:T(8,128)(2,1)S(1)}, u32[]{:S(2)}) copy-start(bf16[4,128,640]{2,1,0:T(8,128)(2,1)S(1)} %collective-permute-done.refs_5_) | copy-start | bytes 1966084
  40.6 41.8 %collective-permute-start.3 = (bf16[4,128,640]{2,1,0:T(8,128)(2,1)}, bf16[4,128,640]{2,1,0:T(8,128)(2,1)}, u32[]{:S(2)}, u32[]{:S(2)}) collective-permute-start(bf16[4,128,640]{2,1,0:T(8,128)(2,1)} %bitcast.17), channel_id=1, source_target_pairs={{0,3},{1,0},{2,1},{3,2},{4,7},{5,4},{6,5},{7,6},{8,11},{9,8},{10,9... | collective-permute-start | bytes 1966088 | tf_op jit(solution)/shard_map/ppermute | solution.py:219
  43.9 33.5 %copy-start.29 = (bf16[2,640]{1,0:T(2,128)(2,1)S(1)}, bf16[2,640]{1,0:T(2,128)(2,1)}, u32[]{:S(2)}) copy-start(bf16[2,640]{1,0:T(2,128)(2,1)} %param.10) | copy-start | bytes 7684
  43.9 43.0 %copy-start.2 = (bf16[448,448]{1,0:T(8,128)(2,1)S(1)}, bf16[448,448]{1,0:T(8,128)(2,1)}, u32[]{:S(2)}) copy-start(bf16[448,448]{1,0:T(8,128)(2,1)} %constant.30.clone.refs_1_) | copy-start | bytes 1204228
  45.7 0.7 copy-start.15
  46.4 63.7 %collective-permute-start.6 = (bf16[2,192,640]{2,1,0:T(8,128)(2,1)}, bf16[2,192,640]{2,1,0:T(8,128)(2,1)}, u32[]{:S(2)}, u32[]{:S(2)}) collective-permute-start(bf16[2,192,640]{2,1,0:T(8,128)(2,1)} %get-tuple-element.45), channel_id=1, source_target_pairs={{4,0},{8,4},{12,8},{16,12},{20,16},{24,20},{28,24},{5,1},{9,5},{13... | collective-permute-start | bytes 1474568 | tf_op jit(solution)/shard_map/ppermute | solution.py:239
  63.8 0.7 copy-start.17
  64.5 45.7 %collective-permute-start.4 = (bf16[2,192,640]{2,1,0:T(8,128)(2,1)}, bf16[2,192,640]{2,1,0:T(8,128)(2,1)}, u32[]{:S(2)}, u32[]{:S(2)}) collective-permute-start(bf16[2,192,640]{2,1,0:T(8,128)(2,1)} %get-tuple-element.46), channel_id=1, source_target_pairs={{0,4},{4,8},{8,12},{12,16},{16,20},{20,24},{24,28},{1,5},{5,9},{9,... | collective-permute-start | bytes 1474568 | tf_op jit(solution)/shard_map/ppermute | solution.py:239
  69.4 0.7 copy-start.19
  70.1 40.1 %collective-permute-start.5 = (bf16[2,256,640]{2,1,0:T(8,128)(2,1)}, bf16[2,256,640]{2,1,0:T(8,128)(2,1)}, u32[]{:S(2)}, u32[]{:S(2)}) collective-permute-start(bf16[2,256,640]{2,1,0:T(8,128)(2,1)} %pad_maximum_fusion), channel_id=1, source_target_pairs={{0,4},{4,8},{8,12},{12,16},{16,20},{20,24},{24,28},{1,5},{5,9},{9,... | collective-permute-start | bytes 1966088 | tf_op jit(solution)/shard_map/ppermute | solution.py:239
  72.0 0.8 copy-start.9
  72.9 37.3 %collective-permute-start.7 = (bf16[2,256,640]{2,1,0:T(8,128)(2,1)}, bf16[2,256,640]{2,1,0:T(8,128)(2,1)}, u32[]{:S(2)}, u32[]{:S(2)}) collective-permute-start(bf16[2,256,640]{2,1,0:T(8,128)(2,1)} %pad_maximum_fusion.1), channel_id=1, source_target_pairs={{4,0},{8,4},{12,8},{16,12},{20,16},{24,20},{28,24},{5,1},{9,5},{13... | collective-permute-start | bytes 1966088 | tf_op jit(solution)/shard_map/ppermute | solution.py:239
  82.5 21.7 %collective-permute-start.8 = (bf16[4,128,256]{2,1,0:T(8,128)(2,1)}, bf16[4,128,256]{2,1,0:T(8,128)(2,1)S(1)}, u32[]{:S(2)}, u32[]{:S(2)}) collective-permute-start(bf16[4,128,256]{2,1,0:T(8,128)(2,1)} %bitcast.52), channel_id=1, source_target_pairs={{0,1},{1,2},{2,3},{3,0},{4,5},{5,6},{6,7},{7,4},{8,9},{9,10},{10,1... | collective-permute-start | bytes 786440 | tf_op jit(solution)/shard_map/ppermute | solution.py:219
  86.9 2.6 copy-start
  89.5 1.1 copy-start.4
  90.6 1.1 copy-start.6
  91.7 0.9 copy-start.7
  92.6 1.1 copy-start.10
  93.7 0.9 copy-start.22
  94.6 3.5 %copy-start.16 = (bf16[4,128,256]{2,1,0:T(8,128)(2,1)S(1)}, bf16[4,128,256]{2,1,0:T(8,128)(2,1)}, u32[]{:S(2)}) copy-start(bf16[4,128,256]{2,1,0:T(8,128)(2,1)} %copy-done.15) | copy-start | bytes 786436
  94.6 3.6 %copy-start.18 = (bf16[4,128,256]{2,1,0:T(8,128)(2,1)S(1)}, bf16[4,128,256]{2,1,0:T(8,128)(2,1)}, u32[]{:S(2)}) copy-start(bf16[4,128,256]{2,1,0:T(8,128)(2,1)} %copy-done.17) | copy-start | bytes 786436
  98.2 6.0 %copy-start.20 = (bf16[4,128,256]{2,1,0:T(8,128)(2,1)S(1)}, bf16[4,128,256]{2,1,0:T(8,128)(2,1)}, u32[]{:S(2)}) copy-start(bf16[4,128,256]{2,1,0:T(8,128)(2,1)} %copy-done.19) | copy-start | bytes 786436
  110.1 11.5 %copy-start.13 = (bf16[640,1280]{1,0:T(8,128)(2,1)S(1)}, bf16[640,1280]{1,0:T(8,128)(2,1)}, u32[]{:S(2)}) copy-start(bf16[640,1280]{1,0:T(8,128)(2,1)} %get-tuple-element.37.w_in) | copy-start | bytes 4915204
  110.2 11.5 %copy-start.14 = (bf16[1280,640]{1,0:T(8,128)(2,1)S(1)}, bf16[1280,640]{1,0:T(8,128)(2,1)}, u32[]{:S(2)}) copy-start(bf16[1280,640]{1,0:T(8,128)(2,1)} %get-tuple-element.35.w_out) | copy-start | bytes 4915204
  125.7 34.7 %collective-permute-start.14 = (bf16[4,128,640]{2,1,0:T(8,128)(2,1)S(1)}, bf16[4,128,640]{2,1,0:T(8,128)(2,1)S(1)}, u32[]{:S(2)}, u32[]{:S(2)}) collective-permute-start(bf16[4,128,640]{2,1,0:T(8,128)(2,1)S(1)} %get-tuple-element.25), channel_id=1, source_target_pairs={{0,1},{1,2},{2,3},{3,0},{4,5},{5,6},{6,7},{7,4},{8,9},{9,10},{10,1... | collective-permute-start | bytes 1966088 | tf_op jit(solution)/shard_map/ppermute | solution.py:219
  130.0 33.2 %collective-permute-start.22 = (bf16[4,128,128]{2,1,0:T(8,128)(2,1)S(1)}, bf16[4,128,128]{2,1,0:T(8,128)(2,1)S(1)}, u32[]{:S(2)}, u32[]{:S(2)}) collective-permute-start(bf16[4,128,128]{2,1,0:T(8,128)(2,1)S(1)} %get-tuple-element.33), channel_id=1, source_target_pairs={{0,1},{1,2},{2,3},{3,0},{4,5},{5,6},{6,7},{7,4},{8,9},{9,10},{10,1... | collective-permute-start | bytes 393224 | tf_op jit(solution)/shard_map/ppermute | solution.py:219
  130.1 33.1 %collective-permute-start.23 = (bf16[4,128,128]{2,1,0:T(8,128)(2,1)S(1)}, bf16[4,128,128]{2,1,0:T(8,128)(2,1)S(1)}, u32[]{:S(2)}, u32[]{:S(2)}) collective-permute-start(bf16[4,128,128]{2,1,0:T(8,128)(2,1)S(1)} %get-tuple-element.34), channel_id=1, source_target_pairs={{0,3},{1,0},{2,1},{3,2},{4,7},{5,4},{6,5},{7,6},{8,11},{9,8},{10,9... | collective-permute-start | bytes 393224 | tf_op jit(solution)/shard_map/ppermute | solution.py:219
  132.2 31.1 %collective-permute-start.17 = (bf16[4,128,640]{2,1,0:T(8,128)(2,1)S(1)}, bf16[4,128,640]{2,1,0:T(8,128)(2,1)S(1)}, u32[]{:S(2)}, u32[]{:S(2)}) collective-permute-start(bf16[4,128,640]{2,1,0:T(8,128)(2,1)S(1)} %get-tuple-element.28), channel_id=1, source_target_pairs={{0,3},{1,0},{2,1},{3,2},{4,7},{5,4},{6,5},{7,6},{8,11},{9,8},{10,9... | collective-permute-start | bytes 1966088 | tf_op jit(solution)/shard_map/ppermute | solution.py:219
  138.1 79.4 %collective-permute-start.15 = (bf16[4,128,640]{2,1,0:T(8,128)(2,1)S(1)}, bf16[4,128,640]{2,1,0:T(8,128)(2,1)S(1)}, u32[]{:S(2)}, u32[]{:S(2)}) collective-permute-start(bf16[4,128,640]{2,1,0:T(8,128)(2,1)S(1)} %get-tuple-element.26), channel_id=1, source_target_pairs={{0,1},{1,2},{2,3},{3,0},{4,5},{5,6},{6,7},{7,4},{8,9},{9,10},{10,1... | collective-permute-start | bytes 1966088 | tf_op jit(solution)/shard_map/ppermute | solution.py:219
  160.4 60.8 %collective-permute-start.18 = (bf16[4,128,640]{2,1,0:T(8,128)(2,1)S(1)}, bf16[4,128,640]{2,1,0:T(8,128)(2,1)S(1)}, u32[]{:S(2)}, u32[]{:S(2)}) collective-permute-start(bf16[4,128,640]{2,1,0:T(8,128)(2,1)S(1)} %get-tuple-element.29), channel_id=1, source_target_pairs={{0,3},{1,0},{2,1},{3,2},{4,7},{5,4},{6,5},{7,6},{8,11},{9,8},{10,9... | collective-permute-start | bytes 1966088 | tf_op jit(solution)/shard_map/ppermute | solution.py:219
  163.2 34.2 %collective-permute-start.16 = (bf16[4,128,256]{2,1,0:T(8,128)(2,1)S(1)}, bf16[4,128,256]{2,1,0:T(8,128)(2,1)S(1)}, u32[]{:S(2)}, u32[]{:S(2)}) collective-permute-start(bf16[4,128,256]{2,1,0:T(8,128)(2,1)S(1)} %get-tuple-element.27), channel_id=1, source_target_pairs={{0,1},{1,2},{2,3},{3,0},{4,5},{5,6},{6,7},{7,4},{8,9},{9,10},{10,1... | collective-permute-start | bytes 786440 | tf_op jit(solution)/shard_map/ppermute | solution.py:219
  163.3 49.8 %collective-permute-start.20 = (bf16[4,128,256]{2,1,0:T(8,128)(2,1)S(1)}, bf16[4,128,256]{2,1,0:T(8,128)(2,1)S(1)}, u32[]{:S(2)}, u32[]{:S(2)}) collective-permute-start(bf16[4,128,256]{2,1,0:T(8,128)(2,1)S(1)} %get-tuple-element.31), channel_id=1, source_target_pairs={{0,1},{1,2},{2,3},{3,0},{4,5},{5,6},{6,7},{7,4},{8,9},{9,10},{10,1... | collective-permute-start | bytes 786440 | tf_op jit(solution)/shard_map/ppermute | solution.py:219
  163.3 52.1 %collective-permute-start.21 = (bf16[4,128,256]{2,1,0:T(8,128)(2,1)S(1)}, bf16[4,128,256]{2,1,0:T(8,128)(2,1)S(1)}, u32[]{:S(2)}, u32[]{:S(2)}) collective-permute-start(bf16[4,128,256]{2,1,0:T(8,128)(2,1)S(1)} %get-tuple-element.32), channel_id=1, source_target_pairs={{0,3},{1,0},{2,1},{3,2},{4,7},{5,4},{6,5},{7,6},{8,11},{9,8},{10,9... | collective-permute-start | bytes 786440 | tf_op jit(solution)/shard_map/ppermute | solution.py:219
  165.3 58.7 %copy-start.26 = (bf16[2,5,256,640]{3,2,1,0:T(8,128)(2,1)S(1)}, bf16[2,5,256,640]{3,2,1,0:T(8,128)(2,1)}, u32[]{:S(2)}) copy-start(bf16[2,5,256,640]{3,2,1,0:T(8,128)(2,1)} %param.9) | copy-start | bytes 9830404
  165.4 58.7 %copy-start.28 = (bf16[448,256,1]{1,0,2:T(8,128)(2,1)S(1)}, bf16[448,256,1]{1,0,2:T(8,128)(2,1)}, u32[]{:S(2)}) copy-start(bf16[448,256,1]{1,0,2:T(8,128)(2,1)} %constant.34) | copy-start | bytes 688132
  197.4 35.9 %collective-permute-start.19 = (bf16[4,128,256]{2,1,0:T(8,128)(2,1)S(1)}, bf16[4,128,256]{2,1,0:T(8,128)(2,1)S(1)}, u32[]{:S(2)}, u32[]{:S(2)}) collective-permute-start(bf16[4,128,256]{2,1,0:T(8,128)(2,1)S(1)} %get-tuple-element.30), channel_id=1, source_target_pairs={{0,3},{1,0},{2,1},{3,2},{4,7},{5,4},{6,5},{7,6},{8,11},{9,8},{10,9... | collective-permute-start | bytes 786440 | tf_op jit(solution)/shard_map/ppermute | solution.py:219
  213.1 25.7 %collective-permute-start.26 = (bf16[2,192,640]{2,1,0:T(8,128)(2,1)S(1)}, bf16[2,192,640]{2,1,0:T(8,128)(2,1)S(1)}, u32[]{:S(2)}, u32[]{:S(2)}) collective-permute-start(bf16[2,192,640]{2,1,0:T(8,128)(2,1)S(1)} %get-tuple-element.49), channel_id=1, source_target_pairs={{4,0},{8,4},{12,8},{16,12},{20,16},{24,20},{28,24},{5,1},{9,5},{13... | collective-permute-start | bytes 1474568 | tf_op jit(solution)/shard_map/ppermute | solution.py:239
  215.4 9.6 %copy-start.8 = (bf16[192,448]{1,0:T(8,128)(2,1)S(1)}, bf16[192,448]{1,0:T(8,128)(2,1)}, u32[]{:S(2)}) copy-start(bf16[192,448]{1,0:T(8,128)(2,1)} %constant.31.clone.refs_2_) | copy-start | bytes 516100
  215.4 23.4 %collective-permute-start.24 = (bf16[2,192,640]{2,1,0:T(8,128)(2,1)S(1)}, bf16[2,192,640]{2,1,0:T(8,128)(2,1)S(1)}, u32[]{:S(2)}, u32[]{:S(2)}) collective-permute-start(bf16[2,192,640]{2,1,0:T(8,128)(2,1)S(1)} %get-tuple-element.50), channel_id=1, source_target_pairs={{0,4},{4,8},{8,12},{12,16},{16,20},{20,24},{24,28},{1,5},{5,9},{9,... | collective-permute-start | bytes 1474568 | tf_op jit(solution)/shard_map/ppermute | solution.py:239
  217.6 25.1 %collective-permute-start.25 = (bf16[2,256,640]{2,1,0:T(8,128)(2,1)S(1)}, bf16[2,256,640]{2,1,0:T(8,128)(2,1)S(1)}, u32[]{:S(2)}, u32[]{:S(2)}) collective-permute-start(bf16[2,256,640]{2,1,0:T(8,128)(2,1)S(1)} %pad_maximum_fusion.2), channel_id=1, source_target_pairs={{0,4},{4,8},{8,12},{12,16},{16,20},{20,24},{24,28},{1,5},{5,9},{9,... | collective-permute-start | bytes 1966088 | tf_op jit(solution)/shard_map/ppermute | solution.py:239
  221.2 21.4 %collective-permute-start.27 = (bf16[2,256,640]{2,1,0:T(8,128)(2,1)S(1)}, bf16[2,256,640]{2,1,0:T(8,128)(2,1)S(1)}, u32[]{:S(2)}, u32[]{:S(2)}) collective-permute-start(bf16[2,256,640]{2,1,0:T(8,128)(2,1)S(1)} %pad_maximum_fusion.3), channel_id=1, source_target_pairs={{4,0},{8,4},{12,8},{16,12},{20,16},{24,20},{28,24},{5,1},{9,5},{13... | collective-permute-start | bytes 1966088 | tf_op jit(solution)/shard_map/ppermute | solution.py:239
  238.7 13.9 %copy-start.11 = (bf16[640,1280]{1,0:T(8,128)(2,1)S(1)}, bf16[640,1280]{1,0:T(8,128)(2,1)}, u32[]{:S(2)}) copy-start(bf16[640,1280]{1,0:T(8,128)(2,1)} %get-tuple-element.38.w_in) | copy-start | bytes 4915204
  238.7 13.9 %copy-start.12 = (bf16[1280,640]{1,0:T(8,128)(2,1)S(1)}, bf16[1280,640]{1,0:T(8,128)(2,1)}, u32[]{:S(2)}) copy-start(bf16[1280,640]{1,0:T(8,128)(2,1)} %get-tuple-element.36.w_out) | copy-start | bytes 4915204
